TPU v7x, 128 devices: a whole 4x4x4 slice. The times are simulated.
128 devices in a mesh: layer: 8 (over z, y_lo), blk: 16 (over x, y_hi, core).
Axes of the slice: x: 4, y: 4 (y_hi: 2, y_lo: 2; y = y_hi * 2 + y_lo), z: 4, core: 2. Of those that a mesh axis runs over, the one named last changes fastest.
Arguments:
- iterate: bfloat16 [8, 1536, 12288], P('layer', 'blk'), may hold values from -0.0546875 to 0.0546875
Outputs:
- update: bfloat16 [8, 1536, 12288], P(None, 'blk', 'layer')
All inputs are finite; a program needn't handle non-finite values.
Results may differ from a plain program's by a relative error of at most 0.0095.
Values may be sent and summed in bfloat16 or wider, within the bound.
No kernel may reach another device: no remote copies, remote signals or barrier semaphores. Data moves between devices by JAX's collectives and lax.ppermute only.
A program may use at most 128 MiB of HBM per device.

v0:
```python
import math

import jax
import jax.numpy as jnp
from jax import lax
from jax.sharding import PartitionSpec as P

coeff_a = 3.4445
coeff_b = -4.775
coeff_c = 2.0315


def shards(iterate):
    local_rows = iterate.shape[1]
    width = iterate.shape[2]
    all_rows = local_rows * lax.axis_size("blk")
    scale = math.sqrt(max(all_rows, width))
    pieces = lax.all_gather(iterate, "blk", axis=1, tiled=True)
    gathered = pieces
    gram_tile = jnp.einsum("lrc,lkc->lrk", iterate, pieces, preferred_element_type=jnp.float32)
    gram_block = gram_tile
    gathered, gram_block = (gathered, gram_block)
    gram_half = gram_block.astype(jnp.bfloat16)
    square = jnp.einsum(
        "lrk,lkm->lrm",
        gram_half,
        lax.all_gather(gram_half, "blk", axis=1, tiled=True),
        preferred_element_type=jnp.float32,
    )
    mixing = (coeff_b * gram_half.astype(jnp.float32) + coeff_c * square).astype(jnp.bfloat16)
    result = coeff_a * iterate.astype(jnp.float32) + jnp.einsum(
        "lrk,lkc->lrc", mixing, gathered, preferred_element_type=jnp.float32
    )
    scaled_rows = (scale * result).astype(jnp.bfloat16)
    return lax.all_to_all(scaled_rows, "layer", split_axis=2, concat_axis=0, tiled=True)


def solution(mesh):
    return jax.shard_map(
        shards,
        mesh=mesh,
        in_specs=(P("layer", "blk", None),),
        out_specs=P(None, "blk", "layer"),
        check_vma=False,
    )
```

profile of v0, /device:TPU:0, one launch (start us, length us, event | category | flops | bytes accessed | tf_op | source)
XLA Modules:
  0.0 465.5 jit_solution(16663097031767835544)
XLA Ops:
  6.5 0.0 all-gather.4.cloned.1.call-start
  6.5 0.7 all-gather.4.cloned.1.call-update
  7.3 0.0 copy-start
  7.3 0.0 all-gather.6.cloned.1.call-start
  7.3 211.9 %all-gather.4.cloned.1.call-done = bf16[1,1536,12288]{2,1,0:T(8,128)(2,1)} async-done(((bf16[1,96,12288]{2,1,0:T(8,128)(2,1)}), bf16[1,1536,12288]{2,1,0:T(8,128)(2,1)}) %all-gather.4.cloned.1.call-update) | async-done | bytes 37748752 | tf_op jit(solution)/shard_map/all_gather | solution.py:18
  219.2 18.5 %fusion.19 = bf16[96,1536]{1,0:T(8,128)(2,1)} fusion(bf16[1,1536,12288]{2,1,0:T(8,128)(2,1)} %all-gather.4.cloned.1.call-done, bf16[1,96,12288]{2,1,0:T(8,128)(2,1)} %param.1), kind=kOutput, calls=%fused_computation.13 | convolution fusion | flops 3624026112 | bytes 40402944 | tf_op jit(solution)/shard_map/lrc,lkc->lrk/dot_general | solution.py:20
  237.7 0.0 all-gather.6.cloned.1.call-update
  237.8 55.6 %all-gather.6.cloned.1.call-done = bf16[1536,1536]{1,0:T(8,128)(2,1)} async-done(((bf16[96,1536]{1,0:T(8,128)(2,1)}), bf16[1536,1536]{1,0:T(8,128)(2,1)}) %all-gather.6.cloned.1.call-update) | async-done | bytes 4718608 | tf_op jit(solution)/shard_map/all_gather | solution.py:27
  293.3 0.0 copy-done
  293.3 22.3 %fusion.13 = bf16[1,96,12288]{2,1,0:T(8,128)(2,1)} fusion(bf16[1,1536,12288]{2,1,0:T(8,128)(2,1)} %all-gather.4.cloned.1.call-done, bf16[1,96,12288]{2,1,0:T(8,128)(2,1)S(1)} %copy-done, bf16[96,1536]{1,0:T(8,128)(2,1)} %fusion.19, bf16[1536,1536]{1,0:T(8,128)(2,1)} %all-gather.6.cloned.1.call-done), kind=kOutput, calls=%fused_computation.7 | convolution fusion | flops 4083499008 | bytes 47480832 | tf_op jit(solution)/shard_map/lrk,lkc->lrc/dot_general | solution.py:31
  315.6 13.5 %copy.5 = bf16[1,96,12288]{1,0,2:T(2,128)(2,1)} copy(bf16[1,96,12288]{2,1,0:T(8,128)(2,1)} %fusion.13) | data formatting | bytes 4718592 | tf_op jit(solution)/shard_map/convert_element_type | solution.py:34
  329.1 0.5 broadcast.2
  329.7 67.2 %reduce = bf16[12288,96]{1,0:T(8,128)(2,1)S(1)} reduce(bf16[12288,1,96]{2,1,0:T(2,128)(2,1)} %bitcast.42, bf16[]{:T(256)} %broadcast.2), dimensions={1}, to_apply=%bitcast.37.reduce_sub_computation | reduce | bytes 4718594
  396.8 6.0 %reshape.28 = bf16[8,2,73728]{2,1,0:T(2,128)(2,1)} reshape(bf16[12288,96]{1,0:T(8,128)(2,1)S(1)} %reduce) | data formatting | bytes 4718592
  402.8 34.6 %all_to_all.18 = bf16[8,2,73728]{2,1,0:T(2,128)(2,1)S(1)} all-to-all(bf16[8,2,73728]{2,1,0:T(2,128)(2,1)} %reshape.28), channel_id=1, replica_groups=mesh['layer'=8,'blk'=16] {'layer'}, dimensions={0} | all-to-all | bytes 4718592 | tf_op jit(solution)/shard_map/all_to_all | solution.py:35
  437.4 6.1 %reshape.29 = bf16[12288,1,96]{2,1,0:T(2,128)(2,1)} reshape(bf16[8,2,73728]{2,1,0:T(2,128)(2,1)S(1)} %all_to_all.18) | data formatting | bytes 4718592
  443.5 12.1 %copy.6 = bf16[1,96,12288]{2,1,0:T(8,128)(2,1)S(1)} copy(bf16[1,96,12288]{1,0,2:T(2,128)(2,1)} %bitcast.43) | data formatting | bytes 4718592 | tf_op jit(solution)/shard_map/all_to_all | solution.py:35
  455.6 0.8 copy.8
  456.4 0.2 bitcast_bitcast_fusion
  456.5 2.1 copy.7
Async XLA Ops:
  6.5 212.7 %all-gather.4.cloned.1.call-start = ((), (), s32[]{:S(2)}) async-start(), calls=%async_computation.1 | async-start | bytes 40108032 | tf_op jit(solution)/shard_map/all_gather | solution.py:18
  7.3 286.1 %copy-start = (bf16[1,96,12288]{2,1,0:T(8,128)(2,1)S(1)}, bf16[1,96,12288]{2,1,0:T(8,128)(2,1)}, u32[]{:S(2)}) copy-start(bf16[1,96,12288]{2,1,0:T(8,128)(2,1)} %param.1) | copy-start | bytes 7077892
  7.3 286.1 %all-gather.6.cloned.1.call-start = ((), (), s32[]{:S(2)}) async-start(), calls=%async_computation.2 | async-start | bytes 5013504 | tf_op jit(solution)/shard_map/all_gather | solution.py:27
Sparse Core Ops, SparseCore 0:
  9.8 209.4 all-gather.3
  237.9 55.3 all-gather.5
where the time goes:
time: 466 us; the launch traced here: 465 us
  waiting for transfers between devices  268 us (58%)
  other arithmetic  67.2 us (14%)
  local copies, waits for them, and re-layouts  41.2 us (9%)
  matrix products  40.8 us (9%)
  blocking collectives  34.6 us (7%)
  between operations  13.4 us (3%)
    all_gather x1, waiting for transfers between devices, shards(): pieces = lax.all_gather(iterate, 'blk', axis=1, tiled=True)  212 us
    unnamed x1, other arithmetic  67.2 us
    all_gather x1, waiting for transfers between devices, shards(): lax.all_gather(gram_half, 'blk', axis=1, tiled=True)  55.6 us
    all_to_all x1, blocking collectives, shards(): lax.all_to_all(scaled_rows, 'layer', split_axis=2, concat_axis=0, tiled=T...  34.6 us
    dot_general x1, matrix products, shards(): jnp.einsum('lrk,lkc->lrc', mixing, gathered, preferred_element_type=jnp.f...  22.3 us
    dot_general x1, matrix products, shards(): jnp.einsum('lrc,lkc->lrk', iterate, pieces, preferred_element_type=jnp.fl...  18.5 us
    all_to_all x3, local copies, waits for them, and re-layouts, shards(): lax.all_to_all(scaled_rows, 'layer', split_axis=2, concat_axis=0, tiled=T...  14.3 us
    convert_element_type x1, local copies, waits for them, and re-layouts, shards(): scaled_rows = (scale * result).astype(jnp.bfloat16)  13.5 us
  transfers between devices with their start and end apart: 2, of which 2 were waited for; matrix products, arithmetic and copies ran while one was open for 0% of the time, Pallas kernels for 0%

commit v1 on v0

v1 whole, which is shorter than its diff:
```python
import math

import jax
import jax.numpy as jnp
from jax import lax
from jax.experimental import pallas as pl
from jax.experimental.pallas import tpu as pltpu
from jax.sharding import Mesh, PartitionSpec as P

coeff_a = 3.4445
coeff_b = -4.775
coeff_c = 2.0315

ROWS = 1536
COLS = 12288
LANES = 128
CHIPS = 8
STRIPES = 8
PANEL = ROWS // (2 * CHIPS)
HALF = ROWS // 2
WIDTH = COLS // CHIPS
TILES = COLS // STRIPES // LANES
MIB = 1 << 20

CHIP_AXES = ("x", "yh")
ALL_CHIPS = ("z", "yl", "x", "yh")


def halves(a, b, first):
    a, b = a.astype(jnp.float32), b.astype(jnp.float32)
    low = lax.broadcasted_iota(jnp.int32, a.shape, a.ndim - 1) < LANES // 2
    if first:
        return jnp.where(low, a, pltpu.roll(b, LANES // 2, a.ndim - 1))
    return jnp.where(low, pltpu.roll(a, LANES // 2, a.ndim - 1), b)


def tile(index):
    return pl.ds(index * LANES, LANES)


def split_kernel(x_ref, out_ref):
    for p in range(CHIPS):
        for j in range(STRIPES):
            out_ref[p, :, tile(j)] = x_ref[:, tile(TILES * j + p)]
        for m in range(STRIPES // 2):
            left = x_ref[:, tile(TILES * (2 * m) + CHIPS + p // 2)]
            right = x_ref[:, tile(TILES * (2 * m + 1) + CHIPS + p // 2)]
            out_ref[p, :, tile(STRIPES + m)] = halves(left, right, p % 2 == 0).astype(out_ref.dtype)


def split_columns(x):
    return pl.pallas_call(
        split_kernel,
        out_shape=jax.ShapeDtypeStruct((CHIPS, PANEL, WIDTH), x.dtype),
        compiler_params=pltpu.CompilerParams(vmem_limit_bytes=16 * MIB),
        name="split_columns",
    )(x)


def gram_kernel(own_ref, other_ref, out_ref):
    for side, ref in enumerate((own_ref, other_ref)):
        for n in range(0, HALF, 256):
            part = lax.dot_general(
                own_ref[...], ref[pl.ds(n, 256), :], (((1,), (1,)), ((), ())), preferred_element_type=jnp.float32
            )
            out_ref[:, pl.ds(side * HALF + n, 256)] = part.astype(out_ref.dtype)


def partial_gram(own, other):
    return pl.pallas_call(
        gram_kernel,
        out_shape=jax.ShapeDtypeStruct((HALF, ROWS), own.dtype),
        compiler_params=pltpu.CompilerParams(vmem_limit_bytes=24 * MIB),
        cost_estimate=pl.CostEstimate(
            flops=2 * HALF * ROWS * WIDTH, bytes_accessed=6 * HALF * ROWS, transcendentals=0
        ),
        name="partial_gram",
    )(own, other)


def update_kernel(gram_ref, gram_other_ref, x_ref, x_other_ref, out_ref, mixing_ref):
    scale = math.sqrt(max(ROWS, COLS))
    step = 256
    for n in range(0, ROWS, step):
        m = (n + HALF) % ROWS
        square = jnp.dot(gram_ref[:, pl.ds(0, HALF)], gram_ref[:, pl.ds(n, step)], preferred_element_type=jnp.float32)
        square += jnp.dot(
            gram_ref[:, pl.ds(HALF, HALF)], gram_other_ref[:, pl.ds(m, step)], preferred_element_type=jnp.float32
        )
        gram = gram_ref[:, pl.ds(n, step)].astype(jnp.float32)
        mixing_ref[:, pl.ds(n, step)] = (coeff_b * gram + coeff_c * square).astype(mixing_ref.dtype)
    for t in range(0, TILES, 2):
        columns = pl.ds(t * LANES, 2 * LANES)
        result = jnp.dot(mixing_ref[:, pl.ds(0, HALF)], x_ref[:, columns], preferred_element_type=jnp.float32)
        result += jnp.dot(mixing_ref[:, pl.ds(HALF, HALF)], x_other_ref[:, columns], preferred_element_type=jnp.float32)
        result = scale * (coeff_a * x_ref[:, columns].astype(jnp.float32) + result)
        for i in range(2):
            block = result[:, i * LANES : (i + 1) * LANES].reshape(CHIPS, PANEL, LANES)
            j = t + i
            if j < STRIPES:
                out_ref[j, :, pl.ds(0, PANEL), :] = block.astype(out_ref.dtype)
            else:
                top, bottom = block[:, : PANEL // 2], block[:, PANEL // 2 :]
                for side in range(2):
                    packed = halves(top, bottom, side == 0).astype(out_ref.dtype)
                    out_ref[2 * (j - STRIPES) + side, :, pl.ds(PANEL, PANEL // 2), :] = packed


def update_rows(gram, gram_other, x, x_other):
    return pl.pallas_call(
        update_kernel,
        out_shape=jax.ShapeDtypeStruct((STRIPES, CHIPS, PANEL + PANEL // 2, LANES), x.dtype),
        scratch_shapes=[pltpu.VMEM((HALF, ROWS), x.dtype)],
        compiler_params=pltpu.CompilerParams(vmem_limit_bytes=32 * MIB),
        cost_estimate=pl.CostEstimate(
            flops=4 * HALF * ROWS * ROWS, bytes_accessed=10 * HALF * ROWS, transcendentals=0
        ),
        name="update_rows",
    )(gram, gram_other, x, x_other)


def join_kernel(pieces_ref, out_ref):
    for p in range(CHIPS):
        out_ref[0, :, tile(p)] = pieces_ref[0, p, pl.ds(0, PANEL), :]
    for pair in range(CHIPS // 2):
        left = pieces_ref[0, 2 * pair, pl.ds(PANEL, PANEL // 2), :]
        right = pieces_ref[0, 2 * pair + 1, pl.ds(PANEL, PANEL // 2), :]
        for part in range(2):
            joined = halves(left, right, part == 0).astype(out_ref.dtype)
            out_ref[0, pl.ds(part * PANEL // 2, PANEL // 2), tile(CHIPS + pair)] = joined


def join_columns(pieces):
    layers = pieces.shape[0]
    return pl.pallas_call(
        join_kernel,
        grid=(layers,),
        in_specs=[pl.BlockSpec((1,) + pieces.shape[1:], lambda i: (i, 0, 0, 0))],
        out_specs=pl.BlockSpec((1, PANEL, TILES * LANES), lambda i: (i, 0, 0)),
        out_shape=jax.ShapeDtypeStruct((layers, PANEL, TILES * LANES), pieces.dtype),
        compiler_params=pltpu.CompilerParams(vmem_limit_bytes=16 * MIB),
        name="join_columns",
    )(pieces)


def swap_cores(value):
    return lax.ppermute(value, "c", [(0, 1), (1, 0)])


def shards(iterate):
    pieces = split_columns(iterate.reshape(PANEL, COLS))
    own = lax.all_to_all(pieces, CHIP_AXES, 0, 0, tiled=True).reshape(HALF, WIDTH)
    other = swap_cores(own)
    partial = partial_gram(own, other).reshape(CHIPS, PANEL, ROWS)
    partials = lax.all_to_all(partial, CHIP_AXES, 0, 0, tiled=True)
    gram = jnp.sum(partials.astype(jnp.float32), axis=0).astype(jnp.bfloat16)
    copies = jnp.broadcast_to(gram, (CHIPS, PANEL, ROWS))
    gram_own = lax.all_to_all(copies, CHIP_AXES, 0, 0, tiled=True).reshape(HALF, ROWS)
    gram_other = swap_cores(gram_own)
    sent = update_rows(gram_own, gram_other, own, other)
    sent = sent.reshape(STRIPES * CHIPS, PANEL + PANEL // 2, LANES)
    received = lax.all_to_all(sent, ALL_CHIPS, 0, 0, tiled=True)
    return join_columns(received.reshape(STRIPES, CHIPS, PANEL + PANEL // 2, LANES))


def solution(mesh):
    fine = Mesh(mesh.devices.reshape(4, 2, 4, 2, 2), ("z", "yl", "x", "yh", "c"))
    return jax.shard_map(
        shards,
        mesh=fine,
        in_specs=(P(("z", "yl"), ("x", "yh", "c"), None),),
        out_specs=P(None, ("x", "yh", "c"), ("z", "yl")),
        check_vma=False,
    )
```

time: 466 us -> 175 us (0.38)
  waiting for transfers between devices: 268 us -> 9.06 us
  blocking collectives: 34.6 us -> 146 us
  other arithmetic: 67.2 us -> 2.04 us
  matrix products: 40.8 us -> 0 us
  local copies, waits for them, and re-layouts: 41.2 us -> 1.87 us
  Pallas kernels: 0 us -> 15.5 us
  between operations: 13.4 us -> 0.05 us
    all_gather x2 -> x0, waiting for transfers between devices: 267 us -> none  [the longest x1 212 us: shards(): pieces = lax.all_gather(iterate, 'blk', axis=1, tiled=True)]
    all_to_all x1 -> x4, blocking collectives: 34.6 us -> 146 us  [the longest x1 40.7 us: shards(): received = lax.all_to_all(sent, ALL_CHIPS, 0, 0, tiled=True)]
    unnamed x1 -> x0, other arithmetic: 67.2 us -> none
    dot_general x2 -> x0, matrix products: 40.8 us -> none  [the longest x1 22.3 us: shards(): jnp.einsum('lrk,lkc->lrc', mixing, gathered, preferred_element_type=jnp.f...]
    pallas_call x0 -> x4, Pallas kernels: none -> 15.5 us  [the longest x1 7.77 us: update_rows(): pl.pallas_call(update_kernel, out_shape=jax.ShapeDtypeStruct((STRIPES, CH...]
    all_to_all x3 -> x0, local copies, waits for them, and re-layouts: 14.3 us -> none  [shards(): lax.all_to_all(scaled_rows, 'layer', split_axis=2, concat_axis=0, tiled=T...]
    convert_element_type x1 -> x0, local copies, waits for them, and re-layouts: 13.5 us -> none  [shards(): scaled_rows = (scale * result).astype(jnp.bfloat16)]
    unnamed x6, local copies, waits for them, and re-layouts: 13.4 us -> 1.67 us
where the time goes in v1:
time: 175 us
  blocking collectives  146 us (83%)
  Pallas kernels  15.5 us (9%)
  waiting for transfers between devices  9.06 us (5%)
  other arithmetic  2.04 us (1%)
  local copies, waits for them, and re-layouts  1.87 us (1%)
    all_to_all x1, blocking collectives, shards(): received = lax.all_to_all(sent, ALL_CHIPS, 0, 0, tiled=True)  40.7 us
    all_to_all x1, blocking collectives, shards(): lax.all_to_all(pieces, CHIP_AXES, 0, 0, tiled=True).reshape(HALF, WIDTH)  37.7 us
    all_to_all x1, blocking collectives, shards(): partials = lax.all_to_all(partial, CHIP_AXES, 0, 0, tiled=True)  34.7 us
    all_to_all x1, blocking collectives, shards(): lax.all_to_all(copies, CHIP_AXES, 0, 0, tiled=True).reshape(HALF, ROWS)  33.3 us
    ppermute x2, waiting for transfers between devices, swap_cores(): return lax.ppermute(value, 'c', [(0, 1), (1, 0)])  9.06 us
    pallas_call x1, Pallas kernels, update_rows(): pl.pallas_call(update_kernel, out_shape=jax.ShapeDtypeStruct((STRIPES, CH...  7.77 us
    pallas_call x1, Pallas kernels, partial_gram(): pl.pallas_call(gram_kernel, out_shape=jax.ShapeDtypeStruct((HALF, ROWS),...  3.84 us
  transfers between devices with their start and end apart: 2, of which 2 were waited for; matrix products, arithmetic and copies ran while one was open for 0% of the time, Pallas kernels for 0%

profile of v1, /device:TPU:0, one launch (start us, length us, event | category | flops | bytes accessed | tf_op | source)
XLA Modules:
  0.0 174.9 jit_solution(11005516036691753941)
XLA Ops:
  0.0 0.0 copy-start
  0.0 1.7 copy-done
  1.7 0.6 split_columns.1
  2.3 37.7 %all_to_all.20 = bf16[8,96,1536]{2,1,0:T(8,128)(2,1)S(1)} all-to-all(bf16[8,96,1536]{2,1,0:T(8,128)(2,1)S(1)} %split_columns.1), channel_id=1, replica_groups=mesh['z'=4,'yl'=2,'x'=4,'yh'=2,'c'=2] {'x','yh'}, dimensions={0} | all-to-all | bytes 4718592 | tf_op jit(solution)/shard_map/all_to_all | solution.py:152
  40.0 0.0 collective-permute-start
  40.0 4.5 %collective-permute-done.other_ref.x_other_ref = bf16[768,1536]{1,0:T(8,128)(2,1)S(1)} collective-permute-done((bf16[768,1536]{1,0:T(8,128)(2,1)S(1)}, bf16[768,1536]{1,0:T(8,128)(2,1)S(1)}, u32[]{:S(2)}, u32[]{:S(2)}) %collective-permute-start) | collective-permute-done | bytes 2359328 | tf_op jit(solution)/shard_map/ppermute | solution.py:147
  44.5 0.0 copy-start.1
  44.5 3.8 %partial_gram.1 = bf16[768,1536]{1,0:T(8,128)(2,1)S(1)} custom-call(bf16[768,1536]{1,0:T(8,128)(2,1)S(1)} %bitcast.9, bf16[768,1536]{1,0:T(8,128)(2,1)S(1)} %collective-permute-done.other_ref.x_other_ref), custom_call_target="tpu_custom_call" | custom-call | flops 3623878656 | bytes 7077888 | tf_op jit(solution)/shard_map/partial_gram/pallas_call | solution.py:70
  48.4 0.0 copy-done.1
  48.4 34.7 %all_to_all.21 = bf16[8,96,1536]{2,1,0:T(8,128)(2,1)} all-to-all(bf16[8,96,1536]{2,1,0:T(8,128)(2,1)S(1)} %bitcast.14), channel_id=1, replica_groups=mesh['z'=4,'yl'=2,'x'=4,'yh'=2,'c'=2] {'x','yh'}, dimensions={0} | all-to-all | bytes 4718592 | tf_op jit(solution)/shard_map/all_to_all | solution.py:155
  83.0 2.0 %reduce_sum.12 = bf16[96,1536]{1,0:T(8,128)(2,1)S(1)} reduce(bf16[8,96,1536]{2,1,0:T(8,128)(2,1)} %all_to_all.21, bf16[]{:T(256)} %constant.2.clone.1), dimensions={0}, to_apply=%region_0.0 | reduce | flops 1032192 | bytes 2654210 | tf_op jit(solution)/shard_map/reduce_sum | solution.py:156
  85.1 0.2 broadcast_in_dim.3
  85.3 0.0 copy-start.2
  85.3 33.3 %all_to_all.22 = bf16[8,96,1536]{2,1,0:T(8,128)(2,1)S(1)} all-to-all(bf16[8,96,1536]{2,1,0:T(8,128)(2,1)S(1)} %broadcast_in_dim.3), channel_id=1, replica_groups=mesh['z'=4,'yl'=2,'x'=4,'yh'=2,'c'=2] {'x','yh'}, dimensions={0} | all-to-all | bytes 4718592 | tf_op jit(solution)/shard_map/all_to_all | solution.py:158
  118.6 0.0 collective-permute-start.1
  118.6 4.5 %collective-permute-done.1.gram_other_ref = bf16[768,1536]{1,0:T(8,128)(2,1)S(1)} collective-permute-done((bf16[768,1536]{1,0:T(8,128)(2,1)S(1)}, bf16[768,1536]{1,0:T(8,128)(2,1)S(1)}, u32[]{:S(2)}, u32[]{:S(2)}) %collective-permute-start.1) | collective-permute-done | bytes 2359328 | tf_op jit(solution)/shard_map/ppermute | solution.py:147
  123.1 0.0 copy-done.2
  123.1 7.8 %update_rows.1 = bf16[8,8,144,128]{3,2,1,0:T(8,128)(2,1)S(1)} custom-call(bf16[768,1536]{1,0:T(8,128)(2,1)S(1)} %bitcast.12, bf16[768,1536]{1,0:T(8,128)(2,1)S(1)} %collective-permute-done.1.gram_other_ref, bf16[768,1536]{1,0:T(8,128)(2,1)S(1)} %bitcast.10, bf16[768,1536]{1,0:T(8,128)(2,1)S(1)} %copy-done.2), custom_call_target="tpu_custom_call" | custom-call | flops 7247757312 | bytes 11796480 | tf_op jit(solution)/shard_map/update_rows/pallas_call | solution.py:110
  130.9 40.7 %all_to_all.23 = bf16[64,144,128]{2,1,0:T(8,128)(2,1)S(1)} all-to-all(bf16[64,144,128]{2,1,0:T(8,128)(2,1)S(1)} %bitcast.13), channel_id=1, replica_groups=mesh['z'=4,'yl'=2,'x'=4,'yh'=2,'c'=2] {'z','yl','x','yh'}, dimensions={0} | all-to-all | bytes 4718592 | tf_op jit(solution)/shard_map/all_to_all | solution.py:162
  171.6 3.3 %join_columns.1 = bf16[8,96,1536]{2,1,0:T(8,128)(2,1)} custom-call(bf16[8,8,144,128]{3,2,1,0:T(8,128)(2,1)S(1)} %bitcast.6), custom_call_target="tpu_custom_call" | custom-call | tf_op jit(solution)/shard_map/join_columns/pallas_call | solution.py:135
Async XLA Ops:
  0.0 1.7 copy-start
  40.0 4.5 %collective-permute-start = (bf16[768,1536]{1,0:T(8,128)(2,1)S(1)}, bf16[768,1536]{1,0:T(8,128)(2,1)S(1)}, u32[]{:S(2)}, u32[]{:S(2)}) collective-permute-start(bf16[768,1536]{1,0:T(8,128)(2,1)S(1)} %bitcast.8), channel_id=1, source_target_pairs={{0,1},{1,0},{2,3},{3,2},{4,5},{5,4},{6,7},{7,6},{8,9},{9,8},{10,11... | collective-permute-start | bytes 7077896 | tf_op jit(solution)/shard_map/ppermute | solution.py:147
  44.5 3.8 %copy-start.1 = (bf16[768,1536]{1,0:T(8,128)(2,1)}, bf16[768,1536]{1,0:T(8,128)(2,1)S(1)}, u32[]{:S(2)}) copy-start(bf16[768,1536]{1,0:T(8,128)(2,1)S(1)} %collective-permute-done.other_ref.x_other_ref) | copy-start | bytes 7077892
  85.3 37.9 %copy-start.2 = (bf16[768,1536]{1,0:T(8,128)(2,1)S(1)}, bf16[768,1536]{1,0:T(8,128)(2,1)}, u32[]{:S(2)}) copy-start(bf16[768,1536]{1,0:T(8,128)(2,1)} %copy-done.1) | copy-start | bytes 7077892
  118.6 4.5 %collective-permute-start.1 = (bf16[768,1536]{1,0:T(8,128)(2,1)S(1)}, bf16[768,1536]{1,0:T(8,128)(2,1)S(1)}, u32[]{:S(2)}, u32[]{:S(2)}) collective-permute-start(bf16[768,1536]{1,0:T(8,128)(2,1)S(1)} %bitcast.11), channel_id=1, source_target_pairs={{0,1},{1,0},{2,3},{3,2},{4,5},{5,4},{6,7},{7,6},{8,9},{9,8},{10,11... | collective-permute-start | bytes 7077896 | tf_op jit(solution)/shard_map/ppermute | solution.py:147

commit v2 on v1

--- a/solution.py
+++ b/solution.py
@@ -20,6 +20,8 @@
 HALF = ROWS // 2
 WIDTH = COLS // CHIPS
 TILES = COLS // STRIPES // LANES
+BLOCKS = HALF // LANES
+PACKED = LANES * BLOCKS * (BLOCKS + 1)
 MIB = 1 << 20
 
 CHIP_AXES = ("x", "yh")
@@ -57,36 +59,89 @@
     )(x)
 
 
+def lower_start(j):
+    return LANES * (BLOCKS * j - j * (j - 1) // 2)
+
+
 def gram_kernel(own_ref, other_ref, out_ref):
     for side, ref in enumerate((own_ref, other_ref)):
-        for n in range(0, HALF, 256):
+        for j in range(0, BLOCKS, 2):
+            first = j * LANES
             part = lax.dot_general(
-                own_ref[...], ref[pl.ds(n, 256), :], (((1,), (1,)), ((), ())), preferred_element_type=jnp.float32
-            )
-            out_ref[:, pl.ds(side * HALF + n, 256)] = part.astype(out_ref.dtype)
+                own_ref[pl.ds(first, HALF - first), :],
+                ref[pl.ds(first, 2 * LANES), :],
+                (((1,), (1,)), ((), ())),
+                preferred_element_type=jnp.float32,
+            ).astype(out_ref.dtype)
+            for i in range(2):
+                start = side * PACKED // 2 + lower_start(j + i)
+                rows = HALF - first - i * LANES
+                out_ref[pl.ds(start, rows), :] = part[i * LANES :, i * LANES : (i + 1) * LANES]
 
 
 def partial_gram(own, other):
     return pl.pallas_call(
         gram_kernel,
-        out_shape=jax.ShapeDtypeStruct((HALF, ROWS), own.dtype),
+        out_shape=jax.ShapeDtypeStruct((PACKED, LANES), own.dtype),
         compiler_params=pltpu.CompilerParams(vmem_limit_bytes=24 * MIB),
         cost_estimate=pl.CostEstimate(
-            flops=2 * HALF * ROWS * WIDTH, bytes_accessed=6 * HALF * ROWS, transcendentals=0
+            flops=2 * PACKED * LANES * WIDTH, bytes_accessed=6 * HALF * ROWS, transcendentals=0
         ),
         name="partial_gram",
     )(own, other)
 
 
-def update_kernel(gram_ref, gram_other_ref, x_ref, x_other_ref, out_ref, mixing_ref):
+def sum_kernel(parts_ref, out_ref):
+    total = jnp.sum(parts_ref[...].astype(jnp.float32), axis=0).astype(out_ref.dtype)
+    for p in range(CHIPS):
+        out_ref[p] = total
+
+
+def sum_copies(parts):
+    return pl.pallas_call(
+        sum_kernel,
+        out_shape=jax.ShapeDtypeStruct(parts.shape, parts.dtype),
+        compiler_params=pltpu.CompilerParams(vmem_limit_bytes=16 * MIB),
+        name="sum_copies",
+    )(parts)
+
+
+def unpack(own_ref, other_ref, gram_ref, gram_other_ref):
+    half = PACKED // 2
+    for j in range(BLOCKS):
+        first = j * LANES
+        rows = HALF - first
+        start = lower_start(j)
+        columns = tile(j)
+        mine = own_ref[pl.ds(start, rows), :]
+        theirs = other_ref[pl.ds(start, rows), :]
+        gram_ref[pl.ds(first, rows), columns] = mine
+        gram_other_ref[pl.ds(first, rows), columns] = theirs
+        gram_ref[pl.ds(first, rows), tile(BLOCKS + j)] = own_ref[pl.ds(half + start, rows), :]
+        if j + 1 < BLOCKS:
+            below = rows - LANES
+            cross = other_ref[pl.ds(half + start + LANES, below), :]
+            gram_ref[pl.ds(first, LANES), pl.ds(first + LANES, below)] = mine[LANES:].T
+            gram_other_ref[pl.ds(first, LANES), pl.ds(first + LANES, below)] = theirs[LANES:].T
+            gram_ref[pl.ds(first, LANES), pl.ds(HALF + first + LANES, below)] = cross.T
+
+
+def update_kernel(own_ref, other_ref, x_ref, x_other_ref, out_ref, gram_ref, gram_other_ref, mixing_ref):
     scale = math.sqrt(max(ROWS, COLS))
     step = 256
+    unpack(own_ref, other_ref, gram_ref, gram_other_ref)
     for n in range(0, ROWS, step):
-        m = (n + HALF) % ROWS
-        square = jnp.dot(gram_ref[:, pl.ds(0, HALF)], gram_ref[:, pl.ds(n, step)], preferred_element_type=jnp.float32)
-        square += jnp.dot(
-            gram_ref[:, pl.ds(HALF, HALF)], gram_other_ref[:, pl.ds(m, step)], preferred_element_type=jnp.float32
-        )
+        left, right = gram_ref[:, pl.ds(0, HALF)], gram_ref[:, pl.ds(HALF, HALF)]
+        square = jnp.dot(left, gram_ref[:, pl.ds(n, step)], preferred_element_type=jnp.float32)
+        if n < HALF:
+            square += lax.dot_general(
+                right,
+                gram_ref[pl.ds(n, step), pl.ds(HALF, HALF)],
+                (((1,), (1,)), ((), ())),
+                preferred_element_type=jnp.float32,
+            )
+        else:
+            square += jnp.dot(right, gram_other_ref[:, pl.ds(n - HALF, step)], preferred_element_type=jnp.float32)
         gram = gram_ref[:, pl.ds(n, step)].astype(jnp.float32)
         mixing_ref[:, pl.ds(n, step)] = (coeff_b * gram + coeff_c * square).astype(mixing_ref.dtype)
     for t in range(0, TILES, 2):
@@ -106,17 +161,21 @@
                     out_ref[2 * (j - STRIPES) + side, :, pl.ds(PANEL, PANEL // 2), :] = packed
 
 
-def update_rows(gram, gram_other, x, x_other):
+def update_rows(own, other, x, x_other):
     return pl.pallas_call(
         update_kernel,
         out_shape=jax.ShapeDtypeStruct((STRIPES, CHIPS, PANEL + PANEL // 2, LANES), x.dtype),
-        scratch_shapes=[pltpu.VMEM((HALF, ROWS), x.dtype)],
+        scratch_shapes=[
+            pltpu.VMEM((HALF, ROWS), x.dtype),
+            pltpu.VMEM((HALF, HALF), x.dtype),
+            pltpu.VMEM((HALF, ROWS), x.dtype),
+        ],
         compiler_params=pltpu.CompilerParams(vmem_limit_bytes=32 * MIB),
         cost_estimate=pl.CostEstimate(
             flops=4 * HALF * ROWS * ROWS, bytes_accessed=10 * HALF * ROWS, transcendentals=0
         ),
         name="update_rows",
-    )(gram, gram_other, x, x_other)
+    )(own, other, x, x_other)
 
 
 def join_kernel(pieces_ref, out_ref):
@@ -151,11 +210,10 @@
     pieces = split_columns(iterate.reshape(PANEL, COLS))
     own = lax.all_to_all(pieces, CHIP_AXES, 0, 0, tiled=True).reshape(HALF, WIDTH)
     other = swap_cores(own)
-    partial = partial_gram(own, other).reshape(CHIPS, PANEL, ROWS)
+    partial = partial_gram(own, other).reshape(CHIPS, PACKED // CHIPS, LANES)
     partials = lax.all_to_all(partial, CHIP_AXES, 0, 0, tiled=True)
-    gram = jnp.sum(partials.astype(jnp.float32), axis=0).astype(jnp.bfloat16)
-    copies = jnp.broadcast_to(gram, (CHIPS, PANEL, ROWS))
-    gram_own = lax.all_to_all(copies, CHIP_AXES, 0, 0, tiled=True).reshape(HALF, ROWS)
+    copies = sum_copies(partials)
+    gram_own = lax.all_to_all(copies, CHIP_AXES, 0, 0, tiled=True).reshape(PACKED, LANES)
     gram_other = swap_cores(gram_own)
     sent = update_rows(gram_own, gram_other, own, other)
     sent = sent.reshape(STRIPES * CHIPS, PANEL + PANEL // 2, LANES)

time: 175 us -> 149 us (0.85)
  blocking collectives: 146 us -> 125 us
  other arithmetic: 2.04 us -> 0 us
    all_to_all x1, blocking collectives: 33.3 us -> 22.6 us  [shards(): lax.all_to_all(copies, CHIP_AXES, 0, 0, tiled=True).reshape(PACKED, LANES)]
    all_to_all x1, blocking collectives: 34.7 us -> 24.3 us  [shards(): partials = lax.all_to_all(partial, CHIP_AXES, 0, 0, tiled=True)]
    reduce_sum x1 -> x0, other arithmetic: 2.04 us -> none  [shards(): gram = jnp.sum(partials.astype(jnp.float32), axis=0).astype(jnp.bfloat16)]
    pallas_call x1 -> x2, Pallas kernels: 3.84 us -> 2.81 us  [the longest x1 2.63 us: partial_gram(): pl.pallas_call(gram_kernel, out_shape=jax.ShapeDtypeStruct((PACKED, LANES...]
where the time goes in v2:
time: 149 us
  blocking collectives  125 us (84%)
  Pallas kernels  14.7 us (10%)
  waiting for transfers between devices  7.66 us (5%)
  local copies, waits for them, and re-layouts  1.66 us (1%)
    all_to_all x1, blocking collectives, shards(): received = lax.all_to_all(sent, ALL_CHIPS, 0, 0, tiled=True)  40.3 us
    all_to_all x1, blocking collectives, shards(): lax.all_to_all(pieces, CHIP_AXES, 0, 0, tiled=True).reshape(HALF, WIDTH)  37.7 us
    all_to_all x1, blocking collectives, shards(): partials = lax.all_to_all(partial, CHIP_AXES, 0, 0, tiled=True)  24.3 us
    all_to_all x1, blocking collectives, shards(): lax.all_to_all(copies, CHIP_AXES, 0, 0, tiled=True).reshape(PACKED, LANES)  22.6 us
    pallas_call x1, Pallas kernels, update_rows(): pl.pallas_call(update_kernel, out_shape=jax.ShapeDtypeStruct((STRIPES, CH...  7.91 us
    ppermute x2, waiting for transfers between devices, swap_cores(): return lax.ppermute(value, 'c', [(0, 1), (1, 0)])  7.66 us
    pallas_call x1, Pallas kernels, join_columns(): pl.pallas_call(join_kernel, grid=(layers,), in_specs=[pl.BlockSpec((1,) +...  3.35 us
  transfers between devices with their start and end apart: 2, of which 2 were waited for; matrix products, arithmetic and copies ran while one was open for 0% of the time, Pallas kernels for 0%

profile of v2, /device:TPU:0, one launch (start us, length us, event | category | flops | bytes accessed | tf_op | source)
XLA Modules:
  0.0 148.8 jit_solution(4809635233262135466)
XLA Ops:
  0.0 0.0 copy-start
  0.0 1.7 %copy-done = bf16[1,96,12288]{2,1,0:T(8,128)(2,1)S(1)} copy-done((bf16[1,96,12288]{2,1,0:T(8,128)(2,1)S(1)}, bf16[1,96,12288]{2,1,0:T(8,128)(2,1)}, u32[]{:S(2)}) %copy-start) | copy-done | bytes 2359320
  1.7 0.6 split_columns.1
  2.3 37.7 %all_to_all.20 = bf16[8,96,1536]{2,1,0:T(8,128)(2,1)S(1)} all-to-all(bf16[8,96,1536]{2,1,0:T(8,128)(2,1)S(1)} %split_columns.1), channel_id=1, replica_groups=mesh['z'=4,'yl'=2,'x'=4,'yh'=2,'c'=2] {'x','yh'}, dimensions={0} | all-to-all | bytes 4718592 | tf_op jit(solution)/shard_map/all_to_all | solution.py:211
  40.0 0.0 collective-permute-start
  40.0 4.5 %collective-permute-done.other_ref.x_other_ref = bf16[768,1536]{1,0:T(8,128)(2,1)S(1)} collective-permute-done((bf16[768,1536]{1,0:T(8,128)(2,1)S(1)}, bf16[768,1536]{1,0:T(8,128)(2,1)S(1)}, u32[]{:S(2)}, u32[]{:S(2)}) %collective-permute-start) | collective-permute-done | bytes 2359328 | tf_op jit(solution)/shard_map/ppermute | solution.py:206
  44.5 2.6 %partial_gram.1 = bf16[5376,128]{1,0:T(8,128)(2,1)S(1)} custom-call(bf16[768,1536]{1,0:T(8,128)(2,1)S(1)} %bitcast.9, bf16[768,1536]{1,0:T(8,128)(2,1)S(1)} %collective-permute-done.other_ref.x_other_ref), custom_call_target="tpu_custom_call" | custom-call | flops 2113929216 | bytes 7077888 | tf_op jit(solution)/shard_map/partial_gram/pallas_call | solution.py:83
  47.1 24.3 %all_to_all.21.parts_ref = bf16[8,672,128]{2,1,0:T(8,128)(2,1)S(1)} all-to-all(bf16[8,672,128]{2,1,0:T(8,128)(2,1)S(1)} %bitcast.14), channel_id=1, replica_groups=mesh['z'=4,'yl'=2,'x'=4,'yh'=2,'c'=2] {'x','yh'}, dimensions={0} | all-to-all | bytes 2752512 | tf_op jit(solution)/shard_map/all_to_all | solution.py:214
  71.4 0.2 sum_copies.1
  71.6 22.6 %all_to_all.22 = bf16[8,672,128]{2,1,0:T(8,128)(2,1)S(1)} all-to-all(bf16[8,672,128]{2,1,0:T(8,128)(2,1)S(1)} %sum_copies.1), channel_id=1, replica_groups=mesh['z'=4,'yl'=2,'x'=4,'yh'=2,'c'=2] {'x','yh'}, dimensions={0} | all-to-all | bytes 2752512 | tf_op jit(solution)/shard_map/all_to_all | solution.py:216
  94.1 0.0 collective-permute-start.1
  94.1 3.1 %collective-permute-done.1.other_ref = bf16[5376,128]{1,0:T(8,128)(2,1)S(1)} collective-permute-done((bf16[5376,128]{1,0:T(8,128)(2,1)S(1)}, bf16[5376,128]{1,0:T(8,128)(2,1)S(1)}, u32[]{:S(2)}, u32[]{:S(2)}) %collective-permute-start.1) | collective-permute-done | bytes 1376288 | tf_op jit(solution)/shard_map/ppermute | solution.py:206
  97.3 7.9 %update_rows.1 = bf16[8,8,144,128]{3,2,1,0:T(8,128)(2,1)S(1)} custom-call(bf16[5376,128]{1,0:T(8,128)(2,1)S(1)} %bitcast.13, bf16[5376,128]{1,0:T(8,128)(2,1)S(1)} %collective-permute-done.1.other_ref, bf16[768,1536]{1,0:T(8,128)(2,1)S(1)} %bitcast.10, bf16[768,1536]{1,0:T(8,128)(2,1)S(1)} %collective-permute-done.other_ref.x_other_ref), custom_call_target="tpu_custom_call" | custom-call | flops 7247757312 | bytes 11796480 | tf_op jit(solution)/shard_map/update_rows/pallas_call | solution.py:165
  105.2 40.3 %all_to_all.23 = bf16[64,144,128]{2,1,0:T(8,128)(2,1)S(1)} all-to-all(bf16[64,144,128]{2,1,0:T(8,128)(2,1)S(1)} %bitcast.11), channel_id=1, replica_groups=mesh['z'=4,'yl'=2,'x'=4,'yh'=2,'c'=2] {'z','yl','x','yh'}, dimensions={0} | all-to-all | bytes 4718592 | tf_op jit(solution)/shard_map/all_to_all | solution.py:220
  145.5 3.3 %join_columns.1 = bf16[8,96,1536]{2,1,0:T(8,128)(2,1)} custom-call(bf16[8,8,144,128]{3,2,1,0:T(8,128)(2,1)S(1)} %bitcast.6), custom_call_target="tpu_custom_call" | custom-call | tf_op jit(solution)/shard_map/join_columns/pallas_call | solution.py:194
Async XLA Ops:
  0.0 1.7 %copy-start = (bf16[1,96,12288]{2,1,0:T(8,128)(2,1)S(1)}, bf16[1,96,12288]{2,1,0:T(8,128)(2,1)}, u32[]{:S(2)}) copy-start(bf16[1,96,12288]{2,1,0:T(8,128)(2,1)} %param.1) | copy-start | bytes 7077892
  40.0 4.5 %collective-permute-start = (bf16[768,1536]{1,0:T(8,128)(2,1)S(1)}, bf16[768,1536]{1,0:T(8,128)(2,1)S(1)}, u32[]{:S(2)}, u32[]{:S(2)}) collective-permute-start(bf16[768,1536]{1,0:T(8,128)(2,1)S(1)} %bitcast.8), channel_id=1, source_target_pairs={{0,1},{1,0},{2,3},{3,2},{4,5},{5,4},{6,7},{7,6},{8,9},{9,8},{10,11... | collective-permute-start | bytes 7077896 | tf_op jit(solution)/shard_map/ppermute | solution.py:206
  94.1 3.1 %collective-permute-start.1 = (bf16[5376,128]{1,0:T(8,128)(2,1)S(1)}, bf16[5376,128]{1,0:T(8,128)(2,1)S(1)}, u32[]{:S(2)}, u32[]{:S(2)}) collective-permute-start(bf16[5376,128]{1,0:T(8,128)(2,1)S(1)} %bitcast.12), channel_id=1, source_target_pairs={{0,1},{1,0},{2,3},{3,2},{4,5},{5,4},{6,7},{7,6},{8,9},{9,8},{10,11... | collective-permute-start | bytes 4128776 | tf_op jit(solution)/shard_map/ppermute | solution.py:206

commit v3 on v1

--- a/solution.py
+++ b/solution.py
@@ -2,6 +2,7 @@
 
 import jax
 import jax.numpy as jnp
+import numpy as np
 from jax import lax
 from jax.experimental import pallas as pl
 from jax.experimental.pallas import tpu as pltpu
@@ -20,10 +21,14 @@
 HALF = ROWS // 2
 WIDTH = COLS // CHIPS
 TILES = COLS // STRIPES // LANES
+BLOCKS = HALF // LANES
+STREAM = LANES * BLOCKS * (BLOCKS + 1) // 3
+PIECE = STREAM // CHIPS
 MIB = 1 << 20
 
 CHIP_AXES = ("x", "yh")
 ALL_CHIPS = ("z", "yl", "x", "yh")
+ORDERS = ("abd", "bda", "dab")
 
 
 def halves(a, b, first):
@@ -36,6 +41,15 @@
 
 def tile(index):
     return pl.ds(index * LANES, LANES)
+
+
+def positions():
+    table = []
+    for x in range(4):
+        for d in range(2):
+            bit = {"a": (x + 1) // 2 % 2, "b": x // 2, "d": d}
+            table.append([4 * bit[i] + 2 * bit[j] + bit[k] for i, j, k in ORDERS])
+    return np.array(table, np.int32)
 
 
 def split_kernel(x_ref, out_ref):
@@ -57,36 +71,148 @@
     )(x)
 
 
-def gram_kernel(own_ref, other_ref, out_ref):
-    for side, ref in enumerate((own_ref, other_ref)):
-        for n in range(0, HALF, 256):
-            part = lax.dot_general(
-                own_ref[...], ref[pl.ds(n, 256), :], (((1,), (1,)), ((), ())), preferred_element_type=jnp.float32
-            )
-            out_ref[:, pl.ds(side * HALF + n, 256)] = part.astype(out_ref.dtype)
-
-
-def partial_gram(own, other):
+STREAMS = (
+    ((0, 0), (0, 1), (0, 3)),
+    ((0, 2), (0, 4), (0, 5), (1, 2), (1, 4), (1, 5)),
+    ((1, 0), (1, 1), (1, 3)),
+)
+
+
+def strip_rows(j):
+    return HALF - j * LANES
+
+
+def strip_starts():
+    starts = {}
+    for s, strips in enumerate(STREAMS):
+        row = 0
+        for side, j in strips:
+            starts[side, j] = s, row
+            row += strip_rows(j)
+        assert row == STREAM
+    return starts
+
+
+def fill_strips(own_ref, ref, side, columns, whole_ref, lead):
+    first = columns[0] * LANES
+    part = lax.dot_general(
+        own_ref[pl.ds(first, HALF - first), :],
+        ref[pl.ds(first, LANES * len(columns)), :],
+        (((1,), (1,)), ((), ())),
+        preferred_element_type=jnp.float32,
+    )
+    for i, j in enumerate(columns):
+        s, start = strip_starts()[side, j]
+        whole_ref[s - lead, pl.ds(start, strip_rows(j)), :] = part[i * LANES :, i * LANES : (i + 1) * LANES]
+
+
+def place(whole_ref, stream, index, position):
+    piece = lax.bitwise_xor(position, index)
+    return whole_ref[stream, pl.ds(pl.multiple_of(piece * PIECE, 32), PIECE), :]
+
+
+def first_kernel(index_ref, own_ref, keep_ref, send_ref, whole_ref):
+    fill_strips(own_ref, own_ref, 0, (0, 1), whole_ref, 0)
+    fill_strips(own_ref, own_ref, 0, (3,), whole_ref, 0)
+    for k in range(CHIPS // 2):
+        keep_ref[k] = place(whole_ref, 0, index_ref[0], k)
+        send_ref[k] = place(whole_ref, 0, index_ref[0], k + CHIPS // 2).astype(send_ref.dtype)
+
+
+def rest_kernel(index_ref, own_ref, other_ref, keep_b_ref, send_b_ref, keep_c_ref, send_c_ref, whole_ref):
+    fill_strips(own_ref, own_ref, 0, (2,), whole_ref, 1)
+    fill_strips(own_ref, own_ref, 0, (4, 5), whole_ref, 1)
+    fill_strips(own_ref, other_ref, 1, (0, 1), whole_ref, 1)
+    fill_strips(own_ref, other_ref, 1, (2, 3), whole_ref, 1)
+    fill_strips(own_ref, other_ref, 1, (4, 5), whole_ref, 1)
+    for s, (keep_ref, send_ref) in enumerate(((keep_b_ref, send_b_ref), (keep_c_ref, send_c_ref))):
+        for k in range(CHIPS // 2):
+            keep_ref[k] = place(whole_ref, s, index_ref[s + 1], k)
+            send_ref[k] = place(whole_ref, s, index_ref[s + 1], k + CHIPS // 2).astype(send_ref.dtype)
+
+
+def partial_gram(kernel, name, streams, blocks, index, *panels):
+    half = (CHIPS // 2, PIECE, LANES)
     return pl.pallas_call(
-        gram_kernel,
-        out_shape=jax.ShapeDtypeStruct((HALF, ROWS), own.dtype),
-        compiler_params=pltpu.CompilerParams(vmem_limit_bytes=24 * MIB),
+        kernel,
+        in_specs=[pl.BlockSpec(memory_space=pltpu.SMEM)] + [pl.BlockSpec(memory_space=pltpu.VMEM)] * len(panels),
+        out_shape=[jax.ShapeDtypeStruct(half, t) for _ in range(streams) for t in (jnp.float32, panels[0].dtype)],
+        scratch_shapes=[pltpu.VMEM((streams, STREAM, LANES), jnp.float32)],
+        compiler_params=pltpu.CompilerParams(vmem_limit_bytes=12 * MIB),
         cost_estimate=pl.CostEstimate(
-            flops=2 * HALF * ROWS * WIDTH, bytes_accessed=6 * HALF * ROWS, transcendentals=0
+            flops=2 * blocks * LANES * LANES * WIDTH, bytes_accessed=6 * streams * STREAM * LANES, transcendentals=0
         ),
-        name="partial_gram",
-    )(own, other)
-
-
-def update_kernel(gram_ref, gram_other_ref, x_ref, x_other_ref, out_ref, mixing_ref):
+        name=name,
+    )(index, *panels)
+
+
+def flip(axis):
+    if axis == "d":
+        return "yh", [(0, 1), (1, 0)]
+    return "x", [(i, i ^ 1 if axis == "a" else 3 - i) for i in range(4)]
+
+
+def exchange(value, axis):
+    return lax.ppermute(value, *flip(axis))
+
+
+def wide(value):
+    return value.astype(jnp.float32)
+
+
+def sum_over_chips(keep, arrived, order):
+    kind = arrived.dtype
+    half = keep + wide(arrived)
+    quarter = half[:2] + wide(exchange(half[2:].astype(kind), order[1]))
+    quarter = quarter.astype(kind)
+    total = (wide(quarter) + wide(exchange(quarter, order[2]))[::-1]).astype(kind)
+    half = jnp.concatenate([total, exchange(total, order[1])])
+    return jnp.concatenate([half, exchange(half, order[0])])
+
+
+def unpack(index_ref, own_refs, other_refs, own_ref, other_ref, gram_ref, gram_other_ref):
+    for s in range(len(STREAMS)):
+        for k in range(CHIPS):
+            rows = pl.ds(pl.multiple_of(lax.bitwise_xor(k, index_ref[s]) * PIECE, 32), PIECE)
+            own_ref[s, rows, :] = own_refs[s][k]
+            other_ref[s, rows, :] = other_refs[s][k]
+    starts = strip_starts()
+    for j in range(BLOCKS):
+        first = j * LANES
+        rows = strip_rows(j)
+        s, start = starts[0, j]
+        t, cross_start = starts[1, j]
+        mine = own_ref[s, pl.ds(start, rows), :]
+        theirs = other_ref[s, pl.ds(start, rows), :]
+        gram_ref[pl.ds(first, rows), tile(j)] = mine
+        gram_other_ref[pl.ds(first, rows), tile(j)] = theirs
+        gram_ref[pl.ds(first, rows), tile(BLOCKS + j)] = own_ref[t, pl.ds(cross_start, rows), :]
+        if j + 1 < BLOCKS:
+            below = rows - LANES
+            cross = other_ref[t, pl.ds(cross_start + LANES, below), :]
+            gram_ref[pl.ds(first, LANES), pl.ds(first + LANES, below)] = mine[LANES:].T
+            gram_other_ref[pl.ds(first, LANES), pl.ds(first + LANES, below)] = theirs[LANES:].T
+            gram_ref[pl.ds(first, LANES), pl.ds(HALF + first + LANES, below)] = cross.T
+
+
+def update_kernel(index_ref, *refs):
+    own_refs, other_refs = refs[:3], refs[3:6]
+    x_ref, x_other_ref, out_ref, own_ref, other_ref, gram_ref, gram_other_ref, mixing_ref = refs[6:]
     scale = math.sqrt(max(ROWS, COLS))
     step = 256
+    unpack(index_ref, own_refs, other_refs, own_ref, other_ref, gram_ref, gram_other_ref)
     for n in range(0, ROWS, step):
-        m = (n + HALF) % ROWS
-        square = jnp.dot(gram_ref[:, pl.ds(0, HALF)], gram_ref[:, pl.ds(n, step)], preferred_element_type=jnp.float32)
-        square += jnp.dot(
-            gram_ref[:, pl.ds(HALF, HALF)], gram_other_ref[:, pl.ds(m, step)], preferred_element_type=jnp.float32
-        )
+        left, right = gram_ref[:, pl.ds(0, HALF)], gram_ref[:, pl.ds(HALF, HALF)]
+        square = jnp.dot(left, gram_ref[:, pl.ds(n, step)], preferred_element_type=jnp.float32)
+        if n < HALF:
+            square += lax.dot_general(
+                right,
+                gram_ref[pl.ds(n, step), pl.ds(HALF, HALF)],
+                (((1,), (1,)), ((), ())),
+                preferred_element_type=jnp.float32,
+            )
+        else:
+            square += jnp.dot(right, gram_other_ref[:, pl.ds(n - HALF, step)], preferred_element_type=jnp.float32)
         gram = gram_ref[:, pl.ds(n, step)].astype(jnp.float32)
         mixing_ref[:, pl.ds(n, step)] = (coeff_b * gram + coeff_c * square).astype(mixing_ref.dtype)
     for t in range(0, TILES, 2):
@@ -106,17 +232,25 @@
                     out_ref[2 * (j - STRIPES) + side, :, pl.ds(PANEL, PANEL // 2), :] = packed
 
 
-def update_rows(gram, gram_other, x, x_other):
+def update_rows(index, own, other, x, x_other):
+    operands = (*own, *other, x, x_other)
     return pl.pallas_call(
         update_kernel,
+        in_specs=[pl.BlockSpec(memory_space=pltpu.SMEM)] + [pl.BlockSpec(memory_space=pltpu.VMEM)] * len(operands),
         out_shape=jax.ShapeDtypeStruct((STRIPES, CHIPS, PANEL + PANEL // 2, LANES), x.dtype),
-        scratch_shapes=[pltpu.VMEM((HALF, ROWS), x.dtype)],
+        scratch_shapes=[
+            pltpu.VMEM((len(STREAMS), STREAM, LANES), x.dtype),
+            pltpu.VMEM((len(STREAMS), STREAM, LANES), x.dtype),
+            pltpu.VMEM((HALF, ROWS), x.dtype),
+            pltpu.VMEM((HALF, HALF), x.dtype),
+            pltpu.VMEM((HALF, ROWS), x.dtype),
+        ],
         compiler_params=pltpu.CompilerParams(vmem_limit_bytes=32 * MIB),
         cost_estimate=pl.CostEstimate(
             flops=4 * HALF * ROWS * ROWS, bytes_accessed=10 * HALF * ROWS, transcendentals=0
         ),
         name="update_rows",
-    )(gram, gram_other, x, x_other)
+    )(index, *operands)
 
 
 def join_kernel(pieces_ref, out_ref):
@@ -151,13 +285,14 @@
     pieces = split_columns(iterate.reshape(PANEL, COLS))
     own = lax.all_to_all(pieces, CHIP_AXES, 0, 0, tiled=True).reshape(HALF, WIDTH)
     other = swap_cores(own)
-    partial = partial_gram(own, other).reshape(CHIPS, PANEL, ROWS)
-    partials = lax.all_to_all(partial, CHIP_AXES, 0, 0, tiled=True)
-    gram = jnp.sum(partials.astype(jnp.float32), axis=0).astype(jnp.bfloat16)
-    copies = jnp.broadcast_to(gram, (CHIPS, PANEL, ROWS))
-    gram_own = lax.all_to_all(copies, CHIP_AXES, 0, 0, tiled=True).reshape(HALF, ROWS)
-    gram_other = swap_cores(gram_own)
-    sent = update_rows(gram_own, gram_other, own, other)
+    index = jnp.asarray(positions())[lax.axis_index(CHIP_AXES)]
+    keep_a, send_a = partial_gram(first_kernel, "gram_first", 1, 15, index, own)
+    arrived_a = exchange(send_a, ORDERS[0][0])
+    rest = partial_gram(rest_kernel, "gram_rest", 2, 33, index, own, other)
+    arrived_a, (keep_b, send_b, keep_c, send_c) = lax.optimization_barrier((arrived_a, rest))
+    arrived = arrived_a, exchange(send_b, ORDERS[1][0]), exchange(send_c, ORDERS[2][0])
+    grams = [sum_over_chips(*stream) for stream in zip((keep_a, keep_b, keep_c), arrived, ORDERS)]
+    sent = update_rows(index, grams, [swap_cores(gram) for gram in grams], own, other)
     sent = sent.reshape(STRIPES * CHIPS, PANEL + PANEL // 2, LANES)
     received = lax.all_to_all(sent, ALL_CHIPS, 0, 0, tiled=True)
     return join_columns(received.reshape(STRIPES, CHIPS, PANEL + PANEL // 2, LANES))

time: 175 us -> 152 us (0.87)
  blocking collectives: 146 us -> 79.6 us
  waiting for transfers between devices: 9.06 us -> 30.6 us
  starting transfers between devices: 0.01 us -> 19.1 us
  Pallas kernels: 15.5 us -> 19.2 us
    all_to_all x2 -> x0, blocking collectives: 68 us -> none  [the longest x1 34.7 us: shards(): partials = lax.all_to_all(partial, CHIP_AXES, 0, 0, tiled=True)]
    ppermute x0 -> x15, waiting for transfers between devices: none -> 27.1 us  [exchange(): return lax.ppermute(value, *flip(axis))]
    ppermute x0 -> x15, starting transfers between devices: none -> 18.6 us  [exchange(): return lax.ppermute(value, *flip(axis))]
    ppermute x2 -> x4, waiting for transfers between devices: 9.06 us -> 3.45 us  [swap_cores(): return lax.ppermute(value, 'c', [(0, 1), (1, 0)])]
    pallas_call x2 -> x3, Pallas kernels: 11.6 us -> 15.2 us  [the longest x1 9.75 us: update_rows(): pl.pallas_call(update_kernel, in_specs=[pl.BlockSpec(memory_space=pltpu.S...]
    reduce_sum x1 -> x0, other arithmetic: 2.04 us -> none  [shards(): gram = jnp.sum(partials.astype(jnp.float32), axis=0).astype(jnp.bfloat16)]
  transfers between devices with their start and end apart: 2 -> 19, of which waited for: 2 -> 13; matrix products, arithmetic and copies ran while one was open for 0% -> 1% of each run, Pallas kernels for 0% -> 4%
where the time goes in v3:
time: 152 us
  blocking collectives  79.6 us (52%)
  waiting for transfers between devices  30.6 us (20%)
  Pallas kernels  19.2 us (13%)
  starting transfers between devices  19.1 us (13%)
  local copies, waits for them, and re-layouts  2.41 us (2%)
    all_to_all x1, blocking collectives, shards(): received = lax.all_to_all(sent, ALL_CHIPS, 0, 0, tiled=True)  41.9 us
    all_to_all x1, blocking collectives, shards(): lax.all_to_all(pieces, CHIP_AXES, 0, 0, tiled=True).reshape(HALF, WIDTH)  37.7 us
    ppermute x15, waiting for transfers between devices, exchange(): return lax.ppermute(value, *flip(axis))  27.1 us
    ppermute x15, starting transfers between devices, exchange(): return lax.ppermute(value, *flip(axis))  18.6 us
    pallas_call x1, Pallas kernels, update_rows(): pl.pallas_call(update_kernel, in_specs=[pl.BlockSpec(memory_space=pltpu.S...  9.75 us
    pallas_call x2, Pallas kernels, partial_gram(): pl.pallas_call(kernel, in_specs=[pl.BlockSpec(memory_space=pltpu.SMEM)] +...  5.47 us
    ppermute x4, waiting for transfers between devices, swap_cores(): return lax.ppermute(value, 'c', [(0, 1), (1, 0)])  3.45 us
    pallas_call x1, Pallas kernels, join_columns(): pl.pallas_call(join_kernel, grid=(layers,), in_specs=[pl.BlockSpec((1,) +...  3.35 us
  transfers between devices with their start and end apart: 19, of which 13 were waited for; matrix products, arithmetic and copies ran while one was open for 1% of the time, Pallas kernels for 4%

profile of v3, /device:TPU:0, one launch (start us, length us, event | category | flops | bytes accessed | tf_op | source)
XLA Modules:
  0.0 151.6 jit_solution(16359192654212269248)
XLA Ops:
  0.0 1.7 %copy-done = bf16[1,96,12288]{2,1,0:T(8,128)(2,1)S(1)} copy-done((bf16[1,96,12288]{2,1,0:T(8,128)(2,1)S(1)}, bf16[1,96,12288]{2,1,0:T(8,128)(2,1)}, u32[]{:S(2)}) %copy-start) | copy-done | bytes 2359320
  1.7 0.6 split_columns.1
  2.3 37.7 %all_to_all.10 = bf16[8,96,1536]{2,1,0:T(8,128)(2,1)S(1)} all-to-all(bf16[8,96,1536]{2,1,0:T(8,128)(2,1)S(1)} %split_columns.1), channel_id=1, replica_groups=mesh['z'=4,'yl'=2,'x'=4,'yh'=2,'c'=2] {'x','yh'}, dimensions={0} | all-to-all | bytes 4718592 | tf_op jit(solution)/shard_map/all_to_all | solution.py:286
  40.0 0.0 collective-permute-start.1
  40.0 0.7 dynamic-slice_bitcast_fusion.index_ref
  40.7 1.7 %gram_first.1 = (f32[4,224,128]{2,1,0:T(8,128)S(1)}, bf16[4,224,128]{2,1,0:T(8,128)(2,1)S(1)}) custom-call(s32[3]{0:T(128)S(1)} %dynamic-slice_bitcast_fusion.index_ref, bf16[768,1536]{1,0:T(8,128)(2,1)S(1)} %bitcast.9), custom_call_target="tpu_custom_call" | custom-call | flops 754974720 | bytes 1376256 | tf_op jit(solution)/shard_map/gram_first/pallas_call | solution.py:136
  42.4 0.6 collective-permute-start
  43.0 1.7 %collective-permute-done.1.other_ref.refs_7_ = bf16[768,1536]{1,0:T(8,128)(2,1)} collective-permute-done((bf16[768,1536]{1,0:T(8,128)(2,1)S(1)}, bf16[768,1536]{1,0:T(8,128)(2,1)}, u32[]{:S(2)}, u32[]{:S(2)}) %collective-permute-start.1) | collective-permute-done | bytes 2359328 | tf_op jit(solution)/shard_map/ppermute | solution.py:281
  44.6 3.8 %gram_rest.1 = (f32[4,224,128]{2,1,0:T(8,128)S(1)}, bf16[4,224,128]{2,1,0:T(8,128)(2,1)S(1)}, f32[4,224,128]{2,1,0:T(8,128)S(1)}, bf16[4,224,128]{2,1,0:T(8,128)(2,1)S(1)}) custom-call(s32[3]{0:T(128)S(1)} %dynamic-slice_bitcast_fusion.index_ref, bf16[768,1536]{1,0:T(8,128)(2,1)S(1)} %bitcast.10, bf16[768,1536]{1,0:T(8,128)(2,1)} %collective-permute-done.1.other_ref.refs_7_), custom_call_target="tpu_custom_call" | custom-call | flops 1660944384 | bytes 2752512 | tf_op jit(solution)/shard_map/gram_rest/pallas_call | solution.py:136
  48.4 2.1 %collective-permute-done = bf16[4,224,128]{2,1,0:T(8,128)(2,1)S(1)} collective-permute-done((bf16[4,224,128]{2,1,0:T(8,128)(2,1)S(1)}, bf16[4,224,128]{2,1,0:T(8,128)(2,1)S(1)}, u32[]{:S(2)}, u32[]{:S(2)}) %collective-permute-start) | collective-permute-done | bytes 229408 | tf_op jit(solution)/shard_map/ppermute | solution.py:156
  50.5 1.5 collective-permute-start.2
  52.0 4.6 %collective-permute-done.2 = bf16[2,224,128]{2,1,0:T(8,128)(2,1)S(1)} collective-permute-done((bf16[2,224,128]{2,1,0:T(8,128)(2,1)S(1)}, bf16[2,224,128]{2,1,0:T(8,128)(2,1)S(1)}, u32[]{:S(2)}, u32[]{:S(2)}) %collective-permute-start.2) | collective-permute-done | bytes 114720 | tf_op jit(solution)/shard_map/ppermute | solution.py:156
  56.7 1.6 %collective-permute-start.3 = (bf16[2,224,128]{2,1,0:T(8,128)(2,1)S(1)}, bf16[2,224,128]{2,1,0:T(8,128)(2,1)S(1)}, u32[]{:S(2)}, u32[]{:S(2)}) collective-permute-start(bf16[2,224,128]{2,1,0:T(8,128)(2,1)S(1)} %fusion.2), channel_id=1, source_target_pairs={{0,2},{2,0},{1,3},{3,1},{4,6},{6,4},{5,7},{7,5},{8,10},{10,8},{9,1... | collective-permute-start | bytes 344072 | tf_op jit(solution)/shard_map/ppermute | solution.py:156
  58.3 1.1 collective-permute-start.6
  59.4 2.2 %collective-permute-start.11 = (bf16[4,224,128]{2,1,0:T(8,128)(2,1)S(1)}, bf16[4,224,128]{2,1,0:T(8,128)(2,1)S(1)}, u32[]{:S(2)}, u32[]{:S(2)}) collective-permute-start(bf16[4,224,128]{2,1,0:T(8,128)(2,1)S(1)} %get-tuple-element.26), channel_id=1, source_target_pairs={{0,2},{2,0},{1,3},{3,1},{4,6},{6,4},{5,7},{7,5},{8,10},{10,8},{9,1... | collective-permute-start | bytes 688136 | tf_op jit(solution)/shard_map/ppermute | solution.py:156
  61.7 2.6 %collective-permute-done.3 = bf16[2,224,128]{2,1,0:T(8,128)(2,1)S(1)} collective-permute-done((bf16[2,224,128]{2,1,0:T(8,128)(2,1)S(1)}, bf16[2,224,128]{2,1,0:T(8,128)(2,1)S(1)}, u32[]{:S(2)}, u32[]{:S(2)}) %collective-permute-start.3) | collective-permute-done | bytes 114720 | tf_op jit(solution)/shard_map/ppermute | solution.py:156
  64.3 1.1 collective-permute-start.4
  65.4 1.2 collective-permute-done.6
  66.6 0.1 convert_add_fusion.1
  66.7 2.2 %collective-permute-start.7 = (bf16[2,224,128]{2,1,0:T(8,128)(2,1)S(1)}, bf16[2,224,128]{2,1,0:T(8,128)(2,1)S(1)}, u32[]{:S(2)}, u32[]{:S(2)}) collective-permute-start(bf16[2,224,128]{2,1,0:T(8,128)(2,1)S(1)} %slice.46), channel_id=1, source_target_pairs={{0,2},{2,0},{1,3},{3,1},{4,6},{6,4},{5,7},{7,5},{8,10},{10,8},{9,1... | collective-permute-start | bytes 344072 | tf_op jit(solution)/shard_map/ppermute | solution.py:156
  68.9 0.0 collective-permute-done.11
  68.9 0.1 convert_add_fusion
  69.0 0.1 collective-permute-start.12
  69.1 1.3 collective-permute-done.4
  70.4 0.8 collective-permute-start.5
  71.2 2.7 %collective-permute-done.12 = bf16[2,224,128]{2,1,0:T(8,128)(2,1)S(1)} collective-permute-done((bf16[2,224,128]{2,1,0:T(8,128)(2,1)S(1)}, bf16[2,224,128]{2,1,0:T(8,128)(2,1)S(1)}, u32[]{:S(2)}, u32[]{:S(2)}) %collective-permute-start.12) | collective-permute-done | bytes 114720 | tf_op jit(solution)/shard_map/ppermute | solution.py:156
  73.9 1.5 collective-permute-start.13
  75.4 0.0 collective-permute-done.7
  75.4 0.1 collective-permute-start.8
  75.5 4.5 %collective-permute-done.13 = bf16[2,224,128]{2,1,0:T(8,128)(2,1)S(1)} collective-permute-done((bf16[2,224,128]{2,1,0:T(8,128)(2,1)S(1)}, bf16[2,224,128]{2,1,0:T(8,128)(2,1)S(1)}, u32[]{:S(2)}, u32[]{:S(2)}) %collective-permute-start.13) | collective-permute-done | bytes 114720 | tf_op jit(solution)/shard_map/ppermute | solution.py:156
  80.0 0.1 collective-permute-start.14
  80.1 0.2 collective-permute-done.8
  80.3 2.0 %collective-permute-start.9 = (bf16[2,224,128]{2,1,0:T(8,128)(2,1)S(1)}, bf16[2,224,128]{2,1,0:T(8,128)(2,1)S(1)}, u32[]{:S(2)}, u32[]{:S(2)}) collective-permute-start(bf16[2,224,128]{2,1,0:T(8,128)(2,1)S(1)} %add_convert_fusion.1), channel_id=1, source_target_pairs={{0,2},{2,0},{1,3},{3,1},{4,6},{6,4},{5,7},{7,5},{8,10},{10,8},{9,1... | collective-permute-start | bytes 344072 | tf_op jit(solution)/shard_map/ppermute | solution.py:156
  82.4 2.5 %collective-permute-done.14 = bf16[2,224,128]{2,1,0:T(8,128)(2,1)S(1)} collective-permute-done((bf16[2,224,128]{2,1,0:T(8,128)(2,1)S(1)}, bf16[2,224,128]{2,1,0:T(8,128)(2,1)S(1)}, u32[]{:S(2)}, u32[]{:S(2)}) %collective-permute-start.14) | collective-permute-done | bytes 114720 | tf_op jit(solution)/shard_map/ppermute | solution.py:156
  84.9 2.2 %collective-permute-start.15 = (bf16[4,224,128]{2,1,0:T(8,128)(2,1)S(1)}, bf16[4,224,128]{2,1,0:T(8,128)(2,1)S(1)}, u32[]{:S(2)}, u32[]{:S(2)}) collective-permute-start(bf16[4,224,128]{2,1,0:T(8,128)(2,1)S(1)} %pad_maximum_fusion.5), channel_id=1, source_target_pairs={{0,2},{2,0},{1,3},{3,1},{4,6},{6,4},{5,7},{7,5},{8,10},{10,8},{9,1... | collective-permute-start | bytes 688136 | tf_op jit(solution)/shard_map/ppermute | solution.py:156
  87.1 0.0 collective-permute-done.9
  87.1 1.5 %collective-permute-start.10 = (bf16[4,224,128]{2,1,0:T(8,128)(2,1)S(1)}, bf16[4,224,128]{2,1,0:T(8,128)(2,1)S(1)}, u32[]{:S(2)}, u32[]{:S(2)}) collective-permute-start(bf16[4,224,128]{2,1,0:T(8,128)(2,1)S(1)} %pad_maximum_fusion.4), channel_id=1, source_target_pairs={{0,12},{4,8},{8,4},{12,0},{1,13},{5,9},{9,5},{13,1},{2,14},{6,10},... | collective-permute-start | bytes 688136 | tf_op jit(solution)/shard_map/ppermute | solution.py:156
  88.7 0.0 collective-permute-done.5
  88.7 0.1 collective-permute-start.16
  88.8 3.7 %collective-permute-done.15 = bf16[4,224,128]{2,1,0:T(8,128)(2,1)S(1)} collective-permute-done((bf16[4,224,128]{2,1,0:T(8,128)(2,1)S(1)}, bf16[4,224,128]{2,1,0:T(8,128)(2,1)S(1)}, u32[]{:S(2)}, u32[]{:S(2)}) %collective-permute-start.15) | collective-permute-done | bytes 229408 | tf_op jit(solution)/shard_map/ppermute | solution.py:156
  92.6 0.1 collective-permute-start.18
  92.7 1.8 %collective-permute-done.10 = bf16[4,224,128]{2,1,0:T(8,128)(2,1)S(1)} collective-permute-done((bf16[4,224,128]{2,1,0:T(8,128)(2,1)S(1)}, bf16[4,224,128]{2,1,0:T(8,128)(2,1)S(1)}, u32[]{:S(2)}, u32[]{:S(2)}) %collective-permute-start.10) | collective-permute-done | bytes 229408 | tf_op jit(solution)/shard_map/ppermute | solution.py:156
  94.5 0.3 collective-permute-start.17
  94.8 0.0 collective-permute-done.16.refs_3_
  94.8 1.8 %collective-permute-done.17.refs_4_ = bf16[8,224,128]{2,1,0:T(8,128)(2,1)S(1)} collective-permute-done((bf16[8,224,128]{2,1,0:T(8,128)(2,1)S(1)}, bf16[8,224,128]{2,1,0:T(8,128)(2,1)S(1)}, u32[]{:S(2)}, u32[]{:S(2)}) %collective-permute-start.17) | collective-permute-done | bytes 458784 | tf_op jit(solution)/shard_map/ppermute | solution.py:281
  96.6 9.8 %update_rows.1 = bf16[8,8,144,128]{3,2,1,0:T(8,128)(2,1)S(1)} custom-call(s32[3]{0:T(128)S(1)} %dynamic-slice_bitcast_fusion.index_ref, bf16[8,224,128]{2,1,0:T(8,128)(2,1)S(1)} %pad_maximum_fusion.refs_0_, bf16[8,224,128]{2,1,0:T(8,128)(2,1)S(1)} %pad_maximum_fusion.1.refs_1_, bf16[8,224,128]{2,1,0:T(8,128)(2,1)S(1)} %pad_maximum_fusion.2.refs_2_, ...), custom_call_target="tpu_custom_call" | custom-call | flops 7247757312 | bytes 11796480 | tf_op jit(solution)/shard_map/update_rows/pallas_call | solution.py:237
  106.3 41.9 %all_to_all.11 = bf16[64,144,128]{2,1,0:T(8,128)(2,1)S(1)} all-to-all(bf16[64,144,128]{2,1,0:T(8,128)(2,1)S(1)} %bitcast.12), channel_id=1, replica_groups=mesh['z'=4,'yl'=2,'x'=4,'yh'=2,'c'=2] {'z','yl','x','yh'}, dimensions={0} | all-to-all | bytes 4718592 | tf_op jit(solution)/shard_map/all_to_all | solution.py:297
  148.2 3.3 %join_columns.1 = bf16[8,96,1536]{2,1,0:T(8,128)(2,1)} custom-call(bf16[8,8,144,128]{3,2,1,0:T(8,128)(2,1)S(1)} %bitcast.6), custom_call_target="tpu_custom_call" | custom-call | tf_op jit(solution)/shard_map/join_columns/pallas_call | solution.py:269
  (21 shorter events, 0.5 us)
Async XLA Ops:
  0.0 1.7 %copy-start = (bf16[1,96,12288]{2,1,0:T(8,128)(2,1)S(1)}, bf16[1,96,12288]{2,1,0:T(8,128)(2,1)}, u32[]{:S(2)}) copy-start(bf16[1,96,12288]{2,1,0:T(8,128)(2,1)} %param.2) | copy-start | bytes 7077892
  40.0 4.7 %collective-permute-start.1 = (bf16[768,1536]{1,0:T(8,128)(2,1)S(1)}, bf16[768,1536]{1,0:T(8,128)(2,1)}, u32[]{:S(2)}, u32[]{:S(2)}) collective-permute-start(bf16[768,1536]{1,0:T(8,128)(2,1)S(1)} %bitcast.8), channel_id=1, source_target_pairs={{0,1},{1,0},{2,3},{3,2},{4,5},{5,4},{6,7},{7,6},{8,9},{9,8},{10,11... | collective-permute-start | bytes 7077896 | tf_op jit(solution)/shard_map/ppermute | solution.py:281
  42.4 8.1 %collective-permute-start = (bf16[4,224,128]{2,1,0:T(8,128)(2,1)S(1)}, bf16[4,224,128]{2,1,0:T(8,128)(2,1)S(1)}, u32[]{:S(2)}, u32[]{:S(2)}) collective-permute-start(bf16[4,224,128]{2,1,0:T(8,128)(2,1)S(1)} %get-tuple-element.17), channel_id=1, source_target_pairs={{0,4},{4,0},{8,12},{12,8},{1,5},{5,1},{9,13},{13,9},{2,6},{6,2},{1... | collective-permute-start | bytes 688136 | tf_op jit(solution)/shard_map/ppermute | solution.py:156
  50.5 6.1 %collective-permute-start.2 = (bf16[2,224,128]{2,1,0:T(8,128)(2,1)S(1)}, bf16[2,224,128]{2,1,0:T(8,128)(2,1)S(1)}, u32[]{:S(2)}, u32[]{:S(2)}) collective-permute-start(bf16[2,224,128]{2,1,0:T(8,128)(2,1)S(1)} %slice.47), channel_id=1, source_target_pairs={{0,12},{4,8},{8,4},{12,0},{1,13},{5,9},{9,5},{13,1},{2,14},{6,10},... | collective-permute-start | bytes 344072 | tf_op jit(solution)/shard_map/ppermute | solution.py:156
  56.7 7.6 %collective-permute-start.3 = (bf16[2,224,128]{2,1,0:T(8,128)(2,1)S(1)}, bf16[2,224,128]{2,1,0:T(8,128)(2,1)S(1)}, u32[]{:S(2)}, u32[]{:S(2)}) collective-permute-start(bf16[2,224,128]{2,1,0:T(8,128)(2,1)S(1)} %fusion.2), channel_id=1, source_target_pairs={{0,2},{2,0},{1,3},{3,1},{4,6},{6,4},{5,7},{7,5},{8,10},{10,8},{9,1... | collective-permute-start | bytes 344072 | tf_op jit(solution)/shard_map/ppermute | solution.py:156
  58.3 8.3 %collective-permute-start.6 = (bf16[4,224,128]{2,1,0:T(8,128)(2,1)S(1)}, bf16[4,224,128]{2,1,0:T(8,128)(2,1)S(1)}, u32[]{:S(2)}, u32[]{:S(2)}) collective-permute-start(bf16[4,224,128]{2,1,0:T(8,128)(2,1)S(1)} %get-tuple-element.24), channel_id=1, source_target_pairs={{0,12},{4,8},{8,4},{12,0},{1,13},{5,9},{9,5},{13,1},{2,14},{6,10},... | collective-permute-start | bytes 688136 | tf_op jit(solution)/shard_map/ppermute | solution.py:156
  59.4 9.5 %collective-permute-start.11 = (bf16[4,224,128]{2,1,0:T(8,128)(2,1)S(1)}, bf16[4,224,128]{2,1,0:T(8,128)(2,1)S(1)}, u32[]{:S(2)}, u32[]{:S(2)}) collective-permute-start(bf16[4,224,128]{2,1,0:T(8,128)(2,1)S(1)} %get-tuple-element.26), channel_id=1, source_target_pairs={{0,2},{2,0},{1,3},{3,1},{4,6},{6,4},{5,7},{7,5},{8,10},{10,8},{9,1... | collective-permute-start | bytes 688136 | tf_op jit(solution)/shard_map/ppermute | solution.py:156
  64.3 6.1 %collective-permute-start.4 = (bf16[2,224,128]{2,1,0:T(8,128)(2,1)S(1)}, bf16[2,224,128]{2,1,0:T(8,128)(2,1)S(1)}, u32[]{:S(2)}, u32[]{:S(2)}) collective-permute-start(bf16[2,224,128]{2,1,0:T(8,128)(2,1)S(1)} %add_convert_fusion.2), channel_id=1, source_target_pairs={{0,12},{4,8},{8,4},{12,0},{1,13},{5,9},{9,5},{13,1},{2,14},{6,10},... | collective-permute-start | bytes 344072 | tf_op jit(solution)/shard_map/ppermute | solution.py:156
  66.7 8.7 %collective-permute-start.7 = (bf16[2,224,128]{2,1,0:T(8,128)(2,1)S(1)}, bf16[2,224,128]{2,1,0:T(8,128)(2,1)S(1)}, u32[]{:S(2)}, u32[]{:S(2)}) collective-permute-start(bf16[2,224,128]{2,1,0:T(8,128)(2,1)S(1)} %slice.46), channel_id=1, source_target_pairs={{0,2},{2,0},{1,3},{3,1},{4,6},{6,4},{5,7},{7,5},{8,10},{10,8},{9,1... | collective-permute-start | bytes 344072 | tf_op jit(solution)/shard_map/ppermute | solution.py:156
  69.0 4.9 %collective-permute-start.12 = (bf16[2,224,128]{2,1,0:T(8,128)(2,1)S(1)}, bf16[2,224,128]{2,1,0:T(8,128)(2,1)S(1)}, u32[]{:S(2)}, u32[]{:S(2)}) collective-permute-start(bf16[2,224,128]{2,1,0:T(8,128)(2,1)S(1)} %slice.45), channel_id=1, source_target_pairs={{0,4},{4,0},{8,12},{12,8},{1,5},{5,1},{9,13},{13,9},{2,6},{6,2},{1... | collective-permute-start | bytes 344072 | tf_op jit(solution)/shard_map/ppermute | solution.py:156
  70.4 18.2 %collective-permute-start.5 = (bf16[4,224,128]{2,1,0:T(8,128)(2,1)S(1)}, bf16[4,224,128]{2,1,0:T(8,128)(2,1)S(1)}, u32[]{:S(2)}, u32[]{:S(2)}) collective-permute-start(bf16[4,224,128]{2,1,0:T(8,128)(2,1)S(1)} %pad_maximum_fusion.3), channel_id=1, source_target_pairs={{0,4},{4,0},{8,12},{12,8},{1,5},{5,1},{9,13},{13,9},{2,6},{6,2},{1... | collective-permute-start | bytes 688136 | tf_op jit(solution)/shard_map/ppermute | solution.py:156
  73.9 6.1 %collective-permute-start.13 = (bf16[2,224,128]{2,1,0:T(8,128)(2,1)S(1)}, bf16[2,224,128]{2,1,0:T(8,128)(2,1)S(1)}, u32[]{:S(2)}, u32[]{:S(2)}) collective-permute-start(bf16[2,224,128]{2,1,0:T(8,128)(2,1)S(1)} %fusion), channel_id=1, source_target_pairs={{0,12},{4,8},{8,4},{12,0},{1,13},{5,9},{9,5},{13,1},{2,14},{6,10},... | collective-permute-start | bytes 344072 | tf_op jit(solution)/shard_map/ppermute | solution.py:156
  75.4 4.9 %collective-permute-start.8 = (bf16[2,224,128]{2,1,0:T(8,128)(2,1)S(1)}, bf16[2,224,128]{2,1,0:T(8,128)(2,1)S(1)}, u32[]{:S(2)}, u32[]{:S(2)}) collective-permute-start(bf16[2,224,128]{2,1,0:T(8,128)(2,1)S(1)} %fusion.1), channel_id=1, source_target_pairs={{0,4},{4,0},{8,12},{12,8},{1,5},{5,1},{9,13},{13,9},{2,6},{6,2},{1... | collective-permute-start | bytes 344072 | tf_op jit(solution)/shard_map/ppermute | solution.py:156
  80.0 4.9 %collective-permute-start.14 = (bf16[2,224,128]{2,1,0:T(8,128)(2,1)S(1)}, bf16[2,224,128]{2,1,0:T(8,128)(2,1)S(1)}, u32[]{:S(2)}, u32[]{:S(2)}) collective-permute-start(bf16[2,224,128]{2,1,0:T(8,128)(2,1)S(1)} %add_convert_fusion), channel_id=1, source_target_pairs={{0,4},{4,0},{8,12},{12,8},{1,5},{5,1},{9,13},{13,9},{2,6},{6,2},{1... | collective-permute-start | bytes 344072 | tf_op jit(solution)/shard_map/ppermute | solution.py:156
  80.3 6.8 %collective-permute-start.9 = (bf16[2,224,128]{2,1,0:T(8,128)(2,1)S(1)}, bf16[2,224,128]{2,1,0:T(8,128)(2,1)S(1)}, u32[]{:S(2)}, u32[]{:S(2)}) collective-permute-start(bf16[2,224,128]{2,1,0:T(8,128)(2,1)S(1)} %add_convert_fusion.1), channel_id=1, source_target_pairs={{0,2},{2,0},{1,3},{3,1},{4,6},{6,4},{5,7},{7,5},{8,10},{10,8},{9,1... | collective-permute-start | bytes 344072 | tf_op jit(solution)/shard_map/ppermute | solution.py:156
  84.9 7.6 %collective-permute-start.15 = (bf16[4,224,128]{2,1,0:T(8,128)(2,1)S(1)}, bf16[4,224,128]{2,1,0:T(8,128)(2,1)S(1)}, u32[]{:S(2)}, u32[]{:S(2)}) collective-permute-start(bf16[4,224,128]{2,1,0:T(8,128)(2,1)S(1)} %pad_maximum_fusion.5), channel_id=1, source_target_pairs={{0,2},{2,0},{1,3},{3,1},{4,6},{6,4},{5,7},{7,5},{8,10},{10,8},{9,1... | collective-permute-start | bytes 688136 | tf_op jit(solution)/shard_map/ppermute | solution.py:156
  87.1 7.3 %collective-permute-start.10 = (bf16[4,224,128]{2,1,0:T(8,128)(2,1)S(1)}, bf16[4,224,128]{2,1,0:T(8,128)(2,1)S(1)}, u32[]{:S(2)}, u32[]{:S(2)}) collective-permute-start(bf16[4,224,128]{2,1,0:T(8,128)(2,1)S(1)} %pad_maximum_fusion.4), channel_id=1, source_target_pairs={{0,12},{4,8},{8,4},{12,0},{1,13},{5,9},{9,5},{13,1},{2,14},{6,10},... | collective-permute-start | bytes 688136 | tf_op jit(solution)/shard_map/ppermute | solution.py:156
  88.7 6.1 %collective-permute-start.16 = (bf16[8,224,128]{2,1,0:T(8,128)(2,1)S(1)}, bf16[8,224,128]{2,1,0:T(8,128)(2,1)S(1)}, u32[]{:S(2)}, u32[]{:S(2)}) collective-permute-start(bf16[8,224,128]{2,1,0:T(8,128)(2,1)S(1)} %pad_maximum_fusion.refs_0_), channel_id=1, source_target_pairs={{0,1},{1,0},{2,3},{3,2},{4,5},{5,4},{6,7},{7,6},{8,9},{9,8},{10,11... | collective-permute-start | bytes 1376264 | tf_op jit(solution)/shard_map/ppermute | solution.py:281
  92.6 2.2 %collective-permute-start.18 = (bf16[8,224,128]{2,1,0:T(8,128)(2,1)S(1)}, bf16[8,224,128]{2,1,0:T(8,128)(2,1)S(1)}, u32[]{:S(2)}, u32[]{:S(2)}) collective-permute-start(bf16[8,224,128]{2,1,0:T(8,128)(2,1)S(1)} %pad_maximum_fusion.2.refs_2_), channel_id=1, source_target_pairs={{0,1},{1,0},{2,3},{3,2},{4,5},{5,4},{6,7},{7,6},{8,9},{9,8},{10,11... | collective-permute-start | bytes 1376264 | tf_op jit(solution)/shard_map/ppermute | solution.py:281
  94.5 2.1 %collective-permute-start.17 = (bf16[8,224,128]{2,1,0:T(8,128)(2,1)S(1)}, bf16[8,224,128]{2,1,0:T(8,128)(2,1)S(1)}, u32[]{:S(2)}, u32[]{:S(2)}) collective-permute-start(bf16[8,224,128]{2,1,0:T(8,128)(2,1)S(1)} %pad_maximum_fusion.1.refs_1_), channel_id=1, source_target_pairs={{0,1},{1,0},{2,3},{3,2},{4,5},{5,4},{6,7},{7,6},{8,9},{9,8},{10,11... | collective-permute-start | bytes 1376264 | tf_op jit(solution)/shard_map/ppermute | solution.py:281

commit v4 on v1

v4 whole, which is shorter than its diff:
```python
import math

import jax
import jax.numpy as jnp
from jax import lax
from jax.experimental import pallas as pl
from jax.experimental.pallas import tpu as pltpu
from jax.sharding import Mesh, PartitionSpec as P

coeff_a = 3.4445
coeff_b = -4.775
coeff_c = 2.0315

ROWS = 1536
COLS = 12288
LANES = 128
CHIPS = 8
STRIPES = 8
PANEL = ROWS // (2 * CHIPS)
HALF = ROWS // 2
WIDTH = COLS // CHIPS
TILES = COLS // STRIPES // LANES
BLOCKS = HALF // LANES
BELOW = LANES * BLOCKS * (BLOCKS - 1) // 2
EDGE = 2 * BELOW + HALF
PACKED = -(-(EDGE + BLOCKS) // (16 * CHIPS)) * 16 * CHIPS
MIB = 1 << 20

CHIP_AXES = ("x", "yh")
ALL_CHIPS = ("z", "yl", "x", "yh")


def halves(a, b, first):
    a, b = a.astype(jnp.float32), b.astype(jnp.float32)
    low = lax.broadcasted_iota(jnp.int32, a.shape, a.ndim - 1) < LANES // 2
    if first:
        return jnp.where(low, a, pltpu.roll(b, LANES // 2, a.ndim - 1))
    return jnp.where(low, pltpu.roll(a, LANES // 2, a.ndim - 1), b)


def tile(index):
    return pl.ds(index * LANES, LANES)


def split_kernel(x_ref, out_ref):
    for p in range(CHIPS):
        for j in range(STRIPES):
            out_ref[p, :, tile(j)] = x_ref[:, tile(TILES * j + p)]
        for m in range(STRIPES // 2):
            left = x_ref[:, tile(TILES * (2 * m) + CHIPS + p // 2)]
            right = x_ref[:, tile(TILES * (2 * m + 1) + CHIPS + p // 2)]
            out_ref[p, :, tile(STRIPES + m)] = halves(left, right, p % 2 == 0).astype(out_ref.dtype)


def split_columns(x):
    return pl.pallas_call(
        split_kernel,
        out_shape=jax.ShapeDtypeStruct((CHIPS, PANEL, WIDTH), x.dtype),
        compiler_params=pltpu.CompilerParams(vmem_limit_bytes=16 * MIB),
        name="split_columns",
    )(x)


def strip(j):
    below = (BLOCKS - 1 - j) * LANES
    start = LANES * sum(BLOCKS - 1 - i for i in range(j))
    return pl.ds(start, below)


def triangle(own_ref, ref, store_below, store_diagonal):
    for j in range(0, BLOCKS, 2):
        first = j * LANES
        part = lax.dot_general(
            own_ref[pl.ds(first, HALF - first), :],
            ref[pl.ds(first, 2 * LANES), :],
            (((1,), (1,)), ((), ())),
            preferred_element_type=jnp.float32,
        )
        for i in range(2):
            columns = part[i * LANES :, i * LANES : (i + 1) * LANES]
            store_diagonal(j + i, columns[:LANES])
            if j + i + 1 < BLOCKS:
                store_below(strip(j + i), columns[LANES:])


def iotas():
    return [lax.broadcasted_iota(jnp.int32, (LANES, LANES), axis) for axis in range(2)]


def own_gram_kernel(own_ref, below_ref, diagonal_ref):
    def store_below(rows, value):
        below_ref[rows, :] = value.astype(below_ref.dtype)

    def store_diagonal(j, value):
        diagonal_ref[j] = value

    triangle(own_ref, own_ref, store_below, store_diagonal)


def own_gram(own):
    return pl.pallas_call(
        own_gram_kernel,
        out_shape=(
            jax.ShapeDtypeStruct((BELOW, LANES), own.dtype),
            jax.ShapeDtypeStruct((BLOCKS, LANES, LANES), jnp.float32),
        ),
        compiler_params=pltpu.CompilerParams(vmem_limit_bytes=8 * MIB),
        cost_estimate=pl.CostEstimate(
            flops=2 * (BELOW + 3 * HALF) * LANES * WIDTH, bytes_accessed=2 * HALF * WIDTH, transcendentals=0
        ),
        name="own_gram",
    )(own)


def cross_gram_kernel(below_ref, diagonal_ref, own_ref, other_ref, out_ref):
    row, column = iotas()
    edges = []

    def store_below(rows, value):
        out_ref[pl.ds(BELOW + rows.start, rows.size), :] = value.astype(out_ref.dtype)

    def store_diagonal(j, value):
        block = jnp.where(row >= column, diagonal_ref[j], value)
        out_ref[pl.ds(2 * BELOW + j * LANES, LANES), :] = block.astype(out_ref.dtype)
        edges.append(jnp.sum(jnp.where(row == column, value, 0.0), axis=0, keepdims=True))

    out_ref[pl.ds(0, BELOW), :] = below_ref[...]
    triangle(own_ref, other_ref, store_below, store_diagonal)
    rest = PACKED - EDGE
    edges.append(jnp.zeros((rest - BLOCKS, LANES), jnp.float32))
    out_ref[pl.ds(EDGE, rest), :] = jnp.concatenate(edges).astype(out_ref.dtype)


def cross_gram(below, diagonal, own, other):
    return pl.pallas_call(
        cross_gram_kernel,
        out_shape=jax.ShapeDtypeStruct((PACKED, LANES), own.dtype),
        compiler_params=pltpu.CompilerParams(vmem_limit_bytes=12 * MIB),
        cost_estimate=pl.CostEstimate(
            flops=2 * (BELOW + 3 * HALF) * LANES * WIDTH, bytes_accessed=4 * HALF * WIDTH, transcendentals=0
        ),
        name="cross_gram",
    )(below, diagonal, own, other)


def sum_kernel(parts_ref, out_ref):
    total = jnp.sum(parts_ref[...].astype(jnp.float32), axis=0).astype(out_ref.dtype)
    for p in range(CHIPS):
        out_ref[p] = total


def sum_copies(parts):
    return pl.pallas_call(
        sum_kernel,
        out_shape=jax.ShapeDtypeStruct(parts.shape, parts.dtype),
        compiler_params=pltpu.CompilerParams(vmem_limit_bytes=16 * MIB),
        name="sum_copies",
    )(parts)


def mirror(packed_ref, out_ref, lower):
    for j in range(BLOCKS):
        first = j * LANES
        block = packed_ref[pl.ds(2 * BELOW + first, LANES), :]
        out_ref[pl.ds(first, LANES), tile(j)] = jnp.where(lower, block, block.T)
        if j + 1 < BLOCKS:
            below = packed_ref[strip(j), :]
            out_ref[pl.ds(first + LANES, below.shape[0]), tile(j)] = below
            out_ref[pl.ds(first, LANES), pl.ds(first + LANES, below.shape[0])] = below.T


def own_square_kernel(packed_ref, gram_ref, square_ref):
    row, column = iotas()
    mirror(packed_ref, gram_ref, row >= column)
    for n in range(0, HALF, 256):
        columns = pl.ds(n, 256)
        square_ref[:, columns] = jnp.dot(gram_ref[...], gram_ref[:, columns], preferred_element_type=jnp.float32)


def own_square(packed):
    return pl.pallas_call(
        own_square_kernel,
        out_shape=(
            jax.ShapeDtypeStruct((HALF, HALF), packed.dtype),
            jax.ShapeDtypeStruct((HALF, HALF), jnp.float32),
        ),
        compiler_params=pltpu.CompilerParams(vmem_limit_bytes=12 * MIB),
        cost_estimate=pl.CostEstimate(
            flops=2 * HALF * HALF * HALF, bytes_accessed=8 * HALF * HALF, transcendentals=0
        ),
        name="own_square",
    )(packed)


def unpack_cross(own_ref, other_ref, cross_ref):
    row, column = iotas()
    for j in range(BLOCKS):
        first = j * LANES
        upper, theirs = (ref[pl.ds(2 * BELOW + first, LANES), :] for ref in (own_ref, other_ref))
        edge = jnp.broadcast_to(own_ref[pl.ds(EDGE, 16), :].astype(jnp.float32)[j : j + 1], (LANES, LANES))
        block = jnp.where(row < column, upper.astype(jnp.float32), theirs.T.astype(jnp.float32))
        cross_ref[pl.ds(first, LANES), tile(j)] = jnp.where(row == column, edge, block).astype(cross_ref.dtype)
        if j + 1 < BLOCKS:
            rows = pl.ds(BELOW + strip(j).start, strip(j).size)
            cross_ref[pl.ds(first + LANES, rows.size), tile(j)] = own_ref[rows, :]
            cross_ref[pl.ds(first, LANES), pl.ds(first + LANES, rows.size)] = other_ref[rows, :].T


def update_kernel(
    own_ref, other_ref, gram_ref, square_ref, x_ref, x_other_ref, out_ref, cross_ref, gram_other_ref, mixing_ref
):
    scale = math.sqrt(max(ROWS, COLS))
    step = 256
    row, column = iotas()
    unpack_cross(own_ref, other_ref, cross_ref)
    mirror(other_ref, gram_other_ref, row >= column)
    for n in range(0, HALF, step):
        columns = pl.ds(n, step)
        square = square_ref[:, columns] + lax.dot_general(
            cross_ref[...], cross_ref[columns, :], (((1,), (1,)), ((), ())), preferred_element_type=jnp.float32
        )
        gram = gram_ref[:, columns].astype(jnp.float32)
        mixing_ref[:, columns] = (coeff_b * gram + coeff_c * square).astype(mixing_ref.dtype)
    for n in range(0, HALF, step):
        columns = pl.ds(n, step)
        square = jnp.dot(gram_ref[...], cross_ref[:, columns], preferred_element_type=jnp.float32)
        square += jnp.dot(cross_ref[...], gram_other_ref[:, columns], preferred_element_type=jnp.float32)
        gram = cross_ref[:, columns].astype(jnp.float32)
        mixing_ref[:, pl.ds(HALF + n, step)] = (coeff_b * gram + coeff_c * square).astype(mixing_ref.dtype)
    for t in range(0, TILES, 2):
        columns = pl.ds(t * LANES, 2 * LANES)
        result = jnp.dot(mixing_ref[:, pl.ds(0, HALF)], x_ref[:, columns], preferred_element_type=jnp.float32)
        result += jnp.dot(mixing_ref[:, pl.ds(HALF, HALF)], x_other_ref[:, columns], preferred_element_type=jnp.float32)
        result = scale * (coeff_a * x_ref[:, columns].astype(jnp.float32) + result)
        for i in range(2):
            block = result[:, i * LANES : (i + 1) * LANES].reshape(CHIPS, PANEL, LANES)
            j = t + i
            if j < STRIPES:
                out_ref[j, :, pl.ds(0, PANEL), :] = block.astype(out_ref.dtype)
            else:
                top, bottom = block[:, : PANEL // 2], block[:, PANEL // 2 :]
                for side in range(2):
                    packed = halves(top, bottom, side == 0).astype(out_ref.dtype)
                    out_ref[2 * (j - STRIPES) + side, :, pl.ds(PANEL, PANEL // 2), :] = packed


def update_rows(packed, packed_other, gram, square, x, x_other):
    return pl.pallas_call(
        update_kernel,
        out_shape=jax.ShapeDtypeStruct((STRIPES, CHIPS, PANEL + PANEL // 2, LANES), x.dtype),
        scratch_shapes=[
            pltpu.VMEM((HALF, HALF), x.dtype),
            pltpu.VMEM((HALF, HALF), x.dtype),
            pltpu.VMEM((HALF, ROWS), x.dtype),
        ],
        compiler_params=pltpu.CompilerParams(vmem_limit_bytes=24 * MIB),
        cost_estimate=pl.CostEstimate(
            flops=4 * HALF * ROWS * ROWS - 2 * HALF * HALF * HALF, bytes_accessed=10 * HALF * ROWS, transcendentals=0
        ),
        name="update_rows",
    )(packed, packed_other, gram, square, x, x_other)


def join_kernel(pieces_ref, out_ref, whole_ref, sems):
    copies = []
    for layer in range(STRIPES):
        for p in range(CHIPS):
            whole_ref[layer, :, tile(p)] = pieces_ref[layer, p, pl.ds(0, PANEL), :]
        for pair in range(CHIPS // 2):
            left = pieces_ref[layer, 2 * pair, pl.ds(PANEL, PANEL // 2), :]
            right = pieces_ref[layer, 2 * pair + 1, pl.ds(PANEL, PANEL // 2), :]
            for part in range(2):
                joined = halves(left, right, part == 0).astype(whole_ref.dtype)
                whole_ref[layer, pl.ds(part * PANEL // 2, PANEL // 2), tile(CHIPS + pair)] = joined
        copies.append(pltpu.make_async_copy(whole_ref.at[layer], out_ref.at[layer], sems.at[layer]))
        copies[-1].start()
    for copy in copies:
        copy.wait()


def join_columns(pieces):
    shape = (pieces.shape[0], PANEL, TILES * LANES)
    return pl.pallas_call(
        join_kernel,
        in_specs=[pl.BlockSpec(memory_space=pltpu.VMEM)],
        out_specs=pl.BlockSpec(memory_space=pl.ANY),
        out_shape=jax.ShapeDtypeStruct(shape, pieces.dtype),
        scratch_shapes=[pltpu.VMEM(shape, pieces.dtype), pltpu.SemaphoreType.DMA((pieces.shape[0],))],
        compiler_params=pltpu.CompilerParams(vmem_limit_bytes=12 * MIB),
        name="join_columns",
    )(pieces)


def swap_cores(value):
    return lax.ppermute(value, "c", [(0, 1), (1, 0)])


def shards(iterate):
    pieces = split_columns(iterate.reshape(PANEL, COLS))
    own = lax.all_to_all(pieces, CHIP_AXES, 0, 0, tiled=True).reshape(HALF, WIDTH)
    other = swap_cores(own)
    partial = cross_gram(*own_gram(own), own, other).reshape(CHIPS, PACKED // CHIPS, LANES)
    partials = lax.all_to_all(partial, CHIP_AXES, 0, 0, tiled=True)
    copies = sum_copies(partials)
    packed = lax.all_to_all(copies, CHIP_AXES, 0, 0, tiled=True).reshape(PACKED, LANES)
    packed_other = swap_cores(packed)
    sent = update_rows(packed, packed_other, *own_square(packed), own, other)
    sent = sent.reshape(STRIPES * CHIPS, PANEL + PANEL // 2, LANES)
    received = lax.all_to_all(sent, ALL_CHIPS, 0, 0, tiled=True)
    return join_columns(received.reshape(STRIPES, CHIPS, PANEL + PANEL // 2, LANES))


def solution(mesh):
    fine = Mesh(mesh.devices.reshape(4, 2, 4, 2, 2), ("z", "yl", "x", "yh", "c"))
    return jax.shard_map(
        shards,
        mesh=fine,
        in_specs=(P(("z", "yl"), ("x", "yh", "c"), None),),
        out_specs=P(None, ("x", "yh", "c"), ("z", "yl")),
        check_vma=False,
    )
```

time: 175 us -> 141 us (0.81)
  blocking collectives: 146 us -> 121 us
  waiting for transfers between devices: 9.06 us -> 4.81 us
  Pallas kernels: 15.5 us -> 13.4 us
  other arithmetic: 2.04 us -> 0 us
    all_to_all x1, blocking collectives: 33.3 us -> 20.6 us  [shards(): lax.all_to_all(copies, CHIP_AXES, 0, 0, tiled=True).reshape(PACKED, LANES)]
    all_to_all x1, blocking collectives: 34.7 us -> 22.2 us  [shards(): partials = lax.all_to_all(partial, CHIP_AXES, 0, 0, tiled=True)]
    ppermute x2, waiting for transfers between devices: 9.06 us -> 4.81 us  [swap_cores(): return lax.ppermute(value, 'c', [(0, 1), (1, 0)])]
    reduce_sum x1 -> x0, other arithmetic: 2.04 us -> none  [shards(): gram = jnp.sum(partials.astype(jnp.float32), axis=0).astype(jnp.bfloat16)]
    pallas_call x2 -> x5, Pallas kernels: 7.18 us -> 5.77 us  [the longest x1 1.58 us: join_columns(): pl.pallas_call(join_kernel, in_specs=[pl.BlockSpec(memory_space=pltpu.VME...]
  transfers between devices with their start and end apart: 2 -> 2, of which waited for: 2 -> 2; matrix products, arithmetic and copies ran while one was open for 0% -> 0% of each run, Pallas kernels for 0% -> 2%
where the time goes in v4:
time: 141 us
  blocking collectives  121 us (86%)
  Pallas kernels  13.4 us (10%)
  waiting for transfers between devices  4.81 us (3%)
  local copies, waits for them, and re-layouts  1.66 us (1%)
    all_to_all x1, blocking collectives, shards(): received = lax.all_to_all(sent, ALL_CHIPS, 0, 0, tiled=True)  40.5 us
    all_to_all x1, blocking collectives, shards(): lax.all_to_all(pieces, CHIP_AXES, 0, 0, tiled=True).reshape(HALF, WIDTH)  37.7 us
    all_to_all x1, blocking collectives, shards(): partials = lax.all_to_all(partial, CHIP_AXES, 0, 0, tiled=True)  22.2 us
    all_to_all x1, blocking collectives, shards(): lax.all_to_all(copies, CHIP_AXES, 0, 0, tiled=True).reshape(PACKED, LANES)  20.6 us
    pallas_call x1, Pallas kernels, update_rows(): pl.pallas_call(update_kernel, out_shape=jax.ShapeDtypeStruct((STRIPES, CH...  7.01 us
    ppermute x2, waiting for transfers between devices, swap_cores(): return lax.ppermute(value, 'c', [(0, 1), (1, 0)])  4.81 us
  transfers between devices with their start and end apart: 2, of which 2 were waited for; matrix products, arithmetic and copies ran while one was open for 0% of the time, Pallas kernels for 2%

profile of v4, /device:TPU:0, one launch (start us, length us, event | category | flops | bytes accessed | tf_op | source)
XLA Modules:
  0.0 141.0 jit_solution(7693729428686385006)
XLA Ops:
  0.0 0.0 copy-start
  0.0 1.7 %copy-done = bf16[1,96,12288]{2,1,0:T(8,128)(2,1)S(1)} copy-done((bf16[1,96,12288]{2,1,0:T(8,128)(2,1)S(1)}, bf16[1,96,12288]{2,1,0:T(8,128)(2,1)}, u32[]{:S(2)}) %copy-start) | copy-done | bytes 2359320
  1.7 0.6 split_columns.1
  2.3 37.7 %all_to_all.20 = bf16[8,96,1536]{2,1,0:T(8,128)(2,1)S(1)} all-to-all(bf16[8,96,1536]{2,1,0:T(8,128)(2,1)S(1)} %split_columns.1), channel_id=1, replica_groups=mesh['z'=4,'yl'=2,'x'=4,'yh'=2,'c'=2] {'x','yh'}, dimensions={0} | all-to-all | bytes 4718592 | tf_op jit(solution)/shard_map/all_to_all | solution.py:300
  40.0 0.0 collective-permute-start
  40.0 1.4 %own_gram.1 = (bf16[1920,128]{1,0:T(8,128)(2,1)S(1)}, f32[6,128,128]{2,1,0:T(8,128)S(1)}) custom-call(bf16[768,1536]{1,0:T(8,128)(2,1)S(1)} %bitcast.7), custom_call_target="tpu_custom_call" | custom-call | flops 1660944384 | bytes 2359296 | tf_op jit(solution)/shard_map/own_gram/pallas_call | solution.py:101
  41.4 3.1 %collective-permute-done.other_ref.x_other_ref = bf16[768,1536]{1,0:T(8,128)(2,1)S(1)} collective-permute-done((bf16[768,1536]{1,0:T(8,128)(2,1)S(1)}, bf16[768,1536]{1,0:T(8,128)(2,1)S(1)}, u32[]{:S(2)}, u32[]{:S(2)}) %collective-permute-start) | collective-permute-done | bytes 2359328 | tf_op jit(solution)/shard_map/ppermute | solution.py:295
  44.5 1.4 %cross_gram.1 = bf16[4736,128]{1,0:T(8,128)(2,1)S(1)} custom-call(bf16[1920,128]{1,0:T(8,128)(2,1)S(1)} %get-tuple-element.9.below_ref, f32[6,128,128]{2,1,0:T(8,128)S(1)} %get-tuple-element.10.diagonal_ref, bf16[768,1536]{1,0:T(8,128)(2,1)S(1)} %bitcast.8, bf16[768,1536]{1,0:T(8,128)(2,1)S(1)} %collective-permute-done.other_ref.x_other_ref), custom_call_target="tpu_custom_call" | custom-call | flops 1660944384 | bytes 4718592 | tf_op jit(solution)/shard_map/cross_gram/pallas_call | solution.py:135
  45.9 22.2 %all_to_all.21.parts_ref = bf16[8,592,128]{2,1,0:T(8,128)(2,1)S(1)} all-to-all(bf16[8,592,128]{2,1,0:T(8,128)(2,1)S(1)} %bitcast.11), channel_id=1, replica_groups=mesh['z'=4,'yl'=2,'x'=4,'yh'=2,'c'=2] {'x','yh'}, dimensions={0} | all-to-all | bytes 2424832 | tf_op jit(solution)/shard_map/all_to_all | solution.py:303
  68.2 0.2 sum_copies.1
  68.3 20.6 %all_to_all.22 = bf16[8,592,128]{2,1,0:T(8,128)(2,1)S(1)} all-to-all(bf16[8,592,128]{2,1,0:T(8,128)(2,1)S(1)} %sum_copies.1), channel_id=1, replica_groups=mesh['z'=4,'yl'=2,'x'=4,'yh'=2,'c'=2] {'x','yh'}, dimensions={0} | all-to-all | bytes 2424832 | tf_op jit(solution)/shard_map/all_to_all | solution.py:305
  89.0 0.0 collective-permute-start.1
  89.0 1.2 own_square.1
  90.2 1.7 %collective-permute-done.1.other_ref = bf16[4736,128]{1,0:T(8,128)(2,1)S(1)} collective-permute-done((bf16[4736,128]{1,0:T(8,128)(2,1)S(1)}, bf16[4736,128]{1,0:T(8,128)(2,1)S(1)}, u32[]{:S(2)}, u32[]{:S(2)}) %collective-permute-start.1) | collective-permute-done | bytes 1212448 | tf_op jit(solution)/shard_map/ppermute | solution.py:295
  91.9 7.0 %update_rows.1 = bf16[8,8,144,128]{3,2,1,0:T(8,128)(2,1)S(1)} custom-call(bf16[4736,128]{1,0:T(8,128)(2,1)S(1)} %bitcast.16, bf16[4736,128]{1,0:T(8,128)(2,1)S(1)} %collective-permute-done.1.other_ref, bf16[768,768]{1,0:T(8,128)(2,1)S(1)} %get-tuple-element.11.gram_ref, f32[768,768]{1,0:T(8,128)S(1)} %get-tuple-element.12.square_ref, ...), custom_call_target="tpu_custom_call" | custom-call | flops 6341787648 | bytes 11796480 | tf_op jit(solution)/shard_map/update_rows/pallas_call | solution.py:248
  98.9 40.5 %all_to_all.23 = bf16[64,144,128]{2,1,0:T(8,128)(2,1)S(1)} all-to-all(bf16[64,144,128]{2,1,0:T(8,128)(2,1)S(1)} %bitcast.13), channel_id=1, replica_groups=mesh['z'=4,'yl'=2,'x'=4,'yh'=2,'c'=2] {'z','yl','x','yh'}, dimensions={0} | all-to-all | bytes 4718592 | tf_op jit(solution)/shard_map/all_to_all | solution.py:309
  139.4 1.6 %join_columns.1 = bf16[8,96,1536]{2,1,0:T(8,128)(2,1)} custom-call(bf16[8,8,144,128]{3,2,1,0:T(8,128)(2,1)S(1)} %bitcast.10), custom_call_target="tpu_custom_call" | custom-call | tf_op jit(solution)/shard_map/join_columns/pallas_call | solution.py:283
Async XLA Ops:
  0.0 1.7 %copy-start = (bf16[1,96,12288]{2,1,0:T(8,128)(2,1)S(1)}, bf16[1,96,12288]{2,1,0:T(8,128)(2,1)}, u32[]{:S(2)}) copy-start(bf16[1,96,12288]{2,1,0:T(8,128)(2,1)} %param.1) | copy-start | bytes 7077892
  40.0 4.5 %collective-permute-start = (bf16[768,1536]{1,0:T(8,128)(2,1)S(1)}, bf16[768,1536]{1,0:T(8,128)(2,1)S(1)}, u32[]{:S(2)}, u32[]{:S(2)}) collective-permute-start(bf16[768,1536]{1,0:T(8,128)(2,1)S(1)} %bitcast.6), channel_id=1, source_target_pairs={{0,1},{1,0},{2,3},{3,2},{4,5},{5,4},{6,7},{7,6},{8,9},{9,8},{10,11... | collective-permute-start | bytes 7077896 | tf_op jit(solution)/shard_map/ppermute | solution.py:295
  89.0 2.9 %collective-permute-start.1 = (bf16[4736,128]{1,0:T(8,128)(2,1)S(1)}, bf16[4736,128]{1,0:T(8,128)(2,1)S(1)}, u32[]{:S(2)}, u32[]{:S(2)}) collective-permute-start(bf16[4736,128]{1,0:T(8,128)(2,1)S(1)} %bitcast.14), channel_id=1, source_target_pairs={{0,1},{1,0},{2,3},{3,2},{4,5},{5,4},{6,7},{7,6},{8,9},{9,8},{10,11... | collective-permute-start | bytes 3637256 | tf_op jit(solution)/shard_map/ppermute | solution.py:295

commit v5 on v4

--- a/solution.py
+++ b/solution.py
@@ -2,6 +2,7 @@
 
 import jax
 import jax.numpy as jnp
+import numpy as np
 from jax import lax
 from jax.experimental import pallas as pl
 from jax.experimental.pallas import tpu as pltpu
@@ -24,10 +25,13 @@
 BELOW = LANES * BLOCKS * (BLOCKS - 1) // 2
 EDGE = 2 * BELOW + HALF
 PACKED = -(-(EDGE + BLOCKS) // (16 * CHIPS)) * 16 * CHIPS
+PIECES = (BELOW // CHIPS,) + ((PACKED - BELOW) // (2 * CHIPS),) * 2
+BASES = (0, BELOW, BELOW + CHIPS * PIECES[1])
 MIB = 1 << 20
 
 CHIP_AXES = ("x", "yh")
 ALL_CHIPS = ("z", "yl", "x", "yh")
+ORDERS = ("abd", "bda", "dab")
 
 
 def halves(a, b, first):
@@ -40,6 +44,36 @@
 
 def tile(index):
     return pl.ds(index * LANES, LANES)
+
+
+def positions():
+    table = []
+    for x in range(4):
+        for d in range(2):
+            bit = {"a": (x + 1) // 2 % 2, "b": x // 2, "d": d}
+            table.append([4 * bit[i] + 2 * bit[j] + bit[k] for i, j, k in ORDERS])
+    return np.array(table, np.int32)
+
+
+def piece_rows(index_ref, stream, position, base=0):
+    piece = lax.bitwise_xor(index_ref[stream], position)
+    return pl.ds(base + pl.multiple_of(piece * PIECES[stream], 16), PIECES[stream])
+
+
+def split_pieces(index_ref, stream, whole_ref, base, keep_ref, send_ref):
+    half = CHIPS // 2
+    for k in range(half):
+        keep_ref[k] = whole_ref[piece_rows(index_ref, stream, k, base), :]
+        send_ref[k] = whole_ref[piece_rows(index_ref, stream, k + half, base), :].astype(send_ref.dtype)
+
+
+def half_shapes(stream, kind):
+    shape = (CHIPS // 2, PIECES[stream], LANES)
+    return [jax.ShapeDtypeStruct(shape, jnp.float32), jax.ShapeDtypeStruct(shape, kind)]
+
+
+def specs(vmem):
+    return [pl.BlockSpec(memory_space=pltpu.SMEM)] + [pl.BlockSpec(memory_space=pltpu.VMEM)] * vmem
 
 
 def split_kernel(x_ref, out_ref):
@@ -87,75 +121,92 @@
     return [lax.broadcasted_iota(jnp.int32, (LANES, LANES), axis) for axis in range(2)]
 
 
-def own_gram_kernel(own_ref, below_ref, diagonal_ref):
+def own_gram_kernel(index_ref, own_ref, keep_ref, send_ref, diagonal_ref, whole_ref):
     def store_below(rows, value):
-        below_ref[rows, :] = value.astype(below_ref.dtype)
+        whole_ref[rows, :] = value
 
     def store_diagonal(j, value):
         diagonal_ref[j] = value
 
     triangle(own_ref, own_ref, store_below, store_diagonal)
-
-
-def own_gram(own):
+    split_pieces(index_ref, 0, whole_ref, 0, keep_ref, send_ref)
+
+
+def own_gram(index, own):
     return pl.pallas_call(
         own_gram_kernel,
-        out_shape=(
-            jax.ShapeDtypeStruct((BELOW, LANES), own.dtype),
-            jax.ShapeDtypeStruct((BLOCKS, LANES, LANES), jnp.float32),
-        ),
+        in_specs=specs(1),
+        out_shape=half_shapes(0, own.dtype) + [jax.ShapeDtypeStruct((BLOCKS, LANES, LANES), jnp.float32)],
+        scratch_shapes=[pltpu.VMEM((BELOW, LANES), jnp.float32)],
         compiler_params=pltpu.CompilerParams(vmem_limit_bytes=8 * MIB),
         cost_estimate=pl.CostEstimate(
             flops=2 * (BELOW + 3 * HALF) * LANES * WIDTH, bytes_accessed=2 * HALF * WIDTH, transcendentals=0
         ),
         name="own_gram",
-    )(own)
-
-
-def cross_gram_kernel(below_ref, diagonal_ref, own_ref, other_ref, out_ref):
+    )(index, own)
+
+
+def cross_gram_kernel(
+    index_ref, diagonal_ref, own_ref, other_ref, keep_b_ref, send_b_ref, keep_c_ref, send_c_ref, whole_ref
+):
     row, column = iotas()
     edges = []
 
     def store_below(rows, value):
-        out_ref[pl.ds(BELOW + rows.start, rows.size), :] = value.astype(out_ref.dtype)
+        whole_ref[rows, :] = value
 
     def store_diagonal(j, value):
-        block = jnp.where(row >= column, diagonal_ref[j], value)
-        out_ref[pl.ds(2 * BELOW + j * LANES, LANES), :] = block.astype(out_ref.dtype)
+        whole_ref[pl.ds(BELOW + j * LANES, LANES), :] = jnp.where(row >= column, diagonal_ref[j], value)
         edges.append(jnp.sum(jnp.where(row == column, value, 0.0), axis=0, keepdims=True))
 
-    out_ref[pl.ds(0, BELOW), :] = below_ref[...]
     triangle(own_ref, other_ref, store_below, store_diagonal)
     rest = PACKED - EDGE
     edges.append(jnp.zeros((rest - BLOCKS, LANES), jnp.float32))
-    out_ref[pl.ds(EDGE, rest), :] = jnp.concatenate(edges).astype(out_ref.dtype)
-
-
-def cross_gram(below, diagonal, own, other):
+    whole_ref[pl.ds(EDGE - BELOW, rest), :] = jnp.concatenate(edges)
+    split_pieces(index_ref, 1, whole_ref, BASES[1] - BELOW, keep_b_ref, send_b_ref)
+    split_pieces(index_ref, 2, whole_ref, BASES[2] - BELOW, keep_c_ref, send_c_ref)
+
+
+def cross_gram(index, diagonal, own, other):
     return pl.pallas_call(
         cross_gram_kernel,
-        out_shape=jax.ShapeDtypeStruct((PACKED, LANES), own.dtype),
+        in_specs=specs(3),
+        out_shape=half_shapes(1, own.dtype) + half_shapes(2, own.dtype),
+        scratch_shapes=[pltpu.VMEM((PACKED - BELOW, LANES), jnp.float32)],
         compiler_params=pltpu.CompilerParams(vmem_limit_bytes=12 * MIB),
         cost_estimate=pl.CostEstimate(
             flops=2 * (BELOW + 3 * HALF) * LANES * WIDTH, bytes_accessed=4 * HALF * WIDTH, transcendentals=0
         ),
         name="cross_gram",
-    )(below, diagonal, own, other)
-
-
-def sum_kernel(parts_ref, out_ref):
-    total = jnp.sum(parts_ref[...].astype(jnp.float32), axis=0).astype(out_ref.dtype)
-    for p in range(CHIPS):
-        out_ref[p] = total
-
-
-def sum_copies(parts):
-    return pl.pallas_call(
-        sum_kernel,
-        out_shape=jax.ShapeDtypeStruct(parts.shape, parts.dtype),
-        compiler_params=pltpu.CompilerParams(vmem_limit_bytes=16 * MIB),
-        name="sum_copies",
-    )(parts)
+    )(index, diagonal, own, other)
+
+
+def exchange(value, axis):
+    if axis == "d":
+        return lax.ppermute(value, "yh", [(0, 1), (1, 0)])
+    return lax.ppermute(value, "x", [(i, i ^ 1 if axis == "a" else 3 - i) for i in range(4)])
+
+
+def wide(value):
+    return value.astype(jnp.float32)
+
+
+def sum_over_chips(keep, arrived, order):
+    kind = arrived.dtype
+    half = keep + wide(arrived)
+    quarter = half[:2] + wide(exchange(half[2:].astype(kind), order[1]))
+    quarter = quarter.astype(kind)
+    total = (wide(quarter) + wide(exchange(quarter, order[2]))[::-1]).astype(kind)
+    half = jnp.concatenate([total, exchange(total, order[1])])
+    return jnp.concatenate([half, exchange(half, order[0])])
+
+
+def unpermute(index_ref, pieces_ref, packed_ref):
+    first = 0
+    for s, rows in enumerate(PIECES):
+        for k in range(CHIPS):
+            packed_ref[piece_rows(index_ref, s, k, BASES[s]), :] = pieces_ref[k, pl.ds(first, rows), :]
+        first += rows
 
 
 def mirror(packed_ref, out_ref, lower):
@@ -169,19 +220,22 @@
             out_ref[pl.ds(first, LANES), pl.ds(first + LANES, below.shape[0])] = below.T
 
 
-def own_square_kernel(packed_ref, gram_ref, square_ref):
+def own_square_kernel(index_ref, pieces_ref, packed_ref, gram_ref, square_ref):
     row, column = iotas()
+    unpermute(index_ref, pieces_ref, packed_ref)
     mirror(packed_ref, gram_ref, row >= column)
     for n in range(0, HALF, 256):
         columns = pl.ds(n, 256)
         square_ref[:, columns] = jnp.dot(gram_ref[...], gram_ref[:, columns], preferred_element_type=jnp.float32)
 
 
-def own_square(packed):
+def own_square(index, pieces):
     return pl.pallas_call(
         own_square_kernel,
+        in_specs=specs(1),
         out_shape=(
-            jax.ShapeDtypeStruct((HALF, HALF), packed.dtype),
+            jax.ShapeDtypeStruct((PACKED, LANES), pieces.dtype),
+            jax.ShapeDtypeStruct((HALF, HALF), pieces.dtype),
             jax.ShapeDtypeStruct((HALF, HALF), jnp.float32),
         ),
         compiler_params=pltpu.CompilerParams(vmem_limit_bytes=12 * MIB),
@@ -189,7 +243,7 @@
             flops=2 * HALF * HALF * HALF, bytes_accessed=8 * HALF * HALF, transcendentals=0
         ),
         name="own_square",
-    )(packed)
+    )(index, pieces)
 
 
 def unpack_cross(own_ref, other_ref, cross_ref):
@@ -207,11 +261,13 @@
 
 
 def update_kernel(
-    own_ref, other_ref, gram_ref, square_ref, x_ref, x_other_ref, out_ref, cross_ref, gram_other_ref, mixing_ref
+    index_ref, own_ref, pieces_ref, gram_ref, square_ref, x_ref, x_other_ref, out_ref,
+    other_ref, cross_ref, gram_other_ref, mixing_ref,
 ):
     scale = math.sqrt(max(ROWS, COLS))
     step = 256
     row, column = iotas()
+    unpermute(index_ref, pieces_ref, other_ref)
     unpack_cross(own_ref, other_ref, cross_ref)
     mirror(other_ref, gram_other_ref, row >= column)
     for n in range(0, HALF, step):
@@ -244,21 +300,24 @@
                     out_ref[2 * (j - STRIPES) + side, :, pl.ds(PANEL, PANEL // 2), :] = packed
 
 
-def update_rows(packed, packed_other, gram, square, x, x_other):
+def update_rows(index, *operands):
+    kind = operands[0].dtype
     return pl.pallas_call(
         update_kernel,
-        out_shape=jax.ShapeDtypeStruct((STRIPES, CHIPS, PANEL + PANEL // 2, LANES), x.dtype),
+        in_specs=specs(len(operands)),
+        out_shape=jax.ShapeDtypeStruct((STRIPES, CHIPS, PANEL + PANEL // 2, LANES), kind),
         scratch_shapes=[
-            pltpu.VMEM((HALF, HALF), x.dtype),
-            pltpu.VMEM((HALF, HALF), x.dtype),
-            pltpu.VMEM((HALF, ROWS), x.dtype),
+            pltpu.VMEM((PACKED, LANES), kind),
+            pltpu.VMEM((HALF, HALF), kind),
+            pltpu.VMEM((HALF, HALF), kind),
+            pltpu.VMEM((HALF, ROWS), kind),
         ],
         compiler_params=pltpu.CompilerParams(vmem_limit_bytes=24 * MIB),
         cost_estimate=pl.CostEstimate(
             flops=4 * HALF * ROWS * ROWS - 2 * HALF * HALF * HALF, bytes_accessed=10 * HALF * ROWS, transcendentals=0
         ),
         name="update_rows",
-    )(packed, packed_other, gram, square, x, x_other)
+    )(index, *operands)
 
 
 def join_kernel(pieces_ref, out_ref, whole_ref, sems):
@@ -299,12 +358,17 @@
     pieces = split_columns(iterate.reshape(PANEL, COLS))
     own = lax.all_to_all(pieces, CHIP_AXES, 0, 0, tiled=True).reshape(HALF, WIDTH)
     other = swap_cores(own)
-    partial = cross_gram(*own_gram(own), own, other).reshape(CHIPS, PACKED // CHIPS, LANES)
-    partials = lax.all_to_all(partial, CHIP_AXES, 0, 0, tiled=True)
-    copies = sum_copies(partials)
-    packed = lax.all_to_all(copies, CHIP_AXES, 0, 0, tiled=True).reshape(PACKED, LANES)
-    packed_other = swap_cores(packed)
-    sent = update_rows(packed, packed_other, *own_square(packed), own, other)
+    index = jnp.asarray(positions())[lax.axis_index(CHIP_AXES)]
+    keep_a, send_a, diagonal = own_gram(index, own)
+    arrived_a = exchange(send_a, ORDERS[0][0])
+    keep_b, send_b, keep_c, send_c = cross_gram(index, diagonal, own, other)
+    arrived = arrived_a, exchange(send_b, ORDERS[1][0]), exchange(send_c, ORDERS[2][0])
+    arrived = lax.optimization_barrier(arrived)
+    streams = [sum_over_chips(*stream) for stream in zip((keep_a, keep_b, keep_c), arrived, ORDERS)]
+    pieces = jnp.concatenate(streams, axis=1)
+    pieces_other = swap_cores(pieces)
+    packed, gram, square = own_square(index, pieces)
+    sent = update_rows(index, packed, pieces_other, gram, square, own, other)
     sent = sent.reshape(STRIPES * CHIPS, PANEL + PANEL // 2, LANES)
     received = lax.all_to_all(sent, ALL_CHIPS, 0, 0, tiled=True)
     return join_columns(received.reshape(STRIPES, CHIPS, PANEL + PANEL // 2, LANES))

time: 141 us -> 143 us (1.014)
  blocking collectives: 121 us -> 79.1 us
  starting transfers between devices: 0.01 us -> 20.2 us
  waiting for transfers between devices: 4.81 us -> 22.1 us
  Pallas kernels: 13.4 us -> 18.1 us
    all_to_all x2 -> x0, blocking collectives: 42.9 us -> none  [the longest x1 22.2 us: shards(): partials = lax.all_to_all(partial, CHIP_AXES, 0, 0, tiled=True)]
    ppermute x0 -> x15, starting transfers between devices: none -> 19.9 us  [the longest x10 12.2 us: exchange(): lax.ppermute(value, 'x', [(i, i ^ 1 if axis == 'a' else 3 - i) for i in r...]
    ppermute x0 -> x15, waiting for transfers between devices: none -> 19.7 us  [the longest x10 11.5 us: exchange(): lax.ppermute(value, 'x', [(i, i ^ 1 if axis == 'a' else 3 - i) for i in r...]
    pallas_call x5 -> x4, Pallas kernels: 11.2 us -> 15.9 us  [the longest x1 8.91 us: update_rows(): pl.pallas_call(update_kernel, in_specs=specs(len(operands)), out_shape=ja...]
    ppermute x2, waiting for transfers between devices: 4.81 us -> 2.42 us  [swap_cores(): return lax.ppermute(value, 'c', [(0, 1), (1, 0)])]
  transfers between devices with their start and end apart: 2 -> 17, of which waited for: 2 -> 13; matrix products, arithmetic and copies ran while one was open for 0% -> 1% of each run, Pallas kernels for 2% -> 5%
where the time goes in v5:
time: 143 us
  blocking collectives  79.1 us (55%)
  waiting for transfers between devices  22.1 us (15%)
  starting transfers between devices  20.2 us (14%)
  Pallas kernels  18.1 us (13%)
  local copies, waits for them, and re-layouts  2.41 us (2%)
    all_to_all x1, blocking collectives, shards(): received = lax.all_to_all(sent, ALL_CHIPS, 0, 0, tiled=True)  41.3 us
    all_to_all x1, blocking collectives, shards(): lax.all_to_all(pieces, CHIP_AXES, 0, 0, tiled=True).reshape(HALF, WIDTH)  37.7 us
    ppermute x10, starting transfers between devices, exchange(): lax.ppermute(value, 'x', [(i, i ^ 1 if axis == 'a' else 3 - i) for i in r...  12.2 us
    ppermute x10, waiting for transfers between devices, exchange(): lax.ppermute(value, 'x', [(i, i ^ 1 if axis == 'a' else 3 - i) for i in r...  11.5 us
    pallas_call x1, Pallas kernels, update_rows(): pl.pallas_call(update_kernel, in_specs=specs(len(operands)), out_shape=ja...  8.91 us
    ppermute x5, waiting for transfers between devices, exchange(): return lax.ppermute(value, 'yh', [(0, 1), (1, 0)])  8.16 us
    ppermute x5, starting transfers between devices, exchange(): return lax.ppermute(value, 'yh', [(0, 1), (1, 0)])  7.7 us
    pallas_call x1, Pallas kernels, cross_gram(): pl.pallas_call(cross_gram_kernel, in_specs=specs(3), out_shape=half_shape...  3.19 us
  transfers between devices with their start and end apart: 17, of which 13 were waited for; matrix products, arithmetic and copies ran while one was open for 1% of the time, Pallas kernels for 5%

profile of v5, /device:TPU:0, one launch (start us, length us, event | category | flops | bytes accessed | tf_op | source)
XLA Modules:
  0.0 142.6 jit_solution(16759338495405360363)
XLA Ops:
  0.0 0.0 copy-start
  0.0 1.7 %copy-done = bf16[1,96,12288]{2,1,0:T(8,128)(2,1)S(1)} copy-done((bf16[1,96,12288]{2,1,0:T(8,128)(2,1)S(1)}, bf16[1,96,12288]{2,1,0:T(8,128)(2,1)}, u32[]{:S(2)}) %copy-start) | copy-done | bytes 2359320
  1.7 0.6 split_columns.1
  2.3 37.7 %all_to_all.10 = bf16[8,96,1536]{2,1,0:T(8,128)(2,1)S(1)} all-to-all(bf16[8,96,1536]{2,1,0:T(8,128)(2,1)S(1)} %split_columns.1), channel_id=1, replica_groups=mesh['z'=4,'yl'=2,'x'=4,'yh'=2,'c'=2] {'x','yh'}, dimensions={0} | all-to-all | bytes 4718592 | tf_op jit(solution)/shard_map/all_to_all | solution.py:359
  40.0 0.0 collective-permute-start.1
  40.0 0.7 dynamic-slice_bitcast_fusion.index_ref
  40.7 2.0 %own_gram.1 = (f32[4,240,128]{2,1,0:T(8,128)S(1)}, bf16[4,240,128]{2,1,0:T(8,128)(2,1)S(1)}, f32[6,128,128]{2,1,0:T(8,128)S(1)}) custom-call(s32[3]{0:T(128)S(1)} %dynamic-slice_bitcast_fusion.index_ref, bf16[768,1536]{1,0:T(8,128)(2,1)S(1)} %bitcast.9), custom_call_target="tpu_custom_call" | custom-call | flops 1660944384 | bytes 2359296 | tf_op jit(solution)/shard_map/own_gram/pallas_call | solution.py:136
  42.7 0.6 collective-permute-start
  43.3 1.4 collective-permute-done.1.other_ref.x_other_ref
  44.6 3.2 %cross_gram.1 = (f32[4,176,128]{2,1,0:T(8,128)S(1)}, bf16[4,176,128]{2,1,0:T(8,128)(2,1)S(1)}, f32[4,176,128]{2,1,0:T(8,128)S(1)}, bf16[4,176,128]{2,1,0:T(8,128)(2,1)S(1)}) custom-call(s32[3]{0:T(128)S(1)} %dynamic-slice_bitcast_fusion.index_ref, f32[6,128,128]{2,1,0:T(8,128)S(1)} %get-tuple-element.20.diagonal_ref, bf16[768,1536]{1,0:T(8,128)(2,1)S(1)} %bitcast.10, ...), custom_call_target="tpu_custom_call" | custom-call | flops 1660944384 | bytes 4718592 | tf_op jit(solution)/shard_map/cross_gram/pallas_call | solution.py:171
  47.8 1.5 %collective-permute-start.2 = (bf16[4,176,128]{2,1,0:T(8,128)(2,1)S(1)}, bf16[4,176,128]{2,1,0:T(8,128)(2,1)S(1)}, u32[]{:S(2)}, u32[]{:S(2)}) collective-permute-start(bf16[4,176,128]{2,1,0:T(8,128)(2,1)S(1)} %get-tuple-element.21), channel_id=1, source_target_pairs={{0,12},{4,8},{8,4},{12,0},{1,13},{5,9},{9,5},{13,1},{2,14},{6,10},... | collective-permute-start | bytes 540680 | tf_op jit(solution)/shard_map/ppermute | solution.py:187
  49.3 1.3 collective-permute-start.3
  50.6 0.5 collective-permute-done
  51.1 4.6 %collective-permute-done.2 = bf16[4,176,128]{2,1,0:T(8,128)(2,1)S(1)} collective-permute-done((bf16[4,176,128]{2,1,0:T(8,128)(2,1)S(1)}, bf16[4,176,128]{2,1,0:T(8,128)(2,1)S(1)}, u32[]{:S(2)}, u32[]{:S(2)}) %collective-permute-start.2) | collective-permute-done | bytes 180256 | tf_op jit(solution)/shard_map/ppermute | solution.py:187
  55.7 1.4 %collective-permute-done.3 = bf16[4,176,128]{2,1,0:T(8,128)(2,1)S(1)} collective-permute-done((bf16[4,176,128]{2,1,0:T(8,128)(2,1)S(1)}, bf16[4,176,128]{2,1,0:T(8,128)(2,1)S(1)}, u32[]{:S(2)}, u32[]{:S(2)}) %collective-permute-start.3) | collective-permute-done | bytes 180256 | tf_op jit(solution)/shard_map/ppermute | solution.py:186
  57.3 0.4 collective-permute-start.12
  57.7 1.0 collective-permute-start.8
  58.8 2.2 %collective-permute-start.4 = (bf16[2,240,128]{2,1,0:T(8,128)(2,1)S(1)}, bf16[2,240,128]{2,1,0:T(8,128)(2,1)S(1)}, u32[]{:S(2)}, u32[]{:S(2)}) collective-permute-start(bf16[2,240,128]{2,1,0:T(8,128)(2,1)S(1)} %slice.45), channel_id=1, source_target_pairs={{0,12},{4,8},{8,4},{12,0},{1,13},{5,9},{9,5},{13,1},{2,14},{6,10},... | collective-permute-start | bytes 368648 | tf_op jit(solution)/shard_map/ppermute | solution.py:187
  61.0 0.9 collective-permute-done.12
  61.9 1.9 %collective-permute-start.13 = (bf16[2,176,128]{2,1,0:T(8,128)(2,1)S(1)}, bf16[2,176,128]{2,1,0:T(8,128)(2,1)S(1)}, u32[]{:S(2)}, u32[]{:S(2)}) collective-permute-start(bf16[2,176,128]{2,1,0:T(8,128)(2,1)S(1)} %fusion.1), channel_id=1, source_target_pairs={{0,12},{4,8},{8,4},{12,0},{1,13},{5,9},{9,5},{13,1},{2,14},{6,10},... | collective-permute-start | bytes 270344 | tf_op jit(solution)/shard_map/ppermute | solution.py:187
  63.8 0.0 collective-permute-done.8
  63.8 1.7 %collective-permute-start.9 = (bf16[2,176,128]{2,1,0:T(8,128)(2,1)S(1)}, bf16[2,176,128]{2,1,0:T(8,128)(2,1)S(1)}, u32[]{:S(2)}, u32[]{:S(2)}) collective-permute-start(bf16[2,176,128]{2,1,0:T(8,128)(2,1)S(1)} %fusion.2), channel_id=1, source_target_pairs={{0,4},{4,0},{8,12},{12,8},{1,5},{5,1},{9,13},{13,9},{2,6},{6,2},{1... | collective-permute-start | bytes 270344 | tf_op jit(solution)/shard_map/ppermute | solution.py:187
  65.5 0.4 collective-permute-done.4
  65.9 1.8 %collective-permute-start.5 = (bf16[2,240,128]{2,1,0:T(8,128)(2,1)S(1)}, bf16[2,240,128]{2,1,0:T(8,128)(2,1)S(1)}, u32[]{:S(2)}, u32[]{:S(2)}) collective-permute-start(bf16[2,240,128]{2,1,0:T(8,128)(2,1)S(1)} %fusion), channel_id=1, source_target_pairs={{0,2},{2,0},{1,3},{3,1},{4,6},{6,4},{5,7},{7,5},{8,10},{10,8},{9,1... | collective-permute-start | bytes 368648 | tf_op jit(solution)/shard_map/ppermute | solution.py:186
  67.7 0.0 collective-permute-done.13
  67.8 0.4 collective-permute-start.14
  68.2 0.4 collective-permute-done.9
  68.6 3.8 %collective-permute-done.5 = bf16[2,240,128]{2,1,0:T(8,128)(2,1)S(1)} collective-permute-done((bf16[2,240,128]{2,1,0:T(8,128)(2,1)S(1)}, bf16[2,240,128]{2,1,0:T(8,128)(2,1)S(1)}, u32[]{:S(2)}, u32[]{:S(2)}) %collective-permute-start.5) | collective-permute-done | bytes 122912 | tf_op jit(solution)/shard_map/ppermute | solution.py:186
  72.5 1.9 %collective-permute-start.6 = (bf16[2,240,128]{2,1,0:T(8,128)(2,1)S(1)}, bf16[2,240,128]{2,1,0:T(8,128)(2,1)S(1)}, u32[]{:S(2)}, u32[]{:S(2)}) collective-permute-start(bf16[2,240,128]{2,1,0:T(8,128)(2,1)S(1)} %add_convert_fusion), channel_id=1, source_target_pairs={{0,12},{4,8},{8,4},{12,0},{1,13},{5,9},{9,5},{13,1},{2,14},{6,10},... | collective-permute-start | bytes 368648 | tf_op jit(solution)/shard_map/ppermute | solution.py:187
  74.4 1.6 %collective-permute-start.10 = (bf16[2,176,128]{2,1,0:T(8,128)(2,1)S(1)}, bf16[2,176,128]{2,1,0:T(8,128)(2,1)S(1)}, u32[]{:S(2)}, u32[]{:S(2)}) collective-permute-start(bf16[2,176,128]{2,1,0:T(8,128)(2,1)S(1)} %add_convert_fusion.2), channel_id=1, source_target_pairs={{0,2},{2,0},{1,3},{3,1},{4,6},{6,4},{5,7},{7,5},{8,10},{10,8},{9,1... | collective-permute-start | bytes 270344 | tf_op jit(solution)/shard_map/ppermute | solution.py:186
  76.0 0.0 collective-permute-done.14
  76.1 2.0 %collective-permute-start.15 = (bf16[4,176,128]{2,1,0:T(8,128)(2,1)S(1)}, bf16[4,176,128]{2,1,0:T(8,128)(2,1)S(1)}, u32[]{:S(2)}, u32[]{:S(2)}) collective-permute-start(bf16[4,176,128]{2,1,0:T(8,128)(2,1)S(1)} %pad_maximum_fusion.2), channel_id=1, source_target_pairs={{0,2},{2,0},{1,3},{3,1},{4,6},{6,4},{5,7},{7,5},{8,10},{10,8},{9,1... | collective-permute-start | bytes 540680 | tf_op jit(solution)/shard_map/ppermute | solution.py:186
  78.1 0.5 collective-permute-done.6
  78.6 0.1 collective-permute-start.7
  78.7 1.8 %collective-permute-done.10 = bf16[2,176,128]{2,1,0:T(8,128)(2,1)S(1)} collective-permute-done((bf16[2,176,128]{2,1,0:T(8,128)(2,1)S(1)}, bf16[2,176,128]{2,1,0:T(8,128)(2,1)S(1)}, u32[]{:S(2)}, u32[]{:S(2)}) %collective-permute-start.10) | collective-permute-done | bytes 90144 | tf_op jit(solution)/shard_map/ppermute | solution.py:186
  80.5 1.5 %collective-permute-start.11 = (bf16[4,176,128]{2,1,0:T(8,128)(2,1)S(1)}, bf16[4,176,128]{2,1,0:T(8,128)(2,1)S(1)}, u32[]{:S(2)}, u32[]{:S(2)}) collective-permute-start(bf16[4,176,128]{2,1,0:T(8,128)(2,1)S(1)} %pad_maximum_fusion.1), channel_id=1, source_target_pairs={{0,12},{4,8},{8,4},{12,0},{1,13},{5,9},{9,5},{13,1},{2,14},{6,10},... | collective-permute-start | bytes 540680 | tf_op jit(solution)/shard_map/ppermute | solution.py:187
  82.0 1.1 collective-permute-done.15
  83.1 4.2 %collective-permute-done.11 = bf16[4,176,128]{2,1,0:T(8,128)(2,1)S(1)} collective-permute-done((bf16[4,176,128]{2,1,0:T(8,128)(2,1)S(1)}, bf16[4,176,128]{2,1,0:T(8,128)(2,1)S(1)}, u32[]{:S(2)}, u32[]{:S(2)}) %collective-permute-start.11) | collective-permute-done | bytes 180256 | tf_op jit(solution)/shard_map/ppermute | solution.py:187
  87.3 0.0 collective-permute-done.7
  87.3 0.1 maximum_maximum_fusion.pieces_ref
  87.4 0.3 collective-permute-start.16
  87.7 1.8 %own_square.1 = (bf16[4736,128]{1,0:T(8,128)(2,1)S(1)}, bf16[768,768]{1,0:T(8,128)(2,1)S(1)}, f32[768,768]{1,0:T(8,128)S(1)}) custom-call(s32[3]{0:T(128)S(1)} %dynamic-slice_bitcast_fusion.index_ref, bf16[8,592,128]{2,1,0:T(8,128)(2,1)S(1)} %maximum_maximum_fusion.pieces_ref), custom_call_target="tpu_custom_call" | custom-call | flops 905969664 | bytes 4718592 | tf_op jit(solution)/shard_map/own_square/pallas_call | solution.py:233
  89.5 1.1 collective-permute-done.16.pieces_ref
  90.6 8.9 %update_rows.1 = bf16[8,8,144,128]{3,2,1,0:T(8,128)(2,1)S(1)} custom-call(s32[3]{0:T(128)S(1)} %dynamic-slice_bitcast_fusion.index_ref, bf16[4736,128]{1,0:T(8,128)(2,1)S(1)} %get-tuple-element.28.own_ref, bf16[8,592,128]{2,1,0:T(8,128)(2,1)S(1)} %collective-permute-done.16.pieces_ref, bf16[768,768]{1,0:T(8,128)(2,1)S(1)} %get-tuple-element.29.gram_ref, ...), custom_call_target="tpu_custom_call" | custom-call | flops 6341787648 | bytes 11796480 | tf_op jit(solution)/shard_map/update_rows/pallas_call | solution.py:305
  99.5 41.3 %all_to_all.11 = bf16[64,144,128]{2,1,0:T(8,128)(2,1)S(1)} all-to-all(bf16[64,144,128]{2,1,0:T(8,128)(2,1)S(1)} %bitcast.12), channel_id=1, replica_groups=mesh['z'=4,'yl'=2,'x'=4,'yh'=2,'c'=2] {'z','yl','x','yh'}, dimensions={0} | all-to-all | bytes 4718592 | tf_op jit(solution)/shard_map/all_to_all | solution.py:373
  140.8 1.6 %join_columns.1 = bf16[8,96,1536]{2,1,0:T(8,128)(2,1)} custom-call(bf16[8,8,144,128]{3,2,1,0:T(8,128)(2,1)S(1)} %bitcast.6), custom_call_target="tpu_custom_call" | custom-call | tf_op jit(solution)/shard_map/join_columns/pallas_call | solution.py:342
  (18 shorter events, 0.4 us)
Async XLA Ops:
  0.0 1.7 %copy-start = (bf16[1,96,12288]{2,1,0:T(8,128)(2,1)S(1)}, bf16[1,96,12288]{2,1,0:T(8,128)(2,1)}, u32[]{:S(2)}) copy-start(bf16[1,96,12288]{2,1,0:T(8,128)(2,1)} %param.2) | copy-start | bytes 7077892
  40.0 4.7 %collective-permute-start.1 = (bf16[768,1536]{1,0:T(8,128)(2,1)S(1)}, bf16[768,1536]{1,0:T(8,128)(2,1)}, u32[]{:S(2)}, u32[]{:S(2)}) collective-permute-start(bf16[768,1536]{1,0:T(8,128)(2,1)S(1)} %bitcast.8), channel_id=1, source_target_pairs={{0,1},{1,0},{2,3},{3,2},{4,5},{5,4},{6,7},{7,6},{8,9},{9,8},{10,11... | collective-permute-start | bytes 7077896 | tf_op jit(solution)/shard_map/ppermute | solution.py:354
  42.7 8.5 %collective-permute-start = (bf16[4,240,128]{2,1,0:T(8,128)(2,1)S(1)}, bf16[4,240,128]{2,1,0:T(8,128)(2,1)S(1)}, u32[]{:S(2)}, u32[]{:S(2)}) collective-permute-start(bf16[4,240,128]{2,1,0:T(8,128)(2,1)S(1)} %get-tuple-element.19), channel_id=1, source_target_pairs={{0,4},{4,0},{8,12},{12,8},{1,5},{5,1},{9,13},{13,9},{2,6},{6,2},{1... | collective-permute-start | bytes 737288 | tf_op jit(solution)/shard_map/ppermute | solution.py:187
  47.8 7.9 %collective-permute-start.2 = (bf16[4,176,128]{2,1,0:T(8,128)(2,1)S(1)}, bf16[4,176,128]{2,1,0:T(8,128)(2,1)S(1)}, u32[]{:S(2)}, u32[]{:S(2)}) collective-permute-start(bf16[4,176,128]{2,1,0:T(8,128)(2,1)S(1)} %get-tuple-element.21), channel_id=1, source_target_pairs={{0,12},{4,8},{8,4},{12,0},{1,13},{5,9},{9,5},{13,1},{2,14},{6,10},... | collective-permute-start | bytes 540680 | tf_op jit(solution)/shard_map/ppermute | solution.py:187
  49.3 7.8 %collective-permute-start.3 = (bf16[4,176,128]{2,1,0:T(8,128)(2,1)S(1)}, bf16[4,176,128]{2,1,0:T(8,128)(2,1)S(1)}, u32[]{:S(2)}, u32[]{:S(2)}) collective-permute-start(bf16[4,176,128]{2,1,0:T(8,128)(2,1)S(1)} %get-tuple-element.22), channel_id=1, source_target_pairs={{0,2},{2,0},{1,3},{3,1},{4,6},{6,4},{5,7},{7,5},{8,10},{10,8},{9,1... | collective-permute-start | bytes 540680 | tf_op jit(solution)/shard_map/ppermute | solution.py:186
  57.3 4.6 %collective-permute-start.12 = (bf16[2,176,128]{2,1,0:T(8,128)(2,1)S(1)}, bf16[2,176,128]{2,1,0:T(8,128)(2,1)S(1)}, u32[]{:S(2)}, u32[]{:S(2)}) collective-permute-start(bf16[2,176,128]{2,1,0:T(8,128)(2,1)S(1)} %slice.46), channel_id=1, source_target_pairs={{0,4},{4,0},{8,12},{12,8},{1,5},{5,1},{9,13},{13,9},{2,6},{6,2},{1... | collective-permute-start | bytes 270344 | tf_op jit(solution)/shard_map/ppermute | solution.py:187
  57.7 6.1 %collective-permute-start.8 = (bf16[2,176,128]{2,1,0:T(8,128)(2,1)S(1)}, bf16[2,176,128]{2,1,0:T(8,128)(2,1)S(1)}, u32[]{:S(2)}, u32[]{:S(2)}) collective-permute-start(bf16[2,176,128]{2,1,0:T(8,128)(2,1)S(1)} %slice.47), channel_id=1, source_target_pairs={{0,2},{2,0},{1,3},{3,1},{4,6},{6,4},{5,7},{7,5},{8,10},{10,8},{9,1... | collective-permute-start | bytes 270344 | tf_op jit(solution)/shard_map/ppermute | solution.py:186
  58.8 7.1 %collective-permute-start.4 = (bf16[2,240,128]{2,1,0:T(8,128)(2,1)S(1)}, bf16[2,240,128]{2,1,0:T(8,128)(2,1)S(1)}, u32[]{:S(2)}, u32[]{:S(2)}) collective-permute-start(bf16[2,240,128]{2,1,0:T(8,128)(2,1)S(1)} %slice.45), channel_id=1, source_target_pairs={{0,12},{4,8},{8,4},{12,0},{1,13},{5,9},{9,5},{13,1},{2,14},{6,10},... | collective-permute-start | bytes 368648 | tf_op jit(solution)/shard_map/ppermute | solution.py:187
  61.9 5.8 %collective-permute-start.13 = (bf16[2,176,128]{2,1,0:T(8,128)(2,1)S(1)}, bf16[2,176,128]{2,1,0:T(8,128)(2,1)S(1)}, u32[]{:S(2)}, u32[]{:S(2)}) collective-permute-start(bf16[2,176,128]{2,1,0:T(8,128)(2,1)S(1)} %fusion.1), channel_id=1, source_target_pairs={{0,12},{4,8},{8,4},{12,0},{1,13},{5,9},{9,5},{13,1},{2,14},{6,10},... | collective-permute-start | bytes 270344 | tf_op jit(solution)/shard_map/ppermute | solution.py:187
  63.8 4.7 %collective-permute-start.9 = (bf16[2,176,128]{2,1,0:T(8,128)(2,1)S(1)}, bf16[2,176,128]{2,1,0:T(8,128)(2,1)S(1)}, u32[]{:S(2)}, u32[]{:S(2)}) collective-permute-start(bf16[2,176,128]{2,1,0:T(8,128)(2,1)S(1)} %fusion.2), channel_id=1, source_target_pairs={{0,4},{4,0},{8,12},{12,8},{1,5},{5,1},{9,13},{13,9},{2,6},{6,2},{1... | collective-permute-start | bytes 270344 | tf_op jit(solution)/shard_map/ppermute | solution.py:187
  65.9 6.5 %collective-permute-start.5 = (bf16[2,240,128]{2,1,0:T(8,128)(2,1)S(1)}, bf16[2,240,128]{2,1,0:T(8,128)(2,1)S(1)}, u32[]{:S(2)}, u32[]{:S(2)}) collective-permute-start(bf16[2,240,128]{2,1,0:T(8,128)(2,1)S(1)} %fusion), channel_id=1, source_target_pairs={{0,2},{2,0},{1,3},{3,1},{4,6},{6,4},{5,7},{7,5},{8,10},{10,8},{9,1... | collective-permute-start | bytes 368648 | tf_op jit(solution)/shard_map/ppermute | solution.py:186
  67.8 8.3 %collective-permute-start.14 = (bf16[2,176,128]{2,1,0:T(8,128)(2,1)S(1)}, bf16[2,176,128]{2,1,0:T(8,128)(2,1)S(1)}, u32[]{:S(2)}, u32[]{:S(2)}) collective-permute-start(bf16[2,176,128]{2,1,0:T(8,128)(2,1)S(1)} %add_convert_fusion.1), channel_id=1, source_target_pairs={{0,4},{4,0},{8,12},{12,8},{1,5},{5,1},{9,13},{13,9},{2,6},{6,2},{1... | collective-permute-start | bytes 270344 | tf_op jit(solution)/shard_map/ppermute | solution.py:187
  72.5 6.2 %collective-permute-start.6 = (bf16[2,240,128]{2,1,0:T(8,128)(2,1)S(1)}, bf16[2,240,128]{2,1,0:T(8,128)(2,1)S(1)}, u32[]{:S(2)}, u32[]{:S(2)}) collective-permute-start(bf16[2,240,128]{2,1,0:T(8,128)(2,1)S(1)} %add_convert_fusion), channel_id=1, source_target_pairs={{0,12},{4,8},{8,4},{12,0},{1,13},{5,9},{9,5},{13,1},{2,14},{6,10},... | collective-permute-start | bytes 368648 | tf_op jit(solution)/shard_map/ppermute | solution.py:187
  74.4 6.1 %collective-permute-start.10 = (bf16[2,176,128]{2,1,0:T(8,128)(2,1)S(1)}, bf16[2,176,128]{2,1,0:T(8,128)(2,1)S(1)}, u32[]{:S(2)}, u32[]{:S(2)}) collective-permute-start(bf16[2,176,128]{2,1,0:T(8,128)(2,1)S(1)} %add_convert_fusion.2), channel_id=1, source_target_pairs={{0,2},{2,0},{1,3},{3,1},{4,6},{6,4},{5,7},{7,5},{8,10},{10,8},{9,1... | collective-permute-start | bytes 270344 | tf_op jit(solution)/shard_map/ppermute | solution.py:186
  76.1 7.1 %collective-permute-start.15 = (bf16[4,176,128]{2,1,0:T(8,128)(2,1)S(1)}, bf16[4,176,128]{2,1,0:T(8,128)(2,1)S(1)}, u32[]{:S(2)}, u32[]{:S(2)}) collective-permute-start(bf16[4,176,128]{2,1,0:T(8,128)(2,1)S(1)} %pad_maximum_fusion.2), channel_id=1, source_target_pairs={{0,2},{2,0},{1,3},{3,1},{4,6},{6,4},{5,7},{7,5},{8,10},{10,8},{9,1... | collective-permute-start | bytes 540680 | tf_op jit(solution)/shard_map/ppermute | solution.py:186
  78.6 8.7 %collective-permute-start.7 = (bf16[4,240,128]{2,1,0:T(8,128)(2,1)S(1)}, bf16[4,240,128]{2,1,0:T(8,128)(2,1)S(1)}, u32[]{:S(2)}, u32[]{:S(2)}) collective-permute-start(bf16[4,240,128]{2,1,0:T(8,128)(2,1)S(1)} %pad_maximum_fusion), channel_id=1, source_target_pairs={{0,4},{4,0},{8,12},{12,8},{1,5},{5,1},{9,13},{13,9},{2,6},{6,2},{1... | collective-permute-start | bytes 737288 | tf_op jit(solution)/shard_map/ppermute | solution.py:187
  80.5 6.8 %collective-permute-start.11 = (bf16[4,176,128]{2,1,0:T(8,128)(2,1)S(1)}, bf16[4,176,128]{2,1,0:T(8,128)(2,1)S(1)}, u32[]{:S(2)}, u32[]{:S(2)}) collective-permute-start(bf16[4,176,128]{2,1,0:T(8,128)(2,1)S(1)} %pad_maximum_fusion.1), channel_id=1, source_target_pairs={{0,12},{4,8},{8,4},{12,0},{1,13},{5,9},{9,5},{13,1},{2,14},{6,10},... | collective-permute-start | bytes 540680 | tf_op jit(solution)/shard_map/ppermute | solution.py:187
  87.4 3.2 %collective-permute-start.16 = (bf16[8,592,128]{2,1,0:T(8,128)(2,1)S(1)}, bf16[8,592,128]{2,1,0:T(8,128)(2,1)S(1)}, u32[]{:S(2)}, u32[]{:S(2)}) collective-permute-start(bf16[8,592,128]{2,1,0:T(8,128)(2,1)S(1)} %maximum_maximum_fusion.pieces_ref), channel_id=1, source_target_pairs={{0,1},{1,0},{2,3},{3,2},{4,5},{5,4},{6,7},{7,6},{8,9},{9,8},{10,11... | collective-permute-start | bytes 3637256 | tf_op jit(solution)/shard_map/ppermute | solution.py:354

commit v6 on v5

--- a/solution.py
+++ b/solution.py
@@ -2,7 +2,6 @@
 
 import jax
 import jax.numpy as jnp
-import numpy as np
 from jax import lax
 from jax.experimental import pallas as pl
 from jax.experimental.pallas import tpu as pltpu
@@ -46,34 +45,28 @@
     return pl.ds(index * LANES, LANES)
 
 
-def positions():
-    table = []
-    for x in range(4):
-        for d in range(2):
-            bit = {"a": (x + 1) // 2 % 2, "b": x // 2, "d": d}
-            table.append([4 * bit[i] + 2 * bit[j] + bit[k] for i, j, k in ORDERS])
-    return np.array(table, np.int32)
-
-
-def piece_rows(index_ref, stream, position, base=0):
-    piece = lax.bitwise_xor(index_ref[stream], position)
+def place(stream):
+    x, d = lax.axis_index("x"), lax.axis_index("yh")
+    bit = {"a": lax.rem((x + 1) // 2, 2), "b": x // 2, "d": d}
+    first, second, third = (bit[axis] for axis in ORDERS[stream])
+    return 4 * first + 2 * second + third
+
+
+def piece_rows(stream, position, base=0):
+    piece = lax.bitwise_xor(place(stream), position)
     return pl.ds(base + pl.multiple_of(piece * PIECES[stream], 16), PIECES[stream])
 
 
-def split_pieces(index_ref, stream, whole_ref, base, keep_ref, send_ref):
+def split_pieces(stream, whole_ref, base, keep_ref, send_ref):
     half = CHIPS // 2
     for k in range(half):
-        keep_ref[k] = whole_ref[piece_rows(index_ref, stream, k, base), :]
-        send_ref[k] = whole_ref[piece_rows(index_ref, stream, k + half, base), :].astype(send_ref.dtype)
+        keep_ref[k] = whole_ref[piece_rows(stream, k, base), :]
+        send_ref[k] = whole_ref[piece_rows(stream, k + half, base), :].astype(send_ref.dtype)
 
 
 def half_shapes(stream, kind):
     shape = (CHIPS // 2, PIECES[stream], LANES)
     return [jax.ShapeDtypeStruct(shape, jnp.float32), jax.ShapeDtypeStruct(shape, kind)]
-
-
-def specs(vmem):
-    return [pl.BlockSpec(memory_space=pltpu.SMEM)] + [pl.BlockSpec(memory_space=pltpu.VMEM)] * vmem
 
 
 def split_kernel(x_ref, out_ref):
@@ -121,7 +114,7 @@
     return [lax.broadcasted_iota(jnp.int32, (LANES, LANES), axis) for axis in range(2)]
 
 
-def own_gram_kernel(index_ref, own_ref, keep_ref, send_ref, diagonal_ref, whole_ref):
+def own_gram_kernel(own_ref, keep_ref, send_ref, diagonal_ref, whole_ref):
     def store_below(rows, value):
         whole_ref[rows, :] = value
 
@@ -129,13 +122,12 @@
         diagonal_ref[j] = value
 
     triangle(own_ref, own_ref, store_below, store_diagonal)
-    split_pieces(index_ref, 0, whole_ref, 0, keep_ref, send_ref)
-
-
-def own_gram(index, own):
+    split_pieces(0, whole_ref, 0, keep_ref, send_ref)
+
+
+def own_gram(own):
     return pl.pallas_call(
         own_gram_kernel,
-        in_specs=specs(1),
         out_shape=half_shapes(0, own.dtype) + [jax.ShapeDtypeStruct((BLOCKS, LANES, LANES), jnp.float32)],
         scratch_shapes=[pltpu.VMEM((BELOW, LANES), jnp.float32)],
         compiler_params=pltpu.CompilerParams(vmem_limit_bytes=8 * MIB),
@@ -143,11 +135,11 @@
             flops=2 * (BELOW + 3 * HALF) * LANES * WIDTH, bytes_accessed=2 * HALF * WIDTH, transcendentals=0
         ),
         name="own_gram",
-    )(index, own)
+    )(own)
 
 
 def cross_gram_kernel(
-    index_ref, diagonal_ref, own_ref, other_ref, keep_b_ref, send_b_ref, keep_c_ref, send_c_ref, whole_ref
+    diagonal_ref, own_ref, other_ref, keep_b_ref, send_b_ref, keep_c_ref, send_c_ref, whole_ref
 ):
     row, column = iotas()
     edges = []
@@ -163,14 +155,13 @@
     rest = PACKED - EDGE
     edges.append(jnp.zeros((rest - BLOCKS, LANES), jnp.float32))
     whole_ref[pl.ds(EDGE - BELOW, rest), :] = jnp.concatenate(edges)
-    split_pieces(index_ref, 1, whole_ref, BASES[1] - BELOW, keep_b_ref, send_b_ref)
-    split_pieces(index_ref, 2, whole_ref, BASES[2] - BELOW, keep_c_ref, send_c_ref)
-
-
-def cross_gram(index, diagonal, own, other):
+    split_pieces(1, whole_ref, BASES[1] - BELOW, keep_b_ref, send_b_ref)
+    split_pieces(2, whole_ref, BASES[2] - BELOW, keep_c_ref, send_c_ref)
+
+
+def cross_gram(diagonal, own, other):
     return pl.pallas_call(
         cross_gram_kernel,
-        in_specs=specs(3),
         out_shape=half_shapes(1, own.dtype) + half_shapes(2, own.dtype),
         scratch_shapes=[pltpu.VMEM((PACKED - BELOW, LANES), jnp.float32)],
         compiler_params=pltpu.CompilerParams(vmem_limit_bytes=12 * MIB),
@@ -178,7 +169,7 @@
             flops=2 * (BELOW + 3 * HALF) * LANES * WIDTH, bytes_accessed=4 * HALF * WIDTH, transcendentals=0
         ),
         name="cross_gram",
-    )(index, diagonal, own, other)
+    )(diagonal, own, other)
 
 
 def exchange(value, axis):
@@ -193,19 +184,17 @@
 
 def sum_over_chips(keep, arrived, order):
     kind = arrived.dtype
-    half = keep + wide(arrived)
-    quarter = half[:2] + wide(exchange(half[2:].astype(kind), order[1]))
-    quarter = quarter.astype(kind)
-    total = (wide(quarter) + wide(exchange(quarter, order[2]))[::-1]).astype(kind)
-    half = jnp.concatenate([total, exchange(total, order[1])])
+    half = (keep + wide(arrived)).astype(kind).reshape(2, 2, *keep.shape[1:])
+    half = (wide(half) + wide(exchange(half, order[1]))[::-1]).astype(kind)
+    half = (wide(half) + wide(exchange(half, order[2]))[:, ::-1]).astype(kind).reshape(arrived.shape)
     return jnp.concatenate([half, exchange(half, order[0])])
 
 
-def unpermute(index_ref, pieces_ref, packed_ref):
+def unpermute(pieces_ref, packed_ref):
     first = 0
     for s, rows in enumerate(PIECES):
         for k in range(CHIPS):
-            packed_ref[piece_rows(index_ref, s, k, BASES[s]), :] = pieces_ref[k, pl.ds(first, rows), :]
+            packed_ref[piece_rows(s, k, BASES[s]), :] = pieces_ref[k, pl.ds(first, rows), :]
         first += rows
 
 
@@ -220,19 +209,18 @@
             out_ref[pl.ds(first, LANES), pl.ds(first + LANES, below.shape[0])] = below.T
 
 
-def own_square_kernel(index_ref, pieces_ref, packed_ref, gram_ref, square_ref):
+def own_square_kernel(pieces_ref, packed_ref, gram_ref, square_ref):
     row, column = iotas()
-    unpermute(index_ref, pieces_ref, packed_ref)
+    unpermute(pieces_ref, packed_ref)
     mirror(packed_ref, gram_ref, row >= column)
     for n in range(0, HALF, 256):
         columns = pl.ds(n, 256)
         square_ref[:, columns] = jnp.dot(gram_ref[...], gram_ref[:, columns], preferred_element_type=jnp.float32)
 
 
-def own_square(index, pieces):
+def own_square(pieces):
     return pl.pallas_call(
         own_square_kernel,
-        in_specs=specs(1),
         out_shape=(
             jax.ShapeDtypeStruct((PACKED, LANES), pieces.dtype),
             jax.ShapeDtypeStruct((HALF, HALF), pieces.dtype),
@@ -243,7 +231,7 @@
             flops=2 * HALF * HALF * HALF, bytes_accessed=8 * HALF * HALF, transcendentals=0
         ),
         name="own_square",
-    )(index, pieces)
+    )(pieces)
 
 
 def unpack_cross(own_ref, other_ref, cross_ref):
@@ -261,13 +249,13 @@
 
 
 def update_kernel(
-    index_ref, own_ref, pieces_ref, gram_ref, square_ref, x_ref, x_other_ref, out_ref,
+    own_ref, pieces_ref, gram_ref, square_ref, x_ref, x_other_ref, out_ref,
     other_ref, cross_ref, gram_other_ref, mixing_ref,
 ):
     scale = math.sqrt(max(ROWS, COLS))
     step = 256
     row, column = iotas()
-    unpermute(index_ref, pieces_ref, other_ref)
+    unpermute(pieces_ref, other_ref)
     unpack_cross(own_ref, other_ref, cross_ref)
     mirror(other_ref, gram_other_ref, row >= column)
     for n in range(0, HALF, step):
@@ -300,11 +288,10 @@
                     out_ref[2 * (j - STRIPES) + side, :, pl.ds(PANEL, PANEL // 2), :] = packed
 
 
-def update_rows(index, *operands):
+def update_rows(*operands):
     kind = operands[0].dtype
     return pl.pallas_call(
         update_kernel,
-        in_specs=specs(len(operands)),
         out_shape=jax.ShapeDtypeStruct((STRIPES, CHIPS, PANEL + PANEL // 2, LANES), kind),
         scratch_shapes=[
             pltpu.VMEM((PACKED, LANES), kind),
@@ -317,7 +304,7 @@
             flops=4 * HALF * ROWS * ROWS - 2 * HALF * HALF * HALF, bytes_accessed=10 * HALF * ROWS, transcendentals=0
         ),
         name="update_rows",
-    )(index, *operands)
+    )(*operands)
 
 
 def join_kernel(pieces_ref, out_ref, whole_ref, sems):
@@ -358,17 +345,16 @@
     pieces = split_columns(iterate.reshape(PANEL, COLS))
     own = lax.all_to_all(pieces, CHIP_AXES, 0, 0, tiled=True).reshape(HALF, WIDTH)
     other = swap_cores(own)
-    index = jnp.asarray(positions())[lax.axis_index(CHIP_AXES)]
-    keep_a, send_a, diagonal = own_gram(index, own)
+    keep_a, send_a, diagonal = own_gram(own)
     arrived_a = exchange(send_a, ORDERS[0][0])
-    keep_b, send_b, keep_c, send_c = cross_gram(index, diagonal, own, other)
+    keep_b, send_b, keep_c, send_c = cross_gram(diagonal, own, other)
     arrived = arrived_a, exchange(send_b, ORDERS[1][0]), exchange(send_c, ORDERS[2][0])
     arrived = lax.optimization_barrier(arrived)
     streams = [sum_over_chips(*stream) for stream in zip((keep_a, keep_b, keep_c), arrived, ORDERS)]
     pieces = jnp.concatenate(streams, axis=1)
     pieces_other = swap_cores(pieces)
-    packed, gram, square = own_square(index, pieces)
-    sent = update_rows(index, packed, pieces_other, gram, square, own, other)
+    packed, gram, square = own_square(pieces)
+    sent = update_rows(packed, pieces_other, gram, square, own, other)
     sent = sent.reshape(STRIPES * CHIPS, PANEL + PANEL // 2, LANES)
     received = lax.all_to_all(sent, ALL_CHIPS, 0, 0, tiled=True)
     return join_columns(received.reshape(STRIPES, CHIPS, PANEL + PANEL // 2, LANES))

time: 143 us -> 138 us (0.965)
  starting transfers between devices: 20.2 us -> 14.9 us
  Pallas kernels: 18.1 us -> 13.6 us
  waiting for transfers between devices: 22.1 us -> 25.9 us
    pallas_call x4, Pallas kernels: 15.9 us -> 11.4 us  [the longest x1 7.11 us: update_rows(): pl.pallas_call(update_kernel, out_shape=jax.ShapeDtypeStruct((STRIPES, CH...]
    ppermute x10 -> x8, starting transfers between devices: 12.2 us -> 8.29 us  [exchange(): lax.ppermute(value, 'x', [(i, i ^ 1 if axis == 'a' else 3 - i) for i in r...]
    ppermute x5 -> x4, waiting for transfers between devices: 8.16 us -> 10.2 us  [exchange(): return lax.ppermute(value, 'yh', [(0, 1), (1, 0)])]
    ppermute x2, waiting for transfers between devices: 2.42 us -> 4.05 us  [swap_cores(): return lax.ppermute(value, 'c', [(0, 1), (1, 0)])]
    ppermute x5 -> x4, starting transfers between devices: 7.7 us -> 6.3 us  [exchange(): return lax.ppermute(value, 'yh', [(0, 1), (1, 0)])]
    ppermute x10 -> x8, waiting for transfers between devices: 11.5 us -> 11.7 us  [exchange(): lax.ppermute(value, 'x', [(i, i ^ 1 if axis == 'a' else 3 - i) for i in r...]
  transfers between devices with their start and end apart: 17 -> 14, of which waited for: 13 -> 9; matrix products, arithmetic and copies ran while one was open for 1% -> 0% of each run, Pallas kernels for 5% -> 3%
where the time goes in v6:
time: 138 us; the launch traced here: 137 us
  blocking collectives  80.3 us (58%)
  waiting for transfers between devices  25.9 us (19%)
  starting transfers between devices  14.9 us (11%)
  Pallas kernels  13.6 us (10%)
  local copies, waits for them, and re-layouts  1.66 us (1%)
    all_to_all x1, blocking collectives, shards(): received = lax.all_to_all(sent, ALL_CHIPS, 0, 0, tiled=True)  42.6 us
    all_to_all x1, blocking collectives, shards(): lax.all_to_all(pieces, CHIP_AXES, 0, 0, tiled=True).reshape(HALF, WIDTH)  37.7 us
    ppermute x8, waiting for transfers between devices, exchange(): lax.ppermute(value, 'x', [(i, i ^ 1 if axis == 'a' else 3 - i) for i in r...  11.7 us
    ppermute x4, waiting for transfers between devices, exchange(): return lax.ppermute(value, 'yh', [(0, 1), (1, 0)])  10.2 us
    ppermute x8, starting transfers between devices, exchange(): lax.ppermute(value, 'x', [(i, i ^ 1 if axis == 'a' else 3 - i) for i in r...  8.29 us
    pallas_call x1, Pallas kernels, update_rows(): pl.pallas_call(update_kernel, out_shape=jax.ShapeDtypeStruct((STRIPES, CH...  7.11 us
    ppermute x4, starting transfers between devices, exchange(): return lax.ppermute(value, 'yh', [(0, 1), (1, 0)])  6.3 us
    ppermute x2, waiting for transfers between devices, swap_cores(): return lax.ppermute(value, 'c', [(0, 1), (1, 0)])  4.05 us
  transfers between devices with their start and end apart: 14, of which 9 were waited for; matrix products, arithmetic and copies ran while one was open for 0% of the time, Pallas kernels for 3%

profile of v6, /device:TPU:0, one launch (start us, length us, event | category | flops | bytes accessed | tf_op | source)
XLA Modules:
  0.0 137.3 jit_solution(5499961679738853480)
XLA Ops:
  0.0 0.0 copy-start
  0.0 1.7 %copy-done = bf16[1,96,12288]{2,1,0:T(8,128)(2,1)S(1)} copy-done((bf16[1,96,12288]{2,1,0:T(8,128)(2,1)S(1)}, bf16[1,96,12288]{2,1,0:T(8,128)(2,1)}, u32[]{:S(2)}) %copy-start) | copy-done | bytes 2359320
  1.7 0.6 split_columns.1
  2.3 37.7 %all_to_all.10 = bf16[8,96,1536]{2,1,0:T(8,128)(2,1)S(1)} all-to-all(bf16[8,96,1536]{2,1,0:T(8,128)(2,1)S(1)} %split_columns.1), channel_id=1, replica_groups=mesh['z'=4,'yl'=2,'x'=4,'yh'=2,'c'=2] {'x','yh'}, dimensions={0} | all-to-all | bytes 4718592 | tf_op jit(solution)/shard_map/all_to_all | solution.py:346
  40.0 0.0 collective-permute-start.1
  40.0 1.5 %own_gram.1 = (f32[4,240,128]{2,1,0:T(8,128)S(1)}, bf16[4,240,128]{2,1,0:T(8,128)(2,1)S(1)}, f32[6,128,128]{2,1,0:T(8,128)S(1)}) custom-call(bf16[768,1536]{1,0:T(8,128)(2,1)S(1)} %bitcast.13), custom_call_target="tpu_custom_call" | custom-call | flops 1660944384 | bytes 2359296 | tf_op jit(solution)/shard_map/own_gram/pallas_call | solution.py:129
  41.4 0.6 collective-permute-start
  42.0 2.5 %collective-permute-done.1.other_ref.x_other_ref = bf16[768,1536]{1,0:T(8,128)(2,1)S(1)} collective-permute-done((bf16[768,1536]{1,0:T(8,128)(2,1)S(1)}, bf16[768,1536]{1,0:T(8,128)(2,1)S(1)}, u32[]{:S(2)}, u32[]{:S(2)}) %collective-permute-start.1) | collective-permute-done | bytes 2359328 | tf_op jit(solution)/shard_map/ppermute | solution.py:341
  44.5 1.5 %cross_gram.1 = (f32[4,176,128]{2,1,0:T(8,128)S(1)}, bf16[4,176,128]{2,1,0:T(8,128)(2,1)S(1)}, f32[4,176,128]{2,1,0:T(8,128)S(1)}, bf16[4,176,128]{2,1,0:T(8,128)(2,1)S(1)}) custom-call(f32[6,128,128]{2,1,0:T(8,128)S(1)} %get-tuple-element.20.diagonal_ref, bf16[768,1536]{1,0:T(8,128)(2,1)S(1)} %bitcast.14, ...), custom_call_target="tpu_custom_call" | custom-call | flops 1660944384 | bytes 4718592 | tf_op jit(solution)/shard_map/cross_gram/pallas_call | solution.py:163
  46.0 1.5 %collective-permute-start.2 = (bf16[4,176,128]{2,1,0:T(8,128)(2,1)S(1)}, bf16[4,176,128]{2,1,0:T(8,128)(2,1)S(1)}, u32[]{:S(2)}, u32[]{:S(2)}) collective-permute-start(bf16[4,176,128]{2,1,0:T(8,128)(2,1)S(1)} %get-tuple-element.21), channel_id=1, source_target_pairs={{0,12},{4,8},{8,4},{12,0},{1,13},{5,9},{9,5},{13,1},{2,14},{6,10},... | collective-permute-start | bytes 540680 | tf_op jit(solution)/shard_map/ppermute | solution.py:178
  47.5 1.3 collective-permute-start.3
  48.8 1.1 collective-permute-done
  49.9 4.0 %collective-permute-done.2 = bf16[4,176,128]{2,1,0:T(8,128)(2,1)S(1)} collective-permute-done((bf16[4,176,128]{2,1,0:T(8,128)(2,1)S(1)}, bf16[4,176,128]{2,1,0:T(8,128)(2,1)S(1)}, u32[]{:S(2)}, u32[]{:S(2)}) %collective-permute-start.2) | collective-permute-done | bytes 180256 | tf_op jit(solution)/shard_map/ppermute | solution.py:178
  53.9 1.4 %collective-permute-done.3 = bf16[4,176,128]{2,1,0:T(8,128)(2,1)S(1)} collective-permute-done((bf16[4,176,128]{2,1,0:T(8,128)(2,1)S(1)}, bf16[4,176,128]{2,1,0:T(8,128)(2,1)S(1)}, u32[]{:S(2)}, u32[]{:S(2)}) %collective-permute-start.3) | collective-permute-done | bytes 180256 | tf_op jit(solution)/shard_map/ppermute | solution.py:177
  55.4 1.3 collective-permute-start.7
  56.7 0.1 add_convert_fusion.2
  56.8 2.2 %collective-permute-start.4 = (bf16[2,2,240,128]{3,2,1,0:T(8,128)(2,1)S(1)}, bf16[2,2,240,128]{3,2,1,0:T(8,128)(2,1)S(1)}, u32[]{:S(2)}, u32[]{:S(2)}) collective-permute-start(bf16[2,2,240,128]{3,2,1,0:T(8,128)(2,1)S(1)} %bitcast.19), channel_id=1, source_target_pairs={{0,12},{4,8},{8,4},{12,0},{1,13},{5,9},{9,5},{13,1},{2,14},{6,10},... | collective-permute-start | bytes 737288 | tf_op jit(solution)/shard_map/ppermute | solution.py:178
  59.0 0.1 collective-permute-start.10
  59.1 3.3 %collective-permute-done.7 = bf16[2,2,176,128]{3,2,1,0:T(8,128)(2,1)S(1)} collective-permute-done((bf16[2,2,176,128]{3,2,1,0:T(8,128)(2,1)S(1)}, bf16[2,2,176,128]{3,2,1,0:T(8,128)(2,1)S(1)}, u32[]{:S(2)}, u32[]{:S(2)}) %collective-permute-start.7) | collective-permute-done | bytes 180256 | tf_op jit(solution)/shard_map/ppermute | solution.py:177
  62.5 0.4 collective-permute-start.8
  63.0 3.3 %collective-permute-done.10 = bf16[2,2,176,128]{3,2,1,0:T(8,128)(2,1)S(1)} collective-permute-done((bf16[2,2,176,128]{3,2,1,0:T(8,128)(2,1)S(1)}, bf16[2,2,176,128]{3,2,1,0:T(8,128)(2,1)S(1)}, u32[]{:S(2)}, u32[]{:S(2)}) %collective-permute-start.10) | collective-permute-done | bytes 180256 | tf_op jit(solution)/shard_map/ppermute | solution.py:178
  66.3 0.0 collective-permute-done.4
  66.3 0.1 add_convert_fusion.1
  66.4 2.0 %collective-permute-start.5 = (bf16[2,2,240,128]{3,2,1,0:T(8,128)(2,1)S(1)}, bf16[2,2,240,128]{3,2,1,0:T(8,128)(2,1)S(1)}, u32[]{:S(2)}, u32[]{:S(2)}) collective-permute-start(bf16[2,2,240,128]{3,2,1,0:T(8,128)(2,1)S(1)} %add_convert_fusion.1), channel_id=1, source_target_pairs={{0,2},{2,0},{1,3},{3,1},{4,6},{6,4},{5,7},{7,5},{8,10},{10,8},{9,1... | collective-permute-start | bytes 737288 | tf_op jit(solution)/shard_map/ppermute | solution.py:177
  68.4 1.5 %collective-permute-start.11 = (bf16[2,2,176,128]{3,2,1,0:T(8,128)(2,1)S(1)}, bf16[2,2,176,128]{3,2,1,0:T(8,128)(2,1)S(1)}, u32[]{:S(2)}, u32[]{:S(2)}) collective-permute-start(bf16[2,2,176,128]{3,2,1,0:T(8,128)(2,1)S(1)} %add_convert_fusion.4), channel_id=1, source_target_pairs={{0,12},{4,8},{8,4},{12,0},{1,13},{5,9},{9,5},{13,1},{2,14},{6,10},... | collective-permute-start | bytes 540680 | tf_op jit(solution)/shard_map/ppermute | solution.py:178
  70.0 0.0 collective-permute-done.8
  70.0 1.9 %collective-permute-start.9 = (bf16[4,176,128]{2,1,0:T(8,128)(2,1)S(1)}, bf16[4,176,128]{2,1,0:T(8,128)(2,1)S(1)}, u32[]{:S(2)}, u32[]{:S(2)}) collective-permute-start(bf16[4,176,128]{2,1,0:T(8,128)(2,1)S(1)} %bitcast.21), channel_id=1, source_target_pairs={{0,12},{4,8},{8,4},{12,0},{1,13},{5,9},{9,5},{13,1},{2,14},{6,10},... | collective-permute-start | bytes 540680 | tf_op jit(solution)/shard_map/ppermute | solution.py:178
  71.9 3.3 %collective-permute-done.11 = bf16[2,2,176,128]{3,2,1,0:T(8,128)(2,1)S(1)} collective-permute-done((bf16[2,2,176,128]{3,2,1,0:T(8,128)(2,1)S(1)}, bf16[2,2,176,128]{3,2,1,0:T(8,128)(2,1)S(1)}, u32[]{:S(2)}, u32[]{:S(2)}) %collective-permute-start.11) | collective-permute-done | bytes 180256 | tf_op jit(solution)/shard_map/ppermute | solution.py:178
  75.3 0.0 collective-permute-done.5
  75.3 0.1 add_convert_fusion
  75.4 0.1 collective-permute-start.6
  75.5 1.7 %collective-permute-start.12 = (bf16[4,176,128]{2,1,0:T(8,128)(2,1)S(1)}, bf16[4,176,128]{2,1,0:T(8,128)(2,1)S(1)}, u32[]{:S(2)}, u32[]{:S(2)}) collective-permute-start(bf16[4,176,128]{2,1,0:T(8,128)(2,1)S(1)} %bitcast.27), channel_id=1, source_target_pairs={{0,2},{2,0},{1,3},{3,1},{4,6},{6,4},{5,7},{7,5},{8,10},{10,8},{9,1... | collective-permute-start | bytes 540680 | tf_op jit(solution)/shard_map/ppermute | solution.py:177
  77.2 0.0 collective-permute-done.9
  77.2 5.4 %collective-permute-done.12 = bf16[4,176,128]{2,1,0:T(8,128)(2,1)S(1)} collective-permute-done((bf16[4,176,128]{2,1,0:T(8,128)(2,1)S(1)}, bf16[4,176,128]{2,1,0:T(8,128)(2,1)S(1)}, u32[]{:S(2)}, u32[]{:S(2)}) %collective-permute-start.12) | collective-permute-done | bytes 180256 | tf_op jit(solution)/shard_map/ppermute | solution.py:177
  82.6 0.0 collective-permute-done.6
  82.6 0.1 maximum_maximum_fusion.pieces_ref
  82.7 0.3 collective-permute-start.13
  83.0 1.3 own_square.1
  84.3 1.6 %collective-permute-done.13.pieces_ref = bf16[8,592,128]{2,1,0:T(8,128)(2,1)S(1)} collective-permute-done((bf16[8,592,128]{2,1,0:T(8,128)(2,1)S(1)}, bf16[8,592,128]{2,1,0:T(8,128)(2,1)S(1)}, u32[]{:S(2)}, u32[]{:S(2)}) %collective-permute-start.13) | collective-permute-done | bytes 1212448 | tf_op jit(solution)/shard_map/ppermute | solution.py:341
  85.8 7.1 %update_rows.1 = bf16[8,8,144,128]{3,2,1,0:T(8,128)(2,1)S(1)} custom-call(bf16[4736,128]{1,0:T(8,128)(2,1)S(1)} %get-tuple-element.28.own_ref, bf16[8,592,128]{2,1,0:T(8,128)(2,1)S(1)} %collective-permute-done.13.pieces_ref, bf16[768,768]{1,0:T(8,128)(2,1)S(1)} %get-tuple-element.29.gram_ref, f32[768,768]{1,0:T(8,128)S(1)} %get-tuple-element.30.square_ref, ...), custom_call_target="tpu_custom_call" | custom-call | flops 6341787648 | bytes 11796480 | tf_op jit(solution)/shard_map/update_rows/pallas_call | solution.py:293
  93.0 42.6 %all_to_all.11 = bf16[64,144,128]{2,1,0:T(8,128)(2,1)S(1)} all-to-all(bf16[64,144,128]{2,1,0:T(8,128)(2,1)S(1)} %bitcast.16), channel_id=1, replica_groups=mesh['z'=4,'yl'=2,'x'=4,'yh'=2,'c'=2] {'z','yl','x','yh'}, dimensions={0} | all-to-all | bytes 4718592 | tf_op jit(solution)/shard_map/all_to_all | solution.py:359
  135.6 1.6 %join_columns.1 = bf16[8,96,1536]{2,1,0:T(8,128)(2,1)} custom-call(bf16[8,8,144,128]{3,2,1,0:T(8,128)(2,1)S(1)} %bitcast.10), custom_call_target="tpu_custom_call" | custom-call | tf_op jit(solution)/shard_map/join_columns/pallas_call | solution.py:329
  (12 shorter events, 0.4 us)
Async XLA Ops:
  0.0 1.7 %copy-start = (bf16[1,96,12288]{2,1,0:T(8,128)(2,1)S(1)}, bf16[1,96,12288]{2,1,0:T(8,128)(2,1)}, u32[]{:S(2)}) copy-start(bf16[1,96,12288]{2,1,0:T(8,128)(2,1)} %param.1) | copy-start | bytes 7077892
  40.0 4.5 %collective-permute-start.1 = (bf16[768,1536]{1,0:T(8,128)(2,1)S(1)}, bf16[768,1536]{1,0:T(8,128)(2,1)S(1)}, u32[]{:S(2)}, u32[]{:S(2)}) collective-permute-start(bf16[768,1536]{1,0:T(8,128)(2,1)S(1)} %bitcast.12), channel_id=1, source_target_pairs={{0,1},{1,0},{2,3},{3,2},{4,5},{5,4},{6,7},{7,6},{8,9},{9,8},{10,11... | collective-permute-start | bytes 7077896 | tf_op jit(solution)/shard_map/ppermute | solution.py:341
  41.4 8.5 %collective-permute-start = (bf16[4,240,128]{2,1,0:T(8,128)(2,1)S(1)}, bf16[4,240,128]{2,1,0:T(8,128)(2,1)S(1)}, u32[]{:S(2)}, u32[]{:S(2)}) collective-permute-start(bf16[4,240,128]{2,1,0:T(8,128)(2,1)S(1)} %get-tuple-element.19), channel_id=1, source_target_pairs={{0,4},{4,0},{8,12},{12,8},{1,5},{5,1},{9,13},{13,9},{2,6},{6,2},{1... | collective-permute-start | bytes 737288 | tf_op jit(solution)/shard_map/ppermute | solution.py:178
  46.0 7.9 %collective-permute-start.2 = (bf16[4,176,128]{2,1,0:T(8,128)(2,1)S(1)}, bf16[4,176,128]{2,1,0:T(8,128)(2,1)S(1)}, u32[]{:S(2)}, u32[]{:S(2)}) collective-permute-start(bf16[4,176,128]{2,1,0:T(8,128)(2,1)S(1)} %get-tuple-element.21), channel_id=1, source_target_pairs={{0,12},{4,8},{8,4},{12,0},{1,13},{5,9},{9,5},{13,1},{2,14},{6,10},... | collective-permute-start | bytes 540680 | tf_op jit(solution)/shard_map/ppermute | solution.py:178
  47.5 7.8 %collective-permute-start.3 = (bf16[4,176,128]{2,1,0:T(8,128)(2,1)S(1)}, bf16[4,176,128]{2,1,0:T(8,128)(2,1)S(1)}, u32[]{:S(2)}, u32[]{:S(2)}) collective-permute-start(bf16[4,176,128]{2,1,0:T(8,128)(2,1)S(1)} %get-tuple-element.22), channel_id=1, source_target_pairs={{0,2},{2,0},{1,3},{3,1},{4,6},{6,4},{5,7},{7,5},{8,10},{10,8},{9,1... | collective-permute-start | bytes 540680 | tf_op jit(solution)/shard_map/ppermute | solution.py:177
  55.4 7.1 %collective-permute-start.7 = (bf16[2,2,176,128]{3,2,1,0:T(8,128)(2,1)S(1)}, bf16[2,2,176,128]{3,2,1,0:T(8,128)(2,1)S(1)}, u32[]{:S(2)}, u32[]{:S(2)}) collective-permute-start(bf16[2,2,176,128]{3,2,1,0:T(8,128)(2,1)S(1)} %bitcast.25), channel_id=1, source_target_pairs={{0,2},{2,0},{1,3},{3,1},{4,6},{6,4},{5,7},{7,5},{8,10},{10,8},{9,1... | collective-permute-start | bytes 540680 | tf_op jit(solution)/shard_map/ppermute | solution.py:177
  56.8 9.5 %collective-permute-start.4 = (bf16[2,2,240,128]{3,2,1,0:T(8,128)(2,1)S(1)}, bf16[2,2,240,128]{3,2,1,0:T(8,128)(2,1)S(1)}, u32[]{:S(2)}, u32[]{:S(2)}) collective-permute-start(bf16[2,2,240,128]{3,2,1,0:T(8,128)(2,1)S(1)} %bitcast.19), channel_id=1, source_target_pairs={{0,12},{4,8},{8,4},{12,0},{1,13},{5,9},{9,5},{13,1},{2,14},{6,10},... | collective-permute-start | bytes 737288 | tf_op jit(solution)/shard_map/ppermute | solution.py:178
  59.0 7.2 %collective-permute-start.10 = (bf16[2,2,176,128]{3,2,1,0:T(8,128)(2,1)S(1)}, bf16[2,2,176,128]{3,2,1,0:T(8,128)(2,1)S(1)}, u32[]{:S(2)}, u32[]{:S(2)}) collective-permute-start(bf16[2,2,176,128]{3,2,1,0:T(8,128)(2,1)S(1)} %bitcast.23), channel_id=1, source_target_pairs={{0,4},{4,0},{8,12},{12,8},{1,5},{5,1},{9,13},{13,9},{2,6},{6,2},{1... | collective-permute-start | bytes 540680 | tf_op jit(solution)/shard_map/ppermute | solution.py:178
  62.5 7.4 %collective-permute-start.8 = (bf16[2,2,176,128]{3,2,1,0:T(8,128)(2,1)S(1)}, bf16[2,2,176,128]{3,2,1,0:T(8,128)(2,1)S(1)}, u32[]{:S(2)}, u32[]{:S(2)}) collective-permute-start(bf16[2,2,176,128]{3,2,1,0:T(8,128)(2,1)S(1)} %add_convert_fusion.7), channel_id=1, source_target_pairs={{0,4},{4,0},{8,12},{12,8},{1,5},{5,1},{9,13},{13,9},{2,6},{6,2},{1... | collective-permute-start | bytes 540680 | tf_op jit(solution)/shard_map/ppermute | solution.py:178
  66.4 8.9 %collective-permute-start.5 = (bf16[2,2,240,128]{3,2,1,0:T(8,128)(2,1)S(1)}, bf16[2,2,240,128]{3,2,1,0:T(8,128)(2,1)S(1)}, u32[]{:S(2)}, u32[]{:S(2)}) collective-permute-start(bf16[2,2,240,128]{3,2,1,0:T(8,128)(2,1)S(1)} %add_convert_fusion.1), channel_id=1, source_target_pairs={{0,2},{2,0},{1,3},{3,1},{4,6},{6,4},{5,7},{7,5},{8,10},{10,8},{9,1... | collective-permute-start | bytes 737288 | tf_op jit(solution)/shard_map/ppermute | solution.py:177
  68.4 6.8 %collective-permute-start.11 = (bf16[2,2,176,128]{3,2,1,0:T(8,128)(2,1)S(1)}, bf16[2,2,176,128]{3,2,1,0:T(8,128)(2,1)S(1)}, u32[]{:S(2)}, u32[]{:S(2)}) collective-permute-start(bf16[2,2,176,128]{3,2,1,0:T(8,128)(2,1)S(1)} %add_convert_fusion.4), channel_id=1, source_target_pairs={{0,12},{4,8},{8,4},{12,0},{1,13},{5,9},{9,5},{13,1},{2,14},{6,10},... | collective-permute-start | bytes 540680 | tf_op jit(solution)/shard_map/ppermute | solution.py:178
  70.0 7.1 %collective-permute-start.9 = (bf16[4,176,128]{2,1,0:T(8,128)(2,1)S(1)}, bf16[4,176,128]{2,1,0:T(8,128)(2,1)S(1)}, u32[]{:S(2)}, u32[]{:S(2)}) collective-permute-start(bf16[4,176,128]{2,1,0:T(8,128)(2,1)S(1)} %bitcast.21), channel_id=1, source_target_pairs={{0,12},{4,8},{8,4},{12,0},{1,13},{5,9},{9,5},{13,1},{2,14},{6,10},... | collective-permute-start | bytes 540680 | tf_op jit(solution)/shard_map/ppermute | solution.py:178
  75.4 7.2 %collective-permute-start.6 = (bf16[4,240,128]{2,1,0:T(8,128)(2,1)S(1)}, bf16[4,240,128]{2,1,0:T(8,128)(2,1)S(1)}, u32[]{:S(2)}, u32[]{:S(2)}) collective-permute-start(bf16[4,240,128]{2,1,0:T(8,128)(2,1)S(1)} %bitcast.17), channel_id=1, source_target_pairs={{0,4},{4,0},{8,12},{12,8},{1,5},{5,1},{9,13},{13,9},{2,6},{6,2},{1... | collective-permute-start | bytes 737288 | tf_op jit(solution)/shard_map/ppermute | solution.py:178
  75.5 7.1 %collective-permute-start.12 = (bf16[4,176,128]{2,1,0:T(8,128)(2,1)S(1)}, bf16[4,176,128]{2,1,0:T(8,128)(2,1)S(1)}, u32[]{:S(2)}, u32[]{:S(2)}) collective-permute-start(bf16[4,176,128]{2,1,0:T(8,128)(2,1)S(1)} %bitcast.27), channel_id=1, source_target_pairs={{0,2},{2,0},{1,3},{3,1},{4,6},{6,4},{5,7},{7,5},{8,10},{10,8},{9,1... | collective-permute-start | bytes 540680 | tf_op jit(solution)/shard_map/ppermute | solution.py:177
  82.7 3.2 %collective-permute-start.13 = (bf16[8,592,128]{2,1,0:T(8,128)(2,1)S(1)}, bf16[8,592,128]{2,1,0:T(8,128)(2,1)S(1)}, u32[]{:S(2)}, u32[]{:S(2)}) collective-permute-start(bf16[8,592,128]{2,1,0:T(8,128)(2,1)S(1)} %maximum_maximum_fusion.pieces_ref), channel_id=1, source_target_pairs={{0,1},{1,0},{2,3},{3,2},{4,5},{5,4},{6,7},{7,6},{8,9},{9,8},{10,11... | collective-permute-start | bytes 3637256 | tf_op jit(solution)/shard_map/ppermute | solution.py:341

commit v7 on v6

--- a/solution.py
+++ b/solution.py
@@ -24,8 +24,8 @@
 BELOW = LANES * BLOCKS * (BLOCKS - 1) // 2
 EDGE = 2 * BELOW + HALF
 PACKED = -(-(EDGE + BLOCKS) // (16 * CHIPS)) * 16 * CHIPS
-PIECES = (BELOW // CHIPS,) + ((PACKED - BELOW) // (2 * CHIPS),) * 2
-BASES = (0, BELOW, BELOW + CHIPS * PIECES[1])
+PIECES = (208, 192, 192)
+BASES = (0, CHIPS * PIECES[0], CHIPS * (PIECES[0] + PIECES[1]))
 MIB = 1 << 20
 
 CHIP_AXES = ("x", "yh")
@@ -69,21 +69,32 @@
     return [jax.ShapeDtypeStruct(shape, jnp.float32), jax.ShapeDtypeStruct(shape, kind)]
 
 
-def split_kernel(x_ref, out_ref):
-    for p in range(CHIPS):
-        for j in range(STRIPES):
-            out_ref[p, :, tile(j)] = x_ref[:, tile(TILES * j + p)]
-        for m in range(STRIPES // 2):
-            left = x_ref[:, tile(TILES * (2 * m) + CHIPS + p // 2)]
-            right = x_ref[:, tile(TILES * (2 * m + 1) + CHIPS + p // 2)]
-            out_ref[p, :, tile(STRIPES + m)] = halves(left, right, p % 2 == 0).astype(out_ref.dtype)
+def split_kernel(x_ref, out_ref, whole_ref, sems):
+    copies = [
+        pltpu.make_async_copy(x_ref.at[pl.ds(r, 16)], whole_ref.at[pl.ds(r, 16)], sems.at[r // 16])
+        for r in range(0, PANEL, 16)
+    ]
+    for copy in copies:
+        copy.start()
+    for r, copy in zip(range(0, PANEL, 16), copies):
+        copy.wait()
+        rows = pl.ds(r, 16)
+        for p in range(CHIPS):
+            for j in range(STRIPES):
+                out_ref[p, rows, tile(j)] = whole_ref[rows, tile(TILES * j + p)]
+            for m in range(STRIPES // 2):
+                left = whole_ref[rows, tile(TILES * (2 * m) + CHIPS + p // 2)]
+                right = whole_ref[rows, tile(TILES * (2 * m + 1) + CHIPS + p // 2)]
+                out_ref[p, rows, tile(STRIPES + m)] = halves(left, right, p % 2 == 0).astype(out_ref.dtype)
 
 
 def split_columns(x):
     return pl.pallas_call(
         split_kernel,
+        in_specs=[pl.BlockSpec(memory_space=pltpu.HBM)],
         out_shape=jax.ShapeDtypeStruct((CHIPS, PANEL, WIDTH), x.dtype),
-        compiler_params=pltpu.CompilerParams(vmem_limit_bytes=16 * MIB),
+        scratch_shapes=[pltpu.VMEM(x.shape, x.dtype), pltpu.SemaphoreType.DMA((PANEL // 16,))],
+        compiler_params=pltpu.CompilerParams(vmem_limit_bytes=57 * MIB),
         name="split_columns",
     )(x)
 
@@ -114,7 +125,7 @@
     return [lax.broadcasted_iota(jnp.int32, (LANES, LANES), axis) for axis in range(2)]
 
 
-def own_gram_kernel(own_ref, keep_ref, send_ref, diagonal_ref, whole_ref):
+def own_gram_kernel(own_ref, keep_ref, send_ref, rest_ref, diagonal_ref, whole_ref):
     def store_below(rows, value):
         whole_ref[rows, :] = value
 
@@ -123,12 +134,17 @@
 
     triangle(own_ref, own_ref, store_below, store_diagonal)
     split_pieces(0, whole_ref, 0, keep_ref, send_ref)
+    rest_ref[...] = whole_ref[pl.ds(BASES[1], BELOW - BASES[1]), :]
 
 
 def own_gram(own):
     return pl.pallas_call(
         own_gram_kernel,
-        out_shape=half_shapes(0, own.dtype) + [jax.ShapeDtypeStruct((BLOCKS, LANES, LANES), jnp.float32)],
+        out_shape=half_shapes(0, own.dtype)
+        + [
+            jax.ShapeDtypeStruct((BELOW - BASES[1], LANES), jnp.float32),
+            jax.ShapeDtypeStruct((BLOCKS, LANES, LANES), jnp.float32),
+        ],
         scratch_shapes=[pltpu.VMEM((BELOW, LANES), jnp.float32)],
         compiler_params=pltpu.CompilerParams(vmem_limit_bytes=8 * MIB),
         cost_estimate=pl.CostEstimate(
@@ -139,37 +155,38 @@
 
 
 def cross_gram_kernel(
-    diagonal_ref, own_ref, other_ref, keep_b_ref, send_b_ref, keep_c_ref, send_c_ref, whole_ref
+    rest_ref, diagonal_ref, own_ref, other_ref, keep_b_ref, send_b_ref, keep_c_ref, send_c_ref, whole_ref
 ):
+    start = BELOW - BASES[1]
+    whole_ref[pl.ds(0, start), :] = rest_ref[...]
     row, column = iotas()
     edges = []
 
     def store_below(rows, value):
-        whole_ref[rows, :] = value
+        whole_ref[pl.ds(start + rows.start, rows.size), :] = value
 
     def store_diagonal(j, value):
-        whole_ref[pl.ds(BELOW + j * LANES, LANES), :] = jnp.where(row >= column, diagonal_ref[j], value)
+        whole_ref[pl.ds(start + BELOW + j * LANES, LANES), :] = jnp.where(row >= column, diagonal_ref[j], value)
         edges.append(jnp.sum(jnp.where(row == column, value, 0.0), axis=0, keepdims=True))
 
     triangle(own_ref, other_ref, store_below, store_diagonal)
-    rest = PACKED - EDGE
-    edges.append(jnp.zeros((rest - BLOCKS, LANES), jnp.float32))
-    whole_ref[pl.ds(EDGE - BELOW, rest), :] = jnp.concatenate(edges)
-    split_pieces(1, whole_ref, BASES[1] - BELOW, keep_b_ref, send_b_ref)
-    split_pieces(2, whole_ref, BASES[2] - BELOW, keep_c_ref, send_c_ref)
-
-
-def cross_gram(diagonal, own, other):
+    edges.append(jnp.zeros((PACKED - EDGE - BLOCKS, LANES), jnp.float32))
+    whole_ref[pl.ds(EDGE - BASES[1], PACKED - EDGE), :] = jnp.concatenate(edges)
+    split_pieces(1, whole_ref, 0, keep_b_ref, send_b_ref)
+    split_pieces(2, whole_ref, BASES[2] - BASES[1], keep_c_ref, send_c_ref)
+
+
+def cross_gram(rest, diagonal, own, other):
     return pl.pallas_call(
         cross_gram_kernel,
         out_shape=half_shapes(1, own.dtype) + half_shapes(2, own.dtype),
-        scratch_shapes=[pltpu.VMEM((PACKED - BELOW, LANES), jnp.float32)],
+        scratch_shapes=[pltpu.VMEM((PACKED - BASES[1], LANES), jnp.float32)],
         compiler_params=pltpu.CompilerParams(vmem_limit_bytes=12 * MIB),
         cost_estimate=pl.CostEstimate(
             flops=2 * (BELOW + 3 * HALF) * LANES * WIDTH, bytes_accessed=4 * HALF * WIDTH, transcendentals=0
         ),
         name="cross_gram",
-    )(diagonal, own, other)
+    )(rest, diagonal, own, other)
 
 
 def exchange(value, axis):
@@ -345,9 +362,9 @@
     pieces = split_columns(iterate.reshape(PANEL, COLS))
     own = lax.all_to_all(pieces, CHIP_AXES, 0, 0, tiled=True).reshape(HALF, WIDTH)
     other = swap_cores(own)
-    keep_a, send_a, diagonal = own_gram(own)
+    keep_a, send_a, *rest = own_gram(own)
     arrived_a = exchange(send_a, ORDERS[0][0])
-    keep_b, send_b, keep_c, send_c = cross_gram(diagonal, own, other)
+    keep_b, send_b, keep_c, send_c = cross_gram(*rest, own, other)
     arrived = arrived_a, exchange(send_b, ORDERS[1][0]), exchange(send_c, ORDERS[2][0])
     arrived = lax.optimization_barrier(arrived)
     streams = [sum_over_chips(*stream) for stream in zip((keep_a, keep_b, keep_c), arrived, ORDERS)]

time: 138 us -> 137 us (level)
  Pallas kernels: 13.6 us -> 16.3 us
  waiting for transfers between devices: 25.9 us -> 23.7 us
  local copies, waits for them, and re-layouts: 1.66 us -> 0 us
    ppermute x8, waiting for transfers between devices: 11.7 us -> 7.7 us  [exchange(): lax.ppermute(value, 'x', [(i, i ^ 1 if axis == 'a' else 3 - i) for i in r...]
    pallas_call x1, Pallas kernels: 0.59 us -> 3.32 us  [split_columns(): pl.pallas_call(split_kernel, in_specs=[pl.BlockSpec(memory_space=pltpu.HB...]
    ppermute x4, waiting for transfers between devices: 10.2 us -> 12 us  [exchange(): return lax.ppermute(value, 'yh', [(0, 1), (1, 0)])]
    unnamed x2 -> x0, local copies, waits for them, and re-layouts: 1.66 us -> none
    ppermute x8, starting transfers between devices: 8.29 us -> 9.74 us  [exchange(): lax.ppermute(value, 'x', [(i, i ^ 1 if axis == 'a' else 3 - i) for i in r...]
  transfers between devices with their start and end apart: 14 -> 14, of which waited for: 9 -> 10; matrix products, arithmetic and copies ran while one was open for 0% -> 0% of each run, Pallas kernels for 3% -> 3%
where the time goes in v7:
time: 137 us
  blocking collectives  79.5 us (58%)
  waiting for transfers between devices  23.7 us (17%)
  Pallas kernels  16.3 us (12%)
  starting transfers between devices  16.2 us (12%)
    all_to_all x1, blocking collectives, shards(): received = lax.all_to_all(sent, ALL_CHIPS, 0, 0, tiled=True)  41.6 us
    all_to_all x1, blocking collectives, shards(): lax.all_to_all(pieces, CHIP_AXES, 0, 0, tiled=True).reshape(HALF, WIDTH)  37.9 us
    ppermute x4, waiting for transfers between devices, exchange(): return lax.ppermute(value, 'yh', [(0, 1), (1, 0)])  12 us
    ppermute x8, starting transfers between devices, exchange(): lax.ppermute(value, 'x', [(i, i ^ 1 if axis == 'a' else 3 - i) for i in r...  9.74 us
    ppermute x8, waiting for transfers between devices, exchange(): lax.ppermute(value, 'x', [(i, i ^ 1 if axis == 'a' else 3 - i) for i in r...  7.7 us
    pallas_call x1, Pallas kernels, update_rows(): pl.pallas_call(update_kernel, out_shape=jax.ShapeDtypeStruct((STRIPES, CH...  7.11 us
    ppermute x4, starting transfers between devices, exchange(): return lax.ppermute(value, 'yh', [(0, 1), (1, 0)])  6.17 us
    ppermute x2, waiting for transfers between devices, swap_cores(): return lax.ppermute(value, 'c', [(0, 1), (1, 0)])  4.06 us
  transfers between devices with their start and end apart: 14, of which 10 were waited for; matrix products, arithmetic and copies ran while one was open for 0% of the time, Pallas kernels for 3%

profile of v7, /device:TPU:0, one launch (start us, length us, event | category | flops | bytes accessed | tf_op | source)
XLA Modules:
  0.0 136.7 jit_solution(3913958298145793982)
XLA Ops:
  0.0 3.3 %split_columns.1 = bf16[8,96,1536]{2,1,0:T(8,128)(2,1)} custom-call(bf16[96,12288]{1,0:T(8,128)(2,1)} %bitcast.16), custom_call_target="tpu_custom_call" | custom-call | tf_op jit(solution)/shard_map/split_columns/pallas_call | solution.py:92
  3.3 37.9 %all_to_all.10 = bf16[8,96,1536]{2,1,0:T(8,128)(2,1)S(1)} all-to-all(bf16[8,96,1536]{2,1,0:T(8,128)(2,1)} %split_columns.1), channel_id=1, replica_groups=mesh['z'=4,'yl'=2,'x'=4,'yh'=2,'c'=2] {'x','yh'}, dimensions={0} | all-to-all | bytes 4718592 | tf_op jit(solution)/shard_map/all_to_all | solution.py:363
  41.2 0.0 collective-permute-start.1
  41.2 1.5 %own_gram.1 = (f32[4,208,128]{2,1,0:T(8,128)S(1)}, bf16[4,208,128]{2,1,0:T(8,128)(2,1)S(1)}, f32[256,128]{1,0:T(8,128)S(1)}, f32[6,128,128]{2,1,0:T(8,128)S(1)}) custom-call(bf16[768,1536]{1,0:T(8,128)(2,1)S(1)} %bitcast.12), custom_call_target="tpu_custom_call" | custom-call | flops 1660944384 | bytes 2359296 | tf_op jit(solution)/shard_map/own_gram/pallas_call | solution.py:141
  42.7 0.6 collective-permute-start
  43.3 2.5 %collective-permute-done.1.other_ref.x_other_ref = bf16[768,1536]{1,0:T(8,128)(2,1)S(1)} collective-permute-done((bf16[768,1536]{1,0:T(8,128)(2,1)S(1)}, bf16[768,1536]{1,0:T(8,128)(2,1)S(1)}, u32[]{:S(2)}, u32[]{:S(2)}) %collective-permute-start.1) | collective-permute-done | bytes 2359328 | tf_op jit(solution)/shard_map/ppermute | solution.py:358
  45.8 1.5 %cross_gram.1 = (f32[4,192,128]{2,1,0:T(8,128)S(1)}, bf16[4,192,128]{2,1,0:T(8,128)(2,1)S(1)}, f32[4,192,128]{2,1,0:T(8,128)S(1)}, bf16[4,192,128]{2,1,0:T(8,128)(2,1)S(1)}) custom-call(f32[256,128]{1,0:T(8,128)S(1)} %get-tuple-element.21.rest_ref, f32[6,128,128]{2,1,0:T(8,128)S(1)} %get-tuple-element.22.diagonal_ref, bf16[768,1536]{1,0:T(8,128)(2,1)S(1)} %bitcast.13, ...), custom_call_target="tpu_custom_call" | custom-call | flops 1660944384 | bytes 4718592 | tf_op jit(solution)/shard_map/cross_gram/pallas_call | solution.py:180
  47.3 1.5 %collective-permute-start.2 = (bf16[4,192,128]{2,1,0:T(8,128)(2,1)S(1)}, bf16[4,192,128]{2,1,0:T(8,128)(2,1)S(1)}, u32[]{:S(2)}, u32[]{:S(2)}) collective-permute-start(bf16[4,192,128]{2,1,0:T(8,128)(2,1)S(1)} %get-tuple-element.23), channel_id=1, source_target_pairs={{0,12},{4,8},{8,4},{12,0},{1,13},{5,9},{9,5},{13,1},{2,14},{6,10},... | collective-permute-start | bytes 589832 | tf_op jit(solution)/shard_map/ppermute | solution.py:195
  48.8 1.3 collective-permute-start.3
  50.1 0.4 collective-permute-done
  50.5 5.1 %collective-permute-done.2 = bf16[4,192,128]{2,1,0:T(8,128)(2,1)S(1)} collective-permute-done((bf16[4,192,128]{2,1,0:T(8,128)(2,1)S(1)}, bf16[4,192,128]{2,1,0:T(8,128)(2,1)S(1)}, u32[]{:S(2)}, u32[]{:S(2)}) %collective-permute-start.2) | collective-permute-done | bytes 196640 | tf_op jit(solution)/shard_map/ppermute | solution.py:195
  55.5 1.4 %collective-permute-done.3 = bf16[4,192,128]{2,1,0:T(8,128)(2,1)S(1)} collective-permute-done((bf16[4,192,128]{2,1,0:T(8,128)(2,1)S(1)}, bf16[4,192,128]{2,1,0:T(8,128)(2,1)S(1)}, u32[]{:S(2)}, u32[]{:S(2)}) %collective-permute-start.3) | collective-permute-done | bytes 196640 | tf_op jit(solution)/shard_map/ppermute | solution.py:194
  57.0 1.3 collective-permute-start.7
  58.4 0.1 collective-permute-start.10
  58.6 2.2 %collective-permute-start.4 = (bf16[2,2,208,128]{3,2,1,0:T(8,128)(2,1)S(1)}, bf16[2,2,208,128]{3,2,1,0:T(8,128)(2,1)S(1)}, u32[]{:S(2)}, u32[]{:S(2)}) collective-permute-start(bf16[2,2,208,128]{3,2,1,0:T(8,128)(2,1)S(1)} %bitcast.19), channel_id=1, source_target_pairs={{0,12},{4,8},{8,4},{12,0},{1,13},{5,9},{9,5},{13,1},{2,14},{6,10},... | collective-permute-start | bytes 638984 | tf_op jit(solution)/shard_map/ppermute | solution.py:195
  60.8 3.6 %collective-permute-done.7 = bf16[2,2,192,128]{3,2,1,0:T(8,128)(2,1)S(1)} collective-permute-done((bf16[2,2,192,128]{3,2,1,0:T(8,128)(2,1)S(1)}, bf16[2,2,192,128]{3,2,1,0:T(8,128)(2,1)S(1)}, u32[]{:S(2)}, u32[]{:S(2)}) %collective-permute-start.7) | collective-permute-done | bytes 196640 | tf_op jit(solution)/shard_map/ppermute | solution.py:194
  64.5 0.4 collective-permute-start.8
  64.9 0.0 collective-permute-done.10
  65.0 1.6 %collective-permute-start.11 = (bf16[2,2,192,128]{3,2,1,0:T(8,128)(2,1)S(1)}, bf16[2,2,192,128]{3,2,1,0:T(8,128)(2,1)S(1)}, u32[]{:S(2)}, u32[]{:S(2)}) collective-permute-start(bf16[2,2,192,128]{3,2,1,0:T(8,128)(2,1)S(1)} %add_convert_fusion.4), channel_id=1, source_target_pairs={{0,12},{4,8},{8,4},{12,0},{1,13},{5,9},{9,5},{13,1},{2,14},{6,10},... | collective-permute-start | bytes 589832 | tf_op jit(solution)/shard_map/ppermute | solution.py:195
  66.6 0.0 collective-permute-done.4
  66.7 1.9 %collective-permute-start.5 = (bf16[2,2,208,128]{3,2,1,0:T(8,128)(2,1)S(1)}, bf16[2,2,208,128]{3,2,1,0:T(8,128)(2,1)S(1)}, u32[]{:S(2)}, u32[]{:S(2)}) collective-permute-start(bf16[2,2,208,128]{3,2,1,0:T(8,128)(2,1)S(1)} %add_convert_fusion.1), channel_id=1, source_target_pairs={{0,2},{2,0},{1,3},{3,1},{4,6},{6,4},{5,7},{7,5},{8,10},{10,8},{9,1... | collective-permute-start | bytes 638984 | tf_op jit(solution)/shard_map/ppermute | solution.py:194
  68.6 1.7 %collective-permute-done.8 = bf16[2,2,192,128]{3,2,1,0:T(8,128)(2,1)S(1)} collective-permute-done((bf16[2,2,192,128]{3,2,1,0:T(8,128)(2,1)S(1)}, bf16[2,2,192,128]{3,2,1,0:T(8,128)(2,1)S(1)}, u32[]{:S(2)}, u32[]{:S(2)}) %collective-permute-start.8) | collective-permute-done | bytes 196640 | tf_op jit(solution)/shard_map/ppermute | solution.py:195
  70.3 1.9 %collective-permute-start.9 = (bf16[4,192,128]{2,1,0:T(8,128)(2,1)S(1)}, bf16[4,192,128]{2,1,0:T(8,128)(2,1)S(1)}, u32[]{:S(2)}, u32[]{:S(2)}) collective-permute-start(bf16[4,192,128]{2,1,0:T(8,128)(2,1)S(1)} %bitcast.21), channel_id=1, source_target_pairs={{0,12},{4,8},{8,4},{12,0},{1,13},{5,9},{9,5},{13,1},{2,14},{6,10},... | collective-permute-start | bytes 589832 | tf_op jit(solution)/shard_map/ppermute | solution.py:195
  72.2 0.6 collective-permute-done.11
  72.8 1.3 collective-permute-done.5
  74.2 1.5 %collective-permute-start.6 = (bf16[4,208,128]{2,1,0:T(8,128)(2,1)S(1)}, bf16[4,208,128]{2,1,0:T(8,128)(2,1)S(1)}, u32[]{:S(2)}, u32[]{:S(2)}) collective-permute-start(bf16[4,208,128]{2,1,0:T(8,128)(2,1)S(1)} %bitcast.17), channel_id=1, source_target_pairs={{0,4},{4,0},{8,12},{12,8},{1,5},{5,1},{9,13},{13,9},{2,6},{6,2},{1... | collective-permute-start | bytes 638984 | tf_op jit(solution)/shard_map/ppermute | solution.py:195
  75.7 1.6 %collective-permute-start.12 = (bf16[4,192,128]{2,1,0:T(8,128)(2,1)S(1)}, bf16[4,192,128]{2,1,0:T(8,128)(2,1)S(1)}, u32[]{:S(2)}, u32[]{:S(2)}) collective-permute-start(bf16[4,192,128]{2,1,0:T(8,128)(2,1)S(1)} %bitcast.23), channel_id=1, source_target_pairs={{0,2},{2,0},{1,3},{3,1},{4,6},{6,4},{5,7},{7,5},{8,10},{10,8},{9,1... | collective-permute-start | bytes 589832 | tf_op jit(solution)/shard_map/ppermute | solution.py:194
  77.3 0.0 collective-permute-done.9
  77.4 5.6 %collective-permute-done.12 = bf16[4,192,128]{2,1,0:T(8,128)(2,1)S(1)} collective-permute-done((bf16[4,192,128]{2,1,0:T(8,128)(2,1)S(1)}, bf16[4,192,128]{2,1,0:T(8,128)(2,1)S(1)}, u32[]{:S(2)}, u32[]{:S(2)}) %collective-permute-start.12) | collective-permute-done | bytes 196640 | tf_op jit(solution)/shard_map/ppermute | solution.py:194
  83.0 0.0 collective-permute-done.6
  83.0 0.1 maximum_maximum_fusion.pieces_ref
  83.1 0.3 collective-permute-start.13
  83.3 1.3 own_square.1
  84.6 1.6 %collective-permute-done.13.pieces_ref = bf16[8,592,128]{2,1,0:T(8,128)(2,1)S(1)} collective-permute-done((bf16[8,592,128]{2,1,0:T(8,128)(2,1)S(1)}, bf16[8,592,128]{2,1,0:T(8,128)(2,1)S(1)}, u32[]{:S(2)}, u32[]{:S(2)}) %collective-permute-start.13) | collective-permute-done | bytes 1212448 | tf_op jit(solution)/shard_map/ppermute | solution.py:358
  86.2 7.1 %update_rows.1 = bf16[8,8,144,128]{3,2,1,0:T(8,128)(2,1)S(1)} custom-call(bf16[4736,128]{1,0:T(8,128)(2,1)S(1)} %get-tuple-element.30.own_ref, bf16[8,592,128]{2,1,0:T(8,128)(2,1)S(1)} %collective-permute-done.13.pieces_ref, bf16[768,768]{1,0:T(8,128)(2,1)S(1)} %get-tuple-element.31.gram_ref, f32[768,768]{1,0:T(8,128)S(1)} %get-tuple-element.32.square_ref, ...), custom_call_target="tpu_custom_call" | custom-call | flops 6341787648 | bytes 11796480 | tf_op jit(solution)/shard_map/update_rows/pallas_call | solution.py:310
  93.3 41.6 %all_to_all.11 = bf16[64,144,128]{2,1,0:T(8,128)(2,1)S(1)} all-to-all(bf16[64,144,128]{2,1,0:T(8,128)(2,1)S(1)} %bitcast.15), channel_id=1, replica_groups=mesh['z'=4,'yl'=2,'x'=4,'yh'=2,'c'=2] {'z','yl','x','yh'}, dimensions={0} | all-to-all | bytes 4718592 | tf_op jit(solution)/shard_map/all_to_all | solution.py:376
  134.9 1.6 %join_columns.1 = bf16[8,96,1536]{2,1,0:T(8,128)(2,1)} custom-call(bf16[8,8,144,128]{3,2,1,0:T(8,128)(2,1)S(1)} %bitcast.10), custom_call_target="tpu_custom_call" | custom-call | tf_op jit(solution)/shard_map/join_columns/pallas_call | solution.py:346
  (15 shorter events, 0.6 us)
Async XLA Ops:
  41.2 4.5 %collective-permute-start.1 = (bf16[768,1536]{1,0:T(8,128)(2,1)S(1)}, bf16[768,1536]{1,0:T(8,128)(2,1)S(1)}, u32[]{:S(2)}, u32[]{:S(2)}) collective-permute-start(bf16[768,1536]{1,0:T(8,128)(2,1)S(1)} %bitcast.11), channel_id=1, source_target_pairs={{0,1},{1,0},{2,3},{3,2},{4,5},{5,4},{6,7},{7,6},{8,9},{9,8},{10,11... | collective-permute-start | bytes 7077896 | tf_op jit(solution)/shard_map/ppermute | solution.py:358
  42.7 7.7 %collective-permute-start = (bf16[4,208,128]{2,1,0:T(8,128)(2,1)S(1)}, bf16[4,208,128]{2,1,0:T(8,128)(2,1)S(1)}, u32[]{:S(2)}, u32[]{:S(2)}) collective-permute-start(bf16[4,208,128]{2,1,0:T(8,128)(2,1)S(1)} %get-tuple-element.20), channel_id=1, source_target_pairs={{0,4},{4,0},{8,12},{12,8},{1,5},{5,1},{9,13},{13,9},{2,6},{6,2},{1... | collective-permute-start | bytes 638984 | tf_op jit(solution)/shard_map/ppermute | solution.py:195
  47.3 8.2 %collective-permute-start.2 = (bf16[4,192,128]{2,1,0:T(8,128)(2,1)S(1)}, bf16[4,192,128]{2,1,0:T(8,128)(2,1)S(1)}, u32[]{:S(2)}, u32[]{:S(2)}) collective-permute-start(bf16[4,192,128]{2,1,0:T(8,128)(2,1)S(1)} %get-tuple-element.23), channel_id=1, source_target_pairs={{0,12},{4,8},{8,4},{12,0},{1,13},{5,9},{9,5},{13,1},{2,14},{6,10},... | collective-permute-start | bytes 589832 | tf_op jit(solution)/shard_map/ppermute | solution.py:195
  48.8 8.2 %collective-permute-start.3 = (bf16[4,192,128]{2,1,0:T(8,128)(2,1)S(1)}, bf16[4,192,128]{2,1,0:T(8,128)(2,1)S(1)}, u32[]{:S(2)}, u32[]{:S(2)}) collective-permute-start(bf16[4,192,128]{2,1,0:T(8,128)(2,1)S(1)} %get-tuple-element.24), channel_id=1, source_target_pairs={{0,2},{2,0},{1,3},{3,1},{4,6},{6,4},{5,7},{7,5},{8,10},{10,8},{9,1... | collective-permute-start | bytes 589832 | tf_op jit(solution)/shard_map/ppermute | solution.py:194
  57.0 7.4 %collective-permute-start.7 = (bf16[2,2,192,128]{3,2,1,0:T(8,128)(2,1)S(1)}, bf16[2,2,192,128]{3,2,1,0:T(8,128)(2,1)S(1)}, u32[]{:S(2)}, u32[]{:S(2)}) collective-permute-start(bf16[2,2,192,128]{3,2,1,0:T(8,128)(2,1)S(1)} %bitcast.27), channel_id=1, source_target_pairs={{0,2},{2,0},{1,3},{3,1},{4,6},{6,4},{5,7},{7,5},{8,10},{10,8},{9,1... | collective-permute-start | bytes 589832 | tf_op jit(solution)/shard_map/ppermute | solution.py:194
  58.4 6.5 %collective-permute-start.10 = (bf16[2,2,192,128]{3,2,1,0:T(8,128)(2,1)S(1)}, bf16[2,2,192,128]{3,2,1,0:T(8,128)(2,1)S(1)}, u32[]{:S(2)}, u32[]{:S(2)}) collective-permute-start(bf16[2,2,192,128]{3,2,1,0:T(8,128)(2,1)S(1)} %bitcast.25), channel_id=1, source_target_pairs={{0,4},{4,0},{8,12},{12,8},{1,5},{5,1},{9,13},{13,9},{2,6},{6,2},{1... | collective-permute-start | bytes 589832 | tf_op jit(solution)/shard_map/ppermute | solution.py:195
  58.6 8.0 %collective-permute-start.4 = (bf16[2,2,208,128]{3,2,1,0:T(8,128)(2,1)S(1)}, bf16[2,2,208,128]{3,2,1,0:T(8,128)(2,1)S(1)}, u32[]{:S(2)}, u32[]{:S(2)}) collective-permute-start(bf16[2,2,208,128]{3,2,1,0:T(8,128)(2,1)S(1)} %bitcast.19), channel_id=1, source_target_pairs={{0,12},{4,8},{8,4},{12,0},{1,13},{5,9},{9,5},{13,1},{2,14},{6,10},... | collective-permute-start | bytes 638984 | tf_op jit(solution)/shard_map/ppermute | solution.py:195
  64.5 5.7 %collective-permute-start.8 = (bf16[2,2,192,128]{3,2,1,0:T(8,128)(2,1)S(1)}, bf16[2,2,192,128]{3,2,1,0:T(8,128)(2,1)S(1)}, u32[]{:S(2)}, u32[]{:S(2)}) collective-permute-start(bf16[2,2,192,128]{3,2,1,0:T(8,128)(2,1)S(1)} %add_convert_fusion.7), channel_id=1, source_target_pairs={{0,4},{4,0},{8,12},{12,8},{1,5},{5,1},{9,13},{13,9},{2,6},{6,2},{1... | collective-permute-start | bytes 589832 | tf_op jit(solution)/shard_map/ppermute | solution.py:195
  65.0 7.8 %collective-permute-start.11 = (bf16[2,2,192,128]{3,2,1,0:T(8,128)(2,1)S(1)}, bf16[2,2,192,128]{3,2,1,0:T(8,128)(2,1)S(1)}, u32[]{:S(2)}, u32[]{:S(2)}) collective-permute-start(bf16[2,2,192,128]{3,2,1,0:T(8,128)(2,1)S(1)} %add_convert_fusion.4), channel_id=1, source_target_pairs={{0,12},{4,8},{8,4},{12,0},{1,13},{5,9},{9,5},{13,1},{2,14},{6,10},... | collective-permute-start | bytes 589832 | tf_op jit(solution)/shard_map/ppermute | solution.py:195
  66.7 7.4 %collective-permute-start.5 = (bf16[2,2,208,128]{3,2,1,0:T(8,128)(2,1)S(1)}, bf16[2,2,208,128]{3,2,1,0:T(8,128)(2,1)S(1)}, u32[]{:S(2)}, u32[]{:S(2)}) collective-permute-start(bf16[2,2,208,128]{3,2,1,0:T(8,128)(2,1)S(1)} %add_convert_fusion.1), channel_id=1, source_target_pairs={{0,2},{2,0},{1,3},{3,1},{4,6},{6,4},{5,7},{7,5},{8,10},{10,8},{9,1... | collective-permute-start | bytes 638984 | tf_op jit(solution)/shard_map/ppermute | solution.py:194
  70.3 7.0 %collective-permute-start.9 = (bf16[4,192,128]{2,1,0:T(8,128)(2,1)S(1)}, bf16[4,192,128]{2,1,0:T(8,128)(2,1)S(1)}, u32[]{:S(2)}, u32[]{:S(2)}) collective-permute-start(bf16[4,192,128]{2,1,0:T(8,128)(2,1)S(1)} %bitcast.21), channel_id=1, source_target_pairs={{0,12},{4,8},{8,4},{12,0},{1,13},{5,9},{9,5},{13,1},{2,14},{6,10},... | collective-permute-start | bytes 589832 | tf_op jit(solution)/shard_map/ppermute | solution.py:195
  74.2 8.8 %collective-permute-start.6 = (bf16[4,208,128]{2,1,0:T(8,128)(2,1)S(1)}, bf16[4,208,128]{2,1,0:T(8,128)(2,1)S(1)}, u32[]{:S(2)}, u32[]{:S(2)}) collective-permute-start(bf16[4,208,128]{2,1,0:T(8,128)(2,1)S(1)} %bitcast.17), channel_id=1, source_target_pairs={{0,4},{4,0},{8,12},{12,8},{1,5},{5,1},{9,13},{13,9},{2,6},{6,2},{1... | collective-permute-start | bytes 638984 | tf_op jit(solution)/shard_map/ppermute | solution.py:195
  75.7 7.3 %collective-permute-start.12 = (bf16[4,192,128]{2,1,0:T(8,128)(2,1)S(1)}, bf16[4,192,128]{2,1,0:T(8,128)(2,1)S(1)}, u32[]{:S(2)}, u32[]{:S(2)}) collective-permute-start(bf16[4,192,128]{2,1,0:T(8,128)(2,1)S(1)} %bitcast.23), channel_id=1, source_target_pairs={{0,2},{2,0},{1,3},{3,1},{4,6},{6,4},{5,7},{7,5},{8,10},{10,8},{9,1... | collective-permute-start | bytes 589832 | tf_op jit(solution)/shard_map/ppermute | solution.py:194
  83.1 3.2 %collective-permute-start.13 = (bf16[8,592,128]{2,1,0:T(8,128)(2,1)S(1)}, bf16[8,592,128]{2,1,0:T(8,128)(2,1)S(1)}, u32[]{:S(2)}, u32[]{:S(2)}) collective-permute-start(bf16[8,592,128]{2,1,0:T(8,128)(2,1)S(1)} %maximum_maximum_fusion.pieces_ref), channel_id=1, source_target_pairs={{0,1},{1,0},{2,3},{3,2},{4,5},{5,4},{6,7},{7,6},{8,9},{9,8},{10,11... | collective-permute-start | bytes 3637256 | tf_op jit(solution)/shard_map/ppermute | solution.py:358

commit v8 on v7

--- a/solution.py
+++ b/solution.py
@@ -30,7 +30,7 @@
 
 CHIP_AXES = ("x", "yh")
 ALL_CHIPS = ("z", "yl", "x", "yh")
-ORDERS = ("abd", "bda", "dab")
+ORDERS = (("abd", "bda", "dab"), ("bda", "dab", "abd"))
 
 
 def halves(a, b, first):
@@ -45,23 +45,23 @@
     return pl.ds(index * LANES, LANES)
 
 
-def place(stream):
+def place(stream, core):
     x, d = lax.axis_index("x"), lax.axis_index("yh")
     bit = {"a": lax.rem((x + 1) // 2, 2), "b": x // 2, "d": d}
-    first, second, third = (bit[axis] for axis in ORDERS[stream])
-    return 4 * first + 2 * second + third
-
-
-def piece_rows(stream, position, base=0):
-    piece = lax.bitwise_xor(place(stream), position)
+    places = [4 * bit[i] + 2 * bit[j] + bit[k] for i, j, k in (orders[stream] for orders in ORDERS)]
+    return places[0] + core * (places[1] - places[0])
+
+
+def piece_rows(stream, position, base, core):
+    piece = lax.bitwise_xor(place(stream, core), position)
     return pl.ds(base + pl.multiple_of(piece * PIECES[stream], 16), PIECES[stream])
 
 
 def split_pieces(stream, whole_ref, base, keep_ref, send_ref):
-    half = CHIPS // 2
+    half, core = CHIPS // 2, lax.axis_index("c")
     for k in range(half):
-        keep_ref[k] = whole_ref[piece_rows(stream, k, base), :]
-        send_ref[k] = whole_ref[piece_rows(stream, k + half, base), :].astype(send_ref.dtype)
+        keep_ref[k] = whole_ref[piece_rows(stream, k, base, core), :]
+        send_ref[k] = whole_ref[piece_rows(stream, k + half, base, core), :].astype(send_ref.dtype)
 
 
 def half_shapes(stream, kind):
@@ -69,32 +69,21 @@
     return [jax.ShapeDtypeStruct(shape, jnp.float32), jax.ShapeDtypeStruct(shape, kind)]
 
 
-def split_kernel(x_ref, out_ref, whole_ref, sems):
-    copies = [
-        pltpu.make_async_copy(x_ref.at[pl.ds(r, 16)], whole_ref.at[pl.ds(r, 16)], sems.at[r // 16])
-        for r in range(0, PANEL, 16)
-    ]
-    for copy in copies:
-        copy.start()
-    for r, copy in zip(range(0, PANEL, 16), copies):
-        copy.wait()
-        rows = pl.ds(r, 16)
-        for p in range(CHIPS):
-            for j in range(STRIPES):
-                out_ref[p, rows, tile(j)] = whole_ref[rows, tile(TILES * j + p)]
-            for m in range(STRIPES // 2):
-                left = whole_ref[rows, tile(TILES * (2 * m) + CHIPS + p // 2)]
-                right = whole_ref[rows, tile(TILES * (2 * m + 1) + CHIPS + p // 2)]
-                out_ref[p, rows, tile(STRIPES + m)] = halves(left, right, p % 2 == 0).astype(out_ref.dtype)
+def split_kernel(x_ref, out_ref):
+    for p in range(CHIPS):
+        for j in range(STRIPES):
+            out_ref[p, :, tile(j)] = x_ref[:, tile(TILES * j + p)]
+        for m in range(STRIPES // 2):
+            left = x_ref[:, tile(TILES * (2 * m) + CHIPS + p // 2)]
+            right = x_ref[:, tile(TILES * (2 * m + 1) + CHIPS + p // 2)]
+            out_ref[p, :, tile(STRIPES + m)] = halves(left, right, p % 2 == 0).astype(out_ref.dtype)
 
 
 def split_columns(x):
     return pl.pallas_call(
         split_kernel,
-        in_specs=[pl.BlockSpec(memory_space=pltpu.HBM)],
         out_shape=jax.ShapeDtypeStruct((CHIPS, PANEL, WIDTH), x.dtype),
-        scratch_shapes=[pltpu.VMEM(x.shape, x.dtype), pltpu.SemaphoreType.DMA((PANEL // 16,))],
-        compiler_params=pltpu.CompilerParams(vmem_limit_bytes=57 * MIB),
+        compiler_params=pltpu.CompilerParams(vmem_limit_bytes=16 * MIB),
         name="split_columns",
     )(x)
 
@@ -189,29 +178,34 @@
     )(rest, diagonal, own, other)
 
 
-def exchange(value, axis):
-    if axis == "d":
-        return lax.ppermute(value, "yh", [(0, 1), (1, 0)])
-    return lax.ppermute(value, "x", [(i, i ^ 1 if axis == "a" else 3 - i) for i in range(4)])
+def exchange(value, stream, hop):
+    pairs = []
+    for x in range(4):
+        for d in range(2):
+            for core in range(2):
+                axis = ORDERS[core][stream][hop]
+                to = {"a": (x ^ 1, d), "b": (3 - x, d), "d": (x, 1 - d)}[axis]
+                pairs.append((4 * x + 2 * d + core, 4 * to[0] + 2 * to[1] + core))
+    return lax.ppermute(value, ("x", "yh", "c"), pairs)
 
 
 def wide(value):
     return value.astype(jnp.float32)
 
 
-def sum_over_chips(keep, arrived, order):
+def sum_over_chips(stream, keep, arrived):
     kind = arrived.dtype
     half = (keep + wide(arrived)).astype(kind).reshape(2, 2, *keep.shape[1:])
-    half = (wide(half) + wide(exchange(half, order[1]))[::-1]).astype(kind)
-    half = (wide(half) + wide(exchange(half, order[2]))[:, ::-1]).astype(kind).reshape(arrived.shape)
-    return jnp.concatenate([half, exchange(half, order[0])])
-
-
-def unpermute(pieces_ref, packed_ref):
+    half = (wide(half) + wide(exchange(half, stream, 1))[::-1]).astype(kind)
+    half = (wide(half) + wide(exchange(half, stream, 2))[:, ::-1]).astype(kind).reshape(arrived.shape)
+    return jnp.concatenate([half, exchange(half, stream, 0)])
+
+
+def unpermute(pieces_ref, packed_ref, core):
     first = 0
     for s, rows in enumerate(PIECES):
         for k in range(CHIPS):
-            packed_ref[piece_rows(s, k, BASES[s]), :] = pieces_ref[k, pl.ds(first, rows), :]
+            packed_ref[piece_rows(s, k, BASES[s], core), :] = pieces_ref[k, pl.ds(first, rows), :]
         first += rows
 
 
@@ -228,7 +222,7 @@
 
 def own_square_kernel(pieces_ref, packed_ref, gram_ref, square_ref):
     row, column = iotas()
-    unpermute(pieces_ref, packed_ref)
+    unpermute(pieces_ref, packed_ref, lax.axis_index("c"))
     mirror(packed_ref, gram_ref, row >= column)
     for n in range(0, HALF, 256):
         columns = pl.ds(n, 256)
@@ -272,7 +266,7 @@
     scale = math.sqrt(max(ROWS, COLS))
     step = 256
     row, column = iotas()
-    unpermute(pieces_ref, other_ref)
+    unpermute(pieces_ref, other_ref, 1 - lax.axis_index("c"))
     unpack_cross(own_ref, other_ref, cross_ref)
     mirror(other_ref, gram_other_ref, row >= column)
     for n in range(0, HALF, step):
@@ -363,11 +357,12 @@
     own = lax.all_to_all(pieces, CHIP_AXES, 0, 0, tiled=True).reshape(HALF, WIDTH)
     other = swap_cores(own)
     keep_a, send_a, *rest = own_gram(own)
-    arrived_a = exchange(send_a, ORDERS[0][0])
+    arrived_a = exchange(send_a, 0, 0)
     keep_b, send_b, keep_c, send_c = cross_gram(*rest, own, other)
-    arrived = arrived_a, exchange(send_b, ORDERS[1][0]), exchange(send_c, ORDERS[2][0])
-    arrived = lax.optimization_barrier(arrived)
-    streams = [sum_over_chips(*stream) for stream in zip((keep_a, keep_b, keep_c), arrived, ORDERS)]
+    arrived_b, arrived_c = exchange(send_b, 1, 0), exchange(send_c, 2, 0)
+    arrived_a, arrived_b = lax.optimization_barrier((arrived_a, arrived_b))
+    first_hops = (keep_a, arrived_a), (keep_b, arrived_b), (keep_c, arrived_c)
+    streams = [sum_over_chips(s, *pair) for s, pair in enumerate(first_hops)]
     pieces = jnp.concatenate(streams, axis=1)
     pieces_other = swap_cores(pieces)
     packed, gram, square = own_square(pieces)

time: 137 us -> 136 us (level)
  Pallas kernels: 16.3 us -> 13.6 us
  local copies, waits for them, and re-layouts: 0 us -> 1.66 us
    pallas_call x1, Pallas kernels: 3.32 us -> 0.59 us  [split_columns(): pl.pallas_call(split_kernel, out_shape=jax.ShapeDtypeStruct((CHIPS, PANEL...]
    unnamed x0 -> x2, local copies, waits for them, and re-layouts: none -> 1.66 us
  transfers between devices with their start and end apart: 14 -> 14, of which waited for: 10 -> 9; matrix products, arithmetic and copies ran while one was open for 0% -> 0% of each run, Pallas kernels for 3% -> 3%
where the time goes in v8:
time: 136 us; the launch traced here: 135 us
  blocking collectives  79.8 us (59%)
  waiting for transfers between devices  23.3 us (17%)
  starting transfers between devices  16.1 us (12%)
  Pallas kernels  13.6 us (10%)
  local copies, waits for them, and re-layouts  1.66 us (1%)
    all_to_all x1, blocking collectives, shards(): received = lax.all_to_all(sent, ALL_CHIPS, 0, 0, tiled=True)  42.1 us
    all_to_all x1, blocking collectives, shards(): lax.all_to_all(pieces, CHIP_AXES, 0, 0, tiled=True).reshape(HALF, WIDTH)  37.7 us
    ppermute x12, waiting for transfers between devices, exchange(): return lax.ppermute(value, ('x', 'yh', 'c'), pairs)  19.2 us
    ppermute x12, starting transfers between devices, exchange(): return lax.ppermute(value, ('x', 'yh', 'c'), pairs)  15.8 us
    pallas_call x1, Pallas kernels, update_rows(): pl.pallas_call(update_kernel, out_shape=jax.ShapeDtypeStruct((STRIPES, CH...  7.11 us
    ppermute x2, waiting for transfers between devices, swap_cores(): return lax.ppermute(value, 'c', [(0, 1), (1, 0)])  4.05 us
  transfers between devices with their start and end apart: 14, of which 9 were waited for; matrix products, arithmetic and copies ran while one was open for 0% of the time, Pallas kernels for 3%

profile of v8, /device:TPU:0, one launch (start us, length us, event | category | flops | bytes accessed | tf_op | source)
XLA Modules:
  0.0 135.3 jit_solution(1357176364218548624)
XLA Ops:
  0.0 0.0 copy-start
  0.0 1.7 %copy-done = bf16[1,96,12288]{2,1,0:T(8,128)(2,1)S(1)} copy-done((bf16[1,96,12288]{2,1,0:T(8,128)(2,1)S(1)}, bf16[1,96,12288]{2,1,0:T(8,128)(2,1)}, u32[]{:S(2)}) %copy-start) | copy-done | bytes 2359320
  1.7 0.6 split_columns.1
  2.3 37.7 %all_to_all.10 = bf16[8,96,1536]{2,1,0:T(8,128)(2,1)S(1)} all-to-all(bf16[8,96,1536]{2,1,0:T(8,128)(2,1)S(1)} %split_columns.1), channel_id=1, replica_groups=mesh['z'=4,'yl'=2,'x'=4,'yh'=2,'c'=2] {'x','yh'}, dimensions={0} | all-to-all | bytes 4718592 | tf_op jit(solution)/shard_map/all_to_all | solution.py:357
  40.0 0.0 collective-permute-start.1
  40.0 1.5 %own_gram.1 = (f32[4,208,128]{2,1,0:T(8,128)S(1)}, bf16[4,208,128]{2,1,0:T(8,128)(2,1)S(1)}, f32[256,128]{1,0:T(8,128)S(1)}, f32[6,128,128]{2,1,0:T(8,128)S(1)}) custom-call(bf16[768,1536]{1,0:T(8,128)(2,1)S(1)} %bitcast.13), custom_call_target="tpu_custom_call" | custom-call | flops 1660944384 | bytes 2359296 | tf_op jit(solution)/shard_map/own_gram/pallas_call | solution.py:130
  41.4 0.6 collective-permute-start
  42.0 2.5 %collective-permute-done.1.other_ref.x_other_ref = bf16[768,1536]{1,0:T(8,128)(2,1)S(1)} collective-permute-done((bf16[768,1536]{1,0:T(8,128)(2,1)S(1)}, bf16[768,1536]{1,0:T(8,128)(2,1)S(1)}, u32[]{:S(2)}, u32[]{:S(2)}) %collective-permute-start.1) | collective-permute-done | bytes 2359328 | tf_op jit(solution)/shard_map/ppermute | solution.py:352
  44.5 1.5 %cross_gram.1 = (f32[4,192,128]{2,1,0:T(8,128)S(1)}, bf16[4,192,128]{2,1,0:T(8,128)(2,1)S(1)}, f32[4,192,128]{2,1,0:T(8,128)S(1)}, bf16[4,192,128]{2,1,0:T(8,128)(2,1)S(1)}) custom-call(f32[256,128]{1,0:T(8,128)S(1)} %get-tuple-element.20.rest_ref, f32[6,128,128]{2,1,0:T(8,128)S(1)} %get-tuple-element.21.diagonal_ref, bf16[768,1536]{1,0:T(8,128)(2,1)S(1)} %bitcast.14, ...), custom_call_target="tpu_custom_call" | custom-call | flops 1660944384 | bytes 4718592 | tf_op jit(solution)/shard_map/cross_gram/pallas_call | solution.py:169
  46.0 1.5 %collective-permute-start.2 = (bf16[4,192,128]{2,1,0:T(8,128)(2,1)S(1)}, bf16[4,192,128]{2,1,0:T(8,128)(2,1)S(1)}, u32[]{:S(2)}, u32[]{:S(2)}) collective-permute-start(bf16[4,192,128]{2,1,0:T(8,128)(2,1)S(1)} %get-tuple-element.22), channel_id=1, source_target_pairs={{0,12},{1,3},{2,14},{3,1},{4,8},{5,7},{6,10},{7,5},{8,4},{9,11},{1... | collective-permute-start | bytes 589832 | tf_op jit(solution)/shard_map/ppermute | solution.py:189
  47.5 1.3 collective-permute-start.9
  48.8 0.0 collective-permute-done
  48.8 4.2 %collective-permute-done.2 = bf16[4,192,128]{2,1,0:T(8,128)(2,1)S(1)} collective-permute-done((bf16[4,192,128]{2,1,0:T(8,128)(2,1)S(1)}, bf16[4,192,128]{2,1,0:T(8,128)(2,1)S(1)}, u32[]{:S(2)}, u32[]{:S(2)}) %collective-permute-start.2) | collective-permute-done | bytes 196640 | tf_op jit(solution)/shard_map/ppermute | solution.py:189
  53.1 1.6 %collective-permute-start.6 = (bf16[2,2,192,128]{3,2,1,0:T(8,128)(2,1)S(1)}, bf16[2,2,192,128]{3,2,1,0:T(8,128)(2,1)S(1)}, u32[]{:S(2)}, u32[]{:S(2)}) collective-permute-start(bf16[2,2,192,128]{3,2,1,0:T(8,128)(2,1)S(1)} %bitcast.25), channel_id=1, source_target_pairs={{0,2},{1,5},{2,0},{3,7},{4,6},{5,1},{6,4},{7,3},{8,10},{9,13},{10,... | collective-permute-start | bytes 589832 | tf_op jit(solution)/shard_map/ppermute | solution.py:189
  54.7 0.0 collective-permute-done.9
  54.8 0.4 collective-permute-start.10
  55.3 2.0 %collective-permute-start.3 = (bf16[2,2,208,128]{3,2,1,0:T(8,128)(2,1)S(1)}, bf16[2,2,208,128]{3,2,1,0:T(8,128)(2,1)S(1)}, u32[]{:S(2)}, u32[]{:S(2)}) collective-permute-start(bf16[2,2,208,128]{3,2,1,0:T(8,128)(2,1)S(1)} %bitcast.19), channel_id=1, source_target_pairs={{0,12},{1,3},{2,14},{3,1},{4,8},{5,7},{6,10},{7,5},{8,4},{9,11},{1... | collective-permute-start | bytes 638984 | tf_op jit(solution)/shard_map/ppermute | solution.py:189
  57.2 4.1 %collective-permute-done.6 = bf16[2,2,192,128]{3,2,1,0:T(8,128)(2,1)S(1)} collective-permute-done((bf16[2,2,192,128]{3,2,1,0:T(8,128)(2,1)S(1)}, bf16[2,2,192,128]{3,2,1,0:T(8,128)(2,1)S(1)}, u32[]{:S(2)}, u32[]{:S(2)}) %collective-permute-start.6) | collective-permute-done | bytes 196640 | tf_op jit(solution)/shard_map/ppermute | solution.py:189
  61.3 0.1 add_convert_fusion.7
  61.4 0.1 collective-permute-start.7
  61.4 0.0 collective-permute-done.10
  61.5 2.3 %collective-permute-start.11 = (bf16[2,2,192,128]{3,2,1,0:T(8,128)(2,1)S(1)}, bf16[2,2,192,128]{3,2,1,0:T(8,128)(2,1)S(1)}, u32[]{:S(2)}, u32[]{:S(2)}) collective-permute-start(bf16[2,2,192,128]{3,2,1,0:T(8,128)(2,1)S(1)} %add_convert_fusion.4), channel_id=1, source_target_pairs={{0,12},{1,3},{2,14},{3,1},{4,8},{5,7},{6,10},{7,5},{8,4},{9,11},{1... | collective-permute-start | bytes 589832 | tf_op jit(solution)/shard_map/ppermute | solution.py:189
  63.8 0.1 collective-permute-done.3
  64.0 1.4 %collective-permute-start.4 = (bf16[2,2,208,128]{3,2,1,0:T(8,128)(2,1)S(1)}, bf16[2,2,208,128]{3,2,1,0:T(8,128)(2,1)S(1)}, u32[]{:S(2)}, u32[]{:S(2)}) collective-permute-start(bf16[2,2,208,128]{3,2,1,0:T(8,128)(2,1)S(1)} %add_convert_fusion.1), channel_id=1, source_target_pairs={{0,2},{1,5},{2,0},{3,7},{4,6},{5,1},{6,4},{7,3},{8,10},{9,13},{10,... | collective-permute-start | bytes 638984 | tf_op jit(solution)/shard_map/ppermute | solution.py:189
  65.4 3.6 %collective-permute-done.7 = bf16[2,2,192,128]{3,2,1,0:T(8,128)(2,1)S(1)} collective-permute-done((bf16[2,2,192,128]{3,2,1,0:T(8,128)(2,1)S(1)}, bf16[2,2,192,128]{3,2,1,0:T(8,128)(2,1)S(1)}, u32[]{:S(2)}, u32[]{:S(2)}) %collective-permute-start.7) | collective-permute-done | bytes 196640 | tf_op jit(solution)/shard_map/ppermute | solution.py:189
  69.1 2.0 %collective-permute-start.8 = (bf16[4,192,128]{2,1,0:T(8,128)(2,1)S(1)}, bf16[4,192,128]{2,1,0:T(8,128)(2,1)S(1)}, u32[]{:S(2)}, u32[]{:S(2)}) collective-permute-start(bf16[4,192,128]{2,1,0:T(8,128)(2,1)S(1)} %bitcast.21), channel_id=1, source_target_pairs={{0,12},{1,3},{2,14},{3,1},{4,8},{5,7},{6,10},{7,5},{8,4},{9,11},{1... | collective-permute-start | bytes 589832 | tf_op jit(solution)/shard_map/ppermute | solution.py:189
  71.1 0.0 collective-permute-done.11
  71.2 1.8 %collective-permute-done.4 = bf16[2,2,208,128]{3,2,1,0:T(8,128)(2,1)S(1)} collective-permute-done((bf16[2,2,208,128]{3,2,1,0:T(8,128)(2,1)S(1)}, bf16[2,2,208,128]{3,2,1,0:T(8,128)(2,1)S(1)}, u32[]{:S(2)}, u32[]{:S(2)}) %collective-permute-start.4) | collective-permute-done | bytes 213024 | tf_op jit(solution)/shard_map/ppermute | solution.py:189
  73.1 0.8 collective-permute-start.5
  73.9 1.8 %collective-permute-start.12 = (bf16[4,192,128]{2,1,0:T(8,128)(2,1)S(1)}, bf16[4,192,128]{2,1,0:T(8,128)(2,1)S(1)}, u32[]{:S(2)}, u32[]{:S(2)}) collective-permute-start(bf16[4,192,128]{2,1,0:T(8,128)(2,1)S(1)} %bitcast.23), channel_id=1, source_target_pairs={{0,2},{1,5},{2,0},{3,7},{4,6},{5,1},{6,4},{7,3},{8,10},{9,13},{10,... | collective-permute-start | bytes 589832 | tf_op jit(solution)/shard_map/ppermute | solution.py:189
  75.7 2.2 %collective-permute-done.8 = bf16[4,192,128]{2,1,0:T(8,128)(2,1)S(1)} collective-permute-done((bf16[4,192,128]{2,1,0:T(8,128)(2,1)S(1)}, bf16[4,192,128]{2,1,0:T(8,128)(2,1)S(1)}, u32[]{:S(2)}, u32[]{:S(2)}) %collective-permute-start.8) | collective-permute-done | bytes 196640 | tf_op jit(solution)/shard_map/ppermute | solution.py:189
  77.9 3.3 %collective-permute-done.12 = bf16[4,192,128]{2,1,0:T(8,128)(2,1)S(1)} collective-permute-done((bf16[4,192,128]{2,1,0:T(8,128)(2,1)S(1)}, bf16[4,192,128]{2,1,0:T(8,128)(2,1)S(1)}, u32[]{:S(2)}, u32[]{:S(2)}) %collective-permute-start.12) | collective-permute-done | bytes 196640 | tf_op jit(solution)/shard_map/ppermute | solution.py:189
  81.1 0.0 collective-permute-done.5
  81.1 0.1 maximum_maximum_fusion.pieces_ref
  81.2 0.3 collective-permute-start.13
  81.5 1.3 own_square.1
  82.8 1.6 %collective-permute-done.13.pieces_ref = bf16[8,592,128]{2,1,0:T(8,128)(2,1)S(1)} collective-permute-done((bf16[8,592,128]{2,1,0:T(8,128)(2,1)S(1)}, bf16[8,592,128]{2,1,0:T(8,128)(2,1)S(1)}, u32[]{:S(2)}, u32[]{:S(2)}) %collective-permute-start.13) | collective-permute-done | bytes 1212448 | tf_op jit(solution)/shard_map/ppermute | solution.py:352
  84.4 7.1 %update_rows.1 = bf16[8,8,144,128]{3,2,1,0:T(8,128)(2,1)S(1)} custom-call(bf16[4736,128]{1,0:T(8,128)(2,1)S(1)} %get-tuple-element.28.own_ref, bf16[8,592,128]{2,1,0:T(8,128)(2,1)S(1)} %collective-permute-done.13.pieces_ref, bf16[768,768]{1,0:T(8,128)(2,1)S(1)} %get-tuple-element.29.gram_ref, f32[768,768]{1,0:T(8,128)S(1)} %get-tuple-element.30.square_ref, ...), custom_call_target="tpu_custom_call" | custom-call | flops 6341787648 | bytes 11796480 | tf_op jit(solution)/shard_map/update_rows/pallas_call | solution.py:304
  91.5 42.1 %all_to_all.11 = bf16[64,144,128]{2,1,0:T(8,128)(2,1)S(1)} all-to-all(bf16[64,144,128]{2,1,0:T(8,128)(2,1)S(1)} %bitcast.16), channel_id=1, replica_groups=mesh['z'=4,'yl'=2,'x'=4,'yh'=2,'c'=2] {'z','yl','x','yh'}, dimensions={0} | all-to-all | bytes 4718592 | tf_op jit(solution)/shard_map/all_to_all | solution.py:371
  133.6 1.6 %join_columns.1 = bf16[8,96,1536]{2,1,0:T(8,128)(2,1)} custom-call(bf16[8,8,144,128]{3,2,1,0:T(8,128)(2,1)S(1)} %bitcast.10), custom_call_target="tpu_custom_call" | custom-call | tf_op jit(solution)/shard_map/join_columns/pallas_call | solution.py:340
  (14 shorter events, 0.5 us)
Async XLA Ops:
  0.0 1.7 %copy-start = (bf16[1,96,12288]{2,1,0:T(8,128)(2,1)S(1)}, bf16[1,96,12288]{2,1,0:T(8,128)(2,1)}, u32[]{:S(2)}) copy-start(bf16[1,96,12288]{2,1,0:T(8,128)(2,1)} %param.1) | copy-start | bytes 7077892
  40.0 4.5 %collective-permute-start.1 = (bf16[768,1536]{1,0:T(8,128)(2,1)S(1)}, bf16[768,1536]{1,0:T(8,128)(2,1)S(1)}, u32[]{:S(2)}, u32[]{:S(2)}) collective-permute-start(bf16[768,1536]{1,0:T(8,128)(2,1)S(1)} %bitcast.12), channel_id=1, source_target_pairs={{0,1},{1,0},{2,3},{3,2},{4,5},{5,4},{6,7},{7,6},{8,9},{9,8},{10,11... | collective-permute-start | bytes 7077896 | tf_op jit(solution)/shard_map/ppermute | solution.py:352
  41.4 7.4 %collective-permute-start = (bf16[4,208,128]{2,1,0:T(8,128)(2,1)S(1)}, bf16[4,208,128]{2,1,0:T(8,128)(2,1)S(1)}, u32[]{:S(2)}, u32[]{:S(2)}) collective-permute-start(bf16[4,208,128]{2,1,0:T(8,128)(2,1)S(1)} %get-tuple-element.19), channel_id=1, source_target_pairs={{0,4},{1,13},{2,6},{3,15},{4,0},{5,9},{6,2},{7,11},{8,12},{9,5},{1... | collective-permute-start | bytes 638984 | tf_op jit(solution)/shard_map/ppermute | solution.py:189
  46.0 7.0 %collective-permute-start.2 = (bf16[4,192,128]{2,1,0:T(8,128)(2,1)S(1)}, bf16[4,192,128]{2,1,0:T(8,128)(2,1)S(1)}, u32[]{:S(2)}, u32[]{:S(2)}) collective-permute-start(bf16[4,192,128]{2,1,0:T(8,128)(2,1)S(1)} %get-tuple-element.22), channel_id=1, source_target_pairs={{0,12},{1,3},{2,14},{3,1},{4,8},{5,7},{6,10},{7,5},{8,4},{9,11},{1... | collective-permute-start | bytes 589832 | tf_op jit(solution)/shard_map/ppermute | solution.py:189
  47.5 7.2 %collective-permute-start.9 = (bf16[4,192,128]{2,1,0:T(8,128)(2,1)S(1)}, bf16[4,192,128]{2,1,0:T(8,128)(2,1)S(1)}, u32[]{:S(2)}, u32[]{:S(2)}) collective-permute-start(bf16[4,192,128]{2,1,0:T(8,128)(2,1)S(1)} %get-tuple-element.27), channel_id=1, source_target_pairs={{0,2},{1,5},{2,0},{3,7},{4,6},{5,1},{6,4},{7,3},{8,10},{9,13},{10,... | collective-permute-start | bytes 589832 | tf_op jit(solution)/shard_map/ppermute | solution.py:189
  53.1 8.2 %collective-permute-start.6 = (bf16[2,2,192,128]{3,2,1,0:T(8,128)(2,1)S(1)}, bf16[2,2,192,128]{3,2,1,0:T(8,128)(2,1)S(1)}, u32[]{:S(2)}, u32[]{:S(2)}) collective-permute-start(bf16[2,2,192,128]{3,2,1,0:T(8,128)(2,1)S(1)} %bitcast.25), channel_id=1, source_target_pairs={{0,2},{1,5},{2,0},{3,7},{4,6},{5,1},{6,4},{7,3},{8,10},{9,13},{10,... | collective-permute-start | bytes 589832 | tf_op jit(solution)/shard_map/ppermute | solution.py:189
  54.8 6.7 %collective-permute-start.10 = (bf16[2,2,192,128]{3,2,1,0:T(8,128)(2,1)S(1)}, bf16[2,2,192,128]{3,2,1,0:T(8,128)(2,1)S(1)}, u32[]{:S(2)}, u32[]{:S(2)}) collective-permute-start(bf16[2,2,192,128]{3,2,1,0:T(8,128)(2,1)S(1)} %bitcast.27), channel_id=1, source_target_pairs={{0,4},{1,13},{2,6},{3,15},{4,0},{5,9},{6,2},{7,11},{8,12},{9,5},{1... | collective-permute-start | bytes 589832 | tf_op jit(solution)/shard_map/ppermute | solution.py:189
  55.3 8.7 %collective-permute-start.3 = (bf16[2,2,208,128]{3,2,1,0:T(8,128)(2,1)S(1)}, bf16[2,2,208,128]{3,2,1,0:T(8,128)(2,1)S(1)}, u32[]{:S(2)}, u32[]{:S(2)}) collective-permute-start(bf16[2,2,208,128]{3,2,1,0:T(8,128)(2,1)S(1)} %bitcast.19), channel_id=1, source_target_pairs={{0,12},{1,3},{2,14},{3,1},{4,8},{5,7},{6,10},{7,5},{8,4},{9,11},{1... | collective-permute-start | bytes 638984 | tf_op jit(solution)/shard_map/ppermute | solution.py:189
  61.4 7.7 %collective-permute-start.7 = (bf16[2,2,192,128]{3,2,1,0:T(8,128)(2,1)S(1)}, bf16[2,2,192,128]{3,2,1,0:T(8,128)(2,1)S(1)}, u32[]{:S(2)}, u32[]{:S(2)}) collective-permute-start(bf16[2,2,192,128]{3,2,1,0:T(8,128)(2,1)S(1)} %add_convert_fusion.7), channel_id=1, source_target_pairs={{0,4},{1,13},{2,6},{3,15},{4,0},{5,9},{6,2},{7,11},{8,12},{9,5},{1... | collective-permute-start | bytes 589832 | tf_op jit(solution)/shard_map/ppermute | solution.py:189
  61.5 9.6 %collective-permute-start.11 = (bf16[2,2,192,128]{3,2,1,0:T(8,128)(2,1)S(1)}, bf16[2,2,192,128]{3,2,1,0:T(8,128)(2,1)S(1)}, u32[]{:S(2)}, u32[]{:S(2)}) collective-permute-start(bf16[2,2,192,128]{3,2,1,0:T(8,128)(2,1)S(1)} %add_convert_fusion.4), channel_id=1, source_target_pairs={{0,12},{1,3},{2,14},{3,1},{4,8},{5,7},{6,10},{7,5},{8,4},{9,11},{1... | collective-permute-start | bytes 589832 | tf_op jit(solution)/shard_map/ppermute | solution.py:189
  64.0 9.0 %collective-permute-start.4 = (bf16[2,2,208,128]{3,2,1,0:T(8,128)(2,1)S(1)}, bf16[2,2,208,128]{3,2,1,0:T(8,128)(2,1)S(1)}, u32[]{:S(2)}, u32[]{:S(2)}) collective-permute-start(bf16[2,2,208,128]{3,2,1,0:T(8,128)(2,1)S(1)} %add_convert_fusion.1), channel_id=1, source_target_pairs={{0,2},{1,5},{2,0},{3,7},{4,6},{5,1},{6,4},{7,3},{8,10},{9,13},{10,... | collective-permute-start | bytes 638984 | tf_op jit(solution)/shard_map/ppermute | solution.py:189
  69.1 8.7 %collective-permute-start.8 = (bf16[4,192,128]{2,1,0:T(8,128)(2,1)S(1)}, bf16[4,192,128]{2,1,0:T(8,128)(2,1)S(1)}, u32[]{:S(2)}, u32[]{:S(2)}) collective-permute-start(bf16[4,192,128]{2,1,0:T(8,128)(2,1)S(1)} %bitcast.21), channel_id=1, source_target_pairs={{0,12},{1,3},{2,14},{3,1},{4,8},{5,7},{6,10},{7,5},{8,4},{9,11},{1... | collective-permute-start | bytes 589832 | tf_op jit(solution)/shard_map/ppermute | solution.py:189
  73.1 8.1 %collective-permute-start.5 = (bf16[4,208,128]{2,1,0:T(8,128)(2,1)S(1)}, bf16[4,208,128]{2,1,0:T(8,128)(2,1)S(1)}, u32[]{:S(2)}, u32[]{:S(2)}) collective-permute-start(bf16[4,208,128]{2,1,0:T(8,128)(2,1)S(1)} %bitcast.17), channel_id=1, source_target_pairs={{0,4},{1,13},{2,6},{3,15},{4,0},{5,9},{6,2},{7,11},{8,12},{9,5},{1... | collective-permute-start | bytes 638984 | tf_op jit(solution)/shard_map/ppermute | solution.py:189
  73.9 7.3 %collective-permute-start.12 = (bf16[4,192,128]{2,1,0:T(8,128)(2,1)S(1)}, bf16[4,192,128]{2,1,0:T(8,128)(2,1)S(1)}, u32[]{:S(2)}, u32[]{:S(2)}) collective-permute-start(bf16[4,192,128]{2,1,0:T(8,128)(2,1)S(1)} %bitcast.23), channel_id=1, source_target_pairs={{0,2},{1,5},{2,0},{3,7},{4,6},{5,1},{6,4},{7,3},{8,10},{9,13},{10,... | collective-permute-start | bytes 589832 | tf_op jit(solution)/shard_map/ppermute | solution.py:189
  81.2 3.2 %collective-permute-start.13 = (bf16[8,592,128]{2,1,0:T(8,128)(2,1)S(1)}, bf16[8,592,128]{2,1,0:T(8,128)(2,1)S(1)}, u32[]{:S(2)}, u32[]{:S(2)}) collective-permute-start(bf16[8,592,128]{2,1,0:T(8,128)(2,1)S(1)} %maximum_maximum_fusion.pieces_ref), channel_id=1, source_target_pairs={{0,1},{1,0},{2,3},{3,2},{4,5},{5,4},{6,7},{7,6},{8,9},{9,8},{10,11... | collective-permute-start | bytes 3637256 | tf_op jit(solution)/shard_map/ppermute | solution.py:352

commit v9 on v8

--- a/solution.py
+++ b/solution.py
@@ -26,6 +26,7 @@
 PACKED = -(-(EDGE + BLOCKS) // (16 * CHIPS)) * 16 * CHIPS
 PIECES = (208, 192, 192)
 BASES = (0, CHIPS * PIECES[0], CHIPS * (PIECES[0] + PIECES[1]))
+TAILS = TILES - CHIPS
 MIB = 1 << 20
 
 CHIP_AXES = ("x", "yh")
@@ -69,23 +70,45 @@
     return [jax.ShapeDtypeStruct(shape, jnp.float32), jax.ShapeDtypeStruct(shape, kind)]
 
 
-def split_kernel(x_ref, out_ref):
+def split_kernel(x_ref, out_ref, tails_ref, sems, tail_sems):
+    tails = [
+        pltpu.make_async_copy(
+            x_ref.at[:, pl.ds((TILES * j + CHIPS) * LANES, TAILS * LANES)],
+            tails_ref.at[:, pl.ds(TAILS * j * LANES, TAILS * LANES)],
+            tail_sems.at[j],
+        )
+        for j in range(STRIPES)
+    ]
+    mains = [
+        pltpu.make_async_copy(x_ref.at[:, tile(TILES * j + p)], out_ref.at[p, :, tile(j)], sems.at[p, j])
+        for j in range(STRIPES)
+        for p in range(CHIPS)
+    ]
+    for copy in tails + mains:
+        copy.start()
+    for copy in tails:
+        copy.wait()
     for p in range(CHIPS):
-        for j in range(STRIPES):
-            out_ref[p, :, tile(j)] = x_ref[:, tile(TILES * j + p)]
         for m in range(STRIPES // 2):
-            left = x_ref[:, tile(TILES * (2 * m) + CHIPS + p // 2)]
-            right = x_ref[:, tile(TILES * (2 * m + 1) + CHIPS + p // 2)]
+            left, right = (tails_ref[:, tile(TAILS * (2 * m + i) + p // 2)] for i in range(2))
             out_ref[p, :, tile(STRIPES + m)] = halves(left, right, p % 2 == 0).astype(out_ref.dtype)
+    for copy in mains:
+        copy.wait()
 
 
 def split_columns(x):
     return pl.pallas_call(
         split_kernel,
+        in_specs=[pl.BlockSpec(memory_space=pltpu.HBM)],
         out_shape=jax.ShapeDtypeStruct((CHIPS, PANEL, WIDTH), x.dtype),
+        scratch_shapes=[
+            pltpu.VMEM((PANEL, STRIPES * TAILS * LANES), x.dtype),
+            pltpu.SemaphoreType.DMA((CHIPS, STRIPES)),
+            pltpu.SemaphoreType.DMA((STRIPES,)),
+        ],
         compiler_params=pltpu.CompilerParams(vmem_limit_bytes=16 * MIB),
         name="split_columns",
-    )(x)
+    )(pltpu.with_memory_space_constraint(x, pltpu.HBM))
 
 
 def strip(j):

time: 136 us -> 136 us (level)
  Pallas kernels: 13.6 us -> 15.8 us
  local copies, waits for them, and re-layouts: 1.66 us -> 0 us
    pallas_call x1, Pallas kernels: 0.59 us -> 2.82 us  [split_columns(): pl.pallas_call(split_kernel, in_specs=[pl.BlockSpec(memory_space=pltpu.HB...]
    unnamed x2 -> x0, local copies, waits for them, and re-layouts: 1.66 us -> none
where the time goes in v9:
time: 136 us
  blocking collectives  79.8 us (59%)
  waiting for transfers between devices  23.3 us (17%)
  starting transfers between devices  16.1 us (12%)
  Pallas kernels  15.8 us (12%)
    all_to_all x1, blocking collectives, shards(): received = lax.all_to_all(sent, ALL_CHIPS, 0, 0, tiled=True)  42.1 us
    all_to_all x1, blocking collectives, shards(): lax.all_to_all(pieces, CHIP_AXES, 0, 0, tiled=True).reshape(HALF, WIDTH)  37.7 us
    ppermute x12, waiting for transfers between devices, exchange(): return lax.ppermute(value, ('x', 'yh', 'c'), pairs)  19.2 us
    ppermute x12, starting transfers between devices, exchange(): return lax.ppermute(value, ('x', 'yh', 'c'), pairs)  15.8 us
    pallas_call x1, Pallas kernels, update_rows(): pl.pallas_call(update_kernel, out_shape=jax.ShapeDtypeStruct((STRIPES, CH...  7.11 us
    ppermute x2, waiting for transfers between devices, swap_cores(): return lax.ppermute(value, 'c', [(0, 1), (1, 0)])  4.05 us
    pallas_call x1, Pallas kernels, split_columns(): pl.pallas_call(split_kernel, in_specs=[pl.BlockSpec(memory_space=pltpu.HB...  2.82 us
  transfers between devices with their start and end apart: 14, of which 9 were waited for; matrix products, arithmetic and copies ran while one was open for 0% of the time, Pallas kernels for 3%

profile of v9, /device:TPU:0, one launch (start us, length us, event | category | flops | bytes accessed | tf_op | source)
XLA Modules:
  0.0 135.9 jit_solution(3219016093280044536)
XLA Ops:
  0.0 2.8 %split_columns.1 = bf16[8,96,1536]{2,1,0:T(8,128)(2,1)S(1)} custom-call(bf16[96,12288]{1,0:T(8,128)(2,1)} %bitcast.16), custom_call_target="tpu_custom_call" | custom-call | tf_op jit(solution)/shard_map/split_columns/pallas_call | solution.py:100
  2.8 37.7 %all_to_all.10 = bf16[8,96,1536]{2,1,0:T(8,128)(2,1)S(1)} all-to-all(bf16[8,96,1536]{2,1,0:T(8,128)(2,1)S(1)} %split_columns.1), channel_id=1, replica_groups=mesh['z'=4,'yl'=2,'x'=4,'yh'=2,'c'=2] {'x','yh'}, dimensions={0} | all-to-all | bytes 4718592 | tf_op jit(solution)/shard_map/all_to_all | solution.py:380
  40.5 0.0 collective-permute-start.1
  40.5 1.5 %own_gram.1 = (f32[4,208,128]{2,1,0:T(8,128)S(1)}, bf16[4,208,128]{2,1,0:T(8,128)(2,1)S(1)}, f32[256,128]{1,0:T(8,128)S(1)}, f32[6,128,128]{2,1,0:T(8,128)S(1)}) custom-call(bf16[768,1536]{1,0:T(8,128)(2,1)S(1)} %bitcast.12), custom_call_target="tpu_custom_call" | custom-call | flops 1660944384 | bytes 2359296 | tf_op jit(solution)/shard_map/own_gram/pallas_call | solution.py:153
  42.0 0.6 collective-permute-start
  42.6 2.5 %collective-permute-done.1.other_ref.x_other_ref = bf16[768,1536]{1,0:T(8,128)(2,1)S(1)} collective-permute-done((bf16[768,1536]{1,0:T(8,128)(2,1)S(1)}, bf16[768,1536]{1,0:T(8,128)(2,1)S(1)}, u32[]{:S(2)}, u32[]{:S(2)}) %collective-permute-start.1) | collective-permute-done | bytes 2359328 | tf_op jit(solution)/shard_map/ppermute | solution.py:375
  45.1 1.5 %cross_gram.1 = (f32[4,192,128]{2,1,0:T(8,128)S(1)}, bf16[4,192,128]{2,1,0:T(8,128)(2,1)S(1)}, f32[4,192,128]{2,1,0:T(8,128)S(1)}, bf16[4,192,128]{2,1,0:T(8,128)(2,1)S(1)}) custom-call(f32[256,128]{1,0:T(8,128)S(1)} %get-tuple-element.20.rest_ref, f32[6,128,128]{2,1,0:T(8,128)S(1)} %get-tuple-element.21.diagonal_ref, bf16[768,1536]{1,0:T(8,128)(2,1)S(1)} %bitcast.13, ...), custom_call_target="tpu_custom_call" | custom-call | flops 1660944384 | bytes 4718592 | tf_op jit(solution)/shard_map/cross_gram/pallas_call | solution.py:192
  46.6 1.5 %collective-permute-start.2 = (bf16[4,192,128]{2,1,0:T(8,128)(2,1)S(1)}, bf16[4,192,128]{2,1,0:T(8,128)(2,1)S(1)}, u32[]{:S(2)}, u32[]{:S(2)}) collective-permute-start(bf16[4,192,128]{2,1,0:T(8,128)(2,1)S(1)} %get-tuple-element.22), channel_id=1, source_target_pairs={{0,12},{1,3},{2,14},{3,1},{4,8},{5,7},{6,10},{7,5},{8,4},{9,11},{1... | collective-permute-start | bytes 589832 | tf_op jit(solution)/shard_map/ppermute | solution.py:212
  48.1 1.3 collective-permute-start.9
  49.4 0.0 collective-permute-done
  49.4 4.2 %collective-permute-done.2 = bf16[4,192,128]{2,1,0:T(8,128)(2,1)S(1)} collective-permute-done((bf16[4,192,128]{2,1,0:T(8,128)(2,1)S(1)}, bf16[4,192,128]{2,1,0:T(8,128)(2,1)S(1)}, u32[]{:S(2)}, u32[]{:S(2)}) %collective-permute-start.2) | collective-permute-done | bytes 196640 | tf_op jit(solution)/shard_map/ppermute | solution.py:212
  53.6 1.6 %collective-permute-start.6 = (bf16[2,2,192,128]{3,2,1,0:T(8,128)(2,1)S(1)}, bf16[2,2,192,128]{3,2,1,0:T(8,128)(2,1)S(1)}, u32[]{:S(2)}, u32[]{:S(2)}) collective-permute-start(bf16[2,2,192,128]{3,2,1,0:T(8,128)(2,1)S(1)} %bitcast.25), channel_id=1, source_target_pairs={{0,2},{1,5},{2,0},{3,7},{4,6},{5,1},{6,4},{7,3},{8,10},{9,13},{10,... | collective-permute-start | bytes 589832 | tf_op jit(solution)/shard_map/ppermute | solution.py:212
  55.3 0.0 collective-permute-done.9
  55.3 0.4 collective-permute-start.10
  55.8 1.9 %collective-permute-start.3 = (bf16[2,2,208,128]{3,2,1,0:T(8,128)(2,1)S(1)}, bf16[2,2,208,128]{3,2,1,0:T(8,128)(2,1)S(1)}, u32[]{:S(2)}, u32[]{:S(2)}) collective-permute-start(bf16[2,2,208,128]{3,2,1,0:T(8,128)(2,1)S(1)} %bitcast.19), channel_id=1, source_target_pairs={{0,12},{1,3},{2,14},{3,1},{4,8},{5,7},{6,10},{7,5},{8,4},{9,11},{1... | collective-permute-start | bytes 638984 | tf_op jit(solution)/shard_map/ppermute | solution.py:212
  57.8 4.1 %collective-permute-done.6 = bf16[2,2,192,128]{3,2,1,0:T(8,128)(2,1)S(1)} collective-permute-done((bf16[2,2,192,128]{3,2,1,0:T(8,128)(2,1)S(1)}, bf16[2,2,192,128]{3,2,1,0:T(8,128)(2,1)S(1)}, u32[]{:S(2)}, u32[]{:S(2)}) %collective-permute-start.6) | collective-permute-done | bytes 196640 | tf_op jit(solution)/shard_map/ppermute | solution.py:212
  61.9 0.1 add_convert_fusion.7
  61.9 0.1 collective-permute-start.7
  62.0 0.0 collective-permute-done.10
  62.1 2.3 %collective-permute-start.11 = (bf16[2,2,192,128]{3,2,1,0:T(8,128)(2,1)S(1)}, bf16[2,2,192,128]{3,2,1,0:T(8,128)(2,1)S(1)}, u32[]{:S(2)}, u32[]{:S(2)}) collective-permute-start(bf16[2,2,192,128]{3,2,1,0:T(8,128)(2,1)S(1)} %add_convert_fusion.4), channel_id=1, source_target_pairs={{0,12},{1,3},{2,14},{3,1},{4,8},{5,7},{6,10},{7,5},{8,4},{9,11},{1... | collective-permute-start | bytes 589832 | tf_op jit(solution)/shard_map/ppermute | solution.py:212
  64.4 0.1 collective-permute-done.3
  64.6 1.4 %collective-permute-start.4 = (bf16[2,2,208,128]{3,2,1,0:T(8,128)(2,1)S(1)}, bf16[2,2,208,128]{3,2,1,0:T(8,128)(2,1)S(1)}, u32[]{:S(2)}, u32[]{:S(2)}) collective-permute-start(bf16[2,2,208,128]{3,2,1,0:T(8,128)(2,1)S(1)} %add_convert_fusion.1), channel_id=1, source_target_pairs={{0,2},{1,5},{2,0},{3,7},{4,6},{5,1},{6,4},{7,3},{8,10},{9,13},{10,... | collective-permute-start | bytes 638984 | tf_op jit(solution)/shard_map/ppermute | solution.py:212
  66.0 3.6 %collective-permute-done.7 = bf16[2,2,192,128]{3,2,1,0:T(8,128)(2,1)S(1)} collective-permute-done((bf16[2,2,192,128]{3,2,1,0:T(8,128)(2,1)S(1)}, bf16[2,2,192,128]{3,2,1,0:T(8,128)(2,1)S(1)}, u32[]{:S(2)}, u32[]{:S(2)}) %collective-permute-start.7) | collective-permute-done | bytes 196640 | tf_op jit(solution)/shard_map/ppermute | solution.py:212
  69.7 2.0 %collective-permute-start.8 = (bf16[4,192,128]{2,1,0:T(8,128)(2,1)S(1)}, bf16[4,192,128]{2,1,0:T(8,128)(2,1)S(1)}, u32[]{:S(2)}, u32[]{:S(2)}) collective-permute-start(bf16[4,192,128]{2,1,0:T(8,128)(2,1)S(1)} %bitcast.21), channel_id=1, source_target_pairs={{0,12},{1,3},{2,14},{3,1},{4,8},{5,7},{6,10},{7,5},{8,4},{9,11},{1... | collective-permute-start | bytes 589832 | tf_op jit(solution)/shard_map/ppermute | solution.py:212
  71.7 0.0 collective-permute-done.11
  71.7 1.8 %collective-permute-done.4 = bf16[2,2,208,128]{3,2,1,0:T(8,128)(2,1)S(1)} collective-permute-done((bf16[2,2,208,128]{3,2,1,0:T(8,128)(2,1)S(1)}, bf16[2,2,208,128]{3,2,1,0:T(8,128)(2,1)S(1)}, u32[]{:S(2)}, u32[]{:S(2)}) %collective-permute-start.4) | collective-permute-done | bytes 213024 | tf_op jit(solution)/shard_map/ppermute | solution.py:212
  73.6 0.8 collective-permute-start.5
  74.5 1.8 %collective-permute-start.12 = (bf16[4,192,128]{2,1,0:T(8,128)(2,1)S(1)}, bf16[4,192,128]{2,1,0:T(8,128)(2,1)S(1)}, u32[]{:S(2)}, u32[]{:S(2)}) collective-permute-start(bf16[4,192,128]{2,1,0:T(8,128)(2,1)S(1)} %bitcast.23), channel_id=1, source_target_pairs={{0,2},{1,5},{2,0},{3,7},{4,6},{5,1},{6,4},{7,3},{8,10},{9,13},{10,... | collective-permute-start | bytes 589832 | tf_op jit(solution)/shard_map/ppermute | solution.py:212
  76.2 2.2 %collective-permute-done.8 = bf16[4,192,128]{2,1,0:T(8,128)(2,1)S(1)} collective-permute-done((bf16[4,192,128]{2,1,0:T(8,128)(2,1)S(1)}, bf16[4,192,128]{2,1,0:T(8,128)(2,1)S(1)}, u32[]{:S(2)}, u32[]{:S(2)}) %collective-permute-start.8) | collective-permute-done | bytes 196640 | tf_op jit(solution)/shard_map/ppermute | solution.py:212
  78.4 3.3 %collective-permute-done.12 = bf16[4,192,128]{2,1,0:T(8,128)(2,1)S(1)} collective-permute-done((bf16[4,192,128]{2,1,0:T(8,128)(2,1)S(1)}, bf16[4,192,128]{2,1,0:T(8,128)(2,1)S(1)}, u32[]{:S(2)}, u32[]{:S(2)}) %collective-permute-start.12) | collective-permute-done | bytes 196640 | tf_op jit(solution)/shard_map/ppermute | solution.py:212
  81.7 0.0 collective-permute-done.5
  81.7 0.1 maximum_maximum_fusion.pieces_ref
  81.8 0.3 collective-permute-start.13
  82.1 1.3 own_square.1
  83.4 1.6 %collective-permute-done.13.pieces_ref = bf16[8,592,128]{2,1,0:T(8,128)(2,1)S(1)} collective-permute-done((bf16[8,592,128]{2,1,0:T(8,128)(2,1)S(1)}, bf16[8,592,128]{2,1,0:T(8,128)(2,1)S(1)}, u32[]{:S(2)}, u32[]{:S(2)}) %collective-permute-start.13) | collective-permute-done | bytes 1212448 | tf_op jit(solution)/shard_map/ppermute | solution.py:375
  85.0 7.1 %update_rows.1 = bf16[8,8,144,128]{3,2,1,0:T(8,128)(2,1)S(1)} custom-call(bf16[4736,128]{1,0:T(8,128)(2,1)S(1)} %get-tuple-element.28.own_ref, bf16[8,592,128]{2,1,0:T(8,128)(2,1)S(1)} %collective-permute-done.13.pieces_ref, bf16[768,768]{1,0:T(8,128)(2,1)S(1)} %get-tuple-element.29.gram_ref, f32[768,768]{1,0:T(8,128)S(1)} %get-tuple-element.30.square_ref, ...), custom_call_target="tpu_custom_call" | custom-call | flops 6341787648 | bytes 11796480 | tf_op jit(solution)/shard_map/update_rows/pallas_call | solution.py:327
  92.1 42.1 %all_to_all.11 = bf16[64,144,128]{2,1,0:T(8,128)(2,1)S(1)} all-to-all(bf16[64,144,128]{2,1,0:T(8,128)(2,1)S(1)} %bitcast.15), channel_id=1, replica_groups=mesh['z'=4,'yl'=2,'x'=4,'yh'=2,'c'=2] {'z','yl','x','yh'}, dimensions={0} | all-to-all | bytes 4718592 | tf_op jit(solution)/shard_map/all_to_all | solution.py:394
  134.1 1.6 %join_columns.1 = bf16[8,96,1536]{2,1,0:T(8,128)(2,1)} custom-call(bf16[8,8,144,128]{3,2,1,0:T(8,128)(2,1)S(1)} %bitcast.10), custom_call_target="tpu_custom_call" | custom-call | tf_op jit(solution)/shard_map/join_columns/pallas_call | solution.py:363
  (14 shorter events, 0.5 us)
Async XLA Ops:
  40.5 4.5 %collective-permute-start.1 = (bf16[768,1536]{1,0:T(8,128)(2,1)S(1)}, bf16[768,1536]{1,0:T(8,128)(2,1)S(1)}, u32[]{:S(2)}, u32[]{:S(2)}) collective-permute-start(bf16[768,1536]{1,0:T(8,128)(2,1)S(1)} %bitcast.11), channel_id=1, source_target_pairs={{0,1},{1,0},{2,3},{3,2},{4,5},{5,4},{6,7},{7,6},{8,9},{9,8},{10,11... | collective-permute-start | bytes 7077896 | tf_op jit(solution)/shard_map/ppermute | solution.py:375
  42.0 7.4 %collective-permute-start = (bf16[4,208,128]{2,1,0:T(8,128)(2,1)S(1)}, bf16[4,208,128]{2,1,0:T(8,128)(2,1)S(1)}, u32[]{:S(2)}, u32[]{:S(2)}) collective-permute-start(bf16[4,208,128]{2,1,0:T(8,128)(2,1)S(1)} %get-tuple-element.19), channel_id=1, source_target_pairs={{0,4},{1,13},{2,6},{3,15},{4,0},{5,9},{6,2},{7,11},{8,12},{9,5},{1... | collective-permute-start | bytes 638984 | tf_op jit(solution)/shard_map/ppermute | solution.py:212
  46.6 7.0 %collective-permute-start.2 = (bf16[4,192,128]{2,1,0:T(8,128)(2,1)S(1)}, bf16[4,192,128]{2,1,0:T(8,128)(2,1)S(1)}, u32[]{:S(2)}, u32[]{:S(2)}) collective-permute-start(bf16[4,192,128]{2,1,0:T(8,128)(2,1)S(1)} %get-tuple-element.22), channel_id=1, source_target_pairs={{0,12},{1,3},{2,14},{3,1},{4,8},{5,7},{6,10},{7,5},{8,4},{9,11},{1... | collective-permute-start | bytes 589832 | tf_op jit(solution)/shard_map/ppermute | solution.py:212
  48.1 7.2 %collective-permute-start.9 = (bf16[4,192,128]{2,1,0:T(8,128)(2,1)S(1)}, bf16[4,192,128]{2,1,0:T(8,128)(2,1)S(1)}, u32[]{:S(2)}, u32[]{:S(2)}) collective-permute-start(bf16[4,192,128]{2,1,0:T(8,128)(2,1)S(1)} %get-tuple-element.27), channel_id=1, source_target_pairs={{0,2},{1,5},{2,0},{3,7},{4,6},{5,1},{6,4},{7,3},{8,10},{9,13},{10,... | collective-permute-start | bytes 589832 | tf_op jit(solution)/shard_map/ppermute | solution.py:212
  53.6 8.2 %collective-permute-start.6 = (bf16[2,2,192,128]{3,2,1,0:T(8,128)(2,1)S(1)}, bf16[2,2,192,128]{3,2,1,0:T(8,128)(2,1)S(1)}, u32[]{:S(2)}, u32[]{:S(2)}) collective-permute-start(bf16[2,2,192,128]{3,2,1,0:T(8,128)(2,1)S(1)} %bitcast.25), channel_id=1, source_target_pairs={{0,2},{1,5},{2,0},{3,7},{4,6},{5,1},{6,4},{7,3},{8,10},{9,13},{10,... | collective-permute-start | bytes 589832 | tf_op jit(solution)/shard_map/ppermute | solution.py:212
  55.3 6.7 %collective-permute-start.10 = (bf16[2,2,192,128]{3,2,1,0:T(8,128)(2,1)S(1)}, bf16[2,2,192,128]{3,2,1,0:T(8,128)(2,1)S(1)}, u32[]{:S(2)}, u32[]{:S(2)}) collective-permute-start(bf16[2,2,192,128]{3,2,1,0:T(8,128)(2,1)S(1)} %bitcast.27), channel_id=1, source_target_pairs={{0,4},{1,13},{2,6},{3,15},{4,0},{5,9},{6,2},{7,11},{8,12},{9,5},{1... | collective-permute-start | bytes 589832 | tf_op jit(solution)/shard_map/ppermute | solution.py:212
  55.8 8.7 %collective-permute-start.3 = (bf16[2,2,208,128]{3,2,1,0:T(8,128)(2,1)S(1)}, bf16[2,2,208,128]{3,2,1,0:T(8,128)(2,1)S(1)}, u32[]{:S(2)}, u32[]{:S(2)}) collective-permute-start(bf16[2,2,208,128]{3,2,1,0:T(8,128)(2,1)S(1)} %bitcast.19), channel_id=1, source_target_pairs={{0,12},{1,3},{2,14},{3,1},{4,8},{5,7},{6,10},{7,5},{8,4},{9,11},{1... | collective-permute-start | bytes 638984 | tf_op jit(solution)/shard_map/ppermute | solution.py:212
  61.9 7.7 %collective-permute-start.7 = (bf16[2,2,192,128]{3,2,1,0:T(8,128)(2,1)S(1)}, bf16[2,2,192,128]{3,2,1,0:T(8,128)(2,1)S(1)}, u32[]{:S(2)}, u32[]{:S(2)}) collective-permute-start(bf16[2,2,192,128]{3,2,1,0:T(8,128)(2,1)S(1)} %add_convert_fusion.7), channel_id=1, source_target_pairs={{0,4},{1,13},{2,6},{3,15},{4,0},{5,9},{6,2},{7,11},{8,12},{9,5},{1... | collective-permute-start | bytes 589832 | tf_op jit(solution)/shard_map/ppermute | solution.py:212
  62.1 9.6 %collective-permute-start.11 = (bf16[2,2,192,128]{3,2,1,0:T(8,128)(2,1)S(1)}, bf16[2,2,192,128]{3,2,1,0:T(8,128)(2,1)S(1)}, u32[]{:S(2)}, u32[]{:S(2)}) collective-permute-start(bf16[2,2,192,128]{3,2,1,0:T(8,128)(2,1)S(1)} %add_convert_fusion.4), channel_id=1, source_target_pairs={{0,12},{1,3},{2,14},{3,1},{4,8},{5,7},{6,10},{7,5},{8,4},{9,11},{1... | collective-permute-start | bytes 589832 | tf_op jit(solution)/shard_map/ppermute | solution.py:212
  64.6 9.0 %collective-permute-start.4 = (bf16[2,2,208,128]{3,2,1,0:T(8,128)(2,1)S(1)}, bf16[2,2,208,128]{3,2,1,0:T(8,128)(2,1)S(1)}, u32[]{:S(2)}, u32[]{:S(2)}) collective-permute-start(bf16[2,2,208,128]{3,2,1,0:T(8,128)(2,1)S(1)} %add_convert_fusion.1), channel_id=1, source_target_pairs={{0,2},{1,5},{2,0},{3,7},{4,6},{5,1},{6,4},{7,3},{8,10},{9,13},{10,... | collective-permute-start | bytes 638984 | tf_op jit(solution)/shard_map/ppermute | solution.py:212
  69.7 8.7 %collective-permute-start.8 = (bf16[4,192,128]{2,1,0:T(8,128)(2,1)S(1)}, bf16[4,192,128]{2,1,0:T(8,128)(2,1)S(1)}, u32[]{:S(2)}, u32[]{:S(2)}) collective-permute-start(bf16[4,192,128]{2,1,0:T(8,128)(2,1)S(1)} %bitcast.21), channel_id=1, source_target_pairs={{0,12},{1,3},{2,14},{3,1},{4,8},{5,7},{6,10},{7,5},{8,4},{9,11},{1... | collective-permute-start | bytes 589832 | tf_op jit(solution)/shard_map/ppermute | solution.py:212
  73.6 8.1 %collective-permute-start.5 = (bf16[4,208,128]{2,1,0:T(8,128)(2,1)S(1)}, bf16[4,208,128]{2,1,0:T(8,128)(2,1)S(1)}, u32[]{:S(2)}, u32[]{:S(2)}) collective-permute-start(bf16[4,208,128]{2,1,0:T(8,128)(2,1)S(1)} %bitcast.17), channel_id=1, source_target_pairs={{0,4},{1,13},{2,6},{3,15},{4,0},{5,9},{6,2},{7,11},{8,12},{9,5},{1... | collective-permute-start | bytes 638984 | tf_op jit(solution)/shard_map/ppermute | solution.py:212
  74.5 7.3 %collective-permute-start.12 = (bf16[4,192,128]{2,1,0:T(8,128)(2,1)S(1)}, bf16[4,192,128]{2,1,0:T(8,128)(2,1)S(1)}, u32[]{:S(2)}, u32[]{:S(2)}) collective-permute-start(bf16[4,192,128]{2,1,0:T(8,128)(2,1)S(1)} %bitcast.23), channel_id=1, source_target_pairs={{0,2},{1,5},{2,0},{3,7},{4,6},{5,1},{6,4},{7,3},{8,10},{9,13},{10,... | collective-permute-start | bytes 589832 | tf_op jit(solution)/shard_map/ppermute | solution.py:212
  81.8 3.2 %collective-permute-start.13 = (bf16[8,592,128]{2,1,0:T(8,128)(2,1)S(1)}, bf16[8,592,128]{2,1,0:T(8,128)(2,1)S(1)}, u32[]{:S(2)}, u32[]{:S(2)}) collective-permute-start(bf16[8,592,128]{2,1,0:T(8,128)(2,1)S(1)} %maximum_maximum_fusion.pieces_ref), channel_id=1, source_target_pairs={{0,1},{1,0},{2,3},{3,2},{4,5},{5,4},{6,7},{7,6},{8,9},{9,8},{10,11... | collective-permute-start | bytes 3637256 | tf_op jit(solution)/shard_map/ppermute | solution.py:375

commit v10 on v8

--- a/solution.py
+++ b/solution.py
@@ -24,7 +24,7 @@
 BELOW = LANES * BLOCKS * (BLOCKS - 1) // 2
 EDGE = 2 * BELOW + HALF
 PACKED = -(-(EDGE + BLOCKS) // (16 * CHIPS)) * 16 * CHIPS
-PIECES = (208, 192, 192)
+PIECES = (240, 176, 176)
 BASES = (0, CHIPS * PIECES[0], CHIPS * (PIECES[0] + PIECES[1]))
 MIB = 1 << 20
 
@@ -53,8 +53,10 @@
 
 
 def piece_rows(stream, position, base, core):
-    piece = lax.bitwise_xor(place(stream, core), position)
-    return pl.ds(base + pl.multiple_of(piece * PIECES[stream], 16), PIECES[stream])
+    if stream > 0:
+        piece = lax.bitwise_xor(place(stream, core), position)
+        return pl.ds(base + pl.multiple_of(piece * PIECES[stream], 16), PIECES[stream])
+    return pl.ds(base + position * PIECES[stream], PIECES[stream])
 
 
 def split_pieces(stream, whole_ref, base, keep_ref, send_ref):
@@ -114,27 +116,23 @@
     return [lax.broadcasted_iota(jnp.int32, (LANES, LANES), axis) for axis in range(2)]
 
 
-def own_gram_kernel(own_ref, keep_ref, send_ref, rest_ref, diagonal_ref, whole_ref):
+def own_gram_kernel(own_ref, below_ref, diagonal_ref):
     def store_below(rows, value):
-        whole_ref[rows, :] = value
+        below_ref[rows, :] = value.astype(below_ref.dtype)
 
     def store_diagonal(j, value):
         diagonal_ref[j] = value
 
     triangle(own_ref, own_ref, store_below, store_diagonal)
-    split_pieces(0, whole_ref, 0, keep_ref, send_ref)
-    rest_ref[...] = whole_ref[pl.ds(BASES[1], BELOW - BASES[1]), :]
 
 
 def own_gram(own):
     return pl.pallas_call(
         own_gram_kernel,
-        out_shape=half_shapes(0, own.dtype)
-        + [
-            jax.ShapeDtypeStruct((BELOW - BASES[1], LANES), jnp.float32),
+        out_shape=(
+            jax.ShapeDtypeStruct((BELOW, LANES), own.dtype),
             jax.ShapeDtypeStruct((BLOCKS, LANES, LANES), jnp.float32),
-        ],
-        scratch_shapes=[pltpu.VMEM((BELOW, LANES), jnp.float32)],
+        ),
         compiler_params=pltpu.CompilerParams(vmem_limit_bytes=8 * MIB),
         cost_estimate=pl.CostEstimate(
             flops=2 * (BELOW + 3 * HALF) * LANES * WIDTH, bytes_accessed=2 * HALF * WIDTH, transcendentals=0
@@ -143,19 +141,32 @@
     )(own)
 
 
+def sum_kernel(parts_ref, out_ref):
+    total = jnp.sum(parts_ref[...].astype(jnp.float32), axis=0).astype(out_ref.dtype)
+    for p in range(CHIPS):
+        out_ref[p] = total
+
+
+def sum_copies(parts):
+    return pl.pallas_call(
+        sum_kernel,
+        out_shape=jax.ShapeDtypeStruct(parts.shape, parts.dtype),
+        compiler_params=pltpu.CompilerParams(vmem_limit_bytes=4 * MIB),
+        name="sum_copies",
+    )(parts)
+
+
 def cross_gram_kernel(
-    rest_ref, diagonal_ref, own_ref, other_ref, keep_b_ref, send_b_ref, keep_c_ref, send_c_ref, whole_ref
+    diagonal_ref, own_ref, other_ref, keep_b_ref, send_b_ref, keep_c_ref, send_c_ref, whole_ref
 ):
-    start = BELOW - BASES[1]
-    whole_ref[pl.ds(0, start), :] = rest_ref[...]
     row, column = iotas()
     edges = []
 
     def store_below(rows, value):
-        whole_ref[pl.ds(start + rows.start, rows.size), :] = value
+        whole_ref[rows, :] = value
 
     def store_diagonal(j, value):
-        whole_ref[pl.ds(start + BELOW + j * LANES, LANES), :] = jnp.where(row >= column, diagonal_ref[j], value)
+        whole_ref[pl.ds(BELOW + j * LANES, LANES), :] = jnp.where(row >= column, diagonal_ref[j], value)
         edges.append(jnp.sum(jnp.where(row == column, value, 0.0), axis=0, keepdims=True))
 
     triangle(own_ref, other_ref, store_below, store_diagonal)
@@ -165,7 +176,7 @@
     split_pieces(2, whole_ref, BASES[2] - BASES[1], keep_c_ref, send_c_ref)
 
 
-def cross_gram(rest, diagonal, own, other):
+def cross_gram(diagonal, own, other):
     return pl.pallas_call(
         cross_gram_kernel,
         out_shape=half_shapes(1, own.dtype) + half_shapes(2, own.dtype),
@@ -175,7 +186,7 @@
             flops=2 * (BELOW + 3 * HALF) * LANES * WIDTH, bytes_accessed=4 * HALF * WIDTH, transcendentals=0
         ),
         name="cross_gram",
-    )(rest, diagonal, own, other)
+    )(diagonal, own, other)
 
 
 def exchange(value, stream, hop):
@@ -355,14 +366,15 @@
 def shards(iterate):
     pieces = split_columns(iterate.reshape(PANEL, COLS))
     own = lax.all_to_all(pieces, CHIP_AXES, 0, 0, tiled=True).reshape(HALF, WIDTH)
-    other = swap_cores(own)
-    keep_a, send_a, *rest = own_gram(own)
-    arrived_a = exchange(send_a, 0, 0)
-    keep_b, send_b, keep_c, send_c = cross_gram(*rest, own, other)
-    arrived_b, arrived_c = exchange(send_b, 1, 0), exchange(send_c, 2, 0)
-    arrived_a, arrived_b = lax.optimization_barrier((arrived_a, arrived_b))
-    first_hops = (keep_a, arrived_a), (keep_b, arrived_b), (keep_c, arrived_c)
-    streams = [sum_over_chips(s, *pair) for s, pair in enumerate(first_hops)]
+    other = pltpu.with_memory_space_constraint(swap_cores(own), pltpu.VMEM)
+    below, diagonal = own_gram(own)
+    below = lax.all_to_all(below.reshape(CHIPS, PIECES[0], LANES), CHIP_AXES, 0, 0, tiled=True)
+    keep_b, send_b, keep_c, send_c = cross_gram(diagonal, own, other)
+    below, arrived_b, arrived_c = lax.optimization_barrier((below, exchange(send_b, 1, 0), exchange(send_c, 2, 0)))
+    first_hops = (keep_b, arrived_b), (keep_c, arrived_c)
+    streams = [sum_over_chips(s + 1, *pair) for s, pair in enumerate(first_hops)]
+    below = lax.all_to_all(sum_copies(below), CHIP_AXES, 0, 0, tiled=True)
+    streams = [below, *streams]
     pieces = jnp.concatenate(streams, axis=1)
     pieces_other = swap_cores(pieces)
     packed, gram, square = own_square(pieces)

time: 136 us -> 152 us (1.12)
  starting transfers between devices: 16.1 us -> 25.3 us
  Pallas kernels: 13.6 us -> 19.1 us
  waiting for transfers between devices: 23.3 us -> 20 us
  other arithmetic: 0.67 us -> 3.29 us
  local copies, waits for them, and re-layouts: 1.66 us -> 4.16 us
    all_to_all x0 -> x2, starting transfers between devices: none -> 8.86 us  [the longest x1 5.38 us: shards(): below = lax.all_to_all(sum_copies(below), CHIP_AXES, 0, 0, tiled=True)]
    unnamed x2 -> x8, local copies, waits for them, and re-layouts: 1.66 us -> 4.16 us
    ppermute x2, waiting for transfers between devices: 4.05 us -> 1.61 us  [swap_cores(): return lax.ppermute(value, 'c', [(0, 1), (1, 0)])]
    pallas_call x1, Pallas kernels: 1.53 us -> 3.84 us  [cross_gram(): pl.pallas_call(cross_gram_kernel, out_shape=half_shapes(1, own.dtype) + h...]
    convert_element_type x3 -> x2, other arithmetic: 0.14 us -> 2.03 us  [sum_over_chips(): half = (keep + wide(arrived)).astype(kind).reshape(2, 2, *keep.shape[1:])]
    pallas_call x1, Pallas kernels: 7.11 us -> 8.75 us  [update_rows(): pl.pallas_call(update_kernel, out_shape=jax.ShapeDtypeStruct((STRIPES, CH...]
    pallas_call x1 -> x2, Pallas kernels: 1.46 us -> 3.04 us  [the longest x1 2.19 us: own_gram(): pl.pallas_call(own_gram_kernel, out_shape=(jax.ShapeDtypeStruct((BELOW, L...]
    ppermute x12 -> x8, waiting for transfers between devices: 19.2 us -> 18.3 us  [exchange(): return lax.ppermute(value, ('x', 'yh', 'c'), pairs)]
  transfers between devices with their start and end apart: 14 -> 12, of which waited for: 9 -> 8; matrix products, arithmetic and copies ran while one was open for 0% -> 2% of each run, Pallas kernels for 3% -> 5%
where the time goes in v10:
time: 152 us; the launch traced here: 151 us
  blocking collectives  79.2 us (52%)
  starting transfers between devices  25.3 us (17%)
  waiting for transfers between devices  20 us (13%)
  Pallas kernels  19.1 us (13%)
  local copies, waits for them, and re-layouts  4.16 us (3%)
  other arithmetic  3.29 us (2%)
    all_to_all x1, blocking collectives, shards(): received = lax.all_to_all(sent, ALL_CHIPS, 0, 0, tiled=True)  41.5 us
    all_to_all x1, blocking collectives, shards(): lax.all_to_all(pieces, CHIP_AXES, 0, 0, tiled=True).reshape(HALF, WIDTH)  37.7 us
    ppermute x8, waiting for transfers between devices, exchange(): return lax.ppermute(value, ('x', 'yh', 'c'), pairs)  18.3 us
    ppermute x8, starting transfers between devices, exchange(): return lax.ppermute(value, ('x', 'yh', 'c'), pairs)  16.2 us
    pallas_call x1, Pallas kernels, update_rows(): pl.pallas_call(update_kernel, out_shape=jax.ShapeDtypeStruct((STRIPES, CH...  8.75 us
    all_to_all x1, starting transfers between devices, shards(): below = lax.all_to_all(sum_copies(below), CHIP_AXES, 0, 0, tiled=True)  5.38 us
    unnamed x8, local copies, waits for them, and re-layouts  4.16 us
    pallas_call x1, Pallas kernels, cross_gram(): pl.pallas_call(cross_gram_kernel, out_shape=half_shapes(1, own.dtype) + h...  3.84 us
  transfers between devices with their start and end apart: 12, of which 8 were waited for; matrix products, arithmetic and copies ran while one was open for 2% of the time, Pallas kernels for 5%

profile of v10, /device:TPU:0, one launch (start us, length us, event | category | flops | bytes accessed | tf_op | source)
XLA Modules:
  0.0 151.3 jit_solution(6555477574706714276)
XLA Ops:
  0.0 0.0 copy-start
  0.0 1.7 %copy-done = bf16[1,96,12288]{2,1,0:T(8,128)(2,1)S(1)} copy-done((bf16[1,96,12288]{2,1,0:T(8,128)(2,1)S(1)}, bf16[1,96,12288]{2,1,0:T(8,128)(2,1)}, u32[]{:S(2)}) %copy-start) | copy-done | bytes 2359320
  1.7 0.6 split_columns.1
  2.3 37.7 %all_to_all.20 = bf16[8,96,1536]{2,1,0:T(8,128)(2,1)S(1)} all-to-all(bf16[8,96,1536]{2,1,0:T(8,128)(2,1)S(1)} %split_columns.1), channel_id=1, replica_groups=mesh['z'=4,'yl'=2,'x'=4,'yh'=2,'c'=2] {'x','yh'}, dimensions={0} | all-to-all | bytes 4718592 | tf_op jit(solution)/shard_map/all_to_all | solution.py:368
  40.0 0.0 collective-permute-start
  40.0 2.2 %own_gram.1 = (bf16[1920,128]{1,0:T(8,128)(2,1)}, f32[6,128,128]{2,1,0:T(8,128)S(1)}) custom-call(bf16[768,1536]{1,0:T(8,128)(2,1)S(1)} %bitcast.12), custom_call_target="tpu_custom_call" | custom-call | flops 1660944384 | bytes 2359296 | tf_op jit(solution)/shard_map/own_gram/pallas_call | solution.py:130
  42.2 0.0 copy-start.2
  42.2 0.8 copy-done.2
  42.9 3.5 %all-to-all-start.1 = ((bf16[8,240,128]{2,1,0:T(8,128)(2,1)}), bf16[8,240,128]{2,1,0:T(8,128)(2,1)S(1)}, u32[]{:S(2)}, u32[]{:S(2)}) async-start(bf16[8,240,128]{2,1,0:T(8,128)(2,1)} %bitcast.2), calls=%async_computation.1 | async-start | bytes 983040 | tf_op jit(solution)/shard_map/all_to_all | solution.py:371
  46.4 0.0 collective-permute-done.other_ref.x_other_ref
  46.4 0.0 copy-start.3
  46.4 1.0 copy-done.3
  47.4 3.8 %cross_gram.1 = (f32[4,176,128]{2,1,0:T(8,128)S(1)}, bf16[4,176,128]{2,1,0:T(8,128)(2,1)}, f32[4,176,128]{2,1,0:T(8,128)S(1)}, bf16[4,176,128]{2,1,0:T(8,128)(2,1)S(1)}) custom-call(f32[6,128,128]{2,1,0:T(8,128)S(1)} %copy-done.3, bf16[768,1536]{1,0:T(8,128)(2,1)S(1)} %bitcast.13, bf16[768,1536]{1,0:T(8,128)(2,1)} %collective-permute-done.other_ref.x_other_ref), custom_call_target="tpu_custom_call" | custom-call | flops 1660944384 | bytes 4718592 | tf_op jit(solution)/shard_map/cross_gram/pallas_call | solution.py:180
  51.3 0.0 copy-start.1
  51.3 0.7 copy-done.1
  52.0 3.2 %collective-permute-start.1 = (bf16[4,176,128]{2,1,0:T(8,128)(2,1)}, bf16[4,176,128]{2,1,0:T(8,128)(2,1)}, u32[]{:S(2)}, u32[]{:S(2)}) collective-permute-start(bf16[4,176,128]{2,1,0:T(8,128)(2,1)} %get-tuple-element.19), channel_id=1, source_target_pairs={{0,12},{1,3},{2,14},{3,1},{4,8},{5,7},{6,10},{7,5},{8,4},{9,11},{1... | collective-permute-start | bytes 540680 | tf_op jit(solution)/shard_map/ppermute | solution.py:200
  55.2 3.0 %collective-permute-start.2 = (bf16[4,176,128]{2,1,0:T(8,128)(2,1)S(1)}, bf16[4,176,128]{2,1,0:T(8,128)(2,1)}, u32[]{:S(2)}, u32[]{:S(2)}) collective-permute-start(bf16[4,176,128]{2,1,0:T(8,128)(2,1)S(1)} %get-tuple-element.20), channel_id=1, source_target_pairs={{0,2},{1,5},{2,0},{3,7},{4,6},{5,1},{6,4},{7,3},{8,10},{9,13},{10,... | collective-permute-start | bytes 540680 | tf_op jit(solution)/shard_map/ppermute | solution.py:200
  58.1 0.0 all-to-all-done.1.parts_ref
  58.1 0.9 collective-permute-done.1
  59.0 3.2 %collective-permute-done.2 = bf16[4,176,128]{2,1,0:T(8,128)(2,1)} collective-permute-done((bf16[4,176,128]{2,1,0:T(8,128)(2,1)S(1)}, bf16[4,176,128]{2,1,0:T(8,128)(2,1)}, u32[]{:S(2)}, u32[]{:S(2)}) %collective-permute-start.2) | collective-permute-done | bytes 180256 | tf_op jit(solution)/shard_map/ppermute | solution.py:200
  62.3 0.8 sum_copies.1
  63.1 5.4 %all-to-all-start.2 = ((bf16[8,240,128]{2,1,0:T(8,128)(2,1)}), bf16[8,240,128]{2,1,0:T(8,128)(2,1)S(1)}, u32[]{:S(2)}, u32[]{:S(2)}) async-start(bf16[8,240,128]{2,1,0:T(8,128)(2,1)} %sum_copies.1), calls=%async_computation.2 | async-start | bytes 983040 | tf_op jit(solution)/shard_map/all_to_all | solution.py:376
  68.5 1.1 add_convert_fusion.5
  69.6 3.6 %collective-permute-start.3 = (bf16[2,2,176,128]{3,2,1,0:T(8,128)(2,1)S(1)}, bf16[2,2,176,128]{3,2,1,0:T(8,128)(2,1)S(1)}, u32[]{:S(2)}, u32[]{:S(2)}) collective-permute-start(bf16[2,2,176,128]{3,2,1,0:T(8,128)(2,1)S(1)} %bitcast.22), channel_id=1, source_target_pairs={{0,2},{1,5},{2,0},{3,7},{4,6},{5,1},{6,4},{7,3},{8,10},{9,13},{10,... | collective-permute-start | bytes 540680 | tf_op jit(solution)/shard_map/ppermute | solution.py:200
  73.2 1.0 add_convert_fusion.2
  74.1 1.5 %collective-permute-start.6 = (bf16[2,2,176,128]{3,2,1,0:T(8,128)(2,1)S(1)}, bf16[2,2,176,128]{3,2,1,0:T(8,128)(2,1)S(1)}, u32[]{:S(2)}, u32[]{:S(2)}) collective-permute-start(bf16[2,2,176,128]{3,2,1,0:T(8,128)(2,1)S(1)} %bitcast.18), channel_id=1, source_target_pairs={{0,4},{1,13},{2,6},{3,15},{4,0},{5,9},{6,2},{7,11},{8,12},{9,5},{1... | collective-permute-start | bytes 540680 | tf_op jit(solution)/shard_map/ppermute | solution.py:200
  75.7 4.6 %collective-permute-done.3 = bf16[2,2,176,128]{3,2,1,0:T(8,128)(2,1)S(1)} collective-permute-done((bf16[2,2,176,128]{3,2,1,0:T(8,128)(2,1)S(1)}, bf16[2,2,176,128]{3,2,1,0:T(8,128)(2,1)S(1)}, u32[]{:S(2)}, u32[]{:S(2)}) %collective-permute-start.3) | collective-permute-done | bytes 180256 | tf_op jit(solution)/shard_map/ppermute | solution.py:200
  80.4 0.6 collective-permute-start.4
  81.0 0.0 collective-permute-done.6
  81.1 1.5 collective-permute-start.7
  82.6 3.4 %collective-permute-done.4 = bf16[2,2,176,128]{3,2,1,0:T(8,128)(2,1)S(1)} collective-permute-done((bf16[2,2,176,128]{3,2,1,0:T(8,128)(2,1)S(1)}, bf16[2,2,176,128]{3,2,1,0:T(8,128)(2,1)S(1)}, u32[]{:S(2)}, u32[]{:S(2)}) %collective-permute-start.4) | collective-permute-done | bytes 180256 | tf_op jit(solution)/shard_map/ppermute | solution.py:200
  86.0 1.3 collective-permute-start.5
  87.3 0.6 collective-permute-done.7
  88.0 1.5 collective-permute-start.8
  89.5 0.0 all-to-all-done.2
  89.5 3.3 %collective-permute-done.5 = bf16[4,176,128]{2,1,0:T(8,128)(2,1)S(1)} collective-permute-done((bf16[4,176,128]{2,1,0:T(8,128)(2,1)S(1)}, bf16[4,176,128]{2,1,0:T(8,128)(2,1)S(1)}, u32[]{:S(2)}, u32[]{:S(2)}) %collective-permute-start.5) | collective-permute-done | bytes 180256 | tf_op jit(solution)/shard_map/ppermute | solution.py:200
  92.8 2.3 %collective-permute-done.8 = bf16[4,176,128]{2,1,0:T(8,128)(2,1)} collective-permute-done((bf16[4,176,128]{2,1,0:T(8,128)(2,1)S(1)}, bf16[4,176,128]{2,1,0:T(8,128)(2,1)}, u32[]{:S(2)}, u32[]{:S(2)}) %collective-permute-start.8) | collective-permute-done | bytes 180256 | tf_op jit(solution)/shard_map/ppermute | solution.py:200
  95.2 1.0 maximum_maximum_fusion.pieces_ref
  96.2 0.3 collective-permute-start.9
  96.4 1.3 own_square.1
  97.7 1.6 %collective-permute-done.9.pieces_ref = bf16[8,592,128]{2,1,0:T(8,128)(2,1)S(1)} collective-permute-done((bf16[8,592,128]{2,1,0:T(8,128)(2,1)S(1)}, bf16[8,592,128]{2,1,0:T(8,128)(2,1)S(1)}, u32[]{:S(2)}, u32[]{:S(2)}) %collective-permute-start.9) | collective-permute-done | bytes 1212448 | tf_op jit(solution)/shard_map/ppermute | solution.py:363
  99.3 8.8 %update_rows.1 = bf16[8,8,144,128]{3,2,1,0:T(8,128)(2,1)S(1)} custom-call(bf16[4736,128]{1,0:T(8,128)(2,1)S(1)} %get-tuple-element.26.own_ref, bf16[8,592,128]{2,1,0:T(8,128)(2,1)S(1)} %collective-permute-done.9.pieces_ref, bf16[768,768]{1,0:T(8,128)(2,1)S(1)} %get-tuple-element.27.gram_ref, f32[768,768]{1,0:T(8,128)S(1)} %get-tuple-element.28.square_ref, ...), custom_call_target="tpu_custom_call" | custom-call | flops 6341787648 | bytes 11796480 | tf_op jit(solution)/shard_map/update_rows/pallas_call | solution.py:315
  108.1 41.5 %all_to_all.21 = bf16[64,144,128]{2,1,0:T(8,128)(2,1)S(1)} all-to-all(bf16[64,144,128]{2,1,0:T(8,128)(2,1)S(1)} %bitcast.15), channel_id=1, replica_groups=mesh['z'=4,'yl'=2,'x'=4,'yh'=2,'c'=2] {'z','yl','x','yh'}, dimensions={0} | all-to-all | bytes 4718592 | tf_op jit(solution)/shard_map/all_to_all | solution.py:383
  149.6 1.6 %join_columns.1 = bf16[8,96,1536]{2,1,0:T(8,128)(2,1)} custom-call(bf16[8,8,144,128]{3,2,1,0:T(8,128)(2,1)S(1)} %bitcast.9), custom_call_target="tpu_custom_call" | custom-call | tf_op jit(solution)/shard_map/join_columns/pallas_call | solution.py:351
  (8 shorter events, 0.3 us)
Async XLA Ops:
  0.0 1.7 %copy-start = (bf16[1,96,12288]{2,1,0:T(8,128)(2,1)S(1)}, bf16[1,96,12288]{2,1,0:T(8,128)(2,1)}, u32[]{:S(2)}) copy-start(bf16[1,96,12288]{2,1,0:T(8,128)(2,1)} %param.1) | copy-start | bytes 7077892
  40.0 6.5 %collective-permute-start = (bf16[768,1536]{1,0:T(8,128)(2,1)S(1)}, bf16[768,1536]{1,0:T(8,128)(2,1)}, u32[]{:S(2)}, u32[]{:S(2)}) collective-permute-start(bf16[768,1536]{1,0:T(8,128)(2,1)S(1)} %bitcast.11), channel_id=1, source_target_pairs={{0,1},{1,0},{2,3},{3,2},{4,5},{5,4},{6,7},{7,6},{8,9},{9,8},{10,11... | collective-permute-start | bytes 7077896 | tf_op jit(solution)/shard_map/ppermute | solution.py:363
  42.2 0.8 copy-start.2
  42.9 15.2 %all-to-all-start.1 = ((bf16[8,240,128]{2,1,0:T(8,128)(2,1)}), bf16[8,240,128]{2,1,0:T(8,128)(2,1)S(1)}, u32[]{:S(2)}, u32[]{:S(2)}) async-start(bf16[8,240,128]{2,1,0:T(8,128)(2,1)} %bitcast.2), calls=%async_computation.1 | async-start | bytes 983040 | tf_op jit(solution)/shard_map/all_to_all | solution.py:371
  46.4 1.0 copy-start.3
  51.3 0.7 copy-start.1
  52.0 7.0 %collective-permute-start.1 = (bf16[4,176,128]{2,1,0:T(8,128)(2,1)}, bf16[4,176,128]{2,1,0:T(8,128)(2,1)}, u32[]{:S(2)}, u32[]{:S(2)}) collective-permute-start(bf16[4,176,128]{2,1,0:T(8,128)(2,1)} %get-tuple-element.19), channel_id=1, source_target_pairs={{0,12},{1,3},{2,14},{3,1},{4,8},{5,7},{6,10},{7,5},{8,4},{9,11},{1... | collective-permute-start | bytes 540680 | tf_op jit(solution)/shard_map/ppermute | solution.py:200
  55.2 7.1 %collective-permute-start.2 = (bf16[4,176,128]{2,1,0:T(8,128)(2,1)S(1)}, bf16[4,176,128]{2,1,0:T(8,128)(2,1)}, u32[]{:S(2)}, u32[]{:S(2)}) collective-permute-start(bf16[4,176,128]{2,1,0:T(8,128)(2,1)S(1)} %get-tuple-element.20), channel_id=1, source_target_pairs={{0,2},{1,5},{2,0},{3,7},{4,6},{5,1},{6,4},{7,3},{8,10},{9,13},{10,... | collective-permute-start | bytes 540680 | tf_op jit(solution)/shard_map/ppermute | solution.py:200
  63.1 26.4 %all-to-all-start.2 = ((bf16[8,240,128]{2,1,0:T(8,128)(2,1)}), bf16[8,240,128]{2,1,0:T(8,128)(2,1)S(1)}, u32[]{:S(2)}, u32[]{:S(2)}) async-start(bf16[8,240,128]{2,1,0:T(8,128)(2,1)} %sum_copies.1), calls=%async_computation.2 | async-start | bytes 983040 | tf_op jit(solution)/shard_map/all_to_all | solution.py:376
  69.6 10.7 %collective-permute-start.3 = (bf16[2,2,176,128]{3,2,1,0:T(8,128)(2,1)S(1)}, bf16[2,2,176,128]{3,2,1,0:T(8,128)(2,1)S(1)}, u32[]{:S(2)}, u32[]{:S(2)}) collective-permute-start(bf16[2,2,176,128]{3,2,1,0:T(8,128)(2,1)S(1)} %bitcast.22), channel_id=1, source_target_pairs={{0,2},{1,5},{2,0},{3,7},{4,6},{5,1},{6,4},{7,3},{8,10},{9,13},{10,... | collective-permute-start | bytes 540680 | tf_op jit(solution)/shard_map/ppermute | solution.py:200
  74.1 6.9 %collective-permute-start.6 = (bf16[2,2,176,128]{3,2,1,0:T(8,128)(2,1)S(1)}, bf16[2,2,176,128]{3,2,1,0:T(8,128)(2,1)S(1)}, u32[]{:S(2)}, u32[]{:S(2)}) collective-permute-start(bf16[2,2,176,128]{3,2,1,0:T(8,128)(2,1)S(1)} %bitcast.18), channel_id=1, source_target_pairs={{0,4},{1,13},{2,6},{3,15},{4,0},{5,9},{6,2},{7,11},{8,12},{9,5},{1... | collective-permute-start | bytes 540680 | tf_op jit(solution)/shard_map/ppermute | solution.py:200
  80.4 5.6 %collective-permute-start.4 = (bf16[2,2,176,128]{3,2,1,0:T(8,128)(2,1)S(1)}, bf16[2,2,176,128]{3,2,1,0:T(8,128)(2,1)S(1)}, u32[]{:S(2)}, u32[]{:S(2)}) collective-permute-start(bf16[2,2,176,128]{3,2,1,0:T(8,128)(2,1)S(1)} %add_convert_fusion.4), channel_id=1, source_target_pairs={{0,4},{1,13},{2,6},{3,15},{4,0},{5,9},{6,2},{7,11},{8,12},{9,5},{1... | collective-permute-start | bytes 540680 | tf_op jit(solution)/shard_map/ppermute | solution.py:200
  81.1 6.8 %collective-permute-start.7 = (bf16[2,2,176,128]{3,2,1,0:T(8,128)(2,1)S(1)}, bf16[2,2,176,128]{3,2,1,0:T(8,128)(2,1)S(1)}, u32[]{:S(2)}, u32[]{:S(2)}) collective-permute-start(bf16[2,2,176,128]{3,2,1,0:T(8,128)(2,1)S(1)} %add_convert_fusion.1), channel_id=1, source_target_pairs={{0,12},{1,3},{2,14},{3,1},{4,8},{5,7},{6,10},{7,5},{8,4},{9,11},{1... | collective-permute-start | bytes 540680 | tf_op jit(solution)/shard_map/ppermute | solution.py:200
  86.0 6.8 %collective-permute-start.5 = (bf16[4,176,128]{2,1,0:T(8,128)(2,1)S(1)}, bf16[4,176,128]{2,1,0:T(8,128)(2,1)S(1)}, u32[]{:S(2)}, u32[]{:S(2)}) collective-permute-start(bf16[4,176,128]{2,1,0:T(8,128)(2,1)S(1)} %bitcast.16), channel_id=1, source_target_pairs={{0,12},{1,3},{2,14},{3,1},{4,8},{5,7},{6,10},{7,5},{8,4},{9,11},{1... | collective-permute-start | bytes 540680 | tf_op jit(solution)/shard_map/ppermute | solution.py:200
  88.0 7.2 %collective-permute-start.8 = (bf16[4,176,128]{2,1,0:T(8,128)(2,1)S(1)}, bf16[4,176,128]{2,1,0:T(8,128)(2,1)}, u32[]{:S(2)}, u32[]{:S(2)}) collective-permute-start(bf16[4,176,128]{2,1,0:T(8,128)(2,1)S(1)} %bitcast.20), channel_id=1, source_target_pairs={{0,2},{1,5},{2,0},{3,7},{4,6},{5,1},{6,4},{7,3},{8,10},{9,13},{10,... | collective-permute-start | bytes 540680 | tf_op jit(solution)/shard_map/ppermute | solution.py:200
  96.2 3.2 %collective-permute-start.9 = (bf16[8,592,128]{2,1,0:T(8,128)(2,1)S(1)}, bf16[8,592,128]{2,1,0:T(8,128)(2,1)S(1)}, u32[]{:S(2)}, u32[]{:S(2)}) collective-permute-start(bf16[8,592,128]{2,1,0:T(8,128)(2,1)S(1)} %maximum_maximum_fusion.pieces_ref), channel_id=1, source_target_pairs={{0,1},{1,0},{2,3},{3,2},{4,5},{5,4},{6,7},{7,6},{8,9},{9,8},{10,11... | collective-permute-start | bytes 3637256 | tf_op jit(solution)/shard_map/ppermute | solution.py:363

commit v11 on v8

--- a/solution.py
+++ b/solution.py
@@ -193,10 +193,14 @@
     return value.astype(jnp.float32)
 
 
-def sum_over_chips(stream, keep, arrived):
+def after(value, *others):
+    return lax.optimization_barrier((value, *others))[0]
+
+
+def sum_over_chips(stream, keep, arrived, *others):
     kind = arrived.dtype
     half = (keep + wide(arrived)).astype(kind).reshape(2, 2, *keep.shape[1:])
-    half = (wide(half) + wide(exchange(half, stream, 1))[::-1]).astype(kind)
+    half = (wide(half) + wide(after(exchange(half, stream, 1), *others))[::-1]).astype(kind)
     half = (wide(half) + wide(exchange(half, stream, 2))[:, ::-1]).astype(kind).reshape(arrived.shape)
     return jnp.concatenate([half, exchange(half, stream, 0)])
 
@@ -360,9 +364,11 @@
     arrived_a = exchange(send_a, 0, 0)
     keep_b, send_b, keep_c, send_c = cross_gram(*rest, own, other)
     arrived_b, arrived_c = exchange(send_b, 1, 0), exchange(send_c, 2, 0)
-    arrived_a, arrived_b = lax.optimization_barrier((arrived_a, arrived_b))
-    first_hops = (keep_a, arrived_a), (keep_b, arrived_b), (keep_c, arrived_c)
-    streams = [sum_over_chips(s, *pair) for s, pair in enumerate(first_hops)]
+    streams = [
+        sum_over_chips(0, keep_a, after(arrived_a, send_b, send_c), arrived_b),
+        sum_over_chips(1, keep_b, arrived_b),
+        sum_over_chips(2, keep_c, arrived_c),
+    ]
     pieces = jnp.concatenate(streams, axis=1)
     pieces_other = swap_cores(pieces)
     packed, gram, square = own_square(pieces)

time: 136 us -> 133 us (0.978)
  waiting for transfers between devices: 23.3 us -> 21.3 us
    ppermute x12, waiting for transfers between devices: 19.2 us -> 17.2 us  [exchange(): return lax.ppermute(value, ('x', 'yh', 'c'), pairs)]
  transfers between devices with their start and end apart: 14 -> 14, of which waited for: 9 -> 11; matrix products, arithmetic and copies ran while one was open for 0% -> 0% of each run, Pallas kernels for 3% -> 3%
where the time goes in v11:
time: 133 us
  blocking collectives  79.4 us (60%)
  waiting for transfers between devices  21.3 us (16%)
  starting transfers between devices  16.1 us (12%)
  Pallas kernels  13.6 us (10%)
  local copies, waits for them, and re-layouts  1.66 us (1%)
    all_to_all x1, blocking collectives, shards(): received = lax.all_to_all(sent, ALL_CHIPS, 0, 0, tiled=True)  41.7 us
    all_to_all x1, blocking collectives, shards(): lax.all_to_all(pieces, CHIP_AXES, 0, 0, tiled=True).reshape(HALF, WIDTH)  37.7 us
    ppermute x12, waiting for transfers between devices, exchange(): return lax.ppermute(value, ('x', 'yh', 'c'), pairs)  17.2 us
    ppermute x12, starting transfers between devices, exchange(): return lax.ppermute(value, ('x', 'yh', 'c'), pairs)  15.9 us
    pallas_call x1, Pallas kernels, update_rows(): pl.pallas_call(update_kernel, out_shape=jax.ShapeDtypeStruct((STRIPES, CH...  7.11 us
    ppermute x2, waiting for transfers between devices, swap_cores(): return lax.ppermute(value, 'c', [(0, 1), (1, 0)])  4.05 us
  transfers between devices with their start and end apart: 14, of which 11 were waited for; matrix products, arithmetic and copies ran while one was open for 0% of the time, Pallas kernels for 3%

profile of v11, /device:TPU:0, one launch (start us, length us, event | category | flops | bytes accessed | tf_op | source)
XLA Modules:
  0.0 133.0 jit_solution(13133108216042555859)
XLA Ops:
  0.0 0.0 copy-start
  0.0 1.7 %copy-done = bf16[1,96,12288]{2,1,0:T(8,128)(2,1)S(1)} copy-done((bf16[1,96,12288]{2,1,0:T(8,128)(2,1)S(1)}, bf16[1,96,12288]{2,1,0:T(8,128)(2,1)}, u32[]{:S(2)}) %copy-start) | copy-done | bytes 2359320
  1.7 0.6 split_columns.1
  2.3 37.7 %all_to_all.10 = bf16[8,96,1536]{2,1,0:T(8,128)(2,1)S(1)} all-to-all(bf16[8,96,1536]{2,1,0:T(8,128)(2,1)S(1)} %split_columns.1), channel_id=1, replica_groups=mesh['z'=4,'yl'=2,'x'=4,'yh'=2,'c'=2] {'x','yh'}, dimensions={0} | all-to-all | bytes 4718592 | tf_op jit(solution)/shard_map/all_to_all | solution.py:361
  40.0 0.0 collective-permute-start.1
  40.0 1.5 %own_gram.1 = (f32[4,208,128]{2,1,0:T(8,128)S(1)}, bf16[4,208,128]{2,1,0:T(8,128)(2,1)S(1)}, f32[256,128]{1,0:T(8,128)S(1)}, f32[6,128,128]{2,1,0:T(8,128)S(1)}) custom-call(bf16[768,1536]{1,0:T(8,128)(2,1)S(1)} %bitcast.13), custom_call_target="tpu_custom_call" | custom-call | flops 1660944384 | bytes 2359296 | tf_op jit(solution)/shard_map/own_gram/pallas_call | solution.py:130
  41.4 0.6 collective-permute-start
  42.0 2.5 %collective-permute-done.1.other_ref.x_other_ref = bf16[768,1536]{1,0:T(8,128)(2,1)S(1)} collective-permute-done((bf16[768,1536]{1,0:T(8,128)(2,1)S(1)}, bf16[768,1536]{1,0:T(8,128)(2,1)S(1)}, u32[]{:S(2)}, u32[]{:S(2)}) %collective-permute-start.1) | collective-permute-done | bytes 2359328 | tf_op jit(solution)/shard_map/ppermute | solution.py:356
  44.5 1.5 %cross_gram.1 = (f32[4,192,128]{2,1,0:T(8,128)S(1)}, bf16[4,192,128]{2,1,0:T(8,128)(2,1)S(1)}, f32[4,192,128]{2,1,0:T(8,128)S(1)}, bf16[4,192,128]{2,1,0:T(8,128)(2,1)S(1)}) custom-call(f32[256,128]{1,0:T(8,128)S(1)} %get-tuple-element.20.rest_ref, f32[6,128,128]{2,1,0:T(8,128)S(1)} %get-tuple-element.21.diagonal_ref, bf16[768,1536]{1,0:T(8,128)(2,1)S(1)} %bitcast.14, ...), custom_call_target="tpu_custom_call" | custom-call | flops 1660944384 | bytes 4718592 | tf_op jit(solution)/shard_map/cross_gram/pallas_call | solution.py:169
  46.0 1.5 %collective-permute-start.3 = (bf16[4,192,128]{2,1,0:T(8,128)(2,1)S(1)}, bf16[4,192,128]{2,1,0:T(8,128)(2,1)S(1)}, u32[]{:S(2)}, u32[]{:S(2)}) collective-permute-start(bf16[4,192,128]{2,1,0:T(8,128)(2,1)S(1)} %get-tuple-element.22), channel_id=1, source_target_pairs={{0,12},{1,3},{2,14},{3,1},{4,8},{5,7},{6,10},{7,5},{8,4},{9,11},{1... | collective-permute-start | bytes 589832 | tf_op jit(solution)/shard_map/ppermute | solution.py:189
  47.5 1.3 collective-permute-start.9
  48.8 0.0 collective-permute-done
  48.9 2.2 %collective-permute-start.2 = (bf16[2,2,208,128]{3,2,1,0:T(8,128)(2,1)S(1)}, bf16[2,2,208,128]{3,2,1,0:T(8,128)(2,1)S(1)}, u32[]{:S(2)}, u32[]{:S(2)}) collective-permute-start(bf16[2,2,208,128]{3,2,1,0:T(8,128)(2,1)S(1)} %bitcast.19), channel_id=1, source_target_pairs={{0,12},{1,3},{2,14},{3,1},{4,8},{5,7},{6,10},{7,5},{8,4},{9,11},{1... | collective-permute-start | bytes 638984 | tf_op jit(solution)/shard_map/ppermute | solution.py:189
  51.0 2.0 %collective-permute-done.3 = bf16[4,192,128]{2,1,0:T(8,128)(2,1)S(1)} collective-permute-done((bf16[4,192,128]{2,1,0:T(8,128)(2,1)S(1)}, bf16[4,192,128]{2,1,0:T(8,128)(2,1)S(1)}, u32[]{:S(2)}, u32[]{:S(2)}) %collective-permute-start.3) | collective-permute-done | bytes 196640 | tf_op jit(solution)/shard_map/ppermute | solution.py:189
  53.1 1.6 %collective-permute-start.6 = (bf16[2,2,192,128]{3,2,1,0:T(8,128)(2,1)S(1)}, bf16[2,2,192,128]{3,2,1,0:T(8,128)(2,1)S(1)}, u32[]{:S(2)}, u32[]{:S(2)}) collective-permute-start(bf16[2,2,192,128]{3,2,1,0:T(8,128)(2,1)S(1)} %bitcast.25), channel_id=1, source_target_pairs={{0,2},{1,5},{2,0},{3,7},{4,6},{5,1},{6,4},{7,3},{8,10},{9,13},{10,... | collective-permute-start | bytes 589832 | tf_op jit(solution)/shard_map/ppermute | solution.py:189
  54.7 2.2 %collective-permute-done.9 = bf16[4,192,128]{2,1,0:T(8,128)(2,1)S(1)} collective-permute-done((bf16[4,192,128]{2,1,0:T(8,128)(2,1)S(1)}, bf16[4,192,128]{2,1,0:T(8,128)(2,1)S(1)}, u32[]{:S(2)}, u32[]{:S(2)}) %collective-permute-start.9) | collective-permute-done | bytes 196640 | tf_op jit(solution)/shard_map/ppermute | solution.py:189
  56.9 0.1 collective-permute-start.10
  57.0 0.0 collective-permute-done.2
  57.1 1.4 %collective-permute-start.4 = (bf16[2,2,208,128]{3,2,1,0:T(8,128)(2,1)S(1)}, bf16[2,2,208,128]{3,2,1,0:T(8,128)(2,1)S(1)}, u32[]{:S(2)}, u32[]{:S(2)}) collective-permute-start(bf16[2,2,208,128]{3,2,1,0:T(8,128)(2,1)S(1)} %add_convert_fusion.1), channel_id=1, source_target_pairs={{0,2},{1,5},{2,0},{3,7},{4,6},{5,1},{6,4},{7,3},{8,10},{9,13},{10,... | collective-permute-start | bytes 638984 | tf_op jit(solution)/shard_map/ppermute | solution.py:189
  58.5 1.8 %collective-permute-done.6 = bf16[2,2,192,128]{3,2,1,0:T(8,128)(2,1)S(1)} collective-permute-done((bf16[2,2,192,128]{3,2,1,0:T(8,128)(2,1)S(1)}, bf16[2,2,192,128]{3,2,1,0:T(8,128)(2,1)S(1)}, u32[]{:S(2)}, u32[]{:S(2)}) %collective-permute-start.6) | collective-permute-done | bytes 196640 | tf_op jit(solution)/shard_map/ppermute | solution.py:189
  60.3 0.1 add_convert_fusion.7
  60.4 0.2 collective-permute-start.7
  60.6 3.4 %collective-permute-done.10 = bf16[2,2,192,128]{3,2,1,0:T(8,128)(2,1)S(1)} collective-permute-done((bf16[2,2,192,128]{3,2,1,0:T(8,128)(2,1)S(1)}, bf16[2,2,192,128]{3,2,1,0:T(8,128)(2,1)S(1)}, u32[]{:S(2)}, u32[]{:S(2)}) %collective-permute-start.10) | collective-permute-done | bytes 196640 | tf_op jit(solution)/shard_map/ppermute | solution.py:189
  64.2 1.1 collective-permute-start.11
  65.2 0.7 collective-permute-done.4
  66.1 2.4 %collective-permute-start.5 = (bf16[4,208,128]{2,1,0:T(8,128)(2,1)S(1)}, bf16[4,208,128]{2,1,0:T(8,128)(2,1)S(1)}, u32[]{:S(2)}, u32[]{:S(2)}) collective-permute-start(bf16[4,208,128]{2,1,0:T(8,128)(2,1)S(1)} %bitcast.17), channel_id=1, source_target_pairs={{0,4},{1,13},{2,6},{3,15},{4,0},{5,9},{6,2},{7,11},{8,12},{9,5},{1... | collective-permute-start | bytes 638984 | tf_op jit(solution)/shard_map/ppermute | solution.py:189
  68.4 0.0 collective-permute-done.7
  68.5 1.8 %collective-permute-start.8 = (bf16[4,192,128]{2,1,0:T(8,128)(2,1)S(1)}, bf16[4,192,128]{2,1,0:T(8,128)(2,1)S(1)}, u32[]{:S(2)}, u32[]{:S(2)}) collective-permute-start(bf16[4,192,128]{2,1,0:T(8,128)(2,1)S(1)} %bitcast.21), channel_id=1, source_target_pairs={{0,12},{1,3},{2,14},{3,1},{4,8},{5,7},{6,10},{7,5},{8,4},{9,11},{1... | collective-permute-start | bytes 589832 | tf_op jit(solution)/shard_map/ppermute | solution.py:189
  70.3 1.5 %collective-permute-done.11 = bf16[2,2,192,128]{3,2,1,0:T(8,128)(2,1)S(1)} collective-permute-done((bf16[2,2,192,128]{3,2,1,0:T(8,128)(2,1)S(1)}, bf16[2,2,192,128]{3,2,1,0:T(8,128)(2,1)S(1)}, u32[]{:S(2)}, u32[]{:S(2)}) %collective-permute-start.11) | collective-permute-done | bytes 196640 | tf_op jit(solution)/shard_map/ppermute | solution.py:189
  72.0 1.7 %collective-permute-start.12 = (bf16[4,192,128]{2,1,0:T(8,128)(2,1)S(1)}, bf16[4,192,128]{2,1,0:T(8,128)(2,1)S(1)}, u32[]{:S(2)}, u32[]{:S(2)}) collective-permute-start(bf16[4,192,128]{2,1,0:T(8,128)(2,1)S(1)} %bitcast.23), channel_id=1, source_target_pairs={{0,2},{1,5},{2,0},{3,7},{4,6},{5,1},{6,4},{7,3},{8,10},{9,13},{10,... | collective-permute-start | bytes 589832 | tf_op jit(solution)/shard_map/ppermute | solution.py:189
  73.7 0.2 collective-permute-done.5
  73.9 1.6 %collective-permute-done.8 = bf16[4,192,128]{2,1,0:T(8,128)(2,1)S(1)} collective-permute-done((bf16[4,192,128]{2,1,0:T(8,128)(2,1)S(1)}, bf16[4,192,128]{2,1,0:T(8,128)(2,1)S(1)}, u32[]{:S(2)}, u32[]{:S(2)}) %collective-permute-start.8) | collective-permute-done | bytes 196640 | tf_op jit(solution)/shard_map/ppermute | solution.py:189
  75.5 3.7 %collective-permute-done.12 = bf16[4,192,128]{2,1,0:T(8,128)(2,1)S(1)} collective-permute-done((bf16[4,192,128]{2,1,0:T(8,128)(2,1)S(1)}, bf16[4,192,128]{2,1,0:T(8,128)(2,1)S(1)}, u32[]{:S(2)}, u32[]{:S(2)}) %collective-permute-start.12) | collective-permute-done | bytes 196640 | tf_op jit(solution)/shard_map/ppermute | solution.py:189
  79.2 0.1 maximum_maximum_fusion.pieces_ref
  79.3 0.3 collective-permute-start.13
  79.6 1.3 own_square.1
  80.9 1.6 %collective-permute-done.13.pieces_ref = bf16[8,592,128]{2,1,0:T(8,128)(2,1)S(1)} collective-permute-done((bf16[8,592,128]{2,1,0:T(8,128)(2,1)S(1)}, bf16[8,592,128]{2,1,0:T(8,128)(2,1)S(1)}, u32[]{:S(2)}, u32[]{:S(2)}) %collective-permute-start.13) | collective-permute-done | bytes 1212448 | tf_op jit(solution)/shard_map/ppermute | solution.py:356
  82.5 7.1 %update_rows.1 = bf16[8,8,144,128]{3,2,1,0:T(8,128)(2,1)S(1)} custom-call(bf16[4736,128]{1,0:T(8,128)(2,1)S(1)} %get-tuple-element.28.own_ref, bf16[8,592,128]{2,1,0:T(8,128)(2,1)S(1)} %collective-permute-done.13.pieces_ref, bf16[768,768]{1,0:T(8,128)(2,1)S(1)} %get-tuple-element.29.gram_ref, f32[768,768]{1,0:T(8,128)S(1)} %get-tuple-element.30.square_ref, ...), custom_call_target="tpu_custom_call" | custom-call | flops 6341787648 | bytes 11796480 | tf_op jit(solution)/shard_map/update_rows/pallas_call | solution.py:308
  89.6 41.7 %all_to_all.11 = bf16[64,144,128]{2,1,0:T(8,128)(2,1)S(1)} all-to-all(bf16[64,144,128]{2,1,0:T(8,128)(2,1)S(1)} %bitcast.16), channel_id=1, replica_groups=mesh['z'=4,'yl'=2,'x'=4,'yh'=2,'c'=2] {'z','yl','x','yh'}, dimensions={0} | all-to-all | bytes 4718592 | tf_op jit(solution)/shard_map/all_to_all | solution.py:377
  131.3 1.6 %join_columns.1 = bf16[8,96,1536]{2,1,0:T(8,128)(2,1)} custom-call(bf16[8,8,144,128]{3,2,1,0:T(8,128)(2,1)S(1)} %bitcast.10), custom_call_target="tpu_custom_call" | custom-call | tf_op jit(solution)/shard_map/join_columns/pallas_call | solution.py:344
  (14 shorter events, 0.5 us)
Async XLA Ops:
  0.0 1.7 %copy-start = (bf16[1,96,12288]{2,1,0:T(8,128)(2,1)S(1)}, bf16[1,96,12288]{2,1,0:T(8,128)(2,1)}, u32[]{:S(2)}) copy-start(bf16[1,96,12288]{2,1,0:T(8,128)(2,1)} %param.1) | copy-start | bytes 7077892
  40.0 4.5 %collective-permute-start.1 = (bf16[768,1536]{1,0:T(8,128)(2,1)S(1)}, bf16[768,1536]{1,0:T(8,128)(2,1)S(1)}, u32[]{:S(2)}, u32[]{:S(2)}) collective-permute-start(bf16[768,1536]{1,0:T(8,128)(2,1)S(1)} %bitcast.12), channel_id=1, source_target_pairs={{0,1},{1,0},{2,3},{3,2},{4,5},{5,4},{6,7},{7,6},{8,9},{9,8},{10,11... | collective-permute-start | bytes 7077896 | tf_op jit(solution)/shard_map/ppermute | solution.py:356
  41.4 7.4 %collective-permute-start = (bf16[4,208,128]{2,1,0:T(8,128)(2,1)S(1)}, bf16[4,208,128]{2,1,0:T(8,128)(2,1)S(1)}, u32[]{:S(2)}, u32[]{:S(2)}) collective-permute-start(bf16[4,208,128]{2,1,0:T(8,128)(2,1)S(1)} %get-tuple-element.19), channel_id=1, source_target_pairs={{0,4},{1,13},{2,6},{3,15},{4,0},{5,9},{6,2},{7,11},{8,12},{9,5},{1... | collective-permute-start | bytes 638984 | tf_op jit(solution)/shard_map/ppermute | solution.py:189
  46.0 7.0 %collective-permute-start.3 = (bf16[4,192,128]{2,1,0:T(8,128)(2,1)S(1)}, bf16[4,192,128]{2,1,0:T(8,128)(2,1)S(1)}, u32[]{:S(2)}, u32[]{:S(2)}) collective-permute-start(bf16[4,192,128]{2,1,0:T(8,128)(2,1)S(1)} %get-tuple-element.22), channel_id=1, source_target_pairs={{0,12},{1,3},{2,14},{3,1},{4,8},{5,7},{6,10},{7,5},{8,4},{9,11},{1... | collective-permute-start | bytes 589832 | tf_op jit(solution)/shard_map/ppermute | solution.py:189
  47.5 9.3 %collective-permute-start.9 = (bf16[4,192,128]{2,1,0:T(8,128)(2,1)S(1)}, bf16[4,192,128]{2,1,0:T(8,128)(2,1)S(1)}, u32[]{:S(2)}, u32[]{:S(2)}) collective-permute-start(bf16[4,192,128]{2,1,0:T(8,128)(2,1)S(1)} %get-tuple-element.23), channel_id=1, source_target_pairs={{0,2},{1,5},{2,0},{3,7},{4,6},{5,1},{6,4},{7,3},{8,10},{9,13},{10,... | collective-permute-start | bytes 589832 | tf_op jit(solution)/shard_map/ppermute | solution.py:189
  48.9 8.1 %collective-permute-start.2 = (bf16[2,2,208,128]{3,2,1,0:T(8,128)(2,1)S(1)}, bf16[2,2,208,128]{3,2,1,0:T(8,128)(2,1)S(1)}, u32[]{:S(2)}, u32[]{:S(2)}) collective-permute-start(bf16[2,2,208,128]{3,2,1,0:T(8,128)(2,1)S(1)} %bitcast.19), channel_id=1, source_target_pairs={{0,12},{1,3},{2,14},{3,1},{4,8},{5,7},{6,10},{7,5},{8,4},{9,11},{1... | collective-permute-start | bytes 638984 | tf_op jit(solution)/shard_map/ppermute | solution.py:189
  53.1 7.3 %collective-permute-start.6 = (bf16[2,2,192,128]{3,2,1,0:T(8,128)(2,1)S(1)}, bf16[2,2,192,128]{3,2,1,0:T(8,128)(2,1)S(1)}, u32[]{:S(2)}, u32[]{:S(2)}) collective-permute-start(bf16[2,2,192,128]{3,2,1,0:T(8,128)(2,1)S(1)} %bitcast.25), channel_id=1, source_target_pairs={{0,2},{1,5},{2,0},{3,7},{4,6},{5,1},{6,4},{7,3},{8,10},{9,13},{10,... | collective-permute-start | bytes 589832 | tf_op jit(solution)/shard_map/ppermute | solution.py:189
  56.9 7.2 %collective-permute-start.10 = (bf16[2,2,192,128]{3,2,1,0:T(8,128)(2,1)S(1)}, bf16[2,2,192,128]{3,2,1,0:T(8,128)(2,1)S(1)}, u32[]{:S(2)}, u32[]{:S(2)}) collective-permute-start(bf16[2,2,192,128]{3,2,1,0:T(8,128)(2,1)S(1)} %bitcast.27), channel_id=1, source_target_pairs={{0,4},{1,13},{2,6},{3,15},{4,0},{5,9},{6,2},{7,11},{8,12},{9,5},{1... | collective-permute-start | bytes 589832 | tf_op jit(solution)/shard_map/ppermute | solution.py:189
  57.1 8.9 %collective-permute-start.4 = (bf16[2,2,208,128]{3,2,1,0:T(8,128)(2,1)S(1)}, bf16[2,2,208,128]{3,2,1,0:T(8,128)(2,1)S(1)}, u32[]{:S(2)}, u32[]{:S(2)}) collective-permute-start(bf16[2,2,208,128]{3,2,1,0:T(8,128)(2,1)S(1)} %add_convert_fusion.1), channel_id=1, source_target_pairs={{0,2},{1,5},{2,0},{3,7},{4,6},{5,1},{6,4},{7,3},{8,10},{9,13},{10,... | collective-permute-start | bytes 638984 | tf_op jit(solution)/shard_map/ppermute | solution.py:189
  60.4 8.1 %collective-permute-start.7 = (bf16[2,2,192,128]{3,2,1,0:T(8,128)(2,1)S(1)}, bf16[2,2,192,128]{3,2,1,0:T(8,128)(2,1)S(1)}, u32[]{:S(2)}, u32[]{:S(2)}) collective-permute-start(bf16[2,2,192,128]{3,2,1,0:T(8,128)(2,1)S(1)} %add_convert_fusion.7), channel_id=1, source_target_pairs={{0,4},{1,13},{2,6},{3,15},{4,0},{5,9},{6,2},{7,11},{8,12},{9,5},{1... | collective-permute-start | bytes 589832 | tf_op jit(solution)/shard_map/ppermute | solution.py:189
  64.2 7.7 %collective-permute-start.11 = (bf16[2,2,192,128]{3,2,1,0:T(8,128)(2,1)S(1)}, bf16[2,2,192,128]{3,2,1,0:T(8,128)(2,1)S(1)}, u32[]{:S(2)}, u32[]{:S(2)}) collective-permute-start(bf16[2,2,192,128]{3,2,1,0:T(8,128)(2,1)S(1)} %add_convert_fusion.4), channel_id=1, source_target_pairs={{0,12},{1,3},{2,14},{3,1},{4,8},{5,7},{6,10},{7,5},{8,4},{9,11},{1... | collective-permute-start | bytes 589832 | tf_op jit(solution)/shard_map/ppermute | solution.py:189
  66.1 7.8 %collective-permute-start.5 = (bf16[4,208,128]{2,1,0:T(8,128)(2,1)S(1)}, bf16[4,208,128]{2,1,0:T(8,128)(2,1)S(1)}, u32[]{:S(2)}, u32[]{:S(2)}) collective-permute-start(bf16[4,208,128]{2,1,0:T(8,128)(2,1)S(1)} %bitcast.17), channel_id=1, source_target_pairs={{0,4},{1,13},{2,6},{3,15},{4,0},{5,9},{6,2},{7,11},{8,12},{9,5},{1... | collective-permute-start | bytes 638984 | tf_op jit(solution)/shard_map/ppermute | solution.py:189
  68.5 7.0 %collective-permute-start.8 = (bf16[4,192,128]{2,1,0:T(8,128)(2,1)S(1)}, bf16[4,192,128]{2,1,0:T(8,128)(2,1)S(1)}, u32[]{:S(2)}, u32[]{:S(2)}) collective-permute-start(bf16[4,192,128]{2,1,0:T(8,128)(2,1)S(1)} %bitcast.21), channel_id=1, source_target_pairs={{0,12},{1,3},{2,14},{3,1},{4,8},{5,7},{6,10},{7,5},{8,4},{9,11},{1... | collective-permute-start | bytes 589832 | tf_op jit(solution)/shard_map/ppermute | solution.py:189
  72.0 7.3 %collective-permute-start.12 = (bf16[4,192,128]{2,1,0:T(8,128)(2,1)S(1)}, bf16[4,192,128]{2,1,0:T(8,128)(2,1)S(1)}, u32[]{:S(2)}, u32[]{:S(2)}) collective-permute-start(bf16[4,192,128]{2,1,0:T(8,128)(2,1)S(1)} %bitcast.23), channel_id=1, source_target_pairs={{0,2},{1,5},{2,0},{3,7},{4,6},{5,1},{6,4},{7,3},{8,10},{9,13},{10,... | collective-permute-start | bytes 589832 | tf_op jit(solution)/shard_map/ppermute | solution.py:189
  79.3 3.2 %collective-permute-start.13 = (bf16[8,592,128]{2,1,0:T(8,128)(2,1)S(1)}, bf16[8,592,128]{2,1,0:T(8,128)(2,1)S(1)}, u32[]{:S(2)}, u32[]{:S(2)}) collective-permute-start(bf16[8,592,128]{2,1,0:T(8,128)(2,1)S(1)} %maximum_maximum_fusion.pieces_ref), channel_id=1, source_target_pairs={{0,1},{1,0},{2,3},{3,2},{4,5},{5,4},{6,7},{7,6},{8,9},{9,8},{10,11... | collective-permute-start | bytes 3637256 | tf_op jit(solution)/shard_map/ppermute | solution.py:356

commit v12 on v11

--- a/solution.py
+++ b/solution.py
@@ -24,7 +24,7 @@
 BELOW = LANES * BLOCKS * (BLOCKS - 1) // 2
 EDGE = 2 * BELOW + HALF
 PACKED = -(-(EDGE + BLOCKS) // (16 * CHIPS)) * 16 * CHIPS
-PIECES = (208, 192, 192)
+PIECES = (240, 176, 176)
 BASES = (0, CHIPS * PIECES[0], CHIPS * (PIECES[0] + PIECES[1]))
 MIB = 1 << 20
 
@@ -114,7 +114,7 @@
     return [lax.broadcasted_iota(jnp.int32, (LANES, LANES), axis) for axis in range(2)]
 
 
-def own_gram_kernel(own_ref, keep_ref, send_ref, rest_ref, diagonal_ref, whole_ref):
+def own_gram_kernel(own_ref, keep_ref, send_ref, diagonal_ref, whole_ref):
     def store_below(rows, value):
         whole_ref[rows, :] = value
 
@@ -123,17 +123,12 @@
 
     triangle(own_ref, own_ref, store_below, store_diagonal)
     split_pieces(0, whole_ref, 0, keep_ref, send_ref)
-    rest_ref[...] = whole_ref[pl.ds(BASES[1], BELOW - BASES[1]), :]
 
 
 def own_gram(own):
     return pl.pallas_call(
         own_gram_kernel,
-        out_shape=half_shapes(0, own.dtype)
-        + [
-            jax.ShapeDtypeStruct((BELOW - BASES[1], LANES), jnp.float32),
-            jax.ShapeDtypeStruct((BLOCKS, LANES, LANES), jnp.float32),
-        ],
+        out_shape=half_shapes(0, own.dtype) + [jax.ShapeDtypeStruct((BLOCKS, LANES, LANES), jnp.float32)],
         scratch_shapes=[pltpu.VMEM((BELOW, LANES), jnp.float32)],
         compiler_params=pltpu.CompilerParams(vmem_limit_bytes=8 * MIB),
         cost_estimate=pl.CostEstimate(
@@ -144,18 +139,16 @@
 
 
 def cross_gram_kernel(
-    rest_ref, diagonal_ref, own_ref, other_ref, keep_b_ref, send_b_ref, keep_c_ref, send_c_ref, whole_ref
+    diagonal_ref, own_ref, other_ref, keep_b_ref, send_b_ref, keep_c_ref, send_c_ref, whole_ref
 ):
-    start = BELOW - BASES[1]
-    whole_ref[pl.ds(0, start), :] = rest_ref[...]
     row, column = iotas()
     edges = []
 
     def store_below(rows, value):
-        whole_ref[pl.ds(start + rows.start, rows.size), :] = value
+        whole_ref[rows, :] = value
 
     def store_diagonal(j, value):
-        whole_ref[pl.ds(start + BELOW + j * LANES, LANES), :] = jnp.where(row >= column, diagonal_ref[j], value)
+        whole_ref[pl.ds(BELOW + j * LANES, LANES), :] = jnp.where(row >= column, diagonal_ref[j], value)
         edges.append(jnp.sum(jnp.where(row == column, value, 0.0), axis=0, keepdims=True))
 
     triangle(own_ref, other_ref, store_below, store_diagonal)
@@ -165,7 +158,7 @@
     split_pieces(2, whole_ref, BASES[2] - BASES[1], keep_c_ref, send_c_ref)
 
 
-def cross_gram(rest, diagonal, own, other):
+def cross_gram(diagonal, own, other):
     return pl.pallas_call(
         cross_gram_kernel,
         out_shape=half_shapes(1, own.dtype) + half_shapes(2, own.dtype),
@@ -175,7 +168,7 @@
             flops=2 * (BELOW + 3 * HALF) * LANES * WIDTH, bytes_accessed=4 * HALF * WIDTH, transcendentals=0
         ),
         name="cross_gram",
-    )(rest, diagonal, own, other)
+    )(diagonal, own, other)
 
 
 def exchange(value, stream, hop):
@@ -205,12 +198,11 @@
     return jnp.concatenate([half, exchange(half, stream, 0)])
 
 
-def unpermute(pieces_ref, packed_ref, core):
-    first = 0
-    for s, rows in enumerate(PIECES):
+def unpermute(first_ref, rest_ref, packed_ref, core):
+    places = ((first_ref, 0), (rest_ref, 0), (rest_ref, PIECES[1]))
+    for s, (pieces_ref, start) in enumerate(places):
         for k in range(CHIPS):
-            packed_ref[piece_rows(s, k, BASES[s], core), :] = pieces_ref[k, pl.ds(first, rows), :]
-        first += rows
+            packed_ref[piece_rows(s, k, BASES[s], core), :] = pieces_ref[k, pl.ds(start, PIECES[s]), :]
 
 
 def mirror(packed_ref, out_ref, lower):
@@ -224,21 +216,21 @@
             out_ref[pl.ds(first, LANES), pl.ds(first + LANES, below.shape[0])] = below.T
 
 
-def own_square_kernel(pieces_ref, packed_ref, gram_ref, square_ref):
+def own_square_kernel(first_ref, rest_ref, packed_ref, gram_ref, square_ref):
     row, column = iotas()
-    unpermute(pieces_ref, packed_ref, lax.axis_index("c"))
+    unpermute(first_ref, rest_ref, packed_ref, lax.axis_index("c"))
     mirror(packed_ref, gram_ref, row >= column)
     for n in range(0, HALF, 256):
         columns = pl.ds(n, 256)
         square_ref[:, columns] = jnp.dot(gram_ref[...], gram_ref[:, columns], preferred_element_type=jnp.float32)
 
 
-def own_square(pieces):
+def own_square(first, rest):
     return pl.pallas_call(
         own_square_kernel,
         out_shape=(
-            jax.ShapeDtypeStruct((PACKED, LANES), pieces.dtype),
-            jax.ShapeDtypeStruct((HALF, HALF), pieces.dtype),
+            jax.ShapeDtypeStruct((PACKED, LANES), first.dtype),
+            jax.ShapeDtypeStruct((HALF, HALF), first.dtype),
             jax.ShapeDtypeStruct((HALF, HALF), jnp.float32),
         ),
         compiler_params=pltpu.CompilerParams(vmem_limit_bytes=12 * MIB),
@@ -246,7 +238,7 @@
             flops=2 * HALF * HALF * HALF, bytes_accessed=8 * HALF * HALF, transcendentals=0
         ),
         name="own_square",
-    )(pieces)
+    )(first, rest)
 
 
 def unpack_cross(own_ref, other_ref, cross_ref):
@@ -264,13 +256,13 @@
 
 
 def update_kernel(
-    own_ref, pieces_ref, gram_ref, square_ref, x_ref, x_other_ref, out_ref,
+    own_ref, first_ref, rest_ref, gram_ref, square_ref, x_ref, x_other_ref, out_ref,
     other_ref, cross_ref, gram_other_ref, mixing_ref,
 ):
     scale = math.sqrt(max(ROWS, COLS))
     step = 256
     row, column = iotas()
-    unpermute(pieces_ref, other_ref, 1 - lax.axis_index("c"))
+    unpermute(first_ref, rest_ref, other_ref, 1 - lax.axis_index("c"))
     unpack_cross(own_ref, other_ref, cross_ref)
     mirror(other_ref, gram_other_ref, row >= column)
     for n in range(0, HALF, step):
@@ -360,19 +352,20 @@
     pieces = split_columns(iterate.reshape(PANEL, COLS))
     own = lax.all_to_all(pieces, CHIP_AXES, 0, 0, tiled=True).reshape(HALF, WIDTH)
     other = swap_cores(own)
-    keep_a, send_a, *rest = own_gram(own)
+    keep_a, send_a, diagonal = own_gram(own)
     arrived_a = exchange(send_a, 0, 0)
-    keep_b, send_b, keep_c, send_c = cross_gram(*rest, own, other)
+    keep_b, send_b, keep_c, send_c = cross_gram(diagonal, own, other)
     arrived_b, arrived_c = exchange(send_b, 1, 0), exchange(send_c, 2, 0)
     streams = [
         sum_over_chips(0, keep_a, after(arrived_a, send_b, send_c), arrived_b),
         sum_over_chips(1, keep_b, arrived_b),
         sum_over_chips(2, keep_c, arrived_c),
     ]
-    pieces = jnp.concatenate(streams, axis=1)
-    pieces_other = swap_cores(pieces)
-    packed, gram, square = own_square(pieces)
-    sent = update_rows(packed, pieces_other, gram, square, own, other)
+    first, rest = streams[0], jnp.concatenate(streams[1:], axis=1)
+    first_other = swap_cores(first)
+    rest_other = swap_cores(after(rest, first_other))
+    packed, gram, square = own_square(first, rest)
+    sent = update_rows(packed, first_other, rest_other, gram, square, own, other)
     sent = sent.reshape(STRIPES * CHIPS, PANEL + PANEL // 2, LANES)
     received = lax.all_to_all(sent, ALL_CHIPS, 0, 0, tiled=True)
     return join_columns(received.reshape(STRIPES, CHIPS, PANEL + PANEL // 2, LANES))

time: 133 us -> 131 us (0.985)
  waiting for transfers between devices: 21.3 us -> 19.9 us
    ppermute x2 -> x3, waiting for transfers between devices: 4.05 us -> 3.34 us  [swap_cores(): return lax.ppermute(value, 'c', [(0, 1), (1, 0)])]
  transfers between devices with their start and end apart: 14 -> 15, of which waited for: 11 -> 10; matrix products, arithmetic and copies ran while one was open for 0% -> 1% of each run, Pallas kernels for 3% -> 3%
where the time goes in v12:
time: 131 us
  blocking collectives  79.6 us (61%)
  waiting for transfers between devices  19.9 us (15%)
  starting transfers between devices  15.5 us (12%)
  Pallas kernels  13.6 us (10%)
  local copies, waits for them, and re-layouts  1.66 us (1%)
    all_to_all x1, blocking collectives, shards(): received = lax.all_to_all(sent, ALL_CHIPS, 0, 0, tiled=True)  41.9 us
    all_to_all x1, blocking collectives, shards(): lax.all_to_all(pieces, CHIP_AXES, 0, 0, tiled=True).reshape(HALF, WIDTH)  37.7 us
    ppermute x12, waiting for transfers between devices, exchange(): return lax.ppermute(value, ('x', 'yh', 'c'), pairs)  16.6 us
    ppermute x12, starting transfers between devices, exchange(): return lax.ppermute(value, ('x', 'yh', 'c'), pairs)  15.1 us
    pallas_call x1, Pallas kernels, update_rows(): pl.pallas_call(update_kernel, out_shape=jax.ShapeDtypeStruct((STRIPES, CH...  7.12 us
    ppermute x3, waiting for transfers between devices, swap_cores(): return lax.ppermute(value, 'c', [(0, 1), (1, 0)])  3.34 us
  transfers between devices with their start and end apart: 15, of which 10 were waited for; matrix products, arithmetic and copies ran while one was open for 1% of the time, Pallas kernels for 3%

profile of v12, /device:TPU:0, one launch (start us, length us, event | category | flops | bytes accessed | tf_op | source)
XLA Modules:
  0.0 131.2 jit_solution(3019674132719452501)
XLA Ops:
  0.0 0.0 copy-start
  0.0 1.7 %copy-done = bf16[1,96,12288]{2,1,0:T(8,128)(2,1)S(1)} copy-done((bf16[1,96,12288]{2,1,0:T(8,128)(2,1)S(1)}, bf16[1,96,12288]{2,1,0:T(8,128)(2,1)}, u32[]{:S(2)}) %copy-start) | copy-done | bytes 2359320
  1.7 0.6 split_columns.1
  2.3 37.7 %all_to_all.10 = bf16[8,96,1536]{2,1,0:T(8,128)(2,1)S(1)} all-to-all(bf16[8,96,1536]{2,1,0:T(8,128)(2,1)S(1)} %split_columns.1), channel_id=1, replica_groups=mesh['z'=4,'yl'=2,'x'=4,'yh'=2,'c'=2] {'x','yh'}, dimensions={0} | all-to-all | bytes 4718592 | tf_op jit(solution)/shard_map/all_to_all | solution.py:353
  40.0 0.0 collective-permute-start.1
  40.0 1.5 %own_gram.1 = (f32[4,240,128]{2,1,0:T(8,128)S(1)}, bf16[4,240,128]{2,1,0:T(8,128)(2,1)S(1)}, f32[6,128,128]{2,1,0:T(8,128)S(1)}) custom-call(bf16[768,1536]{1,0:T(8,128)(2,1)S(1)} %bitcast.13), custom_call_target="tpu_custom_call" | custom-call | flops 1660944384 | bytes 2359296 | tf_op jit(solution)/shard_map/own_gram/pallas_call | solution.py:129
  41.4 0.6 collective-permute-start
  42.0 2.5 %collective-permute-done.1.other_ref.x_other_ref = bf16[768,1536]{1,0:T(8,128)(2,1)S(1)} collective-permute-done((bf16[768,1536]{1,0:T(8,128)(2,1)S(1)}, bf16[768,1536]{1,0:T(8,128)(2,1)S(1)}, u32[]{:S(2)}, u32[]{:S(2)}) %collective-permute-start.1) | collective-permute-done | bytes 2359328 | tf_op jit(solution)/shard_map/ppermute | solution.py:348
  44.5 1.5 %cross_gram.1 = (f32[4,176,128]{2,1,0:T(8,128)S(1)}, bf16[4,176,128]{2,1,0:T(8,128)(2,1)S(1)}, f32[4,176,128]{2,1,0:T(8,128)S(1)}, bf16[4,176,128]{2,1,0:T(8,128)(2,1)S(1)}) custom-call(f32[6,128,128]{2,1,0:T(8,128)S(1)} %get-tuple-element.20.diagonal_ref, bf16[768,1536]{1,0:T(8,128)(2,1)S(1)} %bitcast.14, ...), custom_call_target="tpu_custom_call" | custom-call | flops 1660944384 | bytes 4718592 | tf_op jit(solution)/shard_map/cross_gram/pallas_call | solution.py:162
  46.0 1.5 %collective-permute-start.3 = (bf16[4,176,128]{2,1,0:T(8,128)(2,1)S(1)}, bf16[4,176,128]{2,1,0:T(8,128)(2,1)S(1)}, u32[]{:S(2)}, u32[]{:S(2)}) collective-permute-start(bf16[4,176,128]{2,1,0:T(8,128)(2,1)S(1)} %get-tuple-element.21), channel_id=1, source_target_pairs={{0,12},{1,3},{2,14},{3,1},{4,8},{5,7},{6,10},{7,5},{8,4},{9,11},{1... | collective-permute-start | bytes 540680 | tf_op jit(solution)/shard_map/ppermute | solution.py:182
  47.5 0.2 collective-permute-done
  47.7 0.1 add_convert_fusion.2
  47.8 1.7 %collective-permute-start.2 = (bf16[2,2,240,128]{3,2,1,0:T(8,128)(2,1)S(1)}, bf16[2,2,240,128]{3,2,1,0:T(8,128)(2,1)S(1)}, u32[]{:S(2)}, u32[]{:S(2)}) collective-permute-start(bf16[2,2,240,128]{3,2,1,0:T(8,128)(2,1)S(1)} %bitcast.19), channel_id=1, source_target_pairs={{0,12},{1,3},{2,14},{3,1},{4,8},{5,7},{6,10},{7,5},{8,4},{9,11},{1... | collective-permute-start | bytes 737288 | tf_op jit(solution)/shard_map/ppermute | solution.py:182
  49.5 1.6 %collective-permute-start.9 = (bf16[4,176,128]{2,1,0:T(8,128)(2,1)S(1)}, bf16[4,176,128]{2,1,0:T(8,128)(2,1)S(1)}, u32[]{:S(2)}, u32[]{:S(2)}) collective-permute-start(bf16[4,176,128]{2,1,0:T(8,128)(2,1)S(1)} %get-tuple-element.22), channel_id=1, source_target_pairs={{0,2},{1,5},{2,0},{3,7},{4,6},{5,1},{6,4},{7,3},{8,10},{9,13},{10,... | collective-permute-start | bytes 540680 | tf_op jit(solution)/shard_map/ppermute | solution.py:182
  51.0 1.8 %collective-permute-done.3 = bf16[4,176,128]{2,1,0:T(8,128)(2,1)S(1)} collective-permute-done((bf16[4,176,128]{2,1,0:T(8,128)(2,1)S(1)}, bf16[4,176,128]{2,1,0:T(8,128)(2,1)S(1)}, u32[]{:S(2)}, u32[]{:S(2)}) %collective-permute-start.3) | collective-permute-done | bytes 180256 | tf_op jit(solution)/shard_map/ppermute | solution.py:182
  52.9 1.6 %collective-permute-start.6 = (bf16[2,2,176,128]{3,2,1,0:T(8,128)(2,1)S(1)}, bf16[2,2,176,128]{3,2,1,0:T(8,128)(2,1)S(1)}, u32[]{:S(2)}, u32[]{:S(2)}) collective-permute-start(bf16[2,2,176,128]{3,2,1,0:T(8,128)(2,1)S(1)} %bitcast.21), channel_id=1, source_target_pairs={{0,2},{1,5},{2,0},{3,7},{4,6},{5,1},{6,4},{7,3},{8,10},{9,13},{10,... | collective-permute-start | bytes 540680 | tf_op jit(solution)/shard_map/ppermute | solution.py:182
  54.5 0.9 collective-permute-done.2
  55.5 0.1 add_convert_fusion.1
  55.5 1.6 %collective-permute-start.4 = (bf16[2,2,240,128]{3,2,1,0:T(8,128)(2,1)S(1)}, bf16[2,2,240,128]{3,2,1,0:T(8,128)(2,1)S(1)}, u32[]{:S(2)}, u32[]{:S(2)}) collective-permute-start(bf16[2,2,240,128]{3,2,1,0:T(8,128)(2,1)S(1)} %add_convert_fusion.1), channel_id=1, source_target_pairs={{0,2},{1,5},{2,0},{3,7},{4,6},{5,1},{6,4},{7,3},{8,10},{9,13},{10,... | collective-permute-start | bytes 737288 | tf_op jit(solution)/shard_map/ppermute | solution.py:182
  57.2 0.0 collective-permute-done.9
  57.2 0.2 collective-permute-start.10
  57.5 2.5 %collective-permute-done.6 = bf16[2,2,176,128]{3,2,1,0:T(8,128)(2,1)S(1)} collective-permute-done((bf16[2,2,176,128]{3,2,1,0:T(8,128)(2,1)S(1)}, bf16[2,2,176,128]{3,2,1,0:T(8,128)(2,1)S(1)}, u32[]{:S(2)}, u32[]{:S(2)}) %collective-permute-start.6) | collective-permute-done | bytes 180256 | tf_op jit(solution)/shard_map/ppermute | solution.py:182
  60.0 0.1 collective-permute-start.7
  60.1 3.1 %collective-permute-done.10 = bf16[2,2,176,128]{3,2,1,0:T(8,128)(2,1)S(1)} collective-permute-done((bf16[2,2,176,128]{3,2,1,0:T(8,128)(2,1)S(1)}, bf16[2,2,176,128]{3,2,1,0:T(8,128)(2,1)S(1)}, u32[]{:S(2)}, u32[]{:S(2)}) %collective-permute-start.10) | collective-permute-done | bytes 180256 | tf_op jit(solution)/shard_map/ppermute | solution.py:182
  63.2 0.1 collective-permute-done.4
  63.4 0.1 add_convert_fusion
  63.4 0.3 collective-permute-start.5
  63.8 2.4 %collective-permute-start.11 = (bf16[2,2,176,128]{3,2,1,0:T(8,128)(2,1)S(1)}, bf16[2,2,176,128]{3,2,1,0:T(8,128)(2,1)S(1)}, u32[]{:S(2)}, u32[]{:S(2)}) collective-permute-start(bf16[2,2,176,128]{3,2,1,0:T(8,128)(2,1)S(1)} %add_convert_fusion.4), channel_id=1, source_target_pairs={{0,12},{1,3},{2,14},{3,1},{4,8},{5,7},{6,10},{7,5},{8,4},{9,11},{1... | collective-permute-start | bytes 540680 | tf_op jit(solution)/shard_map/ppermute | solution.py:182
  66.2 0.0 collective-permute-done.7
  66.3 0.9 collective-permute-start.8
  67.2 3.4 %collective-permute-done.11 = bf16[2,2,176,128]{3,2,1,0:T(8,128)(2,1)S(1)} collective-permute-done((bf16[2,2,176,128]{3,2,1,0:T(8,128)(2,1)S(1)}, bf16[2,2,176,128]{3,2,1,0:T(8,128)(2,1)S(1)}, u32[]{:S(2)}, u32[]{:S(2)}) %collective-permute-start.11) | collective-permute-done | bytes 180256 | tf_op jit(solution)/shard_map/ppermute | solution.py:182
  70.7 0.0 collective-permute-done.5
  70.7 0.1 collective-permute-start.13
  70.9 2.5 %collective-permute-start.12 = (bf16[4,176,128]{2,1,0:T(8,128)(2,1)S(1)}, bf16[4,176,128]{2,1,0:T(8,128)(2,1)S(1)}, u32[]{:S(2)}, u32[]{:S(2)}) collective-permute-start(bf16[4,176,128]{2,1,0:T(8,128)(2,1)S(1)} %bitcast.27), channel_id=1, source_target_pairs={{0,2},{1,5},{2,0},{3,7},{4,6},{5,1},{6,4},{7,3},{8,10},{9,13},{10,... | collective-permute-start | bytes 540680 | tf_op jit(solution)/shard_map/ppermute | solution.py:182
  73.3 0.0 collective-permute-done.8
  73.3 4.6 %collective-permute-done.12 = bf16[4,176,128]{2,1,0:T(8,128)(2,1)S(1)} collective-permute-done((bf16[4,176,128]{2,1,0:T(8,128)(2,1)S(1)}, bf16[4,176,128]{2,1,0:T(8,128)(2,1)S(1)}, u32[]{:S(2)}, u32[]{:S(2)}) %collective-permute-start.12) | collective-permute-done | bytes 180256 | tf_op jit(solution)/shard_map/ppermute | solution.py:182
  78.0 0.0 collective-permute-done.13.first_ref
  78.0 0.3 collective-permute-start.14
  78.3 1.3 own_square.1
  79.6 0.9 collective-permute-done.14.rest_ref
  80.5 7.1 %update_rows.1 = bf16[8,8,144,128]{3,2,1,0:T(8,128)(2,1)S(1)} custom-call(bf16[4736,128]{1,0:T(8,128)(2,1)S(1)} %get-tuple-element.27.own_ref, bf16[8,240,128]{2,1,0:T(8,128)(2,1)S(1)} %collective-permute-done.13.first_ref, bf16[8,352,128]{2,1,0:T(8,128)(2,1)S(1)} %collective-permute-done.14.rest_ref, bf16[768,768]{1,0:T(8,128)(2,1)S(1)} %get-tuple-element.29.gram_ref, ...), custom_call_target="tpu_custom_call" | custom-call | flops 6341787648 | bytes 11796480 | tf_op jit(solution)/shard_map/update_rows/pallas_call | solution.py:300
  87.6 41.9 %all_to_all.11 = bf16[64,144,128]{2,1,0:T(8,128)(2,1)S(1)} all-to-all(bf16[64,144,128]{2,1,0:T(8,128)(2,1)S(1)} %bitcast.16), channel_id=1, replica_groups=mesh['z'=4,'yl'=2,'x'=4,'yh'=2,'c'=2] {'z','yl','x','yh'}, dimensions={0} | all-to-all | bytes 4718592 | tf_op jit(solution)/shard_map/all_to_all | solution.py:370
  129.5 1.6 %join_columns.1 = bf16[8,96,1536]{2,1,0:T(8,128)(2,1)} custom-call(bf16[8,8,144,128]{3,2,1,0:T(8,128)(2,1)S(1)} %bitcast.10), custom_call_target="tpu_custom_call" | custom-call | tf_op jit(solution)/shard_map/join_columns/pallas_call | solution.py:336
  (14 shorter events, 0.5 us)
Async XLA Ops:
  0.0 1.7 %copy-start = (bf16[1,96,12288]{2,1,0:T(8,128)(2,1)S(1)}, bf16[1,96,12288]{2,1,0:T(8,128)(2,1)}, u32[]{:S(2)}) copy-start(bf16[1,96,12288]{2,1,0:T(8,128)(2,1)} %param.1) | copy-start | bytes 7077892
  40.0 4.5 %collective-permute-start.1 = (bf16[768,1536]{1,0:T(8,128)(2,1)S(1)}, bf16[768,1536]{1,0:T(8,128)(2,1)S(1)}, u32[]{:S(2)}, u32[]{:S(2)}) collective-permute-start(bf16[768,1536]{1,0:T(8,128)(2,1)S(1)} %bitcast.12), channel_id=1, source_target_pairs={{0,1},{1,0},{2,3},{3,2},{4,5},{5,4},{6,7},{7,6},{8,9},{9,8},{10,11... | collective-permute-start | bytes 7077896 | tf_op jit(solution)/shard_map/ppermute | solution.py:348
  41.4 6.3 %collective-permute-start = (bf16[4,240,128]{2,1,0:T(8,128)(2,1)S(1)}, bf16[4,240,128]{2,1,0:T(8,128)(2,1)S(1)}, u32[]{:S(2)}, u32[]{:S(2)}) collective-permute-start(bf16[4,240,128]{2,1,0:T(8,128)(2,1)S(1)} %get-tuple-element.19), channel_id=1, source_target_pairs={{0,4},{1,13},{2,6},{3,15},{4,0},{5,9},{6,2},{7,11},{8,12},{9,5},{1... | collective-permute-start | bytes 737288 | tf_op jit(solution)/shard_map/ppermute | solution.py:182
  46.0 6.8 %collective-permute-start.3 = (bf16[4,176,128]{2,1,0:T(8,128)(2,1)S(1)}, bf16[4,176,128]{2,1,0:T(8,128)(2,1)S(1)}, u32[]{:S(2)}, u32[]{:S(2)}) collective-permute-start(bf16[4,176,128]{2,1,0:T(8,128)(2,1)S(1)} %get-tuple-element.21), channel_id=1, source_target_pairs={{0,12},{1,3},{2,14},{3,1},{4,8},{5,7},{6,10},{7,5},{8,4},{9,11},{1... | collective-permute-start | bytes 540680 | tf_op jit(solution)/shard_map/ppermute | solution.py:182
  47.8 7.7 %collective-permute-start.2 = (bf16[2,2,240,128]{3,2,1,0:T(8,128)(2,1)S(1)}, bf16[2,2,240,128]{3,2,1,0:T(8,128)(2,1)S(1)}, u32[]{:S(2)}, u32[]{:S(2)}) collective-permute-start(bf16[2,2,240,128]{3,2,1,0:T(8,128)(2,1)S(1)} %bitcast.19), channel_id=1, source_target_pairs={{0,12},{1,3},{2,14},{3,1},{4,8},{5,7},{6,10},{7,5},{8,4},{9,11},{1... | collective-permute-start | bytes 737288 | tf_op jit(solution)/shard_map/ppermute | solution.py:182
  49.5 7.7 %collective-permute-start.9 = (bf16[4,176,128]{2,1,0:T(8,128)(2,1)S(1)}, bf16[4,176,128]{2,1,0:T(8,128)(2,1)S(1)}, u32[]{:S(2)}, u32[]{:S(2)}) collective-permute-start(bf16[4,176,128]{2,1,0:T(8,128)(2,1)S(1)} %get-tuple-element.22), channel_id=1, source_target_pairs={{0,2},{1,5},{2,0},{3,7},{4,6},{5,1},{6,4},{7,3},{8,10},{9,13},{10,... | collective-permute-start | bytes 540680 | tf_op jit(solution)/shard_map/ppermute | solution.py:182
  52.9 7.1 %collective-permute-start.6 = (bf16[2,2,176,128]{3,2,1,0:T(8,128)(2,1)S(1)}, bf16[2,2,176,128]{3,2,1,0:T(8,128)(2,1)S(1)}, u32[]{:S(2)}, u32[]{:S(2)}) collective-permute-start(bf16[2,2,176,128]{3,2,1,0:T(8,128)(2,1)S(1)} %bitcast.21), channel_id=1, source_target_pairs={{0,2},{1,5},{2,0},{3,7},{4,6},{5,1},{6,4},{7,3},{8,10},{9,13},{10,... | collective-permute-start | bytes 540680 | tf_op jit(solution)/shard_map/ppermute | solution.py:182
  55.5 7.8 %collective-permute-start.4 = (bf16[2,2,240,128]{3,2,1,0:T(8,128)(2,1)S(1)}, bf16[2,2,240,128]{3,2,1,0:T(8,128)(2,1)S(1)}, u32[]{:S(2)}, u32[]{:S(2)}) collective-permute-start(bf16[2,2,240,128]{3,2,1,0:T(8,128)(2,1)S(1)} %add_convert_fusion.1), channel_id=1, source_target_pairs={{0,2},{1,5},{2,0},{3,7},{4,6},{5,1},{6,4},{7,3},{8,10},{9,13},{10,... | collective-permute-start | bytes 737288 | tf_op jit(solution)/shard_map/ppermute | solution.py:182
  57.2 5.9 %collective-permute-start.10 = (bf16[2,2,176,128]{3,2,1,0:T(8,128)(2,1)S(1)}, bf16[2,2,176,128]{3,2,1,0:T(8,128)(2,1)S(1)}, u32[]{:S(2)}, u32[]{:S(2)}) collective-permute-start(bf16[2,2,176,128]{3,2,1,0:T(8,128)(2,1)S(1)} %bitcast.23), channel_id=1, source_target_pairs={{0,4},{1,13},{2,6},{3,15},{4,0},{5,9},{6,2},{7,11},{8,12},{9,5},{1... | collective-permute-start | bytes 540680 | tf_op jit(solution)/shard_map/ppermute | solution.py:182
  60.0 6.2 %collective-permute-start.7 = (bf16[2,2,176,128]{3,2,1,0:T(8,128)(2,1)S(1)}, bf16[2,2,176,128]{3,2,1,0:T(8,128)(2,1)S(1)}, u32[]{:S(2)}, u32[]{:S(2)}) collective-permute-start(bf16[2,2,176,128]{3,2,1,0:T(8,128)(2,1)S(1)} %add_convert_fusion.7), channel_id=1, source_target_pairs={{0,4},{1,13},{2,6},{3,15},{4,0},{5,9},{6,2},{7,11},{8,12},{9,5},{1... | collective-permute-start | bytes 540680 | tf_op jit(solution)/shard_map/ppermute | solution.py:182
  63.4 7.3 %collective-permute-start.5 = (bf16[4,240,128]{2,1,0:T(8,128)(2,1)S(1)}, bf16[4,240,128]{2,1,0:T(8,128)(2,1)S(1)}, u32[]{:S(2)}, u32[]{:S(2)}) collective-permute-start(bf16[4,240,128]{2,1,0:T(8,128)(2,1)S(1)} %bitcast.17), channel_id=1, source_target_pairs={{0,4},{1,13},{2,6},{3,15},{4,0},{5,9},{6,2},{7,11},{8,12},{9,5},{1... | collective-permute-start | bytes 737288 | tf_op jit(solution)/shard_map/ppermute | solution.py:182
  63.8 6.9 %collective-permute-start.11 = (bf16[2,2,176,128]{3,2,1,0:T(8,128)(2,1)S(1)}, bf16[2,2,176,128]{3,2,1,0:T(8,128)(2,1)S(1)}, u32[]{:S(2)}, u32[]{:S(2)}) collective-permute-start(bf16[2,2,176,128]{3,2,1,0:T(8,128)(2,1)S(1)} %add_convert_fusion.4), channel_id=1, source_target_pairs={{0,12},{1,3},{2,14},{3,1},{4,8},{5,7},{6,10},{7,5},{8,4},{9,11},{1... | collective-permute-start | bytes 540680 | tf_op jit(solution)/shard_map/ppermute | solution.py:182
  66.3 7.0 %collective-permute-start.8 = (bf16[4,176,128]{2,1,0:T(8,128)(2,1)S(1)}, bf16[4,176,128]{2,1,0:T(8,128)(2,1)S(1)}, u32[]{:S(2)}, u32[]{:S(2)}) collective-permute-start(bf16[4,176,128]{2,1,0:T(8,128)(2,1)S(1)} %bitcast.25), channel_id=1, source_target_pairs={{0,12},{1,3},{2,14},{3,1},{4,8},{5,7},{6,10},{7,5},{8,4},{9,11},{1... | collective-permute-start | bytes 540680 | tf_op jit(solution)/shard_map/ppermute | solution.py:182
  70.7 7.3 %collective-permute-start.13 = (bf16[8,240,128]{2,1,0:T(8,128)(2,1)S(1)}, bf16[8,240,128]{2,1,0:T(8,128)(2,1)S(1)}, u32[]{:S(2)}, u32[]{:S(2)}) collective-permute-start(bf16[8,240,128]{2,1,0:T(8,128)(2,1)S(1)} %pad_maximum_fusion.first_ref), channel_id=1, source_target_pairs={{0,1},{1,0},{2,3},{3,2},{4,5},{5,4},{6,7},{7,6},{8,9},{9,8},{10,11... | collective-permute-start | bytes 1474568 | tf_op jit(solution)/shard_map/ppermute | solution.py:348
  70.9 7.1 %collective-permute-start.12 = (bf16[4,176,128]{2,1,0:T(8,128)(2,1)S(1)}, bf16[4,176,128]{2,1,0:T(8,128)(2,1)S(1)}, u32[]{:S(2)}, u32[]{:S(2)}) collective-permute-start(bf16[4,176,128]{2,1,0:T(8,128)(2,1)S(1)} %bitcast.27), channel_id=1, source_target_pairs={{0,2},{1,5},{2,0},{3,7},{4,6},{5,1},{6,4},{7,3},{8,10},{9,13},{10,... | collective-permute-start | bytes 540680 | tf_op jit(solution)/shard_map/ppermute | solution.py:182
  78.0 2.5 %collective-permute-start.14 = (bf16[8,352,128]{2,1,0:T(8,128)(2,1)S(1)}, bf16[8,352,128]{2,1,0:T(8,128)(2,1)S(1)}, u32[]{:S(2)}, u32[]{:S(2)}) collective-permute-start(bf16[8,352,128]{2,1,0:T(8,128)(2,1)S(1)} %maximum_maximum_fusion.rest_ref), channel_id=1, source_target_pairs={{0,1},{1,0},{2,3},{3,2},{4,5},{5,4},{6,7},{7,6},{8,9},{9,8},{10,11... | collective-permute-start | bytes 2162696 | tf_op jit(solution)/shard_map/ppermute | solution.py:348

commit v13 on v12

--- a/solution.py
+++ b/solution.py
@@ -24,7 +24,7 @@
 BELOW = LANES * BLOCKS * (BLOCKS - 1) // 2
 EDGE = 2 * BELOW + HALF
 PACKED = -(-(EDGE + BLOCKS) // (16 * CHIPS)) * 16 * CHIPS
-PIECES = (240, 176, 176)
+PIECES = (240, 192, 160)
 BASES = (0, CHIPS * PIECES[0], CHIPS * (PIECES[0] + PIECES[1]))
 MIB = 1 << 20
 
@@ -94,20 +94,20 @@
     return pl.ds(start, below)
 
 
-def triangle(own_ref, ref, store_below, store_diagonal):
-    for j in range(0, BLOCKS, 2):
-        first = j * LANES
+def triangle(own_ref, ref, groups, store_below, store_diagonal):
+    for group in groups:
+        first = group[0] * LANES
         part = lax.dot_general(
             own_ref[pl.ds(first, HALF - first), :],
-            ref[pl.ds(first, 2 * LANES), :],
+            ref[pl.ds(first, len(group) * LANES), :],
             (((1,), (1,)), ((), ())),
             preferred_element_type=jnp.float32,
         )
-        for i in range(2):
+        for i, j in enumerate(group):
             columns = part[i * LANES :, i * LANES : (i + 1) * LANES]
-            store_diagonal(j + i, columns[:LANES])
-            if j + i + 1 < BLOCKS:
-                store_below(strip(j + i), columns[LANES:])
+            store_diagonal(j, columns[:LANES])
+            if j + 1 < BLOCKS:
+                store_below(strip(j), columns[LANES:])
 
 
 def iotas():
@@ -121,7 +121,7 @@
     def store_diagonal(j, value):
         diagonal_ref[j] = value
 
-    triangle(own_ref, own_ref, store_below, store_diagonal)
+    triangle(own_ref, own_ref, ((0, 1), (2, 3), (4, 5)), store_below, store_diagonal)
     split_pieces(0, whole_ref, 0, keep_ref, send_ref)
 
 
@@ -138,37 +138,61 @@
     )(own)
 
 
-def cross_gram_kernel(
-    diagonal_ref, own_ref, other_ref, keep_b_ref, send_b_ref, keep_c_ref, send_c_ref, whole_ref
-):
+def cross_first_kernel(own_ref, other_ref, keep_ref, send_ref, diagonal_ref, whole_ref):
+    def store_below(rows, value):
+        whole_ref[rows, :] = value
+
+    def store_diagonal(j, value):
+        diagonal_ref[j] = value
+
+    triangle(own_ref, other_ref, ((0, 1), (2,)), store_below, store_diagonal)
+    split_pieces(1, whole_ref, 0, keep_ref, send_ref)
+
+
+def cross_first(own, other):
+    return pl.pallas_call(
+        cross_first_kernel,
+        out_shape=half_shapes(1, own.dtype) + [jax.ShapeDtypeStruct((BLOCKS // 2, LANES, LANES), jnp.float32)],
+        scratch_shapes=[pltpu.VMEM((BASES[2] - BASES[1], LANES), jnp.float32)],
+        compiler_params=pltpu.CompilerParams(vmem_limit_bytes=8 * MIB),
+        cost_estimate=pl.CostEstimate(
+            flops=4 * HALF * 2 * LANES * WIDTH, bytes_accessed=4 * HALF * WIDTH, transcendentals=0
+        ),
+        name="cross_first",
+    )(own, other)
+
+
+def cross_rest_kernel(diagonal_ref, cross_ref, own_ref, other_ref, keep_ref, send_ref, whole_ref):
     row, column = iotas()
     edges = []
 
     def store_below(rows, value):
-        whole_ref[rows, :] = value
+        whole_ref[pl.ds(BELOW + rows.start - BASES[2], rows.size), :] = value
 
     def store_diagonal(j, value):
-        whole_ref[pl.ds(BELOW + j * LANES, LANES), :] = jnp.where(row >= column, diagonal_ref[j], value)
+        block = pl.ds(2 * BELOW + j * LANES - BASES[2], LANES)
+        whole_ref[block, :] = jnp.where(row >= column, diagonal_ref[j], value)
         edges.append(jnp.sum(jnp.where(row == column, value, 0.0), axis=0, keepdims=True))
 
-    triangle(own_ref, other_ref, store_below, store_diagonal)
+    for j in range(BLOCKS // 2):
+        store_diagonal(j, cross_ref[j])
+    triangle(own_ref, other_ref, ((3,), (4, 5)), store_below, store_diagonal)
     edges.append(jnp.zeros((PACKED - EDGE - BLOCKS, LANES), jnp.float32))
-    whole_ref[pl.ds(EDGE - BASES[1], PACKED - EDGE), :] = jnp.concatenate(edges)
-    split_pieces(1, whole_ref, 0, keep_b_ref, send_b_ref)
-    split_pieces(2, whole_ref, BASES[2] - BASES[1], keep_c_ref, send_c_ref)
-
-
-def cross_gram(diagonal, own, other):
-    return pl.pallas_call(
-        cross_gram_kernel,
-        out_shape=half_shapes(1, own.dtype) + half_shapes(2, own.dtype),
-        scratch_shapes=[pltpu.VMEM((PACKED - BASES[1], LANES), jnp.float32)],
-        compiler_params=pltpu.CompilerParams(vmem_limit_bytes=12 * MIB),
+    whole_ref[pl.ds(EDGE - BASES[2], PACKED - EDGE), :] = jnp.concatenate(edges)
+    split_pieces(2, whole_ref, 0, keep_ref, send_ref)
+
+
+def cross_rest(diagonal, cross, own, other):
+    return pl.pallas_call(
+        cross_rest_kernel,
+        out_shape=half_shapes(2, own.dtype),
+        scratch_shapes=[pltpu.VMEM((PACKED - BASES[2], LANES), jnp.float32)],
+        compiler_params=pltpu.CompilerParams(vmem_limit_bytes=8 * MIB),
         cost_estimate=pl.CostEstimate(
-            flops=2 * (BELOW + 3 * HALF) * LANES * WIDTH, bytes_accessed=4 * HALF * WIDTH, transcendentals=0
-        ),
-        name="cross_gram",
-    )(diagonal, own, other)
+            flops=2 * HALF * 2 * LANES * WIDTH, bytes_accessed=2 * HALF * WIDTH, transcendentals=0
+        ),
+        name="cross_rest",
+    )(diagonal, cross, own, other)
 
 
 def exchange(value, stream, hop):
@@ -198,11 +222,10 @@
     return jnp.concatenate([half, exchange(half, stream, 0)])
 
 
-def unpermute(first_ref, rest_ref, packed_ref, core):
-    places = ((first_ref, 0), (rest_ref, 0), (rest_ref, PIECES[1]))
-    for s, (pieces_ref, start) in enumerate(places):
+def unpermute(streams, packed_ref, core):
+    for s, pieces_ref in enumerate(streams):
         for k in range(CHIPS):
-            packed_ref[piece_rows(s, k, BASES[s], core), :] = pieces_ref[k, pl.ds(start, PIECES[s]), :]
+            packed_ref[piece_rows(s, k, BASES[s], core), :] = pieces_ref[k]
 
 
 def mirror(packed_ref, out_ref, lower):
@@ -216,21 +239,21 @@
             out_ref[pl.ds(first, LANES), pl.ds(first + LANES, below.shape[0])] = below.T
 
 
-def own_square_kernel(first_ref, rest_ref, packed_ref, gram_ref, square_ref):
+def own_square_kernel(a_ref, b_ref, c_ref, packed_ref, gram_ref, square_ref):
     row, column = iotas()
-    unpermute(first_ref, rest_ref, packed_ref, lax.axis_index("c"))
+    unpermute((a_ref, b_ref, c_ref), packed_ref, lax.axis_index("c"))
     mirror(packed_ref, gram_ref, row >= column)
     for n in range(0, HALF, 256):
         columns = pl.ds(n, 256)
         square_ref[:, columns] = jnp.dot(gram_ref[...], gram_ref[:, columns], preferred_element_type=jnp.float32)
 
 
-def own_square(first, rest):
+def own_square(*streams):
     return pl.pallas_call(
         own_square_kernel,
         out_shape=(
-            jax.ShapeDtypeStruct((PACKED, LANES), first.dtype),
-            jax.ShapeDtypeStruct((HALF, HALF), first.dtype),
+            jax.ShapeDtypeStruct((PACKED, LANES), streams[0].dtype),
+            jax.ShapeDtypeStruct((HALF, HALF), streams[0].dtype),
             jax.ShapeDtypeStruct((HALF, HALF), jnp.float32),
         ),
         compiler_params=pltpu.CompilerParams(vmem_limit_bytes=12 * MIB),
@@ -238,7 +261,7 @@
             flops=2 * HALF * HALF * HALF, bytes_accessed=8 * HALF * HALF, transcendentals=0
         ),
         name="own_square",
-    )(first, rest)
+    )(*streams)
 
 
 def unpack_cross(own_ref, other_ref, cross_ref):
@@ -256,13 +279,13 @@
 
 
 def update_kernel(
-    own_ref, first_ref, rest_ref, gram_ref, square_ref, x_ref, x_other_ref, out_ref,
+    own_ref, a_ref, b_ref, c_ref, gram_ref, square_ref, x_ref, x_other_ref, out_ref,
     other_ref, cross_ref, gram_other_ref, mixing_ref,
 ):
     scale = math.sqrt(max(ROWS, COLS))
     step = 256
     row, column = iotas()
-    unpermute(first_ref, rest_ref, other_ref, 1 - lax.axis_index("c"))
+    unpermute((a_ref, b_ref, c_ref), other_ref, 1 - lax.axis_index("c"))
     unpack_cross(own_ref, other_ref, cross_ref)
     mirror(other_ref, gram_other_ref, row >= column)
     for n in range(0, HALF, step):
@@ -354,18 +377,19 @@
     other = swap_cores(own)
     keep_a, send_a, diagonal = own_gram(own)
     arrived_a = exchange(send_a, 0, 0)
-    keep_b, send_b, keep_c, send_c = cross_gram(diagonal, own, other)
-    arrived_b, arrived_c = exchange(send_b, 1, 0), exchange(send_c, 2, 0)
+    keep_b, send_b, cross = cross_first(own, other)
+    arrived_b = exchange(send_b, 1, 0)
+    keep_c, send_c = cross_rest(diagonal, cross, own, other)
+    arrived_c = exchange(send_c, 2, 0)
     streams = [
-        sum_over_chips(0, keep_a, after(arrived_a, send_b, send_c), arrived_b),
+        sum_over_chips(0, keep_a, after(arrived_a, send_b), arrived_b),
         sum_over_chips(1, keep_b, arrived_b),
         sum_over_chips(2, keep_c, arrived_c),
     ]
-    first, rest = streams[0], jnp.concatenate(streams[1:], axis=1)
-    first_other = swap_cores(first)
-    rest_other = swap_cores(after(rest, first_other))
-    packed, gram, square = own_square(first, rest)
-    sent = update_rows(packed, first_other, rest_other, gram, square, own, other)
+    others = [swap_cores(streams[0])]
+    others += [swap_cores(after(stream, others[0])) for stream in streams[1:]]
+    packed, gram, square = own_square(*streams)
+    sent = update_rows(packed, *others, gram, square, own, other)
     sent = sent.reshape(STRIPES * CHIPS, PANEL + PANEL // 2, LANES)
     received = lax.all_to_all(sent, ALL_CHIPS, 0, 0, tiled=True)
     return join_columns(received.reshape(STRIPES, CHIPS, PANEL + PANEL // 2, LANES))

time: 131 us -> 138 us (1.053)
  waiting for transfers between devices: 19.9 us -> 22.9 us
  starting transfers between devices: 15.5 us -> 18.3 us
    ppermute x12, waiting for transfers between devices: 16.6 us -> 20.1 us  [exchange(): return lax.ppermute(value, ('x', 'yh', 'c'), pairs)]
    ppermute x12, starting transfers between devices: 15.1 us -> 17.8 us  [exchange(): return lax.ppermute(value, ('x', 'yh', 'c'), pairs)]
    ppermute x3 -> x4, waiting for transfers between devices: 3.34 us -> 2.79 us  [swap_cores(): return lax.ppermute(value, 'c', [(0, 1), (1, 0)])]
  transfers between devices with their start and end apart: 15 -> 16, of which waited for: 10 -> 10; matrix products, arithmetic and copies ran while one was open for 1% -> 0% of each run, Pallas kernels for 3% -> 3%
where the time goes in v13:
time: 138 us; the launch traced here: 137 us
  blocking collectives  79.4 us (58%)
  waiting for transfers between devices  22.9 us (17%)
  starting transfers between devices  18.3 us (13%)
  Pallas kernels  14 us (10%)
  local copies, waits for them, and re-layouts  1.66 us (1%)
    all_to_all x1, blocking collectives, shards(): received = lax.all_to_all(sent, ALL_CHIPS, 0, 0, tiled=True)  41.7 us
    all_to_all x1, blocking collectives, shards(): lax.all_to_all(pieces, CHIP_AXES, 0, 0, tiled=True).reshape(HALF, WIDTH)  37.7 us
    ppermute x12, waiting for transfers between devices, exchange(): return lax.ppermute(value, ('x', 'yh', 'c'), pairs)  20.1 us
    ppermute x12, starting transfers between devices, exchange(): return lax.ppermute(value, ('x', 'yh', 'c'), pairs)  17.8 us
    pallas_call x1, Pallas kernels, update_rows(): pl.pallas_call(update_kernel, out_shape=jax.ShapeDtypeStruct((STRIPES, CH...  7.11 us
    ppermute x4, waiting for transfers between devices, swap_cores(): return lax.ppermute(value, 'c', [(0, 1), (1, 0)])  2.79 us
  transfers between devices with their start and end apart: 16, of which 10 were waited for; matrix products, arithmetic and copies ran while one was open for 0% of the time, Pallas kernels for 3%

profile of v13, /device:TPU:0, one launch (start us, length us, event | category | flops | bytes accessed | tf_op | source)
XLA Modules:
  0.0 137.3 jit_solution(15932337976159778614)
XLA Ops:
  0.0 0.0 copy-start
  0.0 1.7 %copy-done = bf16[1,96,12288]{2,1,0:T(8,128)(2,1)S(1)} copy-done((bf16[1,96,12288]{2,1,0:T(8,128)(2,1)S(1)}, bf16[1,96,12288]{2,1,0:T(8,128)(2,1)}, u32[]{:S(2)}) %copy-start) | copy-done | bytes 2359320
  1.7 0.6 split_columns.1
  2.3 37.7 %all_to_all.10 = bf16[8,96,1536]{2,1,0:T(8,128)(2,1)S(1)} all-to-all(bf16[8,96,1536]{2,1,0:T(8,128)(2,1)S(1)} %split_columns.1), channel_id=1, replica_groups=mesh['z'=4,'yl'=2,'x'=4,'yh'=2,'c'=2] {'x','yh'}, dimensions={0} | all-to-all | bytes 4718592 | tf_op jit(solution)/shard_map/all_to_all | solution.py:376
  40.0 0.0 collective-permute-start.1
  40.0 1.5 %own_gram.1 = (f32[4,240,128]{2,1,0:T(8,128)S(1)}, bf16[4,240,128]{2,1,0:T(8,128)(2,1)S(1)}, f32[6,128,128]{2,1,0:T(8,128)S(1)}) custom-call(bf16[768,1536]{1,0:T(8,128)(2,1)S(1)} %bitcast.11), custom_call_target="tpu_custom_call" | custom-call | flops 1660944384 | bytes 2359296 | tf_op jit(solution)/shard_map/own_gram/pallas_call | solution.py:129
  41.4 0.6 collective-permute-start
  42.0 2.5 %collective-permute-done.1.other_ref.x_other_ref = bf16[768,1536]{1,0:T(8,128)(2,1)S(1)} collective-permute-done((bf16[768,1536]{1,0:T(8,128)(2,1)S(1)}, bf16[768,1536]{1,0:T(8,128)(2,1)S(1)}, u32[]{:S(2)}, u32[]{:S(2)}) %collective-permute-start.1) | collective-permute-done | bytes 2359328 | tf_op jit(solution)/shard_map/ppermute | solution.py:371
  44.5 1.3 cross_first.1
  45.8 1.5 %collective-permute-start.3 = (bf16[4,192,128]{2,1,0:T(8,128)(2,1)S(1)}, bf16[4,192,128]{2,1,0:T(8,128)(2,1)S(1)}, u32[]{:S(2)}, u32[]{:S(2)}) collective-permute-start(bf16[4,192,128]{2,1,0:T(8,128)(2,1)S(1)} %get-tuple-element.22), channel_id=1, source_target_pairs={{0,12},{1,3},{2,14},{3,1},{4,8},{5,7},{6,10},{7,5},{8,4},{9,11},{1... | collective-permute-start | bytes 589832 | tf_op jit(solution)/shard_map/ppermute | solution.py:206
  47.3 0.5 collective-permute-done
  47.7 0.7 cross_rest.1
  48.4 1.7 %collective-permute-start.9 = (bf16[4,160,128]{2,1,0:T(8,128)(2,1)S(1)}, bf16[4,160,128]{2,1,0:T(8,128)(2,1)S(1)}, u32[]{:S(2)}, u32[]{:S(2)}) collective-permute-start(bf16[4,160,128]{2,1,0:T(8,128)(2,1)S(1)} %get-tuple-element.29), channel_id=1, source_target_pairs={{0,2},{1,5},{2,0},{3,7},{4,6},{5,1},{6,4},{7,3},{8,10},{9,13},{10,... | collective-permute-start | bytes 491528 | tf_op jit(solution)/shard_map/ppermute | solution.py:206
  50.1 0.1 add_convert_fusion.2
  50.2 1.4 %collective-permute-start.2 = (bf16[2,2,240,128]{3,2,1,0:T(8,128)(2,1)S(1)}, bf16[2,2,240,128]{3,2,1,0:T(8,128)(2,1)S(1)}, u32[]{:S(2)}, u32[]{:S(2)}) collective-permute-start(bf16[2,2,240,128]{3,2,1,0:T(8,128)(2,1)S(1)} %bitcast.18), channel_id=1, source_target_pairs={{0,12},{1,3},{2,14},{3,1},{4,8},{5,7},{6,10},{7,5},{8,4},{9,11},{1... | collective-permute-start | bytes 737288 | tf_op jit(solution)/shard_map/ppermute | solution.py:206
  51.6 5.5 %collective-permute-done.9 = bf16[4,160,128]{2,1,0:T(8,128)(2,1)S(1)} collective-permute-done((bf16[4,160,128]{2,1,0:T(8,128)(2,1)S(1)}, bf16[4,160,128]{2,1,0:T(8,128)(2,1)S(1)}, u32[]{:S(2)}, u32[]{:S(2)}) %collective-permute-start.9) | collective-permute-done | bytes 163872 | tf_op jit(solution)/shard_map/ppermute | solution.py:206
  57.1 0.1 collective-permute-start.10
  57.2 0.0 collective-permute-done.3
  57.2 0.1 add_convert_fusion.5
  57.3 1.7 %collective-permute-start.6 = (bf16[2,2,192,128]{3,2,1,0:T(8,128)(2,1)S(1)}, bf16[2,2,192,128]{3,2,1,0:T(8,128)(2,1)S(1)}, u32[]{:S(2)}, u32[]{:S(2)}) collective-permute-start(bf16[2,2,192,128]{3,2,1,0:T(8,128)(2,1)S(1)} %bitcast.22), channel_id=1, source_target_pairs={{0,2},{1,5},{2,0},{3,7},{4,6},{5,1},{6,4},{7,3},{8,10},{9,13},{10,... | collective-permute-start | bytes 589832 | tf_op jit(solution)/shard_map/ppermute | solution.py:206
  59.0 0.0 collective-permute-done.2
  59.0 0.1 add_convert_fusion.1
  59.1 2.0 %collective-permute-start.4 = (bf16[2,2,240,128]{3,2,1,0:T(8,128)(2,1)S(1)}, bf16[2,2,240,128]{3,2,1,0:T(8,128)(2,1)S(1)}, u32[]{:S(2)}, u32[]{:S(2)}) collective-permute-start(bf16[2,2,240,128]{3,2,1,0:T(8,128)(2,1)S(1)} %add_convert_fusion.1), channel_id=1, source_target_pairs={{0,2},{1,5},{2,0},{3,7},{4,6},{5,1},{6,4},{7,3},{8,10},{9,13},{10,... | collective-permute-start | bytes 737288 | tf_op jit(solution)/shard_map/ppermute | solution.py:206
  61.1 3.1 %collective-permute-done.10 = bf16[2,2,160,128]{3,2,1,0:T(8,128)(2,1)S(1)} collective-permute-done((bf16[2,2,160,128]{3,2,1,0:T(8,128)(2,1)S(1)}, bf16[2,2,160,128]{3,2,1,0:T(8,128)(2,1)S(1)}, u32[]{:S(2)}, u32[]{:S(2)}) %collective-permute-start.10) | collective-permute-done | bytes 163872 | tf_op jit(solution)/shard_map/ppermute | solution.py:206
  64.2 0.3 collective-permute-done.6
  64.6 2.1 %collective-permute-start.7 = (bf16[2,2,192,128]{3,2,1,0:T(8,128)(2,1)S(1)}, bf16[2,2,192,128]{3,2,1,0:T(8,128)(2,1)S(1)}, u32[]{:S(2)}, u32[]{:S(2)}) collective-permute-start(bf16[2,2,192,128]{3,2,1,0:T(8,128)(2,1)S(1)} %add_convert_fusion.4), channel_id=1, source_target_pairs={{0,4},{1,13},{2,6},{3,15},{4,0},{5,9},{6,2},{7,11},{8,12},{9,5},{1... | collective-permute-start | bytes 589832 | tf_op jit(solution)/shard_map/ppermute | solution.py:206
  66.7 0.5 collective-permute-done.4
  67.2 0.1 add_convert_fusion
  67.3 2.1 %collective-permute-start.5 = (bf16[4,240,128]{2,1,0:T(8,128)(2,1)S(1)}, bf16[4,240,128]{2,1,0:T(8,128)(2,1)S(1)}, u32[]{:S(2)}, u32[]{:S(2)}) collective-permute-start(bf16[4,240,128]{2,1,0:T(8,128)(2,1)S(1)} %bitcast.20), channel_id=1, source_target_pairs={{0,4},{1,13},{2,6},{3,15},{4,0},{5,9},{6,2},{7,11},{8,12},{9,5},{1... | collective-permute-start | bytes 737288 | tf_op jit(solution)/shard_map/ppermute | solution.py:206
  69.4 1.5 %collective-permute-start.11 = (bf16[2,2,160,128]{3,2,1,0:T(8,128)(2,1)S(1)}, bf16[2,2,160,128]{3,2,1,0:T(8,128)(2,1)S(1)}, u32[]{:S(2)}, u32[]{:S(2)}) collective-permute-start(bf16[2,2,160,128]{3,2,1,0:T(8,128)(2,1)S(1)} %add_convert_fusion.7), channel_id=1, source_target_pairs={{0,12},{1,3},{2,14},{3,1},{4,8},{5,7},{6,10},{7,5},{8,4},{9,11},{1... | collective-permute-start | bytes 491528 | tf_op jit(solution)/shard_map/ppermute | solution.py:206
  70.9 5.1 %collective-permute-done.11 = bf16[2,2,160,128]{3,2,1,0:T(8,128)(2,1)S(1)} collective-permute-done((bf16[2,2,160,128]{3,2,1,0:T(8,128)(2,1)S(1)}, bf16[2,2,160,128]{3,2,1,0:T(8,128)(2,1)S(1)}, u32[]{:S(2)}, u32[]{:S(2)}) %collective-permute-start.11) | collective-permute-done | bytes 163872 | tf_op jit(solution)/shard_map/ppermute | solution.py:206
  76.0 0.0 collective-permute-done.7
  76.1 0.0 collective-permute-done.5
  76.2 0.1 collective-permute-start.13
  76.3 1.5 %collective-permute-start.8 = (bf16[4,192,128]{2,1,0:T(8,128)(2,1)S(1)}, bf16[4,192,128]{2,1,0:T(8,128)(2,1)S(1)}, u32[]{:S(2)}, u32[]{:S(2)}) collective-permute-start(bf16[4,192,128]{2,1,0:T(8,128)(2,1)S(1)} %bitcast.24), channel_id=1, source_target_pairs={{0,12},{1,3},{2,14},{3,1},{4,8},{5,7},{6,10},{7,5},{8,4},{9,11},{1... | collective-permute-start | bytes 589832 | tf_op jit(solution)/shard_map/ppermute | solution.py:206
  77.9 1.7 %collective-permute-start.12 = (bf16[4,160,128]{2,1,0:T(8,128)(2,1)S(1)}, bf16[4,160,128]{2,1,0:T(8,128)(2,1)S(1)}, u32[]{:S(2)}, u32[]{:S(2)}) collective-permute-start(bf16[4,160,128]{2,1,0:T(8,128)(2,1)S(1)} %bitcast.28), channel_id=1, source_target_pairs={{0,2},{1,5},{2,0},{3,7},{4,6},{5,1},{6,4},{7,3},{8,10},{9,13},{10,... | collective-permute-start | bytes 491528 | tf_op jit(solution)/shard_map/ppermute | solution.py:206
  79.5 3.7 %collective-permute-done.8 = bf16[4,192,128]{2,1,0:T(8,128)(2,1)S(1)} collective-permute-done((bf16[4,192,128]{2,1,0:T(8,128)(2,1)S(1)}, bf16[4,192,128]{2,1,0:T(8,128)(2,1)S(1)}, u32[]{:S(2)}, u32[]{:S(2)}) %collective-permute-start.8) | collective-permute-done | bytes 196640 | tf_op jit(solution)/shard_map/ppermute | solution.py:206
  83.3 0.0 collective-permute-done.13.a_ref
  83.3 0.1 collective-permute-start.14
  83.4 1.4 %collective-permute-done.12 = bf16[4,160,128]{2,1,0:T(8,128)(2,1)S(1)} collective-permute-done((bf16[4,160,128]{2,1,0:T(8,128)(2,1)S(1)}, bf16[4,160,128]{2,1,0:T(8,128)(2,1)S(1)}, u32[]{:S(2)}, u32[]{:S(2)}) %collective-permute-start.12) | collective-permute-done | bytes 163872 | tf_op jit(solution)/shard_map/ppermute | solution.py:206
  84.9 0.3 collective-permute-start.15
  85.1 1.3 own_square.1
  86.4 0.3 collective-permute-done.15.c_ref
  86.8 0.0 collective-permute-done.14.b_ref
  86.8 7.1 %update_rows.1 = bf16[8,8,144,128]{3,2,1,0:T(8,128)(2,1)S(1)} custom-call(bf16[4736,128]{1,0:T(8,128)(2,1)S(1)} %get-tuple-element.30.own_ref, bf16[8,240,128]{2,1,0:T(8,128)(2,1)S(1)} %collective-permute-done.13.a_ref, bf16[8,192,128]{2,1,0:T(8,128)(2,1)S(1)} %collective-permute-done.14.b_ref, bf16[8,160,128]{2,1,0:T(8,128)(2,1)S(1)} %collective-permute-done.15.c_ref, ...), custom_call_target="tpu_custom_call" | custom-call | flops 6341787648 | bytes 11796480 | tf_op jit(solution)/shard_map/update_rows/pallas_call | solution.py:323
  93.9 41.7 %all_to_all.11 = bf16[64,144,128]{2,1,0:T(8,128)(2,1)S(1)} all-to-all(bf16[64,144,128]{2,1,0:T(8,128)(2,1)S(1)} %bitcast.17), channel_id=1, replica_groups=mesh['z'=4,'yl'=2,'x'=4,'yh'=2,'c'=2] {'z','yl','x','yh'}, dimensions={0} | all-to-all | bytes 4718592 | tf_op jit(solution)/shard_map/all_to_all | solution.py:394
  135.6 1.6 %join_columns.1 = bf16[8,96,1536]{2,1,0:T(8,128)(2,1)} custom-call(bf16[8,8,144,128]{3,2,1,0:T(8,128)(2,1)S(1)} %bitcast.15), custom_call_target="tpu_custom_call" | custom-call | tf_op jit(solution)/shard_map/join_columns/pallas_call | solution.py:359
  (14 shorter events, 0.5 us)
Async XLA Ops:
  0.0 1.7 %copy-start = (bf16[1,96,12288]{2,1,0:T(8,128)(2,1)S(1)}, bf16[1,96,12288]{2,1,0:T(8,128)(2,1)}, u32[]{:S(2)}) copy-start(bf16[1,96,12288]{2,1,0:T(8,128)(2,1)} %param.1) | copy-start | bytes 7077892
  40.0 4.5 %collective-permute-start.1 = (bf16[768,1536]{1,0:T(8,128)(2,1)S(1)}, bf16[768,1536]{1,0:T(8,128)(2,1)S(1)}, u32[]{:S(2)}, u32[]{:S(2)}) collective-permute-start(bf16[768,1536]{1,0:T(8,128)(2,1)S(1)} %bitcast.10), channel_id=1, source_target_pairs={{0,1},{1,0},{2,3},{3,2},{4,5},{5,4},{6,7},{7,6},{8,9},{9,8},{10,11... | collective-permute-start | bytes 7077896 | tf_op jit(solution)/shard_map/ppermute | solution.py:371
  41.4 6.3 %collective-permute-start = (bf16[4,240,128]{2,1,0:T(8,128)(2,1)S(1)}, bf16[4,240,128]{2,1,0:T(8,128)(2,1)S(1)}, u32[]{:S(2)}, u32[]{:S(2)}) collective-permute-start(bf16[4,240,128]{2,1,0:T(8,128)(2,1)S(1)} %get-tuple-element.21), channel_id=1, source_target_pairs={{0,4},{1,13},{2,6},{3,15},{4,0},{5,9},{6,2},{7,11},{8,12},{9,5},{1... | collective-permute-start | bytes 737288 | tf_op jit(solution)/shard_map/ppermute | solution.py:206
  45.8 11.5 %collective-permute-start.3 = (bf16[4,192,128]{2,1,0:T(8,128)(2,1)S(1)}, bf16[4,192,128]{2,1,0:T(8,128)(2,1)S(1)}, u32[]{:S(2)}, u32[]{:S(2)}) collective-permute-start(bf16[4,192,128]{2,1,0:T(8,128)(2,1)S(1)} %get-tuple-element.22), channel_id=1, source_target_pairs={{0,12},{1,3},{2,14},{3,1},{4,8},{5,7},{6,10},{7,5},{8,4},{9,11},{1... | collective-permute-start | bytes 589832 | tf_op jit(solution)/shard_map/ppermute | solution.py:206
  48.4 8.7 %collective-permute-start.9 = (bf16[4,160,128]{2,1,0:T(8,128)(2,1)S(1)}, bf16[4,160,128]{2,1,0:T(8,128)(2,1)S(1)}, u32[]{:S(2)}, u32[]{:S(2)}) collective-permute-start(bf16[4,160,128]{2,1,0:T(8,128)(2,1)S(1)} %get-tuple-element.29), channel_id=1, source_target_pairs={{0,2},{1,5},{2,0},{3,7},{4,6},{5,1},{6,4},{7,3},{8,10},{9,13},{10,... | collective-permute-start | bytes 491528 | tf_op jit(solution)/shard_map/ppermute | solution.py:206
  50.2 8.8 %collective-permute-start.2 = (bf16[2,2,240,128]{3,2,1,0:T(8,128)(2,1)S(1)}, bf16[2,2,240,128]{3,2,1,0:T(8,128)(2,1)S(1)}, u32[]{:S(2)}, u32[]{:S(2)}) collective-permute-start(bf16[2,2,240,128]{3,2,1,0:T(8,128)(2,1)S(1)} %bitcast.18), channel_id=1, source_target_pairs={{0,12},{1,3},{2,14},{3,1},{4,8},{5,7},{6,10},{7,5},{8,4},{9,11},{1... | collective-permute-start | bytes 737288 | tf_op jit(solution)/shard_map/ppermute | solution.py:206
  57.1 7.1 %collective-permute-start.10 = (bf16[2,2,160,128]{3,2,1,0:T(8,128)(2,1)S(1)}, bf16[2,2,160,128]{3,2,1,0:T(8,128)(2,1)S(1)}, u32[]{:S(2)}, u32[]{:S(2)}) collective-permute-start(bf16[2,2,160,128]{3,2,1,0:T(8,128)(2,1)S(1)} %bitcast.26), channel_id=1, source_target_pairs={{0,4},{1,13},{2,6},{3,15},{4,0},{5,9},{6,2},{7,11},{8,12},{9,5},{1... | collective-permute-start | bytes 491528 | tf_op jit(solution)/shard_map/ppermute | solution.py:206
  57.3 7.3 %collective-permute-start.6 = (bf16[2,2,192,128]{3,2,1,0:T(8,128)(2,1)S(1)}, bf16[2,2,192,128]{3,2,1,0:T(8,128)(2,1)S(1)}, u32[]{:S(2)}, u32[]{:S(2)}) collective-permute-start(bf16[2,2,192,128]{3,2,1,0:T(8,128)(2,1)S(1)} %bitcast.22), channel_id=1, source_target_pairs={{0,2},{1,5},{2,0},{3,7},{4,6},{5,1},{6,4},{7,3},{8,10},{9,13},{10,... | collective-permute-start | bytes 589832 | tf_op jit(solution)/shard_map/ppermute | solution.py:206
  59.1 8.1 %collective-permute-start.4 = (bf16[2,2,240,128]{3,2,1,0:T(8,128)(2,1)S(1)}, bf16[2,2,240,128]{3,2,1,0:T(8,128)(2,1)S(1)}, u32[]{:S(2)}, u32[]{:S(2)}) collective-permute-start(bf16[2,2,240,128]{3,2,1,0:T(8,128)(2,1)S(1)} %add_convert_fusion.1), channel_id=1, source_target_pairs={{0,2},{1,5},{2,0},{3,7},{4,6},{5,1},{6,4},{7,3},{8,10},{9,13},{10,... | collective-permute-start | bytes 737288 | tf_op jit(solution)/shard_map/ppermute | solution.py:206
  64.6 11.4 %collective-permute-start.7 = (bf16[2,2,192,128]{3,2,1,0:T(8,128)(2,1)S(1)}, bf16[2,2,192,128]{3,2,1,0:T(8,128)(2,1)S(1)}, u32[]{:S(2)}, u32[]{:S(2)}) collective-permute-start(bf16[2,2,192,128]{3,2,1,0:T(8,128)(2,1)S(1)} %add_convert_fusion.4), channel_id=1, source_target_pairs={{0,4},{1,13},{2,6},{3,15},{4,0},{5,9},{6,2},{7,11},{8,12},{9,5},{1... | collective-permute-start | bytes 589832 | tf_op jit(solution)/shard_map/ppermute | solution.py:206
  67.3 8.8 %collective-permute-start.5 = (bf16[4,240,128]{2,1,0:T(8,128)(2,1)S(1)}, bf16[4,240,128]{2,1,0:T(8,128)(2,1)S(1)}, u32[]{:S(2)}, u32[]{:S(2)}) collective-permute-start(bf16[4,240,128]{2,1,0:T(8,128)(2,1)S(1)} %bitcast.20), channel_id=1, source_target_pairs={{0,4},{1,13},{2,6},{3,15},{4,0},{5,9},{6,2},{7,11},{8,12},{9,5},{1... | collective-permute-start | bytes 737288 | tf_op jit(solution)/shard_map/ppermute | solution.py:206
  69.4 6.6 %collective-permute-start.11 = (bf16[2,2,160,128]{3,2,1,0:T(8,128)(2,1)S(1)}, bf16[2,2,160,128]{3,2,1,0:T(8,128)(2,1)S(1)}, u32[]{:S(2)}, u32[]{:S(2)}) collective-permute-start(bf16[2,2,160,128]{3,2,1,0:T(8,128)(2,1)S(1)} %add_convert_fusion.7), channel_id=1, source_target_pairs={{0,12},{1,3},{2,14},{3,1},{4,8},{5,7},{6,10},{7,5},{8,4},{9,11},{1... | collective-permute-start | bytes 491528 | tf_op jit(solution)/shard_map/ppermute | solution.py:206
  76.2 7.1 %collective-permute-start.13 = (bf16[8,240,128]{2,1,0:T(8,128)(2,1)S(1)}, bf16[8,240,128]{2,1,0:T(8,128)(2,1)S(1)}, u32[]{:S(2)}, u32[]{:S(2)}) collective-permute-start(bf16[8,240,128]{2,1,0:T(8,128)(2,1)S(1)} %pad_maximum_fusion.a_ref), channel_id=1, source_target_pairs={{0,1},{1,0},{2,3},{3,2},{4,5},{5,4},{6,7},{7,6},{8,9},{9,8},{10,11... | collective-permute-start | bytes 1474568 | tf_op jit(solution)/shard_map/ppermute | solution.py:371
  76.3 7.0 %collective-permute-start.8 = (bf16[4,192,128]{2,1,0:T(8,128)(2,1)S(1)}, bf16[4,192,128]{2,1,0:T(8,128)(2,1)S(1)}, u32[]{:S(2)}, u32[]{:S(2)}) collective-permute-start(bf16[4,192,128]{2,1,0:T(8,128)(2,1)S(1)} %bitcast.24), channel_id=1, source_target_pairs={{0,12},{1,3},{2,14},{3,1},{4,8},{5,7},{6,10},{7,5},{8,4},{9,11},{1... | collective-permute-start | bytes 589832 | tf_op jit(solution)/shard_map/ppermute | solution.py:206
  77.9 7.0 %collective-permute-start.12 = (bf16[4,160,128]{2,1,0:T(8,128)(2,1)S(1)}, bf16[4,160,128]{2,1,0:T(8,128)(2,1)S(1)}, u32[]{:S(2)}, u32[]{:S(2)}) collective-permute-start(bf16[4,160,128]{2,1,0:T(8,128)(2,1)S(1)} %bitcast.28), channel_id=1, source_target_pairs={{0,2},{1,5},{2,0},{3,7},{4,6},{5,1},{6,4},{7,3},{8,10},{9,13},{10,... | collective-permute-start | bytes 491528 | tf_op jit(solution)/shard_map/ppermute | solution.py:206
  83.3 3.4 %collective-permute-start.14 = (bf16[8,192,128]{2,1,0:T(8,128)(2,1)S(1)}, bf16[8,192,128]{2,1,0:T(8,128)(2,1)S(1)}, u32[]{:S(2)}, u32[]{:S(2)}) collective-permute-start(bf16[8,192,128]{2,1,0:T(8,128)(2,1)S(1)} %pad_maximum_fusion.1.b_ref), channel_id=1, source_target_pairs={{0,1},{1,0},{2,3},{3,2},{4,5},{5,4},{6,7},{7,6},{8,9},{9,8},{10,11... | collective-permute-start | bytes 1179656 | tf_op jit(solution)/shard_map/ppermute | solution.py:371
  84.9 1.9 %collective-permute-start.15 = (bf16[8,160,128]{2,1,0:T(8,128)(2,1)S(1)}, bf16[8,160,128]{2,1,0:T(8,128)(2,1)S(1)}, u32[]{:S(2)}, u32[]{:S(2)}) collective-permute-start(bf16[8,160,128]{2,1,0:T(8,128)(2,1)S(1)} %pad_maximum_fusion.2.c_ref), channel_id=1, source_target_pairs={{0,1},{1,0},{2,3},{3,2},{4,5},{5,4},{6,7},{7,6},{8,9},{9,8},{10,11... | collective-permute-start | bytes 983048 | tf_op jit(solution)/shard_map/ppermute | solution.py:371

commit v14 on v12

--- a/solution.py
+++ b/solution.py
@@ -190,12 +190,16 @@
     return lax.optimization_barrier((value, *others))[0]
 
 
-def sum_over_chips(stream, keep, arrived, *others):
-    kind = arrived.dtype
-    half = (keep + wide(arrived)).astype(kind).reshape(2, 2, *keep.shape[1:])
-    half = (wide(half) + wide(after(exchange(half, stream, 1), *others))[::-1]).astype(kind)
-    half = (wide(half) + wide(exchange(half, stream, 2))[:, ::-1]).astype(kind).reshape(arrived.shape)
-    return jnp.concatenate([half, exchange(half, stream, 0)])
+def add_first(keep, arrived):
+    return (keep + wide(arrived)).astype(arrived.dtype).reshape(2, 2, *keep.shape[1:])
+
+
+def add_second(half, arrived):
+    return (wide(half) + wide(arrived)[::-1]).astype(half.dtype)
+
+
+def add_third(half, arrived):
+    return (wide(half) + wide(arrived)[:, ::-1]).astype(half.dtype).reshape(CHIPS // 2, *half.shape[2:])
 
 
 def unpermute(first_ref, rest_ref, packed_ref, core):
@@ -356,12 +360,20 @@
     arrived_a = exchange(send_a, 0, 0)
     keep_b, send_b, keep_c, send_c = cross_gram(diagonal, own, other)
     arrived_b, arrived_c = exchange(send_b, 1, 0), exchange(send_c, 2, 0)
-    streams = [
-        sum_over_chips(0, keep_a, after(arrived_a, send_b, send_c), arrived_b),
-        sum_over_chips(1, keep_b, arrived_b),
-        sum_over_chips(2, keep_c, arrived_c),
-    ]
-    first, rest = streams[0], jnp.concatenate(streams[1:], axis=1)
+    half_a = add_first(keep_a, after(arrived_a, send_b, send_c))
+    half_b, half_c = add_first(keep_b, arrived_b), add_first(keep_c, arrived_c)
+    next_a, next_b, next_c = exchange(half_a, 0, 1), exchange(half_b, 1, 1), exchange(half_c, 2, 1)
+    half_a = add_second(half_a, after(next_a, arrived_b))
+    half_a = add_third(half_a, exchange(half_a, 0, 2))
+    half_b = add_second(half_b, next_b)
+    next_b = exchange(half_b, 1, 2)
+    half_c = add_second(half_c, after(next_c, half_a))
+    next_c = exchange(half_c, 2, 2)
+    first = jnp.concatenate([half_a, exchange(half_a, 0, 0)])
+    half_b = add_third(half_b, next_b)
+    half_c = add_third(half_c, after(next_c, first))
+    rest = [jnp.concatenate([half, exchange(half, s, 0)]) for s, half in ((1, half_b), (2, half_c))]
+    rest = jnp.concatenate(rest, axis=1)
     first_other = swap_cores(first)
     rest_other = swap_cores(after(rest, first_other))
     packed, gram, square = own_square(first, rest)

time: 131 us -> 131 us (level)
  starting transfers between devices: 15.5 us -> 14.1 us
    ppermute x12, starting transfers between devices: 15.1 us -> 13.7 us  [exchange(): return lax.ppermute(value, ('x', 'yh', 'c'), pairs)]
  transfers between devices with their start and end apart: 15 -> 15, of which waited for: 10 -> 12; matrix products, arithmetic and copies ran while one was open for 1% -> 1% of each run, Pallas kernels for 3% -> 3%
where the time goes in v14:
time: 131 us; the launch traced here: 130 us
  blocking collectives  79.2 us (60%)
  waiting for transfers between devices  20.9 us (16%)
  starting transfers between devices  14.1 us (11%)
  Pallas kernels  13.6 us (10%)
  local copies, waits for them, and re-layouts  1.66 us (1%)
    all_to_all x1, blocking collectives, shards(): received = lax.all_to_all(sent, ALL_CHIPS, 0, 0, tiled=True)  41.5 us
    all_to_all x1, blocking collectives, shards(): lax.all_to_all(pieces, CHIP_AXES, 0, 0, tiled=True).reshape(HALF, WIDTH)  37.7 us
    ppermute x12, waiting for transfers between devices, exchange(): return lax.ppermute(value, ('x', 'yh', 'c'), pairs)  17.6 us
    ppermute x12, starting transfers between devices, exchange(): return lax.ppermute(value, ('x', 'yh', 'c'), pairs)  13.7 us
    pallas_call x1, Pallas kernels, update_rows(): pl.pallas_call(update_kernel, out_shape=jax.ShapeDtypeStruct((STRIPES, CH...  7.12 us
    ppermute x3, waiting for transfers between devices, swap_cores(): return lax.ppermute(value, 'c', [(0, 1), (1, 0)])  3.34 us
  transfers between devices with their start and end apart: 15, of which 12 were waited for; matrix products, arithmetic and copies ran while one was open for 1% of the time, Pallas kernels for 3%

profile of v14, /device:TPU:0, one launch (start us, length us, event | category | flops | bytes accessed | tf_op | source)
XLA Modules:
  0.0 130.4 jit_solution(11924901537263104184)
XLA Ops:
  0.0 0.0 copy-start
  0.0 1.7 %copy-done = bf16[1,96,12288]{2,1,0:T(8,128)(2,1)S(1)} copy-done((bf16[1,96,12288]{2,1,0:T(8,128)(2,1)S(1)}, bf16[1,96,12288]{2,1,0:T(8,128)(2,1)}, u32[]{:S(2)}) %copy-start) | copy-done | bytes 2359320
  1.7 0.6 split_columns.1
  2.3 37.7 %all_to_all.10 = bf16[8,96,1536]{2,1,0:T(8,128)(2,1)S(1)} all-to-all(bf16[8,96,1536]{2,1,0:T(8,128)(2,1)S(1)} %split_columns.1), channel_id=1, replica_groups=mesh['z'=4,'yl'=2,'x'=4,'yh'=2,'c'=2] {'x','yh'}, dimensions={0} | all-to-all | bytes 4718592 | tf_op jit(solution)/shard_map/all_to_all | solution.py:357
  40.0 0.0 collective-permute-start.1
  40.0 1.5 %own_gram.1 = (f32[4,240,128]{2,1,0:T(8,128)S(1)}, bf16[4,240,128]{2,1,0:T(8,128)(2,1)S(1)}, f32[6,128,128]{2,1,0:T(8,128)S(1)}) custom-call(bf16[768,1536]{1,0:T(8,128)(2,1)S(1)} %bitcast.13), custom_call_target="tpu_custom_call" | custom-call | flops 1660944384 | bytes 2359296 | tf_op jit(solution)/shard_map/own_gram/pallas_call | solution.py:129
  41.4 0.6 collective-permute-start
  42.0 2.5 %collective-permute-done.1.other_ref.x_other_ref = bf16[768,1536]{1,0:T(8,128)(2,1)S(1)} collective-permute-done((bf16[768,1536]{1,0:T(8,128)(2,1)S(1)}, bf16[768,1536]{1,0:T(8,128)(2,1)S(1)}, u32[]{:S(2)}, u32[]{:S(2)}) %collective-permute-start.1) | collective-permute-done | bytes 2359328 | tf_op jit(solution)/shard_map/ppermute | solution.py:352
  44.5 1.5 %cross_gram.1 = (f32[4,176,128]{2,1,0:T(8,128)S(1)}, bf16[4,176,128]{2,1,0:T(8,128)(2,1)S(1)}, f32[4,176,128]{2,1,0:T(8,128)S(1)}, bf16[4,176,128]{2,1,0:T(8,128)(2,1)S(1)}) custom-call(f32[6,128,128]{2,1,0:T(8,128)S(1)} %get-tuple-element.22.diagonal_ref, bf16[768,1536]{1,0:T(8,128)(2,1)S(1)} %bitcast.14, ...), custom_call_target="tpu_custom_call" | custom-call | flops 1660944384 | bytes 4718592 | tf_op jit(solution)/shard_map/cross_gram/pallas_call | solution.py:162
  46.0 1.5 %collective-permute-start.3 = (bf16[4,176,128]{2,1,0:T(8,128)(2,1)S(1)}, bf16[4,176,128]{2,1,0:T(8,128)(2,1)S(1)}, u32[]{:S(2)}, u32[]{:S(2)}) collective-permute-start(bf16[4,176,128]{2,1,0:T(8,128)(2,1)S(1)} %get-tuple-element.23), channel_id=1, source_target_pairs={{0,12},{1,3},{2,14},{3,1},{4,8},{5,7},{6,10},{7,5},{8,4},{9,11},{1... | collective-permute-start | bytes 540680 | tf_op jit(solution)/shard_map/ppermute | solution.py:182
  47.5 0.2 collective-permute-done
  47.7 0.1 add_convert_fusion.2
  47.8 1.7 %collective-permute-start.2 = (bf16[2,2,240,128]{3,2,1,0:T(8,128)(2,1)S(1)}, bf16[2,2,240,128]{3,2,1,0:T(8,128)(2,1)S(1)}, u32[]{:S(2)}, u32[]{:S(2)}) collective-permute-start(bf16[2,2,240,128]{3,2,1,0:T(8,128)(2,1)S(1)} %bitcast.19), channel_id=1, source_target_pairs={{0,12},{1,3},{2,14},{3,1},{4,8},{5,7},{6,10},{7,5},{8,4},{9,11},{1... | collective-permute-start | bytes 737288 | tf_op jit(solution)/shard_map/ppermute | solution.py:182
  49.5 1.6 %collective-permute-start.9 = (bf16[4,176,128]{2,1,0:T(8,128)(2,1)S(1)}, bf16[4,176,128]{2,1,0:T(8,128)(2,1)S(1)}, u32[]{:S(2)}, u32[]{:S(2)}) collective-permute-start(bf16[4,176,128]{2,1,0:T(8,128)(2,1)S(1)} %get-tuple-element.24), channel_id=1, source_target_pairs={{0,2},{1,5},{2,0},{3,7},{4,6},{5,1},{6,4},{7,3},{8,10},{9,13},{10,... | collective-permute-start | bytes 540680 | tf_op jit(solution)/shard_map/ppermute | solution.py:182
  51.0 1.8 %collective-permute-done.3 = bf16[4,176,128]{2,1,0:T(8,128)(2,1)S(1)} collective-permute-done((bf16[4,176,128]{2,1,0:T(8,128)(2,1)S(1)}, bf16[4,176,128]{2,1,0:T(8,128)(2,1)S(1)}, u32[]{:S(2)}, u32[]{:S(2)}) %collective-permute-start.3) | collective-permute-done | bytes 180256 | tf_op jit(solution)/shard_map/ppermute | solution.py:182
  52.9 1.6 %collective-permute-start.6 = (bf16[2,2,176,128]{3,2,1,0:T(8,128)(2,1)S(1)}, bf16[2,2,176,128]{3,2,1,0:T(8,128)(2,1)S(1)}, u32[]{:S(2)}, u32[]{:S(2)}) collective-permute-start(bf16[2,2,176,128]{3,2,1,0:T(8,128)(2,1)S(1)} %bitcast.21), channel_id=1, source_target_pairs={{0,2},{1,5},{2,0},{3,7},{4,6},{5,1},{6,4},{7,3},{8,10},{9,13},{10,... | collective-permute-start | bytes 540680 | tf_op jit(solution)/shard_map/ppermute | solution.py:182
  54.5 0.9 collective-permute-done.2
  55.5 0.1 add_convert_fusion.1
  55.5 1.6 %collective-permute-start.4 = (bf16[2,2,240,128]{3,2,1,0:T(8,128)(2,1)S(1)}, bf16[2,2,240,128]{3,2,1,0:T(8,128)(2,1)S(1)}, u32[]{:S(2)}, u32[]{:S(2)}) collective-permute-start(bf16[2,2,240,128]{3,2,1,0:T(8,128)(2,1)S(1)} %add_convert_fusion.1), channel_id=1, source_target_pairs={{0,2},{1,5},{2,0},{3,7},{4,6},{5,1},{6,4},{7,3},{8,10},{9,13},{10,... | collective-permute-start | bytes 737288 | tf_op jit(solution)/shard_map/ppermute | solution.py:182
  57.2 0.0 collective-permute-done.9
  57.2 0.2 collective-permute-start.10
  57.5 2.5 %collective-permute-done.6 = bf16[2,2,176,128]{3,2,1,0:T(8,128)(2,1)S(1)} collective-permute-done((bf16[2,2,176,128]{3,2,1,0:T(8,128)(2,1)S(1)}, bf16[2,2,176,128]{3,2,1,0:T(8,128)(2,1)S(1)}, u32[]{:S(2)}, u32[]{:S(2)}) %collective-permute-start.6) | collective-permute-done | bytes 180256 | tf_op jit(solution)/shard_map/ppermute | solution.py:182
  60.0 0.1 collective-permute-start.7
  60.1 3.2 %collective-permute-done.4 = bf16[2,2,240,128]{3,2,1,0:T(8,128)(2,1)S(1)} collective-permute-done((bf16[2,2,240,128]{3,2,1,0:T(8,128)(2,1)S(1)}, bf16[2,2,240,128]{3,2,1,0:T(8,128)(2,1)S(1)}, u32[]{:S(2)}, u32[]{:S(2)}) %collective-permute-start.4) | collective-permute-done | bytes 245792 | tf_op jit(solution)/shard_map/ppermute | solution.py:182
  63.4 0.1 add_convert_fusion
  63.4 0.1 collective-permute-start.5
  63.5 0.0 collective-permute-done.10
  63.6 1.5 %collective-permute-start.11 = (bf16[2,2,176,128]{3,2,1,0:T(8,128)(2,1)S(1)}, bf16[2,2,176,128]{3,2,1,0:T(8,128)(2,1)S(1)}, u32[]{:S(2)}, u32[]{:S(2)}) collective-permute-start(bf16[2,2,176,128]{3,2,1,0:T(8,128)(2,1)S(1)} %add_convert_fusion.4), channel_id=1, source_target_pairs={{0,12},{1,3},{2,14},{3,1},{4,8},{5,7},{6,10},{7,5},{8,4},{9,11},{1... | collective-permute-start | bytes 540680 | tf_op jit(solution)/shard_map/ppermute | solution.py:182
  65.1 0.5 collective-permute-done.7
  65.7 1.5 %collective-permute-start.8 = (bf16[4,176,128]{2,1,0:T(8,128)(2,1)S(1)}, bf16[4,176,128]{2,1,0:T(8,128)(2,1)S(1)}, u32[]{:S(2)}, u32[]{:S(2)}) collective-permute-start(bf16[4,176,128]{2,1,0:T(8,128)(2,1)S(1)} %bitcast.25), channel_id=1, source_target_pairs={{0,12},{1,3},{2,14},{3,1},{4,8},{5,7},{6,10},{7,5},{8,4},{9,11},{1... | collective-permute-start | bytes 540680 | tf_op jit(solution)/shard_map/ppermute | solution.py:182
  67.2 2.5 %collective-permute-done.5 = bf16[4,240,128]{2,1,0:T(8,128)(2,1)S(1)} collective-permute-done((bf16[4,240,128]{2,1,0:T(8,128)(2,1)S(1)}, bf16[4,240,128]{2,1,0:T(8,128)(2,1)S(1)}, u32[]{:S(2)}, u32[]{:S(2)}) %collective-permute-start.5) | collective-permute-done | bytes 245792 | tf_op jit(solution)/shard_map/ppermute | solution.py:182
  69.7 0.1 collective-permute-start.13
  69.8 0.6 collective-permute-done.11
  70.5 1.6 %collective-permute-start.12 = (bf16[4,176,128]{2,1,0:T(8,128)(2,1)S(1)}, bf16[4,176,128]{2,1,0:T(8,128)(2,1)S(1)}, u32[]{:S(2)}, u32[]{:S(2)}) collective-permute-start(bf16[4,176,128]{2,1,0:T(8,128)(2,1)S(1)} %bitcast.27), channel_id=1, source_target_pairs={{0,2},{1,5},{2,0},{3,7},{4,6},{5,1},{6,4},{7,3},{8,10},{9,13},{10,... | collective-permute-start | bytes 540680 | tf_op jit(solution)/shard_map/ppermute | solution.py:182
  72.1 0.3 collective-permute-done.8
  72.4 5.1 %collective-permute-done.12 = bf16[4,176,128]{2,1,0:T(8,128)(2,1)S(1)} collective-permute-done((bf16[4,176,128]{2,1,0:T(8,128)(2,1)S(1)}, bf16[4,176,128]{2,1,0:T(8,128)(2,1)S(1)}, u32[]{:S(2)}, u32[]{:S(2)}) %collective-permute-start.12) | collective-permute-done | bytes 180256 | tf_op jit(solution)/shard_map/ppermute | solution.py:182
  77.6 0.0 collective-permute-done.13.first_ref
  77.6 0.3 collective-permute-start.14
  77.9 1.3 own_square.1
  79.2 0.9 collective-permute-done.14.rest_ref
  80.1 7.1 %update_rows.1 = bf16[8,8,144,128]{3,2,1,0:T(8,128)(2,1)S(1)} custom-call(bf16[4736,128]{1,0:T(8,128)(2,1)S(1)} %get-tuple-element.31.own_ref, bf16[8,240,128]{2,1,0:T(8,128)(2,1)S(1)} %collective-permute-done.13.first_ref, bf16[8,352,128]{2,1,0:T(8,128)(2,1)S(1)} %collective-permute-done.14.rest_ref, bf16[768,768]{1,0:T(8,128)(2,1)S(1)} %get-tuple-element.33.gram_ref, ...), custom_call_target="tpu_custom_call" | custom-call | flops 6341787648 | bytes 11796480 | tf_op jit(solution)/shard_map/update_rows/pallas_call | solution.py:304
  87.2 41.5 %all_to_all.11 = bf16[64,144,128]{2,1,0:T(8,128)(2,1)S(1)} all-to-all(bf16[64,144,128]{2,1,0:T(8,128)(2,1)S(1)} %bitcast.16), channel_id=1, replica_groups=mesh['z'=4,'yl'=2,'x'=4,'yh'=2,'c'=2] {'z','yl','x','yh'}, dimensions={0} | all-to-all | bytes 4718592 | tf_op jit(solution)/shard_map/all_to_all | solution.py:382
  128.7 1.6 %join_columns.1 = bf16[8,96,1536]{2,1,0:T(8,128)(2,1)} custom-call(bf16[8,8,144,128]{3,2,1,0:T(8,128)(2,1)S(1)} %bitcast.10), custom_call_target="tpu_custom_call" | custom-call | tf_op jit(solution)/shard_map/join_columns/pallas_call | solution.py:340
  (14 shorter events, 0.5 us)
Async XLA Ops:
  0.0 1.7 %copy-start = (bf16[1,96,12288]{2,1,0:T(8,128)(2,1)S(1)}, bf16[1,96,12288]{2,1,0:T(8,128)(2,1)}, u32[]{:S(2)}) copy-start(bf16[1,96,12288]{2,1,0:T(8,128)(2,1)} %param.1) | copy-start | bytes 7077892
  40.0 4.5 %collective-permute-start.1 = (bf16[768,1536]{1,0:T(8,128)(2,1)S(1)}, bf16[768,1536]{1,0:T(8,128)(2,1)S(1)}, u32[]{:S(2)}, u32[]{:S(2)}) collective-permute-start(bf16[768,1536]{1,0:T(8,128)(2,1)S(1)} %bitcast.12), channel_id=1, source_target_pairs={{0,1},{1,0},{2,3},{3,2},{4,5},{5,4},{6,7},{7,6},{8,9},{9,8},{10,11... | collective-permute-start | bytes 7077896 | tf_op jit(solution)/shard_map/ppermute | solution.py:352
  41.4 6.3 %collective-permute-start = (bf16[4,240,128]{2,1,0:T(8,128)(2,1)S(1)}, bf16[4,240,128]{2,1,0:T(8,128)(2,1)S(1)}, u32[]{:S(2)}, u32[]{:S(2)}) collective-permute-start(bf16[4,240,128]{2,1,0:T(8,128)(2,1)S(1)} %get-tuple-element.21), channel_id=1, source_target_pairs={{0,4},{1,13},{2,6},{3,15},{4,0},{5,9},{6,2},{7,11},{8,12},{9,5},{1... | collective-permute-start | bytes 737288 | tf_op jit(solution)/shard_map/ppermute | solution.py:182
  46.0 6.8 %collective-permute-start.3 = (bf16[4,176,128]{2,1,0:T(8,128)(2,1)S(1)}, bf16[4,176,128]{2,1,0:T(8,128)(2,1)S(1)}, u32[]{:S(2)}, u32[]{:S(2)}) collective-permute-start(bf16[4,176,128]{2,1,0:T(8,128)(2,1)S(1)} %get-tuple-element.23), channel_id=1, source_target_pairs={{0,12},{1,3},{2,14},{3,1},{4,8},{5,7},{6,10},{7,5},{8,4},{9,11},{1... | collective-permute-start | bytes 540680 | tf_op jit(solution)/shard_map/ppermute | solution.py:182
  47.8 7.7 %collective-permute-start.2 = (bf16[2,2,240,128]{3,2,1,0:T(8,128)(2,1)S(1)}, bf16[2,2,240,128]{3,2,1,0:T(8,128)(2,1)S(1)}, u32[]{:S(2)}, u32[]{:S(2)}) collective-permute-start(bf16[2,2,240,128]{3,2,1,0:T(8,128)(2,1)S(1)} %bitcast.19), channel_id=1, source_target_pairs={{0,12},{1,3},{2,14},{3,1},{4,8},{5,7},{6,10},{7,5},{8,4},{9,11},{1... | collective-permute-start | bytes 737288 | tf_op jit(solution)/shard_map/ppermute | solution.py:182
  49.5 7.7 %collective-permute-start.9 = (bf16[4,176,128]{2,1,0:T(8,128)(2,1)S(1)}, bf16[4,176,128]{2,1,0:T(8,128)(2,1)S(1)}, u32[]{:S(2)}, u32[]{:S(2)}) collective-permute-start(bf16[4,176,128]{2,1,0:T(8,128)(2,1)S(1)} %get-tuple-element.24), channel_id=1, source_target_pairs={{0,2},{1,5},{2,0},{3,7},{4,6},{5,1},{6,4},{7,3},{8,10},{9,13},{10,... | collective-permute-start | bytes 540680 | tf_op jit(solution)/shard_map/ppermute | solution.py:182
  52.9 7.1 %collective-permute-start.6 = (bf16[2,2,176,128]{3,2,1,0:T(8,128)(2,1)S(1)}, bf16[2,2,176,128]{3,2,1,0:T(8,128)(2,1)S(1)}, u32[]{:S(2)}, u32[]{:S(2)}) collective-permute-start(bf16[2,2,176,128]{3,2,1,0:T(8,128)(2,1)S(1)} %bitcast.21), channel_id=1, source_target_pairs={{0,2},{1,5},{2,0},{3,7},{4,6},{5,1},{6,4},{7,3},{8,10},{9,13},{10,... | collective-permute-start | bytes 540680 | tf_op jit(solution)/shard_map/ppermute | solution.py:182
  55.5 7.8 %collective-permute-start.4 = (bf16[2,2,240,128]{3,2,1,0:T(8,128)(2,1)S(1)}, bf16[2,2,240,128]{3,2,1,0:T(8,128)(2,1)S(1)}, u32[]{:S(2)}, u32[]{:S(2)}) collective-permute-start(bf16[2,2,240,128]{3,2,1,0:T(8,128)(2,1)S(1)} %add_convert_fusion.1), channel_id=1, source_target_pairs={{0,2},{1,5},{2,0},{3,7},{4,6},{5,1},{6,4},{7,3},{8,10},{9,13},{10,... | collective-permute-start | bytes 737288 | tf_op jit(solution)/shard_map/ppermute | solution.py:182
  57.2 6.3 %collective-permute-start.10 = (bf16[2,2,176,128]{3,2,1,0:T(8,128)(2,1)S(1)}, bf16[2,2,176,128]{3,2,1,0:T(8,128)(2,1)S(1)}, u32[]{:S(2)}, u32[]{:S(2)}) collective-permute-start(bf16[2,2,176,128]{3,2,1,0:T(8,128)(2,1)S(1)} %bitcast.23), channel_id=1, source_target_pairs={{0,4},{1,13},{2,6},{3,15},{4,0},{5,9},{6,2},{7,11},{8,12},{9,5},{1... | collective-permute-start | bytes 540680 | tf_op jit(solution)/shard_map/ppermute | solution.py:182
  60.0 5.6 %collective-permute-start.7 = (bf16[2,2,176,128]{3,2,1,0:T(8,128)(2,1)S(1)}, bf16[2,2,176,128]{3,2,1,0:T(8,128)(2,1)S(1)}, u32[]{:S(2)}, u32[]{:S(2)}) collective-permute-start(bf16[2,2,176,128]{3,2,1,0:T(8,128)(2,1)S(1)} %add_convert_fusion.7), channel_id=1, source_target_pairs={{0,4},{1,13},{2,6},{3,15},{4,0},{5,9},{6,2},{7,11},{8,12},{9,5},{1... | collective-permute-start | bytes 540680 | tf_op jit(solution)/shard_map/ppermute | solution.py:182
  63.4 6.3 %collective-permute-start.5 = (bf16[4,240,128]{2,1,0:T(8,128)(2,1)S(1)}, bf16[4,240,128]{2,1,0:T(8,128)(2,1)S(1)}, u32[]{:S(2)}, u32[]{:S(2)}) collective-permute-start(bf16[4,240,128]{2,1,0:T(8,128)(2,1)S(1)} %bitcast.17), channel_id=1, source_target_pairs={{0,4},{1,13},{2,6},{3,15},{4,0},{5,9},{6,2},{7,11},{8,12},{9,5},{1... | collective-permute-start | bytes 737288 | tf_op jit(solution)/shard_map/ppermute | solution.py:182
  63.6 6.8 %collective-permute-start.11 = (bf16[2,2,176,128]{3,2,1,0:T(8,128)(2,1)S(1)}, bf16[2,2,176,128]{3,2,1,0:T(8,128)(2,1)S(1)}, u32[]{:S(2)}, u32[]{:S(2)}) collective-permute-start(bf16[2,2,176,128]{3,2,1,0:T(8,128)(2,1)S(1)} %add_convert_fusion.4), channel_id=1, source_target_pairs={{0,12},{1,3},{2,14},{3,1},{4,8},{5,7},{6,10},{7,5},{8,4},{9,11},{1... | collective-permute-start | bytes 540680 | tf_op jit(solution)/shard_map/ppermute | solution.py:182
  65.7 6.8 %collective-permute-start.8 = (bf16[4,176,128]{2,1,0:T(8,128)(2,1)S(1)}, bf16[4,176,128]{2,1,0:T(8,128)(2,1)S(1)}, u32[]{:S(2)}, u32[]{:S(2)}) collective-permute-start(bf16[4,176,128]{2,1,0:T(8,128)(2,1)S(1)} %bitcast.25), channel_id=1, source_target_pairs={{0,12},{1,3},{2,14},{3,1},{4,8},{5,7},{6,10},{7,5},{8,4},{9,11},{1... | collective-permute-start | bytes 540680 | tf_op jit(solution)/shard_map/ppermute | solution.py:182
  69.7 7.9 %collective-permute-start.13 = (bf16[8,240,128]{2,1,0:T(8,128)(2,1)S(1)}, bf16[8,240,128]{2,1,0:T(8,128)(2,1)S(1)}, u32[]{:S(2)}, u32[]{:S(2)}) collective-permute-start(bf16[8,240,128]{2,1,0:T(8,128)(2,1)S(1)} %pad_maximum_fusion.first_ref), channel_id=1, source_target_pairs={{0,1},{1,0},{2,3},{3,2},{4,5},{5,4},{6,7},{7,6},{8,9},{9,8},{10,11... | collective-permute-start | bytes 1474568 | tf_op jit(solution)/shard_map/ppermute | solution.py:352
  70.5 7.1 %collective-permute-start.12 = (bf16[4,176,128]{2,1,0:T(8,128)(2,1)S(1)}, bf16[4,176,128]{2,1,0:T(8,128)(2,1)S(1)}, u32[]{:S(2)}, u32[]{:S(2)}) collective-permute-start(bf16[4,176,128]{2,1,0:T(8,128)(2,1)S(1)} %bitcast.27), channel_id=1, source_target_pairs={{0,2},{1,5},{2,0},{3,7},{4,6},{5,1},{6,4},{7,3},{8,10},{9,13},{10,... | collective-permute-start | bytes 540680 | tf_op jit(solution)/shard_map/ppermute | solution.py:182
  77.6 2.5 %collective-permute-start.14 = (bf16[8,352,128]{2,1,0:T(8,128)(2,1)S(1)}, bf16[8,352,128]{2,1,0:T(8,128)(2,1)S(1)}, u32[]{:S(2)}, u32[]{:S(2)}) collective-permute-start(bf16[8,352,128]{2,1,0:T(8,128)(2,1)S(1)} %maximum_maximum_fusion.rest_ref), channel_id=1, source_target_pairs={{0,1},{1,0},{2,3},{3,2},{4,5},{5,4},{6,7},{7,6},{8,9},{9,8},{10,11... | collective-permute-start | bytes 2162696 | tf_op jit(solution)/shard_map/ppermute | solution.py:352

commit v15 on v14

--- a/solution.py
+++ b/solution.py
@@ -24,7 +24,7 @@
 BELOW = LANES * BLOCKS * (BLOCKS - 1) // 2
 EDGE = 2 * BELOW + HALF
 PACKED = -(-(EDGE + BLOCKS) // (16 * CHIPS)) * 16 * CHIPS
-PIECES = (240, 176, 176)
+PIECES = (240, 192, 160)
 BASES = (0, CHIPS * PIECES[0], CHIPS * (PIECES[0] + PIECES[1]))
 MIB = 1 << 20
 
@@ -202,11 +202,10 @@
     return (wide(half) + wide(arrived)[:, ::-1]).astype(half.dtype).reshape(CHIPS // 2, *half.shape[2:])
 
 
-def unpermute(first_ref, rest_ref, packed_ref, core):
-    places = ((first_ref, 0), (rest_ref, 0), (rest_ref, PIECES[1]))
-    for s, (pieces_ref, start) in enumerate(places):
+def unpermute(streams, packed_ref, core):
+    for s, pieces_ref in enumerate(streams):
         for k in range(CHIPS):
-            packed_ref[piece_rows(s, k, BASES[s], core), :] = pieces_ref[k, pl.ds(start, PIECES[s]), :]
+            packed_ref[piece_rows(s, k, BASES[s], core), :] = pieces_ref[k]
 
 
 def mirror(packed_ref, out_ref, lower):
@@ -220,21 +219,21 @@
             out_ref[pl.ds(first, LANES), pl.ds(first + LANES, below.shape[0])] = below.T
 
 
-def own_square_kernel(first_ref, rest_ref, packed_ref, gram_ref, square_ref):
+def own_square_kernel(a_ref, b_ref, c_ref, packed_ref, gram_ref, square_ref):
     row, column = iotas()
-    unpermute(first_ref, rest_ref, packed_ref, lax.axis_index("c"))
+    unpermute((a_ref, b_ref, c_ref), packed_ref, lax.axis_index("c"))
     mirror(packed_ref, gram_ref, row >= column)
     for n in range(0, HALF, 256):
         columns = pl.ds(n, 256)
         square_ref[:, columns] = jnp.dot(gram_ref[...], gram_ref[:, columns], preferred_element_type=jnp.float32)
 
 
-def own_square(first, rest):
+def own_square(*streams):
     return pl.pallas_call(
         own_square_kernel,
         out_shape=(
-            jax.ShapeDtypeStruct((PACKED, LANES), first.dtype),
-            jax.ShapeDtypeStruct((HALF, HALF), first.dtype),
+            jax.ShapeDtypeStruct((PACKED, LANES), streams[0].dtype),
+            jax.ShapeDtypeStruct((HALF, HALF), streams[0].dtype),
             jax.ShapeDtypeStruct((HALF, HALF), jnp.float32),
         ),
         compiler_params=pltpu.CompilerParams(vmem_limit_bytes=12 * MIB),
@@ -242,7 +241,7 @@
             flops=2 * HALF * HALF * HALF, bytes_accessed=8 * HALF * HALF, transcendentals=0
         ),
         name="own_square",
-    )(first, rest)
+    )(*streams)
 
 
 def unpack_cross(own_ref, other_ref, cross_ref):
@@ -260,13 +259,13 @@
 
 
 def update_kernel(
-    own_ref, first_ref, rest_ref, gram_ref, square_ref, x_ref, x_other_ref, out_ref,
+    own_ref, a_ref, b_ref, c_ref, gram_ref, square_ref, x_ref, x_other_ref, out_ref,
     other_ref, cross_ref, gram_other_ref, mixing_ref,
 ):
     scale = math.sqrt(max(ROWS, COLS))
     step = 256
     row, column = iotas()
-    unpermute(first_ref, rest_ref, other_ref, 1 - lax.axis_index("c"))
+    unpermute((a_ref, b_ref, c_ref), other_ref, 1 - lax.axis_index("c"))
     unpack_cross(own_ref, other_ref, cross_ref)
     mirror(other_ref, gram_other_ref, row >= column)
     for n in range(0, HALF, step):
@@ -363,21 +362,21 @@
     half_a = add_first(keep_a, after(arrived_a, send_b, send_c))
     half_b, half_c = add_first(keep_b, arrived_b), add_first(keep_c, arrived_c)
     next_a, next_b, next_c = exchange(half_a, 0, 1), exchange(half_b, 1, 1), exchange(half_c, 2, 1)
-    half_a = add_second(half_a, after(next_a, arrived_b))
-    half_a = add_third(half_a, exchange(half_a, 0, 2))
+    half_a = add_second(half_a, after(next_a, half_b))
+    next_a = exchange(half_a, 0, 2)
     half_b = add_second(half_b, next_b)
+    half_a = add_third(half_a, after(next_a, half_b))
     next_b = exchange(half_b, 1, 2)
     half_c = add_second(half_c, after(next_c, half_a))
     next_c = exchange(half_c, 2, 2)
-    first = jnp.concatenate([half_a, exchange(half_a, 0, 0)])
     half_b = add_third(half_b, next_b)
+    first = jnp.concatenate([half_a, after(exchange(half_a, 0, 0), half_b)])
     half_c = add_third(half_c, after(next_c, first))
-    rest = [jnp.concatenate([half, exchange(half, s, 0)]) for s, half in ((1, half_b), (2, half_c))]
-    rest = jnp.concatenate(rest, axis=1)
-    first_other = swap_cores(first)
-    rest_other = swap_cores(after(rest, first_other))
-    packed, gram, square = own_square(first, rest)
-    sent = update_rows(packed, first_other, rest_other, gram, square, own, other)
+    streams = [first] + [jnp.concatenate([half, exchange(half, s, 0)]) for s, half in ((1, half_b), (2, half_c))]
+    others = [swap_cores(first)]
+    others += [swap_cores(after(stream, others[0])) for stream in streams[1:]]
+    packed, gram, square = own_square(*streams)
+    sent = update_rows(packed, *others, gram, square, own, other)
     sent = sent.reshape(STRIPES * CHIPS, PANEL + PANEL // 2, LANES)
     received = lax.all_to_all(sent, ALL_CHIPS, 0, 0, tiled=True)
     return join_columns(received.reshape(STRIPES, CHIPS, PANEL + PANEL // 2, LANES))

time: 131 us -> 131 us (level)
    ppermute x3 -> x4, waiting for transfers between devices: 3.34 us -> 2.79 us  [swap_cores(): return lax.ppermute(value, 'c', [(0, 1), (1, 0)])]
  transfers between devices with their start and end apart: 15 -> 16, of which waited for: 12 -> 11; matrix products, arithmetic and copies ran while one was open for 1% -> 1% of each run, Pallas kernels for 3% -> 3%
where the time goes in v15:
time: 131 us
  blocking collectives  79.4 us (61%)
  waiting for transfers between devices  21.5 us (16%)
  starting transfers between devices  13.8 us (11%)
  Pallas kernels  13.6 us (10%)
  local copies, waits for them, and re-layouts  1.66 us (1%)
    all_to_all x1, blocking collectives, shards(): received = lax.all_to_all(sent, ALL_CHIPS, 0, 0, tiled=True)  41.7 us
    all_to_all x1, blocking collectives, shards(): lax.all_to_all(pieces, CHIP_AXES, 0, 0, tiled=True).reshape(HALF, WIDTH)  37.7 us
    ppermute x12, waiting for transfers between devices, exchange(): return lax.ppermute(value, ('x', 'yh', 'c'), pairs)  18.7 us
    ppermute x12, starting transfers between devices, exchange(): return lax.ppermute(value, ('x', 'yh', 'c'), pairs)  13.4 us
    pallas_call x1, Pallas kernels, update_rows(): pl.pallas_call(update_kernel, out_shape=jax.ShapeDtypeStruct((STRIPES, CH...  7.11 us
    ppermute x4, waiting for transfers between devices, swap_cores(): return lax.ppermute(value, 'c', [(0, 1), (1, 0)])  2.79 us
  transfers between devices with their start and end apart: 16, of which 11 were waited for; matrix products, arithmetic and copies ran while one was open for 1% of the time, Pallas kernels for 3%

profile of v15, /device:TPU:0, one launch (start us, length us, event | category | flops | bytes accessed | tf_op | source)
XLA Modules:
  0.0 131.0 jit_solution(229358545097285249)
XLA Ops:
  0.0 0.0 copy-start
  0.0 1.7 %copy-done = bf16[1,96,12288]{2,1,0:T(8,128)(2,1)S(1)} copy-done((bf16[1,96,12288]{2,1,0:T(8,128)(2,1)S(1)}, bf16[1,96,12288]{2,1,0:T(8,128)(2,1)}, u32[]{:S(2)}) %copy-start) | copy-done | bytes 2359320
  1.7 0.6 split_columns.1
  2.3 37.7 %all_to_all.10 = bf16[8,96,1536]{2,1,0:T(8,128)(2,1)S(1)} all-to-all(bf16[8,96,1536]{2,1,0:T(8,128)(2,1)S(1)} %split_columns.1), channel_id=1, replica_groups=mesh['z'=4,'yl'=2,'x'=4,'yh'=2,'c'=2] {'x','yh'}, dimensions={0} | all-to-all | bytes 4718592 | tf_op jit(solution)/shard_map/all_to_all | solution.py:356
  40.0 0.0 collective-permute-start.1
  40.0 1.5 %own_gram.1 = (f32[4,240,128]{2,1,0:T(8,128)S(1)}, bf16[4,240,128]{2,1,0:T(8,128)(2,1)S(1)}, f32[6,128,128]{2,1,0:T(8,128)S(1)}) custom-call(bf16[768,1536]{1,0:T(8,128)(2,1)S(1)} %bitcast.13), custom_call_target="tpu_custom_call" | custom-call | flops 1660944384 | bytes 2359296 | tf_op jit(solution)/shard_map/own_gram/pallas_call | solution.py:129
  41.4 0.6 collective-permute-start
  42.0 2.5 %collective-permute-done.1.other_ref.x_other_ref = bf16[768,1536]{1,0:T(8,128)(2,1)S(1)} collective-permute-done((bf16[768,1536]{1,0:T(8,128)(2,1)S(1)}, bf16[768,1536]{1,0:T(8,128)(2,1)S(1)}, u32[]{:S(2)}, u32[]{:S(2)}) %collective-permute-start.1) | collective-permute-done | bytes 2359328 | tf_op jit(solution)/shard_map/ppermute | solution.py:351
  44.5 1.5 %cross_gram.1 = (f32[4,192,128]{2,1,0:T(8,128)S(1)}, bf16[4,192,128]{2,1,0:T(8,128)(2,1)S(1)}, f32[4,160,128]{2,1,0:T(8,128)S(1)}, bf16[4,160,128]{2,1,0:T(8,128)(2,1)S(1)}) custom-call(f32[6,128,128]{2,1,0:T(8,128)S(1)} %get-tuple-element.25.diagonal_ref, bf16[768,1536]{1,0:T(8,128)(2,1)S(1)} %bitcast.14, ...), custom_call_target="tpu_custom_call" | custom-call | flops 1660944384 | bytes 4718592 | tf_op jit(solution)/shard_map/cross_gram/pallas_call | solution.py:162
  46.0 1.5 %collective-permute-start.3 = (bf16[4,192,128]{2,1,0:T(8,128)(2,1)S(1)}, bf16[4,192,128]{2,1,0:T(8,128)(2,1)S(1)}, u32[]{:S(2)}, u32[]{:S(2)}) collective-permute-start(bf16[4,192,128]{2,1,0:T(8,128)(2,1)S(1)} %get-tuple-element.26), channel_id=1, source_target_pairs={{0,12},{1,3},{2,14},{3,1},{4,8},{5,7},{6,10},{7,5},{8,4},{9,11},{1... | collective-permute-start | bytes 589832 | tf_op jit(solution)/shard_map/ppermute | solution.py:182
  47.5 0.2 collective-permute-done
  47.7 0.1 add_convert_fusion.2
  47.8 1.7 %collective-permute-start.2 = (bf16[2,2,240,128]{3,2,1,0:T(8,128)(2,1)S(1)}, bf16[2,2,240,128]{3,2,1,0:T(8,128)(2,1)S(1)}, u32[]{:S(2)}, u32[]{:S(2)}) collective-permute-start(bf16[2,2,240,128]{3,2,1,0:T(8,128)(2,1)S(1)} %bitcast.19), channel_id=1, source_target_pairs={{0,12},{1,3},{2,14},{3,1},{4,8},{5,7},{6,10},{7,5},{8,4},{9,11},{1... | collective-permute-start | bytes 737288 | tf_op jit(solution)/shard_map/ppermute | solution.py:182
  49.5 1.6 %collective-permute-start.9 = (bf16[4,160,128]{2,1,0:T(8,128)(2,1)S(1)}, bf16[4,160,128]{2,1,0:T(8,128)(2,1)S(1)}, u32[]{:S(2)}, u32[]{:S(2)}) collective-permute-start(bf16[4,160,128]{2,1,0:T(8,128)(2,1)S(1)} %get-tuple-element.27), channel_id=1, source_target_pairs={{0,2},{1,5},{2,0},{3,7},{4,6},{5,1},{6,4},{7,3},{8,10},{9,13},{10,... | collective-permute-start | bytes 491528 | tf_op jit(solution)/shard_map/ppermute | solution.py:182
  51.0 1.9 %collective-permute-done.3 = bf16[4,192,128]{2,1,0:T(8,128)(2,1)S(1)} collective-permute-done((bf16[4,192,128]{2,1,0:T(8,128)(2,1)S(1)}, bf16[4,192,128]{2,1,0:T(8,128)(2,1)S(1)}, u32[]{:S(2)}, u32[]{:S(2)}) %collective-permute-start.3) | collective-permute-done | bytes 196640 | tf_op jit(solution)/shard_map/ppermute | solution.py:182
  53.0 1.6 %collective-permute-start.5 = (bf16[2,2,192,128]{3,2,1,0:T(8,128)(2,1)S(1)}, bf16[2,2,192,128]{3,2,1,0:T(8,128)(2,1)S(1)}, u32[]{:S(2)}, u32[]{:S(2)}) collective-permute-start(bf16[2,2,192,128]{3,2,1,0:T(8,128)(2,1)S(1)} %bitcast.21), channel_id=1, source_target_pairs={{0,2},{1,5},{2,0},{3,7},{4,6},{5,1},{6,4},{7,3},{8,10},{9,13},{10,... | collective-permute-start | bytes 589832 | tf_op jit(solution)/shard_map/ppermute | solution.py:182
  54.7 0.9 collective-permute-done.2
  55.7 0.1 add_convert_fusion.1
  55.7 1.6 %collective-permute-start.4 = (bf16[2,2,240,128]{3,2,1,0:T(8,128)(2,1)S(1)}, bf16[2,2,240,128]{3,2,1,0:T(8,128)(2,1)S(1)}, u32[]{:S(2)}, u32[]{:S(2)}) collective-permute-start(bf16[2,2,240,128]{3,2,1,0:T(8,128)(2,1)S(1)} %add_convert_fusion.1), channel_id=1, source_target_pairs={{0,2},{1,5},{2,0},{3,7},{4,6},{5,1},{6,4},{7,3},{8,10},{9,13},{10,... | collective-permute-start | bytes 737288 | tf_op jit(solution)/shard_map/ppermute | solution.py:182
  57.4 0.0 collective-permute-done.9
  57.4 0.1 collective-permute-start.10
  57.5 2.8 %collective-permute-done.5 = bf16[2,2,192,128]{3,2,1,0:T(8,128)(2,1)S(1)} collective-permute-done((bf16[2,2,192,128]{3,2,1,0:T(8,128)(2,1)S(1)}, bf16[2,2,192,128]{3,2,1,0:T(8,128)(2,1)S(1)}, u32[]{:S(2)}, u32[]{:S(2)}) %collective-permute-start.5) | collective-permute-done | bytes 196640 | tf_op jit(solution)/shard_map/ppermute | solution.py:182
  60.3 0.1 add_convert_fusion.4
  60.4 0.1 collective-permute-start.7
  60.5 3.0 %collective-permute-done.4 = bf16[2,2,240,128]{3,2,1,0:T(8,128)(2,1)S(1)} collective-permute-done((bf16[2,2,240,128]{3,2,1,0:T(8,128)(2,1)S(1)}, bf16[2,2,240,128]{3,2,1,0:T(8,128)(2,1)S(1)}, u32[]{:S(2)}, u32[]{:S(2)}) %collective-permute-start.4) | collective-permute-done | bytes 245792 | tf_op jit(solution)/shard_map/ppermute | solution.py:182
  63.5 0.1 add_convert_fusion
  63.6 0.1 collective-permute-start.6
  63.7 0.0 collective-permute-done.10
  63.8 1.5 %collective-permute-start.11 = (bf16[2,2,160,128]{3,2,1,0:T(8,128)(2,1)S(1)}, bf16[2,2,160,128]{3,2,1,0:T(8,128)(2,1)S(1)}, u32[]{:S(2)}, u32[]{:S(2)}) collective-permute-start(bf16[2,2,160,128]{3,2,1,0:T(8,128)(2,1)S(1)} %add_convert_fusion.7), channel_id=1, source_target_pairs={{0,12},{1,3},{2,14},{3,1},{4,8},{5,7},{6,10},{7,5},{8,4},{9,11},{1... | collective-permute-start | bytes 491528 | tf_op jit(solution)/shard_map/ppermute | solution.py:182
  65.3 0.9 collective-permute-done.7
  66.2 3.7 %collective-permute-done.6 = bf16[4,240,128]{2,1,0:T(8,128)(2,1)S(1)} collective-permute-done((bf16[4,240,128]{2,1,0:T(8,128)(2,1)S(1)}, bf16[4,240,128]{2,1,0:T(8,128)(2,1)S(1)}, u32[]{:S(2)}, u32[]{:S(2)}) %collective-permute-start.6) | collective-permute-done | bytes 245792 | tf_op jit(solution)/shard_map/ppermute | solution.py:182
  69.9 0.1 collective-permute-start.13
  70.0 1.5 %collective-permute-start.8 = (bf16[4,192,128]{2,1,0:T(8,128)(2,1)S(1)}, bf16[4,192,128]{2,1,0:T(8,128)(2,1)S(1)}, u32[]{:S(2)}, u32[]{:S(2)}) collective-permute-start(bf16[4,192,128]{2,1,0:T(8,128)(2,1)S(1)} %bitcast.23), channel_id=1, source_target_pairs={{0,12},{1,3},{2,14},{3,1},{4,8},{5,7},{6,10},{7,5},{8,4},{9,11},{1... | collective-permute-start | bytes 589832 | tf_op jit(solution)/shard_map/ppermute | solution.py:182
  71.5 0.0 collective-permute-done.11
  71.6 1.5 %collective-permute-start.12 = (bf16[4,160,128]{2,1,0:T(8,128)(2,1)S(1)}, bf16[4,160,128]{2,1,0:T(8,128)(2,1)S(1)}, u32[]{:S(2)}, u32[]{:S(2)}) collective-permute-start(bf16[4,160,128]{2,1,0:T(8,128)(2,1)S(1)} %bitcast.27), channel_id=1, source_target_pairs={{0,2},{1,5},{2,0},{3,7},{4,6},{5,1},{6,4},{7,3},{8,10},{9,13},{10,... | collective-permute-start | bytes 491528 | tf_op jit(solution)/shard_map/ppermute | solution.py:182
  73.1 3.9 %collective-permute-done.8 = bf16[4,192,128]{2,1,0:T(8,128)(2,1)S(1)} collective-permute-done((bf16[4,192,128]{2,1,0:T(8,128)(2,1)S(1)}, bf16[4,192,128]{2,1,0:T(8,128)(2,1)S(1)}, u32[]{:S(2)}, u32[]{:S(2)}) %collective-permute-start.8) | collective-permute-done | bytes 196640 | tf_op jit(solution)/shard_map/ppermute | solution.py:182
  77.0 0.0 collective-permute-done.13.a_ref
  77.0 0.1 collective-permute-start.14
  77.1 1.4 %collective-permute-done.12 = bf16[4,160,128]{2,1,0:T(8,128)(2,1)S(1)} collective-permute-done((bf16[4,160,128]{2,1,0:T(8,128)(2,1)S(1)}, bf16[4,160,128]{2,1,0:T(8,128)(2,1)S(1)}, u32[]{:S(2)}, u32[]{:S(2)}) %collective-permute-start.12) | collective-permute-done | bytes 163872 | tf_op jit(solution)/shard_map/ppermute | solution.py:182
  78.5 0.3 collective-permute-start.15
  78.8 1.3 own_square.1
  80.1 0.3 collective-permute-done.15.c_ref
  80.4 0.0 collective-permute-done.14.b_ref
  80.4 7.1 %update_rows.1 = bf16[8,8,144,128]{3,2,1,0:T(8,128)(2,1)S(1)} custom-call(bf16[4736,128]{1,0:T(8,128)(2,1)S(1)} %get-tuple-element.36.own_ref, bf16[8,240,128]{2,1,0:T(8,128)(2,1)S(1)} %collective-permute-done.13.a_ref, bf16[8,192,128]{2,1,0:T(8,128)(2,1)S(1)} %collective-permute-done.14.b_ref, bf16[8,160,128]{2,1,0:T(8,128)(2,1)S(1)} %collective-permute-done.15.c_ref, ...), custom_call_target="tpu_custom_call" | custom-call | flops 6341787648 | bytes 11796480 | tf_op jit(solution)/shard_map/update_rows/pallas_call | solution.py:303
  87.5 41.7 %all_to_all.11 = bf16[64,144,128]{2,1,0:T(8,128)(2,1)S(1)} all-to-all(bf16[64,144,128]{2,1,0:T(8,128)(2,1)S(1)} %bitcast.16), channel_id=1, replica_groups=mesh['z'=4,'yl'=2,'x'=4,'yh'=2,'c'=2] {'z','yl','x','yh'}, dimensions={0} | all-to-all | bytes 4718592 | tf_op jit(solution)/shard_map/all_to_all | solution.py:381
  129.3 1.6 %join_columns.1 = bf16[8,96,1536]{2,1,0:T(8,128)(2,1)} custom-call(bf16[8,8,144,128]{3,2,1,0:T(8,128)(2,1)S(1)} %bitcast.10), custom_call_target="tpu_custom_call" | custom-call | tf_op jit(solution)/shard_map/join_columns/pallas_call | solution.py:339
  (14 shorter events, 0.5 us)
Async XLA Ops:
  0.0 1.7 %copy-start = (bf16[1,96,12288]{2,1,0:T(8,128)(2,1)S(1)}, bf16[1,96,12288]{2,1,0:T(8,128)(2,1)}, u32[]{:S(2)}) copy-start(bf16[1,96,12288]{2,1,0:T(8,128)(2,1)} %param.1) | copy-start | bytes 7077892
  40.0 4.5 %collective-permute-start.1 = (bf16[768,1536]{1,0:T(8,128)(2,1)S(1)}, bf16[768,1536]{1,0:T(8,128)(2,1)S(1)}, u32[]{:S(2)}, u32[]{:S(2)}) collective-permute-start(bf16[768,1536]{1,0:T(8,128)(2,1)S(1)} %bitcast.12), channel_id=1, source_target_pairs={{0,1},{1,0},{2,3},{3,2},{4,5},{5,4},{6,7},{7,6},{8,9},{9,8},{10,11... | collective-permute-start | bytes 7077896 | tf_op jit(solution)/shard_map/ppermute | solution.py:351
  41.4 6.3 %collective-permute-start = (bf16[4,240,128]{2,1,0:T(8,128)(2,1)S(1)}, bf16[4,240,128]{2,1,0:T(8,128)(2,1)S(1)}, u32[]{:S(2)}, u32[]{:S(2)}) collective-permute-start(bf16[4,240,128]{2,1,0:T(8,128)(2,1)S(1)} %get-tuple-element.24), channel_id=1, source_target_pairs={{0,4},{1,13},{2,6},{3,15},{4,0},{5,9},{6,2},{7,11},{8,12},{9,5},{1... | collective-permute-start | bytes 737288 | tf_op jit(solution)/shard_map/ppermute | solution.py:182
  46.0 7.0 %collective-permute-start.3 = (bf16[4,192,128]{2,1,0:T(8,128)(2,1)S(1)}, bf16[4,192,128]{2,1,0:T(8,128)(2,1)S(1)}, u32[]{:S(2)}, u32[]{:S(2)}) collective-permute-start(bf16[4,192,128]{2,1,0:T(8,128)(2,1)S(1)} %get-tuple-element.26), channel_id=1, source_target_pairs={{0,12},{1,3},{2,14},{3,1},{4,8},{5,7},{6,10},{7,5},{8,4},{9,11},{1... | collective-permute-start | bytes 589832 | tf_op jit(solution)/shard_map/ppermute | solution.py:182
  47.8 7.8 %collective-permute-start.2 = (bf16[2,2,240,128]{3,2,1,0:T(8,128)(2,1)S(1)}, bf16[2,2,240,128]{3,2,1,0:T(8,128)(2,1)S(1)}, u32[]{:S(2)}, u32[]{:S(2)}) collective-permute-start(bf16[2,2,240,128]{3,2,1,0:T(8,128)(2,1)S(1)} %bitcast.19), channel_id=1, source_target_pairs={{0,12},{1,3},{2,14},{3,1},{4,8},{5,7},{6,10},{7,5},{8,4},{9,11},{1... | collective-permute-start | bytes 737288 | tf_op jit(solution)/shard_map/ppermute | solution.py:182
  49.5 7.9 %collective-permute-start.9 = (bf16[4,160,128]{2,1,0:T(8,128)(2,1)S(1)}, bf16[4,160,128]{2,1,0:T(8,128)(2,1)S(1)}, u32[]{:S(2)}, u32[]{:S(2)}) collective-permute-start(bf16[4,160,128]{2,1,0:T(8,128)(2,1)S(1)} %get-tuple-element.27), channel_id=1, source_target_pairs={{0,2},{1,5},{2,0},{3,7},{4,6},{5,1},{6,4},{7,3},{8,10},{9,13},{10,... | collective-permute-start | bytes 491528 | tf_op jit(solution)/shard_map/ppermute | solution.py:182
  53.0 7.3 %collective-permute-start.5 = (bf16[2,2,192,128]{3,2,1,0:T(8,128)(2,1)S(1)}, bf16[2,2,192,128]{3,2,1,0:T(8,128)(2,1)S(1)}, u32[]{:S(2)}, u32[]{:S(2)}) collective-permute-start(bf16[2,2,192,128]{3,2,1,0:T(8,128)(2,1)S(1)} %bitcast.21), channel_id=1, source_target_pairs={{0,2},{1,5},{2,0},{3,7},{4,6},{5,1},{6,4},{7,3},{8,10},{9,13},{10,... | collective-permute-start | bytes 589832 | tf_op jit(solution)/shard_map/ppermute | solution.py:182
  55.7 7.8 %collective-permute-start.4 = (bf16[2,2,240,128]{3,2,1,0:T(8,128)(2,1)S(1)}, bf16[2,2,240,128]{3,2,1,0:T(8,128)(2,1)S(1)}, u32[]{:S(2)}, u32[]{:S(2)}) collective-permute-start(bf16[2,2,240,128]{3,2,1,0:T(8,128)(2,1)S(1)} %add_convert_fusion.1), channel_id=1, source_target_pairs={{0,2},{1,5},{2,0},{3,7},{4,6},{5,1},{6,4},{7,3},{8,10},{9,13},{10,... | collective-permute-start | bytes 737288 | tf_op jit(solution)/shard_map/ppermute | solution.py:182
  57.4 6.3 %collective-permute-start.10 = (bf16[2,2,160,128]{3,2,1,0:T(8,128)(2,1)S(1)}, bf16[2,2,160,128]{3,2,1,0:T(8,128)(2,1)S(1)}, u32[]{:S(2)}, u32[]{:S(2)}) collective-permute-start(bf16[2,2,160,128]{3,2,1,0:T(8,128)(2,1)S(1)} %bitcast.25), channel_id=1, source_target_pairs={{0,4},{1,13},{2,6},{3,15},{4,0},{5,9},{6,2},{7,11},{8,12},{9,5},{1... | collective-permute-start | bytes 491528 | tf_op jit(solution)/shard_map/ppermute | solution.py:182
  60.4 5.7 %collective-permute-start.7 = (bf16[2,2,192,128]{3,2,1,0:T(8,128)(2,1)S(1)}, bf16[2,2,192,128]{3,2,1,0:T(8,128)(2,1)S(1)}, u32[]{:S(2)}, u32[]{:S(2)}) collective-permute-start(bf16[2,2,192,128]{3,2,1,0:T(8,128)(2,1)S(1)} %add_convert_fusion.4), channel_id=1, source_target_pairs={{0,4},{1,13},{2,6},{3,15},{4,0},{5,9},{6,2},{7,11},{8,12},{9,5},{1... | collective-permute-start | bytes 589832 | tf_op jit(solution)/shard_map/ppermute | solution.py:182
  63.6 6.3 %collective-permute-start.6 = (bf16[4,240,128]{2,1,0:T(8,128)(2,1)S(1)}, bf16[4,240,128]{2,1,0:T(8,128)(2,1)S(1)}, u32[]{:S(2)}, u32[]{:S(2)}) collective-permute-start(bf16[4,240,128]{2,1,0:T(8,128)(2,1)S(1)} %bitcast.17), channel_id=1, source_target_pairs={{0,4},{1,13},{2,6},{3,15},{4,0},{5,9},{6,2},{7,11},{8,12},{9,5},{1... | collective-permute-start | bytes 737288 | tf_op jit(solution)/shard_map/ppermute | solution.py:182
  63.8 7.7 %collective-permute-start.11 = (bf16[2,2,160,128]{3,2,1,0:T(8,128)(2,1)S(1)}, bf16[2,2,160,128]{3,2,1,0:T(8,128)(2,1)S(1)}, u32[]{:S(2)}, u32[]{:S(2)}) collective-permute-start(bf16[2,2,160,128]{3,2,1,0:T(8,128)(2,1)S(1)} %add_convert_fusion.7), channel_id=1, source_target_pairs={{0,12},{1,3},{2,14},{3,1},{4,8},{5,7},{6,10},{7,5},{8,4},{9,11},{1... | collective-permute-start | bytes 491528 | tf_op jit(solution)/shard_map/ppermute | solution.py:182
  69.9 7.1 %collective-permute-start.13 = (bf16[8,240,128]{2,1,0:T(8,128)(2,1)S(1)}, bf16[8,240,128]{2,1,0:T(8,128)(2,1)S(1)}, u32[]{:S(2)}, u32[]{:S(2)}) collective-permute-start(bf16[8,240,128]{2,1,0:T(8,128)(2,1)S(1)} %pad_maximum_fusion.a_ref), channel_id=1, source_target_pairs={{0,1},{1,0},{2,3},{3,2},{4,5},{5,4},{6,7},{7,6},{8,9},{9,8},{10,11... | collective-permute-start | bytes 1474568 | tf_op jit(solution)/shard_map/ppermute | solution.py:351
  70.0 7.0 %collective-permute-start.8 = (bf16[4,192,128]{2,1,0:T(8,128)(2,1)S(1)}, bf16[4,192,128]{2,1,0:T(8,128)(2,1)S(1)}, u32[]{:S(2)}, u32[]{:S(2)}) collective-permute-start(bf16[4,192,128]{2,1,0:T(8,128)(2,1)S(1)} %bitcast.23), channel_id=1, source_target_pairs={{0,12},{1,3},{2,14},{3,1},{4,8},{5,7},{6,10},{7,5},{8,4},{9,11},{1... | collective-permute-start | bytes 589832 | tf_op jit(solution)/shard_map/ppermute | solution.py:182
  71.6 6.9 %collective-permute-start.12 = (bf16[4,160,128]{2,1,0:T(8,128)(2,1)S(1)}, bf16[4,160,128]{2,1,0:T(8,128)(2,1)S(1)}, u32[]{:S(2)}, u32[]{:S(2)}) collective-permute-start(bf16[4,160,128]{2,1,0:T(8,128)(2,1)S(1)} %bitcast.27), channel_id=1, source_target_pairs={{0,2},{1,5},{2,0},{3,7},{4,6},{5,1},{6,4},{7,3},{8,10},{9,13},{10,... | collective-permute-start | bytes 491528 | tf_op jit(solution)/shard_map/ppermute | solution.py:182
  77.0 3.4 %collective-permute-start.14 = (bf16[8,192,128]{2,1,0:T(8,128)(2,1)S(1)}, bf16[8,192,128]{2,1,0:T(8,128)(2,1)S(1)}, u32[]{:S(2)}, u32[]{:S(2)}) collective-permute-start(bf16[8,192,128]{2,1,0:T(8,128)(2,1)S(1)} %pad_maximum_fusion.1.b_ref), channel_id=1, source_target_pairs={{0,1},{1,0},{2,3},{3,2},{4,5},{5,4},{6,7},{7,6},{8,9},{9,8},{10,11... | collective-permute-start | bytes 1179656 | tf_op jit(solution)/shard_map/ppermute | solution.py:351
  78.5 1.9 %collective-permute-start.15 = (bf16[8,160,128]{2,1,0:T(8,128)(2,1)S(1)}, bf16[8,160,128]{2,1,0:T(8,128)(2,1)S(1)}, u32[]{:S(2)}, u32[]{:S(2)}) collective-permute-start(bf16[8,160,128]{2,1,0:T(8,128)(2,1)S(1)} %pad_maximum_fusion.2.c_ref), channel_id=1, source_target_pairs={{0,1},{1,0},{2,3},{3,2},{4,5},{5,4},{6,7},{7,6},{8,9},{9,8},{10,11... | collective-permute-start | bytes 983048 | tf_op jit(solution)/shard_map/ppermute | solution.py:351

commit v16 on v15

--- a/solution.py
+++ b/solution.py
@@ -370,11 +370,11 @@
     half_c = add_second(half_c, after(next_c, half_a))
     next_c = exchange(half_c, 2, 2)
     half_b = add_third(half_b, next_b)
-    first = jnp.concatenate([half_a, after(exchange(half_a, 0, 0), half_b)])
-    half_c = add_third(half_c, after(next_c, first))
+    first = jnp.concatenate([half_a, after(exchange(half_a, 0, 0), half_b, next_c)])
+    half_c = add_third(half_c, next_c)
     streams = [first] + [jnp.concatenate([half, exchange(half, s, 0)]) for s, half in ((1, half_b), (2, half_c))]
     others = [swap_cores(first)]
-    others += [swap_cores(after(stream, others[0])) for stream in streams[1:]]
+    others += [swap_cores(stream) for stream in streams[1:]]
     packed, gram, square = own_square(*streams)
     sent = update_rows(packed, *others, gram, square, own, other)
     sent = sent.reshape(STRIPES * CHIPS, PANEL + PANEL // 2, LANES)

time: 131 us -> 130 us (level)
  no operation moved by 1% of the time
where the time goes in v16:
time: 130 us
  blocking collectives  79.1 us (61%)
  waiting for transfers between devices  20.2 us (16%)
  starting transfers between devices  14 us (11%)
  Pallas kernels  13.6 us (10%)
  local copies, waits for them, and re-layouts  1.66 us (1%)
    all_to_all x1, blocking collectives, shards(): received = lax.all_to_all(sent, ALL_CHIPS, 0, 0, tiled=True)  41.4 us
    all_to_all x1, blocking collectives, shards(): lax.all_to_all(pieces, CHIP_AXES, 0, 0, tiled=True).reshape(HALF, WIDTH)  37.7 us
    ppermute x12, waiting for transfers between devices, exchange(): return lax.ppermute(value, ('x', 'yh', 'c'), pairs)  17.4 us
    ppermute x12, starting transfers between devices, exchange(): return lax.ppermute(value, ('x', 'yh', 'c'), pairs)  13.5 us
    pallas_call x1, Pallas kernels, update_rows(): pl.pallas_call(update_kernel, out_shape=jax.ShapeDtypeStruct((STRIPES, CH...  7.11 us
    ppermute x4, waiting for transfers between devices, swap_cores(): return lax.ppermute(value, 'c', [(0, 1), (1, 0)])  2.79 us
  transfers between devices with their start and end apart: 16, of which 11 were waited for; matrix products, arithmetic and copies ran while one was open for 1% of the time, Pallas kernels for 3%

profile of v16, /device:TPU:0, one launch (start us, length us, event | category | flops | bytes accessed | tf_op | source)
XLA Modules:
  0.0 129.6 jit_solution(3251867908138024816)
XLA Ops:
  0.0 0.0 copy-start
  0.0 1.7 %copy-done = bf16[1,96,12288]{2,1,0:T(8,128)(2,1)S(1)} copy-done((bf16[1,96,12288]{2,1,0:T(8,128)(2,1)S(1)}, bf16[1,96,12288]{2,1,0:T(8,128)(2,1)}, u32[]{:S(2)}) %copy-start) | copy-done | bytes 2359320
  1.7 0.6 split_columns.1
  2.3 37.7 %all_to_all.10 = bf16[8,96,1536]{2,1,0:T(8,128)(2,1)S(1)} all-to-all(bf16[8,96,1536]{2,1,0:T(8,128)(2,1)S(1)} %split_columns.1), channel_id=1, replica_groups=mesh['z'=4,'yl'=2,'x'=4,'yh'=2,'c'=2] {'x','yh'}, dimensions={0} | all-to-all | bytes 4718592 | tf_op jit(solution)/shard_map/all_to_all | solution.py:356
  40.0 0.0 collective-permute-start.1
  40.0 1.5 %own_gram.1 = (f32[4,240,128]{2,1,0:T(8,128)S(1)}, bf16[4,240,128]{2,1,0:T(8,128)(2,1)S(1)}, f32[6,128,128]{2,1,0:T(8,128)S(1)}) custom-call(bf16[768,1536]{1,0:T(8,128)(2,1)S(1)} %bitcast.13), custom_call_target="tpu_custom_call" | custom-call | flops 1660944384 | bytes 2359296 | tf_op jit(solution)/shard_map/own_gram/pallas_call | solution.py:129
  41.4 0.6 collective-permute-start
  42.0 2.5 %collective-permute-done.1.other_ref.x_other_ref = bf16[768,1536]{1,0:T(8,128)(2,1)S(1)} collective-permute-done((bf16[768,1536]{1,0:T(8,128)(2,1)S(1)}, bf16[768,1536]{1,0:T(8,128)(2,1)S(1)}, u32[]{:S(2)}, u32[]{:S(2)}) %collective-permute-start.1) | collective-permute-done | bytes 2359328 | tf_op jit(solution)/shard_map/ppermute | solution.py:351
  44.5 1.5 %cross_gram.1 = (f32[4,192,128]{2,1,0:T(8,128)S(1)}, bf16[4,192,128]{2,1,0:T(8,128)(2,1)S(1)}, f32[4,160,128]{2,1,0:T(8,128)S(1)}, bf16[4,160,128]{2,1,0:T(8,128)(2,1)S(1)}) custom-call(f32[6,128,128]{2,1,0:T(8,128)S(1)} %get-tuple-element.22.diagonal_ref, bf16[768,1536]{1,0:T(8,128)(2,1)S(1)} %bitcast.14, ...), custom_call_target="tpu_custom_call" | custom-call | flops 1660944384 | bytes 4718592 | tf_op jit(solution)/shard_map/cross_gram/pallas_call | solution.py:162
  46.0 1.5 %collective-permute-start.3 = (bf16[4,192,128]{2,1,0:T(8,128)(2,1)S(1)}, bf16[4,192,128]{2,1,0:T(8,128)(2,1)S(1)}, u32[]{:S(2)}, u32[]{:S(2)}) collective-permute-start(bf16[4,192,128]{2,1,0:T(8,128)(2,1)S(1)} %get-tuple-element.23), channel_id=1, source_target_pairs={{0,12},{1,3},{2,14},{3,1},{4,8},{5,7},{6,10},{7,5},{8,4},{9,11},{1... | collective-permute-start | bytes 589832 | tf_op jit(solution)/shard_map/ppermute | solution.py:182
  47.5 0.2 collective-permute-done
  47.7 0.1 add_convert_fusion.2
  47.8 1.7 %collective-permute-start.2 = (bf16[2,2,240,128]{3,2,1,0:T(8,128)(2,1)S(1)}, bf16[2,2,240,128]{3,2,1,0:T(8,128)(2,1)S(1)}, u32[]{:S(2)}, u32[]{:S(2)}) collective-permute-start(bf16[2,2,240,128]{3,2,1,0:T(8,128)(2,1)S(1)} %bitcast.19), channel_id=1, source_target_pairs={{0,12},{1,3},{2,14},{3,1},{4,8},{5,7},{6,10},{7,5},{8,4},{9,11},{1... | collective-permute-start | bytes 737288 | tf_op jit(solution)/shard_map/ppermute | solution.py:182
  49.5 1.6 %collective-permute-start.8 = (bf16[4,160,128]{2,1,0:T(8,128)(2,1)S(1)}, bf16[4,160,128]{2,1,0:T(8,128)(2,1)S(1)}, u32[]{:S(2)}, u32[]{:S(2)}) collective-permute-start(bf16[4,160,128]{2,1,0:T(8,128)(2,1)S(1)} %get-tuple-element.24), channel_id=1, source_target_pairs={{0,2},{1,5},{2,0},{3,7},{4,6},{5,1},{6,4},{7,3},{8,10},{9,13},{10,... | collective-permute-start | bytes 491528 | tf_op jit(solution)/shard_map/ppermute | solution.py:182
  51.0 1.9 %collective-permute-done.3 = bf16[4,192,128]{2,1,0:T(8,128)(2,1)S(1)} collective-permute-done((bf16[4,192,128]{2,1,0:T(8,128)(2,1)S(1)}, bf16[4,192,128]{2,1,0:T(8,128)(2,1)S(1)}, u32[]{:S(2)}, u32[]{:S(2)}) %collective-permute-start.3) | collective-permute-done | bytes 196640 | tf_op jit(solution)/shard_map/ppermute | solution.py:182
  53.0 1.6 %collective-permute-start.5 = (bf16[2,2,192,128]{3,2,1,0:T(8,128)(2,1)S(1)}, bf16[2,2,192,128]{3,2,1,0:T(8,128)(2,1)S(1)}, u32[]{:S(2)}, u32[]{:S(2)}) collective-permute-start(bf16[2,2,192,128]{3,2,1,0:T(8,128)(2,1)S(1)} %bitcast.21), channel_id=1, source_target_pairs={{0,2},{1,5},{2,0},{3,7},{4,6},{5,1},{6,4},{7,3},{8,10},{9,13},{10,... | collective-permute-start | bytes 589832 | tf_op jit(solution)/shard_map/ppermute | solution.py:182
  54.7 0.9 collective-permute-done.2
  55.7 0.1 add_convert_fusion.1
  55.7 1.6 %collective-permute-start.4 = (bf16[2,2,240,128]{3,2,1,0:T(8,128)(2,1)S(1)}, bf16[2,2,240,128]{3,2,1,0:T(8,128)(2,1)S(1)}, u32[]{:S(2)}, u32[]{:S(2)}) collective-permute-start(bf16[2,2,240,128]{3,2,1,0:T(8,128)(2,1)S(1)} %add_convert_fusion.1), channel_id=1, source_target_pairs={{0,2},{1,5},{2,0},{3,7},{4,6},{5,1},{6,4},{7,3},{8,10},{9,13},{10,... | collective-permute-start | bytes 737288 | tf_op jit(solution)/shard_map/ppermute | solution.py:182
  57.4 0.0 collective-permute-done.8
  57.4 0.1 collective-permute-start.9
  57.5 2.8 %collective-permute-done.5 = bf16[2,2,192,128]{3,2,1,0:T(8,128)(2,1)S(1)} collective-permute-done((bf16[2,2,192,128]{3,2,1,0:T(8,128)(2,1)S(1)}, bf16[2,2,192,128]{3,2,1,0:T(8,128)(2,1)S(1)}, u32[]{:S(2)}, u32[]{:S(2)}) %collective-permute-start.5) | collective-permute-done | bytes 196640 | tf_op jit(solution)/shard_map/ppermute | solution.py:182
  60.3 0.1 add_convert_fusion.4
  60.4 0.1 collective-permute-start.7
  60.5 3.0 %collective-permute-done.4 = bf16[2,2,240,128]{3,2,1,0:T(8,128)(2,1)S(1)} collective-permute-done((bf16[2,2,240,128]{3,2,1,0:T(8,128)(2,1)S(1)}, bf16[2,2,240,128]{3,2,1,0:T(8,128)(2,1)S(1)}, u32[]{:S(2)}, u32[]{:S(2)}) %collective-permute-start.4) | collective-permute-done | bytes 245792 | tf_op jit(solution)/shard_map/ppermute | solution.py:182
  63.5 0.1 add_convert_fusion
  63.6 0.1 collective-permute-start.6
  63.7 0.0 collective-permute-done.9
  63.8 1.5 %collective-permute-start.10 = (bf16[2,2,160,128]{3,2,1,0:T(8,128)(2,1)S(1)}, bf16[2,2,160,128]{3,2,1,0:T(8,128)(2,1)S(1)}, u32[]{:S(2)}, u32[]{:S(2)}) collective-permute-start(bf16[2,2,160,128]{3,2,1,0:T(8,128)(2,1)S(1)} %add_convert_fusion.7), channel_id=1, source_target_pairs={{0,12},{1,3},{2,14},{3,1},{4,8},{5,7},{6,10},{7,5},{8,4},{9,11},{1... | collective-permute-start | bytes 491528 | tf_op jit(solution)/shard_map/ppermute | solution.py:182
  65.3 0.9 collective-permute-done.7
  66.2 1.5 %collective-permute-start.11 = (bf16[4,192,128]{2,1,0:T(8,128)(2,1)S(1)}, bf16[4,192,128]{2,1,0:T(8,128)(2,1)S(1)}, u32[]{:S(2)}, u32[]{:S(2)}) collective-permute-start(bf16[4,192,128]{2,1,0:T(8,128)(2,1)S(1)} %bitcast.23), channel_id=1, source_target_pairs={{0,12},{1,3},{2,14},{3,1},{4,8},{5,7},{6,10},{7,5},{8,4},{9,11},{1... | collective-permute-start | bytes 589832 | tf_op jit(solution)/shard_map/ppermute | solution.py:182
  67.7 2.7 %collective-permute-done.10 = bf16[2,2,160,128]{3,2,1,0:T(8,128)(2,1)S(1)} collective-permute-done((bf16[2,2,160,128]{3,2,1,0:T(8,128)(2,1)S(1)}, bf16[2,2,160,128]{3,2,1,0:T(8,128)(2,1)S(1)}, u32[]{:S(2)}, u32[]{:S(2)}) %collective-permute-start.10) | collective-permute-done | bytes 163872 | tf_op jit(solution)/shard_map/ppermute | solution.py:182
  70.5 1.6 %collective-permute-start.12 = (bf16[4,160,128]{2,1,0:T(8,128)(2,1)S(1)}, bf16[4,160,128]{2,1,0:T(8,128)(2,1)S(1)}, u32[]{:S(2)}, u32[]{:S(2)}) collective-permute-start(bf16[4,160,128]{2,1,0:T(8,128)(2,1)S(1)} %bitcast.27), channel_id=1, source_target_pairs={{0,2},{1,5},{2,0},{3,7},{4,6},{5,1},{6,4},{7,3},{8,10},{9,13},{10,... | collective-permute-start | bytes 491528 | tf_op jit(solution)/shard_map/ppermute | solution.py:182
  72.1 0.0 collective-permute-done.6
  72.1 0.1 collective-permute-start.13
  72.2 0.9 collective-permute-done.11
  73.2 0.1 collective-permute-start.14
  73.3 4.0 %collective-permute-done.12 = bf16[4,160,128]{2,1,0:T(8,128)(2,1)S(1)} collective-permute-done((bf16[4,160,128]{2,1,0:T(8,128)(2,1)S(1)}, bf16[4,160,128]{2,1,0:T(8,128)(2,1)S(1)}, u32[]{:S(2)}, u32[]{:S(2)}) %collective-permute-start.12) | collective-permute-done | bytes 163872 | tf_op jit(solution)/shard_map/ppermute | solution.py:182
  77.4 0.3 collective-permute-start.15
  77.7 1.3 %own_square.1 = (bf16[4736,128]{1,0:T(8,128)(2,1)S(1)}, bf16[768,768]{1,0:T(8,128)(2,1)S(1)}, f32[768,768]{1,0:T(8,128)S(1)}) custom-call(bf16[8,240,128]{2,1,0:T(8,128)(2,1)S(1)} %pad_maximum_fusion.a_ref, bf16[8,192,128]{2,1,0:T(8,128)(2,1)S(1)} %pad_maximum_fusion.1.b_ref, bf16[8,160,128]{2,1,0:T(8,128)(2,1)S(1)} %pad_maximum_fusion.2.c_ref), custom_call_target="tpu_custom_call" | custom-call | flops 905969664 | bytes 4718592 | tf_op jit(solution)/shard_map/own_square/pallas_call | solution.py:232
  79.0 0.3 collective-permute-done.15.c_ref
  79.3 0.0 collective-permute-done.14.b_ref
  79.3 0.0 collective-permute-done.13.a_ref
  79.3 7.1 %update_rows.1 = bf16[8,8,144,128]{3,2,1,0:T(8,128)(2,1)S(1)} custom-call(bf16[4736,128]{1,0:T(8,128)(2,1)S(1)} %get-tuple-element.32.own_ref, bf16[8,240,128]{2,1,0:T(8,128)(2,1)S(1)} %collective-permute-done.13.a_ref, bf16[8,192,128]{2,1,0:T(8,128)(2,1)S(1)} %collective-permute-done.14.b_ref, bf16[8,160,128]{2,1,0:T(8,128)(2,1)S(1)} %collective-permute-done.15.c_ref, ...), custom_call_target="tpu_custom_call" | custom-call | flops 6341787648 | bytes 11796480 | tf_op jit(solution)/shard_map/update_rows/pallas_call | solution.py:303
  86.4 41.4 %all_to_all.11 = bf16[64,144,128]{2,1,0:T(8,128)(2,1)S(1)} all-to-all(bf16[64,144,128]{2,1,0:T(8,128)(2,1)S(1)} %bitcast.16), channel_id=1, replica_groups=mesh['z'=4,'yl'=2,'x'=4,'yh'=2,'c'=2] {'z','yl','x','yh'}, dimensions={0} | all-to-all | bytes 4718592 | tf_op jit(solution)/shard_map/all_to_all | solution.py:381
  127.8 1.6 %join_columns.1 = bf16[8,96,1536]{2,1,0:T(8,128)(2,1)} custom-call(bf16[8,8,144,128]{3,2,1,0:T(8,128)(2,1)S(1)} %bitcast.10), custom_call_target="tpu_custom_call" | custom-call | tf_op jit(solution)/shard_map/join_columns/pallas_call | solution.py:339
  (14 shorter events, 0.5 us)
Async XLA Ops:
  0.0 1.7 %copy-start = (bf16[1,96,12288]{2,1,0:T(8,128)(2,1)S(1)}, bf16[1,96,12288]{2,1,0:T(8,128)(2,1)}, u32[]{:S(2)}) copy-start(bf16[1,96,12288]{2,1,0:T(8,128)(2,1)} %param.1) | copy-start | bytes 7077892
  40.0 4.5 %collective-permute-start.1 = (bf16[768,1536]{1,0:T(8,128)(2,1)S(1)}, bf16[768,1536]{1,0:T(8,128)(2,1)S(1)}, u32[]{:S(2)}, u32[]{:S(2)}) collective-permute-start(bf16[768,1536]{1,0:T(8,128)(2,1)S(1)} %bitcast.12), channel_id=1, source_target_pairs={{0,1},{1,0},{2,3},{3,2},{4,5},{5,4},{6,7},{7,6},{8,9},{9,8},{10,11... | collective-permute-start | bytes 7077896 | tf_op jit(solution)/shard_map/ppermute | solution.py:351
  41.4 6.3 %collective-permute-start = (bf16[4,240,128]{2,1,0:T(8,128)(2,1)S(1)}, bf16[4,240,128]{2,1,0:T(8,128)(2,1)S(1)}, u32[]{:S(2)}, u32[]{:S(2)}) collective-permute-start(bf16[4,240,128]{2,1,0:T(8,128)(2,1)S(1)} %get-tuple-element.21), channel_id=1, source_target_pairs={{0,4},{1,13},{2,6},{3,15},{4,0},{5,9},{6,2},{7,11},{8,12},{9,5},{1... | collective-permute-start | bytes 737288 | tf_op jit(solution)/shard_map/ppermute | solution.py:182
  46.0 7.0 %collective-permute-start.3 = (bf16[4,192,128]{2,1,0:T(8,128)(2,1)S(1)}, bf16[4,192,128]{2,1,0:T(8,128)(2,1)S(1)}, u32[]{:S(2)}, u32[]{:S(2)}) collective-permute-start(bf16[4,192,128]{2,1,0:T(8,128)(2,1)S(1)} %get-tuple-element.23), channel_id=1, source_target_pairs={{0,12},{1,3},{2,14},{3,1},{4,8},{5,7},{6,10},{7,5},{8,4},{9,11},{1... | collective-permute-start | bytes 589832 | tf_op jit(solution)/shard_map/ppermute | solution.py:182
  47.8 7.8 %collective-permute-start.2 = (bf16[2,2,240,128]{3,2,1,0:T(8,128)(2,1)S(1)}, bf16[2,2,240,128]{3,2,1,0:T(8,128)(2,1)S(1)}, u32[]{:S(2)}, u32[]{:S(2)}) collective-permute-start(bf16[2,2,240,128]{3,2,1,0:T(8,128)(2,1)S(1)} %bitcast.19), channel_id=1, source_target_pairs={{0,12},{1,3},{2,14},{3,1},{4,8},{5,7},{6,10},{7,5},{8,4},{9,11},{1... | collective-permute-start | bytes 737288 | tf_op jit(solution)/shard_map/ppermute | solution.py:182
  49.5 7.9 %collective-permute-start.8 = (bf16[4,160,128]{2,1,0:T(8,128)(2,1)S(1)}, bf16[4,160,128]{2,1,0:T(8,128)(2,1)S(1)}, u32[]{:S(2)}, u32[]{:S(2)}) collective-permute-start(bf16[4,160,128]{2,1,0:T(8,128)(2,1)S(1)} %get-tuple-element.24), channel_id=1, source_target_pairs={{0,2},{1,5},{2,0},{3,7},{4,6},{5,1},{6,4},{7,3},{8,10},{9,13},{10,... | collective-permute-start | bytes 491528 | tf_op jit(solution)/shard_map/ppermute | solution.py:182
  53.0 7.3 %collective-permute-start.5 = (bf16[2,2,192,128]{3,2,1,0:T(8,128)(2,1)S(1)}, bf16[2,2,192,128]{3,2,1,0:T(8,128)(2,1)S(1)}, u32[]{:S(2)}, u32[]{:S(2)}) collective-permute-start(bf16[2,2,192,128]{3,2,1,0:T(8,128)(2,1)S(1)} %bitcast.21), channel_id=1, source_target_pairs={{0,2},{1,5},{2,0},{3,7},{4,6},{5,1},{6,4},{7,3},{8,10},{9,13},{10,... | collective-permute-start | bytes 589832 | tf_op jit(solution)/shard_map/ppermute | solution.py:182
  55.7 7.8 %collective-permute-start.4 = (bf16[2,2,240,128]{3,2,1,0:T(8,128)(2,1)S(1)}, bf16[2,2,240,128]{3,2,1,0:T(8,128)(2,1)S(1)}, u32[]{:S(2)}, u32[]{:S(2)}) collective-permute-start(bf16[2,2,240,128]{3,2,1,0:T(8,128)(2,1)S(1)} %add_convert_fusion.1), channel_id=1, source_target_pairs={{0,2},{1,5},{2,0},{3,7},{4,6},{5,1},{6,4},{7,3},{8,10},{9,13},{10,... | collective-permute-start | bytes 737288 | tf_op jit(solution)/shard_map/ppermute | solution.py:182
  57.4 6.3 %collective-permute-start.9 = (bf16[2,2,160,128]{3,2,1,0:T(8,128)(2,1)S(1)}, bf16[2,2,160,128]{3,2,1,0:T(8,128)(2,1)S(1)}, u32[]{:S(2)}, u32[]{:S(2)}) collective-permute-start(bf16[2,2,160,128]{3,2,1,0:T(8,128)(2,1)S(1)} %bitcast.25), channel_id=1, source_target_pairs={{0,4},{1,13},{2,6},{3,15},{4,0},{5,9},{6,2},{7,11},{8,12},{9,5},{1... | collective-permute-start | bytes 491528 | tf_op jit(solution)/shard_map/ppermute | solution.py:182
  60.4 5.7 %collective-permute-start.7 = (bf16[2,2,192,128]{3,2,1,0:T(8,128)(2,1)S(1)}, bf16[2,2,192,128]{3,2,1,0:T(8,128)(2,1)S(1)}, u32[]{:S(2)}, u32[]{:S(2)}) collective-permute-start(bf16[2,2,192,128]{3,2,1,0:T(8,128)(2,1)S(1)} %add_convert_fusion.4), channel_id=1, source_target_pairs={{0,4},{1,13},{2,6},{3,15},{4,0},{5,9},{6,2},{7,11},{8,12},{9,5},{1... | collective-permute-start | bytes 589832 | tf_op jit(solution)/shard_map/ppermute | solution.py:182
  63.6 8.5 %collective-permute-start.6 = (bf16[4,240,128]{2,1,0:T(8,128)(2,1)S(1)}, bf16[4,240,128]{2,1,0:T(8,128)(2,1)S(1)}, u32[]{:S(2)}, u32[]{:S(2)}) collective-permute-start(bf16[4,240,128]{2,1,0:T(8,128)(2,1)S(1)} %bitcast.17), channel_id=1, source_target_pairs={{0,4},{1,13},{2,6},{3,15},{4,0},{5,9},{6,2},{7,11},{8,12},{9,5},{1... | collective-permute-start | bytes 737288 | tf_op jit(solution)/shard_map/ppermute | solution.py:182
  63.8 6.6 %collective-permute-start.10 = (bf16[2,2,160,128]{3,2,1,0:T(8,128)(2,1)S(1)}, bf16[2,2,160,128]{3,2,1,0:T(8,128)(2,1)S(1)}, u32[]{:S(2)}, u32[]{:S(2)}) collective-permute-start(bf16[2,2,160,128]{3,2,1,0:T(8,128)(2,1)S(1)} %add_convert_fusion.7), channel_id=1, source_target_pairs={{0,12},{1,3},{2,14},{3,1},{4,8},{5,7},{6,10},{7,5},{8,4},{9,11},{1... | collective-permute-start | bytes 491528 | tf_op jit(solution)/shard_map/ppermute | solution.py:182
  66.2 7.0 %collective-permute-start.11 = (bf16[4,192,128]{2,1,0:T(8,128)(2,1)S(1)}, bf16[4,192,128]{2,1,0:T(8,128)(2,1)S(1)}, u32[]{:S(2)}, u32[]{:S(2)}) collective-permute-start(bf16[4,192,128]{2,1,0:T(8,128)(2,1)S(1)} %bitcast.23), channel_id=1, source_target_pairs={{0,12},{1,3},{2,14},{3,1},{4,8},{5,7},{6,10},{7,5},{8,4},{9,11},{1... | collective-permute-start | bytes 589832 | tf_op jit(solution)/shard_map/ppermute | solution.py:182
  70.5 6.9 %collective-permute-start.12 = (bf16[4,160,128]{2,1,0:T(8,128)(2,1)S(1)}, bf16[4,160,128]{2,1,0:T(8,128)(2,1)S(1)}, u32[]{:S(2)}, u32[]{:S(2)}) collective-permute-start(bf16[4,160,128]{2,1,0:T(8,128)(2,1)S(1)} %bitcast.27), channel_id=1, source_target_pairs={{0,2},{1,5},{2,0},{3,7},{4,6},{5,1},{6,4},{7,3},{8,10},{9,13},{10,... | collective-permute-start | bytes 491528 | tf_op jit(solution)/shard_map/ppermute | solution.py:182
  72.1 7.1 %collective-permute-start.13 = (bf16[8,240,128]{2,1,0:T(8,128)(2,1)S(1)}, bf16[8,240,128]{2,1,0:T(8,128)(2,1)S(1)}, u32[]{:S(2)}, u32[]{:S(2)}) collective-permute-start(bf16[8,240,128]{2,1,0:T(8,128)(2,1)S(1)} %pad_maximum_fusion.a_ref), channel_id=1, source_target_pairs={{0,1},{1,0},{2,3},{3,2},{4,5},{5,4},{6,7},{7,6},{8,9},{9,8},{10,11... | collective-permute-start | bytes 1474568 | tf_op jit(solution)/shard_map/ppermute | solution.py:351
  73.2 6.1 %collective-permute-start.14 = (bf16[8,192,128]{2,1,0:T(8,128)(2,1)S(1)}, bf16[8,192,128]{2,1,0:T(8,128)(2,1)S(1)}, u32[]{:S(2)}, u32[]{:S(2)}) collective-permute-start(bf16[8,192,128]{2,1,0:T(8,128)(2,1)S(1)} %pad_maximum_fusion.1.b_ref), channel_id=1, source_target_pairs={{0,1},{1,0},{2,3},{3,2},{4,5},{5,4},{6,7},{7,6},{8,9},{9,8},{10,11... | collective-permute-start | bytes 1179656 | tf_op jit(solution)/shard_map/ppermute | solution.py:351
  77.4 1.9 %collective-permute-start.15 = (bf16[8,160,128]{2,1,0:T(8,128)(2,1)S(1)}, bf16[8,160,128]{2,1,0:T(8,128)(2,1)S(1)}, u32[]{:S(2)}, u32[]{:S(2)}) collective-permute-start(bf16[8,160,128]{2,1,0:T(8,128)(2,1)S(1)} %pad_maximum_fusion.2.c_ref), channel_id=1, source_target_pairs={{0,1},{1,0},{2,3},{3,2},{4,5},{5,4},{6,7},{7,6},{8,9},{9,8},{10,11... | collective-permute-start | bytes 983048 | tf_op jit(solution)/shard_map/ppermute | solution.py:351

commit v17 on v16

--- a/solution.py
+++ b/solution.py
@@ -24,7 +24,7 @@
 BELOW = LANES * BLOCKS * (BLOCKS - 1) // 2
 EDGE = 2 * BELOW + HALF
 PACKED = -(-(EDGE + BLOCKS) // (16 * CHIPS)) * 16 * CHIPS
-PIECES = (240, 192, 160)
+PIECES = (240, 208, 144)
 BASES = (0, CHIPS * PIECES[0], CHIPS * (PIECES[0] + PIECES[1]))
 MIB = 1 << 20
 

time: 130 us -> 132 us (1.015)
  transfers between devices with their start and end apart: 16 -> 16, of which waited for: 11 -> 10; matrix products, arithmetic and copies ran while one was open for 1% -> 1% of each run, Pallas kernels for 3% -> 3%
where the time goes in v17:
time: 132 us; the launch traced here: 131 us
  blocking collectives  79.7 us (60%)
  waiting for transfers between devices  20.7 us (16%)
  starting transfers between devices  14.8 us (11%)
  Pallas kernels  13.6 us (10%)
  local copies, waits for them, and re-layouts  1.66 us (1%)
    all_to_all x1, blocking collectives, shards(): received = lax.all_to_all(sent, ALL_CHIPS, 0, 0, tiled=True)  42 us
    all_to_all x1, blocking collectives, shards(): lax.all_to_all(pieces, CHIP_AXES, 0, 0, tiled=True).reshape(HALF, WIDTH)  37.7 us
    ppermute x12, waiting for transfers between devices, exchange(): return lax.ppermute(value, ('x', 'yh', 'c'), pairs)  17.9 us
    ppermute x12, starting transfers between devices, exchange(): return lax.ppermute(value, ('x', 'yh', 'c'), pairs)  14.4 us
    pallas_call x1, Pallas kernels, update_rows(): pl.pallas_call(update_kernel, out_shape=jax.ShapeDtypeStruct((STRIPES, CH...  7.12 us
    ppermute x4, waiting for transfers between devices, swap_cores(): return lax.ppermute(value, 'c', [(0, 1), (1, 0)])  2.74 us
  transfers between devices with their start and end apart: 16, of which 10 were waited for; matrix products, arithmetic and copies ran while one was open for 1% of the time, Pallas kernels for 3%

profile of v17, /device:TPU:0, one launch (start us, length us, event | category | flops | bytes accessed | tf_op | source)
XLA Modules:
  0.0 131.5 jit_solution(10570213470646961532)
XLA Ops:
  0.0 0.0 copy-start
  0.0 1.7 %copy-done = bf16[1,96,12288]{2,1,0:T(8,128)(2,1)S(1)} copy-done((bf16[1,96,12288]{2,1,0:T(8,128)(2,1)S(1)}, bf16[1,96,12288]{2,1,0:T(8,128)(2,1)}, u32[]{:S(2)}) %copy-start) | copy-done | bytes 2359320
  1.7 0.6 split_columns.1
  2.3 37.7 %all_to_all.10 = bf16[8,96,1536]{2,1,0:T(8,128)(2,1)S(1)} all-to-all(bf16[8,96,1536]{2,1,0:T(8,128)(2,1)S(1)} %split_columns.1), channel_id=1, replica_groups=mesh['z'=4,'yl'=2,'x'=4,'yh'=2,'c'=2] {'x','yh'}, dimensions={0} | all-to-all | bytes 4718592 | tf_op jit(solution)/shard_map/all_to_all | solution.py:356
  40.0 0.0 collective-permute-start.1
  40.0 1.5 %own_gram.1 = (f32[4,240,128]{2,1,0:T(8,128)S(1)}, bf16[4,240,128]{2,1,0:T(8,128)(2,1)S(1)}, f32[6,128,128]{2,1,0:T(8,128)S(1)}) custom-call(bf16[768,1536]{1,0:T(8,128)(2,1)S(1)} %bitcast.13), custom_call_target="tpu_custom_call" | custom-call | flops 1660944384 | bytes 2359296 | tf_op jit(solution)/shard_map/own_gram/pallas_call | solution.py:129
  41.4 0.6 collective-permute-start
  42.0 2.5 %collective-permute-done.1.other_ref.x_other_ref = bf16[768,1536]{1,0:T(8,128)(2,1)S(1)} collective-permute-done((bf16[768,1536]{1,0:T(8,128)(2,1)S(1)}, bf16[768,1536]{1,0:T(8,128)(2,1)S(1)}, u32[]{:S(2)}, u32[]{:S(2)}) %collective-permute-start.1) | collective-permute-done | bytes 2359328 | tf_op jit(solution)/shard_map/ppermute | solution.py:351
  44.5 1.5 %cross_gram.1 = (f32[4,208,128]{2,1,0:T(8,128)S(1)}, bf16[4,208,128]{2,1,0:T(8,128)(2,1)S(1)}, f32[4,144,128]{2,1,0:T(8,128)S(1)}, bf16[4,144,128]{2,1,0:T(8,128)(2,1)S(1)}) custom-call(f32[6,128,128]{2,1,0:T(8,128)S(1)} %get-tuple-element.22.diagonal_ref, bf16[768,1536]{1,0:T(8,128)(2,1)S(1)} %bitcast.14, ...), custom_call_target="tpu_custom_call" | custom-call | flops 1660944384 | bytes 4718592 | tf_op jit(solution)/shard_map/cross_gram/pallas_call | solution.py:162
  46.0 1.6 %collective-permute-start.8 = (bf16[4,144,128]{2,1,0:T(8,128)(2,1)S(1)}, bf16[4,144,128]{2,1,0:T(8,128)(2,1)S(1)}, u32[]{:S(2)}, u32[]{:S(2)}) collective-permute-start(bf16[4,144,128]{2,1,0:T(8,128)(2,1)S(1)} %get-tuple-element.24), channel_id=1, source_target_pairs={{0,2},{1,5},{2,0},{3,7},{4,6},{5,1},{6,4},{7,3},{8,10},{9,13},{10,... | collective-permute-start | bytes 442376 | tf_op jit(solution)/shard_map/ppermute | solution.py:182
  47.7 1.1 collective-permute-start.3
  48.8 0.0 collective-permute-done
  48.8 0.1 add_convert_fusion.2
  48.8 2.2 %collective-permute-start.2 = (bf16[2,2,240,128]{3,2,1,0:T(8,128)(2,1)S(1)}, bf16[2,2,240,128]{3,2,1,0:T(8,128)(2,1)S(1)}, u32[]{:S(2)}, u32[]{:S(2)}) collective-permute-start(bf16[2,2,240,128]{3,2,1,0:T(8,128)(2,1)S(1)} %bitcast.19), channel_id=1, source_target_pairs={{0,12},{1,3},{2,14},{3,1},{4,8},{5,7},{6,10},{7,5},{8,4},{9,11},{1... | collective-permute-start | bytes 737288 | tf_op jit(solution)/shard_map/ppermute | solution.py:182
  51.0 3.7 %collective-permute-done.3 = bf16[4,208,128]{2,1,0:T(8,128)(2,1)S(1)} collective-permute-done((bf16[4,208,128]{2,1,0:T(8,128)(2,1)S(1)}, bf16[4,208,128]{2,1,0:T(8,128)(2,1)S(1)}, u32[]{:S(2)}, u32[]{:S(2)}) %collective-permute-start.3) | collective-permute-done | bytes 213024 | tf_op jit(solution)/shard_map/ppermute | solution.py:182
  54.7 0.1 add_convert_fusion.5
  54.8 2.1 %collective-permute-start.5 = (bf16[2,2,208,128]{3,2,1,0:T(8,128)(2,1)S(1)}, bf16[2,2,208,128]{3,2,1,0:T(8,128)(2,1)S(1)}, u32[]{:S(2)}, u32[]{:S(2)}) collective-permute-start(bf16[2,2,208,128]{3,2,1,0:T(8,128)(2,1)S(1)} %bitcast.21), channel_id=1, source_target_pairs={{0,2},{1,5},{2,0},{3,7},{4,6},{5,1},{6,4},{7,3},{8,10},{9,13},{10,... | collective-permute-start | bytes 638984 | tf_op jit(solution)/shard_map/ppermute | solution.py:182
  56.8 0.5 collective-permute-done.2
  57.4 0.1 add_convert_fusion.1
  57.5 2.1 %collective-permute-start.4 = (bf16[2,2,240,128]{3,2,1,0:T(8,128)(2,1)S(1)}, bf16[2,2,240,128]{3,2,1,0:T(8,128)(2,1)S(1)}, u32[]{:S(2)}, u32[]{:S(2)}) collective-permute-start(bf16[2,2,240,128]{3,2,1,0:T(8,128)(2,1)S(1)} %add_convert_fusion.1), channel_id=1, source_target_pairs={{0,2},{1,5},{2,0},{3,7},{4,6},{5,1},{6,4},{7,3},{8,10},{9,13},{10,... | collective-permute-start | bytes 737288 | tf_op jit(solution)/shard_map/ppermute | solution.py:182
  59.5 0.0 collective-permute-done.8
  59.6 0.1 collective-permute-start.9
  59.7 2.6 %collective-permute-done.5 = bf16[2,2,208,128]{3,2,1,0:T(8,128)(2,1)S(1)} collective-permute-done((bf16[2,2,208,128]{3,2,1,0:T(8,128)(2,1)S(1)}, bf16[2,2,208,128]{3,2,1,0:T(8,128)(2,1)S(1)}, u32[]{:S(2)}, u32[]{:S(2)}) %collective-permute-start.5) | collective-permute-done | bytes 213024 | tf_op jit(solution)/shard_map/ppermute | solution.py:182
  62.2 0.1 add_convert_fusion.4
  62.3 0.1 collective-permute-start.7
  62.4 2.8 %collective-permute-done.4 = bf16[2,2,240,128]{3,2,1,0:T(8,128)(2,1)S(1)} collective-permute-done((bf16[2,2,240,128]{3,2,1,0:T(8,128)(2,1)S(1)}, bf16[2,2,240,128]{3,2,1,0:T(8,128)(2,1)S(1)}, u32[]{:S(2)}, u32[]{:S(2)}) %collective-permute-start.4) | collective-permute-done | bytes 245792 | tf_op jit(solution)/shard_map/ppermute | solution.py:182
  65.3 0.1 add_convert_fusion
  65.3 0.1 collective-permute-start.6
  65.4 0.0 collective-permute-done.9
  65.5 1.2 collective-permute-start.10
  66.7 1.5 %collective-permute-done.7 = bf16[2,2,208,128]{3,2,1,0:T(8,128)(2,1)S(1)} collective-permute-done((bf16[2,2,208,128]{3,2,1,0:T(8,128)(2,1)S(1)}, bf16[2,2,208,128]{3,2,1,0:T(8,128)(2,1)S(1)}, u32[]{:S(2)}, u32[]{:S(2)}) %collective-permute-start.7) | collective-permute-done | bytes 213024 | tf_op jit(solution)/shard_map/ppermute | solution.py:182
  68.3 1.2 collective-permute-start.11
  69.5 2.4 %collective-permute-done.10 = bf16[2,2,144,128]{3,2,1,0:T(8,128)(2,1)S(1)} collective-permute-done((bf16[2,2,144,128]{3,2,1,0:T(8,128)(2,1)S(1)}, bf16[2,2,144,128]{3,2,1,0:T(8,128)(2,1)S(1)}, u32[]{:S(2)}, u32[]{:S(2)}) %collective-permute-start.10) | collective-permute-done | bytes 147488 | tf_op jit(solution)/shard_map/ppermute | solution.py:182
  72.0 2.1 %collective-permute-start.12 = (bf16[4,144,128]{2,1,0:T(8,128)(2,1)S(1)}, bf16[4,144,128]{2,1,0:T(8,128)(2,1)S(1)}, u32[]{:S(2)}, u32[]{:S(2)}) collective-permute-start(bf16[4,144,128]{2,1,0:T(8,128)(2,1)S(1)} %bitcast.27), channel_id=1, source_target_pairs={{0,2},{1,5},{2,0},{3,7},{4,6},{5,1},{6,4},{7,3},{8,10},{9,13},{10,... | collective-permute-start | bytes 442376 | tf_op jit(solution)/shard_map/ppermute | solution.py:182
  74.1 0.0 collective-permute-done.6
  74.1 0.1 collective-permute-start.13
  74.2 1.2 collective-permute-done.11
  75.5 0.1 collective-permute-start.14
  75.6 3.2 %collective-permute-done.12 = bf16[4,144,128]{2,1,0:T(8,128)(2,1)S(1)} collective-permute-done((bf16[4,144,128]{2,1,0:T(8,128)(2,1)S(1)}, bf16[4,144,128]{2,1,0:T(8,128)(2,1)S(1)}, u32[]{:S(2)}, u32[]{:S(2)}) %collective-permute-start.12) | collective-permute-done | bytes 147488 | tf_op jit(solution)/shard_map/ppermute | solution.py:182
  78.8 0.3 collective-permute-start.15
  79.0 1.3 own_square.1
  80.3 0.3 collective-permute-done.15.c_ref
  80.6 0.0 collective-permute-done.13.a_ref
  80.6 0.0 collective-permute-done.14.b_ref
  80.6 7.1 %update_rows.1 = bf16[8,8,144,128]{3,2,1,0:T(8,128)(2,1)S(1)} custom-call(bf16[4736,128]{1,0:T(8,128)(2,1)S(1)} %get-tuple-element.32.own_ref, bf16[8,240,128]{2,1,0:T(8,128)(2,1)S(1)} %collective-permute-done.13.a_ref, bf16[8,208,128]{2,1,0:T(8,128)(2,1)S(1)} %collective-permute-done.14.b_ref, bf16[8,144,128]{2,1,0:T(8,128)(2,1)S(1)} %collective-permute-done.15.c_ref, ...), custom_call_target="tpu_custom_call" | custom-call | flops 6341787648 | bytes 11796480 | tf_op jit(solution)/shard_map/update_rows/pallas_call | solution.py:303
  87.7 42.0 %all_to_all.11 = bf16[64,144,128]{2,1,0:T(8,128)(2,1)S(1)} all-to-all(bf16[64,144,128]{2,1,0:T(8,128)(2,1)S(1)} %bitcast.16), channel_id=1, replica_groups=mesh['z'=4,'yl'=2,'x'=4,'yh'=2,'c'=2] {'z','yl','x','yh'}, dimensions={0} | all-to-all | bytes 4718592 | tf_op jit(solution)/shard_map/all_to_all | solution.py:381
  129.7 1.6 %join_columns.1 = bf16[8,96,1536]{2,1,0:T(8,128)(2,1)} custom-call(bf16[8,8,144,128]{3,2,1,0:T(8,128)(2,1)S(1)} %bitcast.10), custom_call_target="tpu_custom_call" | custom-call | tf_op jit(solution)/shard_map/join_columns/pallas_call | solution.py:339
  (13 shorter events, 0.4 us)
Async XLA Ops:
  0.0 1.7 %copy-start = (bf16[1,96,12288]{2,1,0:T(8,128)(2,1)S(1)}, bf16[1,96,12288]{2,1,0:T(8,128)(2,1)}, u32[]{:S(2)}) copy-start(bf16[1,96,12288]{2,1,0:T(8,128)(2,1)} %param.1) | copy-start | bytes 7077892
  40.0 4.5 %collective-permute-start.1 = (bf16[768,1536]{1,0:T(8,128)(2,1)S(1)}, bf16[768,1536]{1,0:T(8,128)(2,1)S(1)}, u32[]{:S(2)}, u32[]{:S(2)}) collective-permute-start(bf16[768,1536]{1,0:T(8,128)(2,1)S(1)} %bitcast.12), channel_id=1, source_target_pairs={{0,1},{1,0},{2,3},{3,2},{4,5},{5,4},{6,7},{7,6},{8,9},{9,8},{10,11... | collective-permute-start | bytes 7077896 | tf_op jit(solution)/shard_map/ppermute | solution.py:351
  41.4 7.3 %collective-permute-start = (bf16[4,240,128]{2,1,0:T(8,128)(2,1)S(1)}, bf16[4,240,128]{2,1,0:T(8,128)(2,1)S(1)}, u32[]{:S(2)}, u32[]{:S(2)}) collective-permute-start(bf16[4,240,128]{2,1,0:T(8,128)(2,1)S(1)} %get-tuple-element.21), channel_id=1, source_target_pairs={{0,4},{1,13},{2,6},{3,15},{4,0},{5,9},{6,2},{7,11},{8,12},{9,5},{1... | collective-permute-start | bytes 737288 | tf_op jit(solution)/shard_map/ppermute | solution.py:182
  46.0 13.5 %collective-permute-start.8 = (bf16[4,144,128]{2,1,0:T(8,128)(2,1)S(1)}, bf16[4,144,128]{2,1,0:T(8,128)(2,1)S(1)}, u32[]{:S(2)}, u32[]{:S(2)}) collective-permute-start(bf16[4,144,128]{2,1,0:T(8,128)(2,1)S(1)} %get-tuple-element.24), channel_id=1, source_target_pairs={{0,2},{1,5},{2,0},{3,7},{4,6},{5,1},{6,4},{7,3},{8,10},{9,13},{10,... | collective-permute-start | bytes 442376 | tf_op jit(solution)/shard_map/ppermute | solution.py:182
  47.7 7.1 %collective-permute-start.3 = (bf16[4,208,128]{2,1,0:T(8,128)(2,1)S(1)}, bf16[4,208,128]{2,1,0:T(8,128)(2,1)S(1)}, u32[]{:S(2)}, u32[]{:S(2)}) collective-permute-start(bf16[4,208,128]{2,1,0:T(8,128)(2,1)S(1)} %get-tuple-element.23), channel_id=1, source_target_pairs={{0,12},{1,3},{2,14},{3,1},{4,8},{5,7},{6,10},{7,5},{8,4},{9,11},{1... | collective-permute-start | bytes 638984 | tf_op jit(solution)/shard_map/ppermute | solution.py:182
  48.8 8.5 %collective-permute-start.2 = (bf16[2,2,240,128]{3,2,1,0:T(8,128)(2,1)S(1)}, bf16[2,2,240,128]{3,2,1,0:T(8,128)(2,1)S(1)}, u32[]{:S(2)}, u32[]{:S(2)}) collective-permute-start(bf16[2,2,240,128]{3,2,1,0:T(8,128)(2,1)S(1)} %bitcast.19), channel_id=1, source_target_pairs={{0,12},{1,3},{2,14},{3,1},{4,8},{5,7},{6,10},{7,5},{8,4},{9,11},{1... | collective-permute-start | bytes 737288 | tf_op jit(solution)/shard_map/ppermute | solution.py:182
  54.8 7.4 %collective-permute-start.5 = (bf16[2,2,208,128]{3,2,1,0:T(8,128)(2,1)S(1)}, bf16[2,2,208,128]{3,2,1,0:T(8,128)(2,1)S(1)}, u32[]{:S(2)}, u32[]{:S(2)}) collective-permute-start(bf16[2,2,208,128]{3,2,1,0:T(8,128)(2,1)S(1)} %bitcast.21), channel_id=1, source_target_pairs={{0,2},{1,5},{2,0},{3,7},{4,6},{5,1},{6,4},{7,3},{8,10},{9,13},{10,... | collective-permute-start | bytes 638984 | tf_op jit(solution)/shard_map/ppermute | solution.py:182
  57.5 7.8 %collective-permute-start.4 = (bf16[2,2,240,128]{3,2,1,0:T(8,128)(2,1)S(1)}, bf16[2,2,240,128]{3,2,1,0:T(8,128)(2,1)S(1)}, u32[]{:S(2)}, u32[]{:S(2)}) collective-permute-start(bf16[2,2,240,128]{3,2,1,0:T(8,128)(2,1)S(1)} %add_convert_fusion.1), channel_id=1, source_target_pairs={{0,2},{1,5},{2,0},{3,7},{4,6},{5,1},{6,4},{7,3},{8,10},{9,13},{10,... | collective-permute-start | bytes 737288 | tf_op jit(solution)/shard_map/ppermute | solution.py:182
  59.6 5.9 %collective-permute-start.9 = (bf16[2,2,144,128]{3,2,1,0:T(8,128)(2,1)S(1)}, bf16[2,2,144,128]{3,2,1,0:T(8,128)(2,1)S(1)}, u32[]{:S(2)}, u32[]{:S(2)}) collective-permute-start(bf16[2,2,144,128]{3,2,1,0:T(8,128)(2,1)S(1)} %bitcast.25), channel_id=1, source_target_pairs={{0,4},{1,13},{2,6},{3,15},{4,0},{5,9},{6,2},{7,11},{8,12},{9,5},{1... | collective-permute-start | bytes 442376 | tf_op jit(solution)/shard_map/ppermute | solution.py:182
  62.3 5.9 %collective-permute-start.7 = (bf16[2,2,208,128]{3,2,1,0:T(8,128)(2,1)S(1)}, bf16[2,2,208,128]{3,2,1,0:T(8,128)(2,1)S(1)}, u32[]{:S(2)}, u32[]{:S(2)}) collective-permute-start(bf16[2,2,208,128]{3,2,1,0:T(8,128)(2,1)S(1)} %add_convert_fusion.4), channel_id=1, source_target_pairs={{0,4},{1,13},{2,6},{3,15},{4,0},{5,9},{6,2},{7,11},{8,12},{9,5},{1... | collective-permute-start | bytes 638984 | tf_op jit(solution)/shard_map/ppermute | solution.py:182
  65.3 8.7 %collective-permute-start.6 = (bf16[4,240,128]{2,1,0:T(8,128)(2,1)S(1)}, bf16[4,240,128]{2,1,0:T(8,128)(2,1)S(1)}, u32[]{:S(2)}, u32[]{:S(2)}) collective-permute-start(bf16[4,240,128]{2,1,0:T(8,128)(2,1)S(1)} %bitcast.17), channel_id=1, source_target_pairs={{0,4},{1,13},{2,6},{3,15},{4,0},{5,9},{6,2},{7,11},{8,12},{9,5},{1... | collective-permute-start | bytes 737288 | tf_op jit(solution)/shard_map/ppermute | solution.py:182
  65.5 6.4 %collective-permute-start.10 = (bf16[2,2,144,128]{3,2,1,0:T(8,128)(2,1)S(1)}, bf16[2,2,144,128]{3,2,1,0:T(8,128)(2,1)S(1)}, u32[]{:S(2)}, u32[]{:S(2)}) collective-permute-start(bf16[2,2,144,128]{3,2,1,0:T(8,128)(2,1)S(1)} %add_convert_fusion.7), channel_id=1, source_target_pairs={{0,12},{1,3},{2,14},{3,1},{4,8},{5,7},{6,10},{7,5},{8,4},{9,11},{1... | collective-permute-start | bytes 442376 | tf_op jit(solution)/shard_map/ppermute | solution.py:182
  68.3 7.1 %collective-permute-start.11 = (bf16[4,208,128]{2,1,0:T(8,128)(2,1)S(1)}, bf16[4,208,128]{2,1,0:T(8,128)(2,1)S(1)}, u32[]{:S(2)}, u32[]{:S(2)}) collective-permute-start(bf16[4,208,128]{2,1,0:T(8,128)(2,1)S(1)} %bitcast.23), channel_id=1, source_target_pairs={{0,12},{1,3},{2,14},{3,1},{4,8},{5,7},{6,10},{7,5},{8,4},{9,11},{1... | collective-permute-start | bytes 638984 | tf_op jit(solution)/shard_map/ppermute | solution.py:182
  72.0 6.7 %collective-permute-start.12 = (bf16[4,144,128]{2,1,0:T(8,128)(2,1)S(1)}, bf16[4,144,128]{2,1,0:T(8,128)(2,1)S(1)}, u32[]{:S(2)}, u32[]{:S(2)}) collective-permute-start(bf16[4,144,128]{2,1,0:T(8,128)(2,1)S(1)} %bitcast.27), channel_id=1, source_target_pairs={{0,2},{1,5},{2,0},{3,7},{4,6},{5,1},{6,4},{7,3},{8,10},{9,13},{10,... | collective-permute-start | bytes 442376 | tf_op jit(solution)/shard_map/ppermute | solution.py:182
  74.1 6.5 %collective-permute-start.13 = (bf16[8,240,128]{2,1,0:T(8,128)(2,1)S(1)}, bf16[8,240,128]{2,1,0:T(8,128)(2,1)S(1)}, u32[]{:S(2)}, u32[]{:S(2)}) collective-permute-start(bf16[8,240,128]{2,1,0:T(8,128)(2,1)S(1)} %pad_maximum_fusion.a_ref), channel_id=1, source_target_pairs={{0,1},{1,0},{2,3},{3,2},{4,5},{5,4},{6,7},{7,6},{8,9},{9,8},{10,11... | collective-permute-start | bytes 1474568 | tf_op jit(solution)/shard_map/ppermute | solution.py:351
  75.5 5.1 %collective-permute-start.14 = (bf16[8,208,128]{2,1,0:T(8,128)(2,1)S(1)}, bf16[8,208,128]{2,1,0:T(8,128)(2,1)S(1)}, u32[]{:S(2)}, u32[]{:S(2)}) collective-permute-start(bf16[8,208,128]{2,1,0:T(8,128)(2,1)S(1)} %pad_maximum_fusion.1.b_ref), channel_id=1, source_target_pairs={{0,1},{1,0},{2,3},{3,2},{4,5},{5,4},{6,7},{7,6},{8,9},{9,8},{10,11... | collective-permute-start | bytes 1277960 | tf_op jit(solution)/shard_map/ppermute | solution.py:351
  78.8 1.8 %collective-permute-start.15 = (bf16[8,144,128]{2,1,0:T(8,128)(2,1)S(1)}, bf16[8,144,128]{2,1,0:T(8,128)(2,1)S(1)}, u32[]{:S(2)}, u32[]{:S(2)}) collective-permute-start(bf16[8,144,128]{2,1,0:T(8,128)(2,1)S(1)} %pad_maximum_fusion.2.c_ref), channel_id=1, source_target_pairs={{0,1},{1,0},{2,3},{3,2},{4,5},{5,4},{6,7},{7,6},{8,9},{9,8},{10,11... | collective-permute-start | bytes 884744 | tf_op jit(solution)/shard_map/ppermute | solution.py:351

commit v18 on v17

--- a/solution.py
+++ b/solution.py
@@ -24,7 +24,7 @@
 BELOW = LANES * BLOCKS * (BLOCKS - 1) // 2
 EDGE = 2 * BELOW + HALF
 PACKED = -(-(EDGE + BLOCKS) // (16 * CHIPS)) * 16 * CHIPS
-PIECES = (240, 208, 144)
+PIECES = (240, 176, 176)
 BASES = (0, CHIPS * PIECES[0], CHIPS * (PIECES[0] + PIECES[1]))
 MIB = 1 << 20
 

time: 132 us -> 130 us (0.985)
  transfers between devices with their start and end apart: 16 -> 16, of which waited for: 10 -> 11; matrix products, arithmetic and copies ran while one was open for 1% -> 1% of each run, Pallas kernels for 3% -> 3%
where the time goes in v18:
time: 130 us
  blocking collectives  79.2 us (61%)
  waiting for transfers between devices  20 us (15%)
  starting transfers between devices  14.4 us (11%)
  Pallas kernels  13.6 us (10%)
  local copies, waits for them, and re-layouts  1.66 us (1%)
    all_to_all x1, blocking collectives, shards(): received = lax.all_to_all(sent, ALL_CHIPS, 0, 0, tiled=True)  41.5 us
    all_to_all x1, blocking collectives, shards(): lax.all_to_all(pieces, CHIP_AXES, 0, 0, tiled=True).reshape(HALF, WIDTH)  37.7 us
    ppermute x12, waiting for transfers between devices, exchange(): return lax.ppermute(value, ('x', 'yh', 'c'), pairs)  17.2 us
    ppermute x12, starting transfers between devices, exchange(): return lax.ppermute(value, ('x', 'yh', 'c'), pairs)  13.7 us
    pallas_call x1, Pallas kernels, update_rows(): pl.pallas_call(update_kernel, out_shape=jax.ShapeDtypeStruct((STRIPES, CH...  7.12 us
    ppermute x4, waiting for transfers between devices, swap_cores(): return lax.ppermute(value, 'c', [(0, 1), (1, 0)])  2.82 us
  transfers between devices with their start and end apart: 16, of which 11 were waited for; matrix products, arithmetic and copies ran while one was open for 1% of the time, Pallas kernels for 3%

profile of v18, /device:TPU:0, one launch (start us, length us, event | category | flops | bytes accessed | tf_op | source)
XLA Modules:
  0.0 129.9 jit_solution(14957316771719015811)
XLA Ops:
  0.0 0.0 copy-start
  0.0 1.7 %copy-done = bf16[1,96,12288]{2,1,0:T(8,128)(2,1)S(1)} copy-done((bf16[1,96,12288]{2,1,0:T(8,128)(2,1)S(1)}, bf16[1,96,12288]{2,1,0:T(8,128)(2,1)}, u32[]{:S(2)}) %copy-start) | copy-done | bytes 2359320
  1.7 0.6 split_columns.1
  2.3 37.7 %all_to_all.10 = bf16[8,96,1536]{2,1,0:T(8,128)(2,1)S(1)} all-to-all(bf16[8,96,1536]{2,1,0:T(8,128)(2,1)S(1)} %split_columns.1), channel_id=1, replica_groups=mesh['z'=4,'yl'=2,'x'=4,'yh'=2,'c'=2] {'x','yh'}, dimensions={0} | all-to-all | bytes 4718592 | tf_op jit(solution)/shard_map/all_to_all | solution.py:356
  40.0 0.0 collective-permute-start.1
  40.0 1.5 %own_gram.1 = (f32[4,240,128]{2,1,0:T(8,128)S(1)}, bf16[4,240,128]{2,1,0:T(8,128)(2,1)S(1)}, f32[6,128,128]{2,1,0:T(8,128)S(1)}) custom-call(bf16[768,1536]{1,0:T(8,128)(2,1)S(1)} %bitcast.13), custom_call_target="tpu_custom_call" | custom-call | flops 1660944384 | bytes 2359296 | tf_op jit(solution)/shard_map/own_gram/pallas_call | solution.py:129
  41.4 0.6 collective-permute-start
  42.0 2.5 %collective-permute-done.1.other_ref.x_other_ref = bf16[768,1536]{1,0:T(8,128)(2,1)S(1)} collective-permute-done((bf16[768,1536]{1,0:T(8,128)(2,1)S(1)}, bf16[768,1536]{1,0:T(8,128)(2,1)S(1)}, u32[]{:S(2)}, u32[]{:S(2)}) %collective-permute-start.1) | collective-permute-done | bytes 2359328 | tf_op jit(solution)/shard_map/ppermute | solution.py:351
  44.5 1.5 %cross_gram.1 = (f32[4,176,128]{2,1,0:T(8,128)S(1)}, bf16[4,176,128]{2,1,0:T(8,128)(2,1)S(1)}, f32[4,176,128]{2,1,0:T(8,128)S(1)}, bf16[4,176,128]{2,1,0:T(8,128)(2,1)S(1)}) custom-call(f32[6,128,128]{2,1,0:T(8,128)S(1)} %get-tuple-element.22.diagonal_ref, bf16[768,1536]{1,0:T(8,128)(2,1)S(1)} %bitcast.14, ...), custom_call_target="tpu_custom_call" | custom-call | flops 1660944384 | bytes 4718592 | tf_op jit(solution)/shard_map/cross_gram/pallas_call | solution.py:162
  46.0 1.5 %collective-permute-start.3 = (bf16[4,176,128]{2,1,0:T(8,128)(2,1)S(1)}, bf16[4,176,128]{2,1,0:T(8,128)(2,1)S(1)}, u32[]{:S(2)}, u32[]{:S(2)}) collective-permute-start(bf16[4,176,128]{2,1,0:T(8,128)(2,1)S(1)} %get-tuple-element.23), channel_id=1, source_target_pairs={{0,12},{1,3},{2,14},{3,1},{4,8},{5,7},{6,10},{7,5},{8,4},{9,11},{1... | collective-permute-start | bytes 540680 | tf_op jit(solution)/shard_map/ppermute | solution.py:182
  47.5 0.2 collective-permute-done
  47.7 0.1 add_convert_fusion.2
  47.8 1.7 %collective-permute-start.2 = (bf16[2,2,240,128]{3,2,1,0:T(8,128)(2,1)S(1)}, bf16[2,2,240,128]{3,2,1,0:T(8,128)(2,1)S(1)}, u32[]{:S(2)}, u32[]{:S(2)}) collective-permute-start(bf16[2,2,240,128]{3,2,1,0:T(8,128)(2,1)S(1)} %bitcast.19), channel_id=1, source_target_pairs={{0,12},{1,3},{2,14},{3,1},{4,8},{5,7},{6,10},{7,5},{8,4},{9,11},{1... | collective-permute-start | bytes 737288 | tf_op jit(solution)/shard_map/ppermute | solution.py:182
  49.5 1.6 %collective-permute-start.8 = (bf16[4,176,128]{2,1,0:T(8,128)(2,1)S(1)}, bf16[4,176,128]{2,1,0:T(8,128)(2,1)S(1)}, u32[]{:S(2)}, u32[]{:S(2)}) collective-permute-start(bf16[4,176,128]{2,1,0:T(8,128)(2,1)S(1)} %get-tuple-element.24), channel_id=1, source_target_pairs={{0,2},{1,5},{2,0},{3,7},{4,6},{5,1},{6,4},{7,3},{8,10},{9,13},{10,... | collective-permute-start | bytes 540680 | tf_op jit(solution)/shard_map/ppermute | solution.py:182
  51.0 1.8 %collective-permute-done.3 = bf16[4,176,128]{2,1,0:T(8,128)(2,1)S(1)} collective-permute-done((bf16[4,176,128]{2,1,0:T(8,128)(2,1)S(1)}, bf16[4,176,128]{2,1,0:T(8,128)(2,1)S(1)}, u32[]{:S(2)}, u32[]{:S(2)}) %collective-permute-start.3) | collective-permute-done | bytes 180256 | tf_op jit(solution)/shard_map/ppermute | solution.py:182
  52.9 1.6 %collective-permute-start.5 = (bf16[2,2,176,128]{3,2,1,0:T(8,128)(2,1)S(1)}, bf16[2,2,176,128]{3,2,1,0:T(8,128)(2,1)S(1)}, u32[]{:S(2)}, u32[]{:S(2)}) collective-permute-start(bf16[2,2,176,128]{3,2,1,0:T(8,128)(2,1)S(1)} %bitcast.21), channel_id=1, source_target_pairs={{0,2},{1,5},{2,0},{3,7},{4,6},{5,1},{6,4},{7,3},{8,10},{9,13},{10,... | collective-permute-start | bytes 540680 | tf_op jit(solution)/shard_map/ppermute | solution.py:182
  54.5 0.9 collective-permute-done.2
  55.5 0.1 add_convert_fusion.1
  55.5 1.6 %collective-permute-start.4 = (bf16[2,2,240,128]{3,2,1,0:T(8,128)(2,1)S(1)}, bf16[2,2,240,128]{3,2,1,0:T(8,128)(2,1)S(1)}, u32[]{:S(2)}, u32[]{:S(2)}) collective-permute-start(bf16[2,2,240,128]{3,2,1,0:T(8,128)(2,1)S(1)} %add_convert_fusion.1), channel_id=1, source_target_pairs={{0,2},{1,5},{2,0},{3,7},{4,6},{5,1},{6,4},{7,3},{8,10},{9,13},{10,... | collective-permute-start | bytes 737288 | tf_op jit(solution)/shard_map/ppermute | solution.py:182
  57.2 0.0 collective-permute-done.8
  57.2 0.2 collective-permute-start.9
  57.5 2.5 %collective-permute-done.5 = bf16[2,2,176,128]{3,2,1,0:T(8,128)(2,1)S(1)} collective-permute-done((bf16[2,2,176,128]{3,2,1,0:T(8,128)(2,1)S(1)}, bf16[2,2,176,128]{3,2,1,0:T(8,128)(2,1)S(1)}, u32[]{:S(2)}, u32[]{:S(2)}) %collective-permute-start.5) | collective-permute-done | bytes 180256 | tf_op jit(solution)/shard_map/ppermute | solution.py:182
  60.0 0.1 collective-permute-start.7
  60.1 3.2 %collective-permute-done.4 = bf16[2,2,240,128]{3,2,1,0:T(8,128)(2,1)S(1)} collective-permute-done((bf16[2,2,240,128]{3,2,1,0:T(8,128)(2,1)S(1)}, bf16[2,2,240,128]{3,2,1,0:T(8,128)(2,1)S(1)}, u32[]{:S(2)}, u32[]{:S(2)}) %collective-permute-start.4) | collective-permute-done | bytes 245792 | tf_op jit(solution)/shard_map/ppermute | solution.py:182
  63.4 0.1 add_convert_fusion
  63.4 0.1 collective-permute-start.6
  63.5 0.0 collective-permute-done.9
  63.6 1.5 %collective-permute-start.10 = (bf16[2,2,176,128]{3,2,1,0:T(8,128)(2,1)S(1)}, bf16[2,2,176,128]{3,2,1,0:T(8,128)(2,1)S(1)}, u32[]{:S(2)}, u32[]{:S(2)}) collective-permute-start(bf16[2,2,176,128]{3,2,1,0:T(8,128)(2,1)S(1)} %add_convert_fusion.4), channel_id=1, source_target_pairs={{0,12},{1,3},{2,14},{3,1},{4,8},{5,7},{6,10},{7,5},{8,4},{9,11},{1... | collective-permute-start | bytes 540680 | tf_op jit(solution)/shard_map/ppermute | solution.py:182
  65.1 0.5 collective-permute-done.7
  65.7 1.5 %collective-permute-start.11 = (bf16[4,176,128]{2,1,0:T(8,128)(2,1)S(1)}, bf16[4,176,128]{2,1,0:T(8,128)(2,1)S(1)}, u32[]{:S(2)}, u32[]{:S(2)}) collective-permute-start(bf16[4,176,128]{2,1,0:T(8,128)(2,1)S(1)} %bitcast.25), channel_id=1, source_target_pairs={{0,12},{1,3},{2,14},{3,1},{4,8},{5,7},{6,10},{7,5},{8,4},{9,11},{1... | collective-permute-start | bytes 540680 | tf_op jit(solution)/shard_map/ppermute | solution.py:182
  67.2 3.2 %collective-permute-done.10 = bf16[2,2,176,128]{3,2,1,0:T(8,128)(2,1)S(1)} collective-permute-done((bf16[2,2,176,128]{3,2,1,0:T(8,128)(2,1)S(1)}, bf16[2,2,176,128]{3,2,1,0:T(8,128)(2,1)S(1)}, u32[]{:S(2)}, u32[]{:S(2)}) %collective-permute-start.10) | collective-permute-done | bytes 180256 | tf_op jit(solution)/shard_map/ppermute | solution.py:182
  70.5 1.6 %collective-permute-start.12 = (bf16[4,176,128]{2,1,0:T(8,128)(2,1)S(1)}, bf16[4,176,128]{2,1,0:T(8,128)(2,1)S(1)}, u32[]{:S(2)}, u32[]{:S(2)}) collective-permute-start(bf16[4,176,128]{2,1,0:T(8,128)(2,1)S(1)} %bitcast.27), channel_id=1, source_target_pairs={{0,2},{1,5},{2,0},{3,7},{4,6},{5,1},{6,4},{7,3},{8,10},{9,13},{10,... | collective-permute-start | bytes 540680 | tf_op jit(solution)/shard_map/ppermute | solution.py:182
  72.1 0.0 collective-permute-done.6
  72.2 0.1 collective-permute-start.13
  72.3 0.2 collective-permute-done.11
  72.5 0.4 collective-permute-start.14
  72.9 4.7 %collective-permute-done.12 = bf16[4,176,128]{2,1,0:T(8,128)(2,1)S(1)} collective-permute-done((bf16[4,176,128]{2,1,0:T(8,128)(2,1)S(1)}, bf16[4,176,128]{2,1,0:T(8,128)(2,1)S(1)}, u32[]{:S(2)}, u32[]{:S(2)}) %collective-permute-start.12) | collective-permute-done | bytes 180256 | tf_op jit(solution)/shard_map/ppermute | solution.py:182
  77.6 0.3 collective-permute-start.15
  77.9 1.3 %own_square.1 = (bf16[4736,128]{1,0:T(8,128)(2,1)S(1)}, bf16[768,768]{1,0:T(8,128)(2,1)S(1)}, f32[768,768]{1,0:T(8,128)S(1)}) custom-call(bf16[8,240,128]{2,1,0:T(8,128)(2,1)S(1)} %pad_maximum_fusion.a_ref, bf16[8,176,128]{2,1,0:T(8,128)(2,1)S(1)} %pad_maximum_fusion.1.b_ref, bf16[8,176,128]{2,1,0:T(8,128)(2,1)S(1)} %pad_maximum_fusion.2.c_ref), custom_call_target="tpu_custom_call" | custom-call | flops 905969664 | bytes 4718592 | tf_op jit(solution)/shard_map/own_square/pallas_call | solution.py:232
  79.2 0.0 collective-permute-done.14.b_ref
  79.2 0.3 collective-permute-done.15.c_ref
  79.5 0.0 collective-permute-done.13.a_ref
  79.5 7.1 %update_rows.1 = bf16[8,8,144,128]{3,2,1,0:T(8,128)(2,1)S(1)} custom-call(bf16[4736,128]{1,0:T(8,128)(2,1)S(1)} %get-tuple-element.32.own_ref, bf16[8,240,128]{2,1,0:T(8,128)(2,1)S(1)} %collective-permute-done.13.a_ref, bf16[8,176,128]{2,1,0:T(8,128)(2,1)S(1)} %collective-permute-done.14.b_ref, bf16[8,176,128]{2,1,0:T(8,128)(2,1)S(1)} %collective-permute-done.15.c_ref, ...), custom_call_target="tpu_custom_call" | custom-call | flops 6341787648 | bytes 11796480 | tf_op jit(solution)/shard_map/update_rows/pallas_call | solution.py:303
  86.6 41.5 %all_to_all.11 = bf16[64,144,128]{2,1,0:T(8,128)(2,1)S(1)} all-to-all(bf16[64,144,128]{2,1,0:T(8,128)(2,1)S(1)} %bitcast.16), channel_id=1, replica_groups=mesh['z'=4,'yl'=2,'x'=4,'yh'=2,'c'=2] {'z','yl','x','yh'}, dimensions={0} | all-to-all | bytes 4718592 | tf_op jit(solution)/shard_map/all_to_all | solution.py:381
  128.2 1.6 %join_columns.1 = bf16[8,96,1536]{2,1,0:T(8,128)(2,1)} custom-call(bf16[8,8,144,128]{3,2,1,0:T(8,128)(2,1)S(1)} %bitcast.10), custom_call_target="tpu_custom_call" | custom-call | tf_op jit(solution)/shard_map/join_columns/pallas_call | solution.py:339
  (15 shorter events, 0.5 us)
Async XLA Ops:
  0.0 1.7 %copy-start = (bf16[1,96,12288]{2,1,0:T(8,128)(2,1)S(1)}, bf16[1,96,12288]{2,1,0:T(8,128)(2,1)}, u32[]{:S(2)}) copy-start(bf16[1,96,12288]{2,1,0:T(8,128)(2,1)} %param.1) | copy-start | bytes 7077892
  40.0 4.5 %collective-permute-start.1 = (bf16[768,1536]{1,0:T(8,128)(2,1)S(1)}, bf16[768,1536]{1,0:T(8,128)(2,1)S(1)}, u32[]{:S(2)}, u32[]{:S(2)}) collective-permute-start(bf16[768,1536]{1,0:T(8,128)(2,1)S(1)} %bitcast.12), channel_id=1, source_target_pairs={{0,1},{1,0},{2,3},{3,2},{4,5},{5,4},{6,7},{7,6},{8,9},{9,8},{10,11... | collective-permute-start | bytes 7077896 | tf_op jit(solution)/shard_map/ppermute | solution.py:351
  41.4 6.3 %collective-permute-start = (bf16[4,240,128]{2,1,0:T(8,128)(2,1)S(1)}, bf16[4,240,128]{2,1,0:T(8,128)(2,1)S(1)}, u32[]{:S(2)}, u32[]{:S(2)}) collective-permute-start(bf16[4,240,128]{2,1,0:T(8,128)(2,1)S(1)} %get-tuple-element.21), channel_id=1, source_target_pairs={{0,4},{1,13},{2,6},{3,15},{4,0},{5,9},{6,2},{7,11},{8,12},{9,5},{1... | collective-permute-start | bytes 737288 | tf_op jit(solution)/shard_map/ppermute | solution.py:182
  46.0 6.8 %collective-permute-start.3 = (bf16[4,176,128]{2,1,0:T(8,128)(2,1)S(1)}, bf16[4,176,128]{2,1,0:T(8,128)(2,1)S(1)}, u32[]{:S(2)}, u32[]{:S(2)}) collective-permute-start(bf16[4,176,128]{2,1,0:T(8,128)(2,1)S(1)} %get-tuple-element.23), channel_id=1, source_target_pairs={{0,12},{1,3},{2,14},{3,1},{4,8},{5,7},{6,10},{7,5},{8,4},{9,11},{1... | collective-permute-start | bytes 540680 | tf_op jit(solution)/shard_map/ppermute | solution.py:182
  47.8 7.7 %collective-permute-start.2 = (bf16[2,2,240,128]{3,2,1,0:T(8,128)(2,1)S(1)}, bf16[2,2,240,128]{3,2,1,0:T(8,128)(2,1)S(1)}, u32[]{:S(2)}, u32[]{:S(2)}) collective-permute-start(bf16[2,2,240,128]{3,2,1,0:T(8,128)(2,1)S(1)} %bitcast.19), channel_id=1, source_target_pairs={{0,12},{1,3},{2,14},{3,1},{4,8},{5,7},{6,10},{7,5},{8,4},{9,11},{1... | collective-permute-start | bytes 737288 | tf_op jit(solution)/shard_map/ppermute | solution.py:182
  49.5 7.7 %collective-permute-start.8 = (bf16[4,176,128]{2,1,0:T(8,128)(2,1)S(1)}, bf16[4,176,128]{2,1,0:T(8,128)(2,1)S(1)}, u32[]{:S(2)}, u32[]{:S(2)}) collective-permute-start(bf16[4,176,128]{2,1,0:T(8,128)(2,1)S(1)} %get-tuple-element.24), channel_id=1, source_target_pairs={{0,2},{1,5},{2,0},{3,7},{4,6},{5,1},{6,4},{7,3},{8,10},{9,13},{10,... | collective-permute-start | bytes 540680 | tf_op jit(solution)/shard_map/ppermute | solution.py:182
  52.9 7.1 %collective-permute-start.5 = (bf16[2,2,176,128]{3,2,1,0:T(8,128)(2,1)S(1)}, bf16[2,2,176,128]{3,2,1,0:T(8,128)(2,1)S(1)}, u32[]{:S(2)}, u32[]{:S(2)}) collective-permute-start(bf16[2,2,176,128]{3,2,1,0:T(8,128)(2,1)S(1)} %bitcast.21), channel_id=1, source_target_pairs={{0,2},{1,5},{2,0},{3,7},{4,6},{5,1},{6,4},{7,3},{8,10},{9,13},{10,... | collective-permute-start | bytes 540680 | tf_op jit(solution)/shard_map/ppermute | solution.py:182
  55.5 7.8 %collective-permute-start.4 = (bf16[2,2,240,128]{3,2,1,0:T(8,128)(2,1)S(1)}, bf16[2,2,240,128]{3,2,1,0:T(8,128)(2,1)S(1)}, u32[]{:S(2)}, u32[]{:S(2)}) collective-permute-start(bf16[2,2,240,128]{3,2,1,0:T(8,128)(2,1)S(1)} %add_convert_fusion.1), channel_id=1, source_target_pairs={{0,2},{1,5},{2,0},{3,7},{4,6},{5,1},{6,4},{7,3},{8,10},{9,13},{10,... | collective-permute-start | bytes 737288 | tf_op jit(solution)/shard_map/ppermute | solution.py:182
  57.2 6.3 %collective-permute-start.9 = (bf16[2,2,176,128]{3,2,1,0:T(8,128)(2,1)S(1)}, bf16[2,2,176,128]{3,2,1,0:T(8,128)(2,1)S(1)}, u32[]{:S(2)}, u32[]{:S(2)}) collective-permute-start(bf16[2,2,176,128]{3,2,1,0:T(8,128)(2,1)S(1)} %bitcast.23), channel_id=1, source_target_pairs={{0,4},{1,13},{2,6},{3,15},{4,0},{5,9},{6,2},{7,11},{8,12},{9,5},{1... | collective-permute-start | bytes 540680 | tf_op jit(solution)/shard_map/ppermute | solution.py:182
  60.0 5.6 %collective-permute-start.7 = (bf16[2,2,176,128]{3,2,1,0:T(8,128)(2,1)S(1)}, bf16[2,2,176,128]{3,2,1,0:T(8,128)(2,1)S(1)}, u32[]{:S(2)}, u32[]{:S(2)}) collective-permute-start(bf16[2,2,176,128]{3,2,1,0:T(8,128)(2,1)S(1)} %add_convert_fusion.7), channel_id=1, source_target_pairs={{0,4},{1,13},{2,6},{3,15},{4,0},{5,9},{6,2},{7,11},{8,12},{9,5},{1... | collective-permute-start | bytes 540680 | tf_op jit(solution)/shard_map/ppermute | solution.py:182
  63.4 8.7 %collective-permute-start.6 = (bf16[4,240,128]{2,1,0:T(8,128)(2,1)S(1)}, bf16[4,240,128]{2,1,0:T(8,128)(2,1)S(1)}, u32[]{:S(2)}, u32[]{:S(2)}) collective-permute-start(bf16[4,240,128]{2,1,0:T(8,128)(2,1)S(1)} %bitcast.17), channel_id=1, source_target_pairs={{0,4},{1,13},{2,6},{3,15},{4,0},{5,9},{6,2},{7,11},{8,12},{9,5},{1... | collective-permute-start | bytes 737288 | tf_op jit(solution)/shard_map/ppermute | solution.py:182
  63.6 6.8 %collective-permute-start.10 = (bf16[2,2,176,128]{3,2,1,0:T(8,128)(2,1)S(1)}, bf16[2,2,176,128]{3,2,1,0:T(8,128)(2,1)S(1)}, u32[]{:S(2)}, u32[]{:S(2)}) collective-permute-start(bf16[2,2,176,128]{3,2,1,0:T(8,128)(2,1)S(1)} %add_convert_fusion.4), channel_id=1, source_target_pairs={{0,12},{1,3},{2,14},{3,1},{4,8},{5,7},{6,10},{7,5},{8,4},{9,11},{1... | collective-permute-start | bytes 540680 | tf_op jit(solution)/shard_map/ppermute | solution.py:182
  65.7 6.8 %collective-permute-start.11 = (bf16[4,176,128]{2,1,0:T(8,128)(2,1)S(1)}, bf16[4,176,128]{2,1,0:T(8,128)(2,1)S(1)}, u32[]{:S(2)}, u32[]{:S(2)}) collective-permute-start(bf16[4,176,128]{2,1,0:T(8,128)(2,1)S(1)} %bitcast.25), channel_id=1, source_target_pairs={{0,12},{1,3},{2,14},{3,1},{4,8},{5,7},{6,10},{7,5},{8,4},{9,11},{1... | collective-permute-start | bytes 540680 | tf_op jit(solution)/shard_map/ppermute | solution.py:182
  70.5 7.1 %collective-permute-start.12 = (bf16[4,176,128]{2,1,0:T(8,128)(2,1)S(1)}, bf16[4,176,128]{2,1,0:T(8,128)(2,1)S(1)}, u32[]{:S(2)}, u32[]{:S(2)}) collective-permute-start(bf16[4,176,128]{2,1,0:T(8,128)(2,1)S(1)} %bitcast.27), channel_id=1, source_target_pairs={{0,2},{1,5},{2,0},{3,7},{4,6},{5,1},{6,4},{7,3},{8,10},{9,13},{10,... | collective-permute-start | bytes 540680 | tf_op jit(solution)/shard_map/ppermute | solution.py:182
  72.2 7.4 %collective-permute-start.13 = (bf16[8,240,128]{2,1,0:T(8,128)(2,1)S(1)}, bf16[8,240,128]{2,1,0:T(8,128)(2,1)S(1)}, u32[]{:S(2)}, u32[]{:S(2)}) collective-permute-start(bf16[8,240,128]{2,1,0:T(8,128)(2,1)S(1)} %pad_maximum_fusion.a_ref), channel_id=1, source_target_pairs={{0,1},{1,0},{2,3},{3,2},{4,5},{5,4},{6,7},{7,6},{8,9},{9,8},{10,11... | collective-permute-start | bytes 1474568 | tf_op jit(solution)/shard_map/ppermute | solution.py:351
  72.5 6.7 %collective-permute-start.14 = (bf16[8,176,128]{2,1,0:T(8,128)(2,1)S(1)}, bf16[8,176,128]{2,1,0:T(8,128)(2,1)S(1)}, u32[]{:S(2)}, u32[]{:S(2)}) collective-permute-start(bf16[8,176,128]{2,1,0:T(8,128)(2,1)S(1)} %pad_maximum_fusion.1.b_ref), channel_id=1, source_target_pairs={{0,1},{1,0},{2,3},{3,2},{4,5},{5,4},{6,7},{7,6},{8,9},{9,8},{10,11... | collective-permute-start | bytes 1081352 | tf_op jit(solution)/shard_map/ppermute | solution.py:351
  77.6 1.9 %collective-permute-start.15 = (bf16[8,176,128]{2,1,0:T(8,128)(2,1)S(1)}, bf16[8,176,128]{2,1,0:T(8,128)(2,1)S(1)}, u32[]{:S(2)}, u32[]{:S(2)}) collective-permute-start(bf16[8,176,128]{2,1,0:T(8,128)(2,1)S(1)} %pad_maximum_fusion.2.c_ref), channel_id=1, source_target_pairs={{0,1},{1,0},{2,3},{3,2},{4,5},{5,4},{6,7},{7,6},{8,9},{9,8},{10,11... | collective-permute-start | bytes 1081352 | tf_op jit(solution)/shard_map/ppermute | solution.py:351

commit v19 on v16

--- a/solution.py
+++ b/solution.py
@@ -30,7 +30,7 @@
 
 CHIP_AXES = ("x", "yh")
 ALL_CHIPS = ("z", "yl", "x", "yh")
-ORDERS = (("abd", "bda", "dab"), ("bda", "dab", "abd"))
+ORDERS = (("abd", "bda", "dab"), ("dab", "abd", "bda"))
 
 
 def halves(a, b, first):

time: 130 us -> 136 us (1.046)
  waiting for transfers between devices: 20.2 us -> 23.5 us
  starting transfers between devices: 14 us -> 17 us
    ppermute x12, waiting for transfers between devices: 17.4 us -> 20.7 us  [exchange(): return lax.ppermute(value, ('x', 'yh', 'c'), pairs)]
    ppermute x12, starting transfers between devices: 13.5 us -> 16.1 us  [exchange(): return lax.ppermute(value, ('x', 'yh', 'c'), pairs)]
  transfers between devices with their start and end apart: 16 -> 16, of which waited for: 11 -> 9; matrix products, arithmetic and copies ran while one was open for 1% -> 1% of each run, Pallas kernels for 3% -> 3%
where the time goes in v19:
time: 136 us
  blocking collectives  79 us (58%)
  waiting for transfers between devices  23.5 us (17%)
  starting transfers between devices  17 us (12%)
  Pallas kernels  13.6 us (10%)
  local copies, waits for them, and re-layouts  1.66 us (1%)
    all_to_all x1, blocking collectives, shards(): received = lax.all_to_all(sent, ALL_CHIPS, 0, 0, tiled=True)  41.3 us
    all_to_all x1, blocking collectives, shards(): lax.all_to_all(pieces, CHIP_AXES, 0, 0, tiled=True).reshape(HALF, WIDTH)  37.7 us
    ppermute x12, waiting for transfers between devices, exchange(): return lax.ppermute(value, ('x', 'yh', 'c'), pairs)  20.7 us
    ppermute x12, starting transfers between devices, exchange(): return lax.ppermute(value, ('x', 'yh', 'c'), pairs)  16.1 us
    pallas_call x1, Pallas kernels, update_rows(): pl.pallas_call(update_kernel, out_shape=jax.ShapeDtypeStruct((STRIPES, CH...  7.11 us
    ppermute x4, waiting for transfers between devices, swap_cores(): return lax.ppermute(value, 'c', [(0, 1), (1, 0)])  2.79 us
  transfers between devices with their start and end apart: 16, of which 9 were waited for; matrix products, arithmetic and copies ran while one was open for 1% of the time, Pallas kernels for 3%

profile of v19, /device:TPU:0, one launch (start us, length us, event | category | flops | bytes accessed | tf_op | source)
XLA Modules:
  0.0 135.8 jit_solution(14651726962177752666)
XLA Ops:
  0.0 0.0 copy-start
  0.0 1.7 %copy-done = bf16[1,96,12288]{2,1,0:T(8,128)(2,1)S(1)} copy-done((bf16[1,96,12288]{2,1,0:T(8,128)(2,1)S(1)}, bf16[1,96,12288]{2,1,0:T(8,128)(2,1)}, u32[]{:S(2)}) %copy-start) | copy-done | bytes 2359320
  1.7 0.6 split_columns.1
  2.3 37.7 %all_to_all.10 = bf16[8,96,1536]{2,1,0:T(8,128)(2,1)S(1)} all-to-all(bf16[8,96,1536]{2,1,0:T(8,128)(2,1)S(1)} %split_columns.1), channel_id=1, replica_groups=mesh['z'=4,'yl'=2,'x'=4,'yh'=2,'c'=2] {'x','yh'}, dimensions={0} | all-to-all | bytes 4718592 | tf_op jit(solution)/shard_map/all_to_all | solution.py:356
  40.0 0.0 collective-permute-start.1
  40.0 1.5 %own_gram.1 = (f32[4,240,128]{2,1,0:T(8,128)S(1)}, bf16[4,240,128]{2,1,0:T(8,128)(2,1)S(1)}, f32[6,128,128]{2,1,0:T(8,128)S(1)}) custom-call(bf16[768,1536]{1,0:T(8,128)(2,1)S(1)} %bitcast.13), custom_call_target="tpu_custom_call" | custom-call | flops 1660944384 | bytes 2359296 | tf_op jit(solution)/shard_map/own_gram/pallas_call | solution.py:129
  41.4 0.6 collective-permute-start
  42.0 2.5 %collective-permute-done.1.other_ref.x_other_ref = bf16[768,1536]{1,0:T(8,128)(2,1)S(1)} collective-permute-done((bf16[768,1536]{1,0:T(8,128)(2,1)S(1)}, bf16[768,1536]{1,0:T(8,128)(2,1)S(1)}, u32[]{:S(2)}, u32[]{:S(2)}) %collective-permute-start.1) | collective-permute-done | bytes 2359328 | tf_op jit(solution)/shard_map/ppermute | solution.py:351
  44.5 1.5 %cross_gram.1 = (f32[4,192,128]{2,1,0:T(8,128)S(1)}, bf16[4,192,128]{2,1,0:T(8,128)(2,1)S(1)}, f32[4,160,128]{2,1,0:T(8,128)S(1)}, bf16[4,160,128]{2,1,0:T(8,128)(2,1)S(1)}) custom-call(f32[6,128,128]{2,1,0:T(8,128)S(1)} %get-tuple-element.22.diagonal_ref, bf16[768,1536]{1,0:T(8,128)(2,1)S(1)} %bitcast.14, ...), custom_call_target="tpu_custom_call" | custom-call | flops 1660944384 | bytes 4718592 | tf_op jit(solution)/shard_map/cross_gram/pallas_call | solution.py:162
  46.0 1.5 %collective-permute-start.3 = (bf16[4,192,128]{2,1,0:T(8,128)(2,1)S(1)}, bf16[4,192,128]{2,1,0:T(8,128)(2,1)S(1)}, u32[]{:S(2)}, u32[]{:S(2)}) collective-permute-start(bf16[4,192,128]{2,1,0:T(8,128)(2,1)S(1)} %get-tuple-element.23), channel_id=1, source_target_pairs={{0,12},{1,5},{2,14},{3,7},{4,8},{5,1},{6,10},{7,3},{8,4},{9,13},{1... | collective-permute-start | bytes 589832 | tf_op jit(solution)/shard_map/ppermute | solution.py:182
  47.5 0.2 collective-permute-done
  47.7 0.1 add_convert_fusion.2
  47.8 1.7 %collective-permute-start.2 = (bf16[2,2,240,128]{3,2,1,0:T(8,128)(2,1)S(1)}, bf16[2,2,240,128]{3,2,1,0:T(8,128)(2,1)S(1)}, u32[]{:S(2)}, u32[]{:S(2)}) collective-permute-start(bf16[2,2,240,128]{3,2,1,0:T(8,128)(2,1)S(1)} %bitcast.19), channel_id=1, source_target_pairs={{0,12},{1,5},{2,14},{3,7},{4,8},{5,1},{6,10},{7,3},{8,4},{9,13},{1... | collective-permute-start | bytes 737288 | tf_op jit(solution)/shard_map/ppermute | solution.py:182
  49.5 1.6 %collective-permute-start.8 = (bf16[4,160,128]{2,1,0:T(8,128)(2,1)S(1)}, bf16[4,160,128]{2,1,0:T(8,128)(2,1)S(1)}, u32[]{:S(2)}, u32[]{:S(2)}) collective-permute-start(bf16[4,160,128]{2,1,0:T(8,128)(2,1)S(1)} %get-tuple-element.24), channel_id=1, source_target_pairs={{0,2},{1,13},{2,0},{3,15},{4,6},{5,9},{6,4},{7,11},{8,10},{9,5},{1... | collective-permute-start | bytes 491528 | tf_op jit(solution)/shard_map/ppermute | solution.py:182
  51.0 2.1 %collective-permute-done.3 = bf16[4,192,128]{2,1,0:T(8,128)(2,1)S(1)} collective-permute-done((bf16[4,192,128]{2,1,0:T(8,128)(2,1)S(1)}, bf16[4,192,128]{2,1,0:T(8,128)(2,1)S(1)}, u32[]{:S(2)}, u32[]{:S(2)}) %collective-permute-start.3) | collective-permute-done | bytes 196640 | tf_op jit(solution)/shard_map/ppermute | solution.py:182
  53.2 1.6 %collective-permute-start.5 = (bf16[2,2,192,128]{3,2,1,0:T(8,128)(2,1)S(1)}, bf16[2,2,192,128]{3,2,1,0:T(8,128)(2,1)S(1)}, u32[]{:S(2)}, u32[]{:S(2)}) collective-permute-start(bf16[2,2,192,128]{3,2,1,0:T(8,128)(2,1)S(1)} %bitcast.21), channel_id=1, source_target_pairs={{0,2},{1,13},{2,0},{3,15},{4,6},{5,9},{6,4},{7,11},{8,10},{9,5},{1... | collective-permute-start | bytes 589832 | tf_op jit(solution)/shard_map/ppermute | solution.py:182
  54.8 3.6 %collective-permute-done.2 = bf16[2,2,240,128]{3,2,1,0:T(8,128)(2,1)S(1)} collective-permute-done((bf16[2,2,240,128]{3,2,1,0:T(8,128)(2,1)S(1)}, bf16[2,2,240,128]{3,2,1,0:T(8,128)(2,1)S(1)}, u32[]{:S(2)}, u32[]{:S(2)}) %collective-permute-start.2) | collective-permute-done | bytes 245792 | tf_op jit(solution)/shard_map/ppermute | solution.py:182
  58.5 0.1 add_convert_fusion.1
  58.5 1.6 %collective-permute-start.4 = (bf16[2,2,240,128]{3,2,1,0:T(8,128)(2,1)S(1)}, bf16[2,2,240,128]{3,2,1,0:T(8,128)(2,1)S(1)}, u32[]{:S(2)}, u32[]{:S(2)}) collective-permute-start(bf16[2,2,240,128]{3,2,1,0:T(8,128)(2,1)S(1)} %add_convert_fusion.1), channel_id=1, source_target_pairs={{0,2},{1,13},{2,0},{3,15},{4,6},{5,9},{6,4},{7,11},{8,10},{9,5},{1... | collective-permute-start | bytes 737288 | tf_op jit(solution)/shard_map/ppermute | solution.py:182
  60.1 0.0 collective-permute-done.8
  60.2 0.1 collective-permute-start.9
  60.2 0.2 collective-permute-done.5
  60.5 0.1 add_convert_fusion.4
  60.6 1.9 %collective-permute-start.7 = (bf16[2,2,192,128]{3,2,1,0:T(8,128)(2,1)S(1)}, bf16[2,2,192,128]{3,2,1,0:T(8,128)(2,1)S(1)}, u32[]{:S(2)}, u32[]{:S(2)}) collective-permute-start(bf16[2,2,192,128]{3,2,1,0:T(8,128)(2,1)S(1)} %add_convert_fusion.4), channel_id=1, source_target_pairs={{0,4},{1,3},{2,6},{3,1},{4,0},{5,7},{6,2},{7,5},{8,12},{9,11},{10,... | collective-permute-start | bytes 589832 | tf_op jit(solution)/shard_map/ppermute | solution.py:182
  62.4 6.3 %collective-permute-done.4 = bf16[2,2,240,128]{3,2,1,0:T(8,128)(2,1)S(1)} collective-permute-done((bf16[2,2,240,128]{3,2,1,0:T(8,128)(2,1)S(1)}, bf16[2,2,240,128]{3,2,1,0:T(8,128)(2,1)S(1)}, u32[]{:S(2)}, u32[]{:S(2)}) %collective-permute-start.4) | collective-permute-done | bytes 245792 | tf_op jit(solution)/shard_map/ppermute | solution.py:182
  68.8 0.1 add_convert_fusion
  68.8 0.1 collective-permute-start.6
  68.9 0.0 collective-permute-done.9
  69.0 0.6 collective-permute-start.10
  69.6 0.0 collective-permute-done.7
  69.7 2.8 %collective-permute-start.11 = (bf16[4,192,128]{2,1,0:T(8,128)(2,1)S(1)}, bf16[4,192,128]{2,1,0:T(8,128)(2,1)S(1)}, u32[]{:S(2)}, u32[]{:S(2)}) collective-permute-start(bf16[4,192,128]{2,1,0:T(8,128)(2,1)S(1)} %bitcast.23), channel_id=1, source_target_pairs={{0,12},{1,5},{2,14},{3,7},{4,8},{5,1},{6,10},{7,3},{8,4},{9,13},{1... | collective-permute-start | bytes 589832 | tf_op jit(solution)/shard_map/ppermute | solution.py:182
  72.5 4.2 %collective-permute-done.10 = bf16[2,2,160,128]{3,2,1,0:T(8,128)(2,1)S(1)} collective-permute-done((bf16[2,2,160,128]{3,2,1,0:T(8,128)(2,1)S(1)}, bf16[2,2,160,128]{3,2,1,0:T(8,128)(2,1)S(1)}, u32[]{:S(2)}, u32[]{:S(2)}) %collective-permute-start.10) | collective-permute-done | bytes 163872 | tf_op jit(solution)/shard_map/ppermute | solution.py:182
  76.8 2.2 %collective-permute-start.12 = (bf16[4,160,128]{2,1,0:T(8,128)(2,1)S(1)}, bf16[4,160,128]{2,1,0:T(8,128)(2,1)S(1)}, u32[]{:S(2)}, u32[]{:S(2)}) collective-permute-start(bf16[4,160,128]{2,1,0:T(8,128)(2,1)S(1)} %bitcast.27), channel_id=1, source_target_pairs={{0,2},{1,13},{2,0},{3,15},{4,6},{5,9},{6,4},{7,11},{8,10},{9,5},{1... | collective-permute-start | bytes 491528 | tf_op jit(solution)/shard_map/ppermute | solution.py:182
  78.9 0.0 collective-permute-done.6
  79.0 0.1 collective-permute-start.13
  79.1 0.0 collective-permute-done.11
  79.1 0.6 collective-permute-start.14
  79.7 4.0 %collective-permute-done.12 = bf16[4,160,128]{2,1,0:T(8,128)(2,1)S(1)} collective-permute-done((bf16[4,160,128]{2,1,0:T(8,128)(2,1)S(1)}, bf16[4,160,128]{2,1,0:T(8,128)(2,1)S(1)}, u32[]{:S(2)}, u32[]{:S(2)}) %collective-permute-start.12) | collective-permute-done | bytes 163872 | tf_op jit(solution)/shard_map/ppermute | solution.py:182
  83.7 0.3 collective-permute-start.15
  84.0 1.3 own_square.1
  85.3 0.3 collective-permute-done.15.c_ref
  85.6 0.0 collective-permute-done.14.b_ref
  85.6 0.0 collective-permute-done.13.a_ref
  85.6 7.1 %update_rows.1 = bf16[8,8,144,128]{3,2,1,0:T(8,128)(2,1)S(1)} custom-call(bf16[4736,128]{1,0:T(8,128)(2,1)S(1)} %get-tuple-element.32.own_ref, bf16[8,240,128]{2,1,0:T(8,128)(2,1)S(1)} %collective-permute-done.13.a_ref, bf16[8,192,128]{2,1,0:T(8,128)(2,1)S(1)} %collective-permute-done.14.b_ref, bf16[8,160,128]{2,1,0:T(8,128)(2,1)S(1)} %collective-permute-done.15.c_ref, ...), custom_call_target="tpu_custom_call" | custom-call | flops 6341787648 | bytes 11796480 | tf_op jit(solution)/shard_map/update_rows/pallas_call | solution.py:303
  92.7 41.3 %all_to_all.11 = bf16[64,144,128]{2,1,0:T(8,128)(2,1)S(1)} all-to-all(bf16[64,144,128]{2,1,0:T(8,128)(2,1)S(1)} %bitcast.16), channel_id=1, replica_groups=mesh['z'=4,'yl'=2,'x'=4,'yh'=2,'c'=2] {'z','yl','x','yh'}, dimensions={0} | all-to-all | bytes 4718592 | tf_op jit(solution)/shard_map/all_to_all | solution.py:381
  134.1 1.6 %join_columns.1 = bf16[8,96,1536]{2,1,0:T(8,128)(2,1)} custom-call(bf16[8,8,144,128]{3,2,1,0:T(8,128)(2,1)S(1)} %bitcast.10), custom_call_target="tpu_custom_call" | custom-call | tf_op jit(solution)/shard_map/join_columns/pallas_call | solution.py:339
  (14 shorter events, 0.5 us)
Async XLA Ops:
  0.0 1.7 %copy-start = (bf16[1,96,12288]{2,1,0:T(8,128)(2,1)S(1)}, bf16[1,96,12288]{2,1,0:T(8,128)(2,1)}, u32[]{:S(2)}) copy-start(bf16[1,96,12288]{2,1,0:T(8,128)(2,1)} %param.1) | copy-start | bytes 7077892
  40.0 4.5 %collective-permute-start.1 = (bf16[768,1536]{1,0:T(8,128)(2,1)S(1)}, bf16[768,1536]{1,0:T(8,128)(2,1)S(1)}, u32[]{:S(2)}, u32[]{:S(2)}) collective-permute-start(bf16[768,1536]{1,0:T(8,128)(2,1)S(1)} %bitcast.12), channel_id=1, source_target_pairs={{0,1},{1,0},{2,3},{3,2},{4,5},{5,4},{6,7},{7,6},{8,9},{9,8},{10,11... | collective-permute-start | bytes 7077896 | tf_op jit(solution)/shard_map/ppermute | solution.py:351
  41.4 6.3 %collective-permute-start = (bf16[4,240,128]{2,1,0:T(8,128)(2,1)S(1)}, bf16[4,240,128]{2,1,0:T(8,128)(2,1)S(1)}, u32[]{:S(2)}, u32[]{:S(2)}) collective-permute-start(bf16[4,240,128]{2,1,0:T(8,128)(2,1)S(1)} %get-tuple-element.21), channel_id=1, source_target_pairs={{0,4},{1,3},{2,6},{3,1},{4,0},{5,7},{6,2},{7,5},{8,12},{9,11},{10,... | collective-permute-start | bytes 737288 | tf_op jit(solution)/shard_map/ppermute | solution.py:182
  46.0 7.1 %collective-permute-start.3 = (bf16[4,192,128]{2,1,0:T(8,128)(2,1)S(1)}, bf16[4,192,128]{2,1,0:T(8,128)(2,1)S(1)}, u32[]{:S(2)}, u32[]{:S(2)}) collective-permute-start(bf16[4,192,128]{2,1,0:T(8,128)(2,1)S(1)} %get-tuple-element.23), channel_id=1, source_target_pairs={{0,12},{1,5},{2,14},{3,7},{4,8},{5,1},{6,10},{7,3},{8,4},{9,13},{1... | collective-permute-start | bytes 589832 | tf_op jit(solution)/shard_map/ppermute | solution.py:182
  47.8 10.6 %collective-permute-start.2 = (bf16[2,2,240,128]{3,2,1,0:T(8,128)(2,1)S(1)}, bf16[2,2,240,128]{3,2,1,0:T(8,128)(2,1)S(1)}, u32[]{:S(2)}, u32[]{:S(2)}) collective-permute-start(bf16[2,2,240,128]{3,2,1,0:T(8,128)(2,1)S(1)} %bitcast.19), channel_id=1, source_target_pairs={{0,12},{1,5},{2,14},{3,7},{4,8},{5,1},{6,10},{7,3},{8,4},{9,13},{1... | collective-permute-start | bytes 737288 | tf_op jit(solution)/shard_map/ppermute | solution.py:182
  49.5 10.6 %collective-permute-start.8 = (bf16[4,160,128]{2,1,0:T(8,128)(2,1)S(1)}, bf16[4,160,128]{2,1,0:T(8,128)(2,1)S(1)}, u32[]{:S(2)}, u32[]{:S(2)}) collective-permute-start(bf16[4,160,128]{2,1,0:T(8,128)(2,1)S(1)} %get-tuple-element.24), channel_id=1, source_target_pairs={{0,2},{1,13},{2,0},{3,15},{4,6},{5,9},{6,4},{7,11},{8,10},{9,5},{1... | collective-permute-start | bytes 491528 | tf_op jit(solution)/shard_map/ppermute | solution.py:182
  53.2 7.3 %collective-permute-start.5 = (bf16[2,2,192,128]{3,2,1,0:T(8,128)(2,1)S(1)}, bf16[2,2,192,128]{3,2,1,0:T(8,128)(2,1)S(1)}, u32[]{:S(2)}, u32[]{:S(2)}) collective-permute-start(bf16[2,2,192,128]{3,2,1,0:T(8,128)(2,1)S(1)} %bitcast.21), channel_id=1, source_target_pairs={{0,2},{1,13},{2,0},{3,15},{4,6},{5,9},{6,4},{7,11},{8,10},{9,5},{1... | collective-permute-start | bytes 589832 | tf_op jit(solution)/shard_map/ppermute | solution.py:182
  58.5 10.2 %collective-permute-start.4 = (bf16[2,2,240,128]{3,2,1,0:T(8,128)(2,1)S(1)}, bf16[2,2,240,128]{3,2,1,0:T(8,128)(2,1)S(1)}, u32[]{:S(2)}, u32[]{:S(2)}) collective-permute-start(bf16[2,2,240,128]{3,2,1,0:T(8,128)(2,1)S(1)} %add_convert_fusion.1), channel_id=1, source_target_pairs={{0,2},{1,13},{2,0},{3,15},{4,6},{5,9},{6,4},{7,11},{8,10},{9,5},{1... | collective-permute-start | bytes 737288 | tf_op jit(solution)/shard_map/ppermute | solution.py:182
  60.2 8.8 %collective-permute-start.9 = (bf16[2,2,160,128]{3,2,1,0:T(8,128)(2,1)S(1)}, bf16[2,2,160,128]{3,2,1,0:T(8,128)(2,1)S(1)}, u32[]{:S(2)}, u32[]{:S(2)}) collective-permute-start(bf16[2,2,160,128]{3,2,1,0:T(8,128)(2,1)S(1)} %bitcast.25), channel_id=1, source_target_pairs={{0,4},{1,3},{2,6},{3,1},{4,0},{5,7},{6,2},{7,5},{8,12},{9,11},{10,... | collective-permute-start | bytes 491528 | tf_op jit(solution)/shard_map/ppermute | solution.py:182
  60.6 9.1 %collective-permute-start.7 = (bf16[2,2,192,128]{3,2,1,0:T(8,128)(2,1)S(1)}, bf16[2,2,192,128]{3,2,1,0:T(8,128)(2,1)S(1)}, u32[]{:S(2)}, u32[]{:S(2)}) collective-permute-start(bf16[2,2,192,128]{3,2,1,0:T(8,128)(2,1)S(1)} %add_convert_fusion.4), channel_id=1, source_target_pairs={{0,4},{1,3},{2,6},{3,1},{4,0},{5,7},{6,2},{7,5},{8,12},{9,11},{10,... | collective-permute-start | bytes 589832 | tf_op jit(solution)/shard_map/ppermute | solution.py:182
  68.8 10.1 %collective-permute-start.6 = (bf16[4,240,128]{2,1,0:T(8,128)(2,1)S(1)}, bf16[4,240,128]{2,1,0:T(8,128)(2,1)S(1)}, u32[]{:S(2)}, u32[]{:S(2)}) collective-permute-start(bf16[4,240,128]{2,1,0:T(8,128)(2,1)S(1)} %bitcast.17), channel_id=1, source_target_pairs={{0,4},{1,3},{2,6},{3,1},{4,0},{5,7},{6,2},{7,5},{8,12},{9,11},{10,... | collective-permute-start | bytes 737288 | tf_op jit(solution)/shard_map/ppermute | solution.py:182
  69.0 7.7 %collective-permute-start.10 = (bf16[2,2,160,128]{3,2,1,0:T(8,128)(2,1)S(1)}, bf16[2,2,160,128]{3,2,1,0:T(8,128)(2,1)S(1)}, u32[]{:S(2)}, u32[]{:S(2)}) collective-permute-start(bf16[2,2,160,128]{3,2,1,0:T(8,128)(2,1)S(1)} %add_convert_fusion.7), channel_id=1, source_target_pairs={{0,12},{1,5},{2,14},{3,7},{4,8},{5,1},{6,10},{7,3},{8,4},{9,13},{1... | collective-permute-start | bytes 491528 | tf_op jit(solution)/shard_map/ppermute | solution.py:182
  69.7 9.4 %collective-permute-start.11 = (bf16[4,192,128]{2,1,0:T(8,128)(2,1)S(1)}, bf16[4,192,128]{2,1,0:T(8,128)(2,1)S(1)}, u32[]{:S(2)}, u32[]{:S(2)}) collective-permute-start(bf16[4,192,128]{2,1,0:T(8,128)(2,1)S(1)} %bitcast.23), channel_id=1, source_target_pairs={{0,12},{1,5},{2,14},{3,7},{4,8},{5,1},{6,10},{7,3},{8,4},{9,13},{1... | collective-permute-start | bytes 589832 | tf_op jit(solution)/shard_map/ppermute | solution.py:182
  76.8 6.9 %collective-permute-start.12 = (bf16[4,160,128]{2,1,0:T(8,128)(2,1)S(1)}, bf16[4,160,128]{2,1,0:T(8,128)(2,1)S(1)}, u32[]{:S(2)}, u32[]{:S(2)}) collective-permute-start(bf16[4,160,128]{2,1,0:T(8,128)(2,1)S(1)} %bitcast.27), channel_id=1, source_target_pairs={{0,2},{1,13},{2,0},{3,15},{4,6},{5,9},{6,4},{7,11},{8,10},{9,5},{1... | collective-permute-start | bytes 491528 | tf_op jit(solution)/shard_map/ppermute | solution.py:182
  79.0 6.6 %collective-permute-start.13 = (bf16[8,240,128]{2,1,0:T(8,128)(2,1)S(1)}, bf16[8,240,128]{2,1,0:T(8,128)(2,1)S(1)}, u32[]{:S(2)}, u32[]{:S(2)}) collective-permute-start(bf16[8,240,128]{2,1,0:T(8,128)(2,1)S(1)} %pad_maximum_fusion.a_ref), channel_id=1, source_target_pairs={{0,1},{1,0},{2,3},{3,2},{4,5},{5,4},{6,7},{7,6},{8,9},{9,8},{10,11... | collective-permute-start | bytes 1474568 | tf_op jit(solution)/shard_map/ppermute | solution.py:351
  79.1 6.5 %collective-permute-start.14 = (bf16[8,192,128]{2,1,0:T(8,128)(2,1)S(1)}, bf16[8,192,128]{2,1,0:T(8,128)(2,1)S(1)}, u32[]{:S(2)}, u32[]{:S(2)}) collective-permute-start(bf16[8,192,128]{2,1,0:T(8,128)(2,1)S(1)} %pad_maximum_fusion.1.b_ref), channel_id=1, source_target_pairs={{0,1},{1,0},{2,3},{3,2},{4,5},{5,4},{6,7},{7,6},{8,9},{9,8},{10,11... | collective-permute-start | bytes 1179656 | tf_op jit(solution)/shard_map/ppermute | solution.py:351
  83.7 1.9 %collective-permute-start.15 = (bf16[8,160,128]{2,1,0:T(8,128)(2,1)S(1)}, bf16[8,160,128]{2,1,0:T(8,128)(2,1)S(1)}, u32[]{:S(2)}, u32[]{:S(2)}) collective-permute-start(bf16[8,160,128]{2,1,0:T(8,128)(2,1)S(1)} %pad_maximum_fusion.2.c_ref), channel_id=1, source_target_pairs={{0,1},{1,0},{2,3},{3,2},{4,5},{5,4},{6,7},{7,6},{8,9},{9,8},{10,11... | collective-permute-start | bytes 983048 | tf_op jit(solution)/shard_map/ppermute | solution.py:351
